TPU v7x, 32 devices: a whole 2x2x4 slice. The times are simulated.
32 devices in a mesh: grp: 4 (over x, core), seq: 8 (over z, y).
Axes of the slice: x: 2, y: 2, z: 4, core: 2. Of those that a mesh axis runs over, the one named last changes fastest.
Arguments:
- inputs: bfloat16 [4, 1024, 768], P('grp', 'seq'), may hold values from -6 to 6
- segment_ids: int32 [4, 1024], P('grp'), may hold values from 0 to 2, never falling along the last dimension, each value on 1 to 512 neighbouring positions
- padding: int32 [4, 1024], P('grp', 'seq'), may hold values 0 or 1
- cotangent: bfloat16 [4, 1024, 768], P('grp', 'seq'), may hold values from -6 to 6
- w_query: bfloat16 [768, 768], P(('grp', 'seq')), may hold values from -0.21875 to 0.21875
- b_query: bfloat16 [768], P(('grp', 'seq')), may hold values from -3 to 3
- w_key: bfloat16 [768, 768], P(('grp', 'seq')), may hold values from -0.21875 to 0.21875
- w_value: bfloat16 [768, 768], P(('grp', 'seq')), may hold values from -0.21875 to 0.21875
- b_value: bfloat16 [768], P(('grp', 'seq')), may hold values from -3 to 3
- w_out: bfloat16 [768, 768], P(('grp', 'seq')), may hold values from -3.5 to 3.5
- b_out: bfloat16 [768], P(('grp', 'seq')), may hold values from -2 to 2
- ln1_gain: bfloat16 [768], P(('grp', 'seq')), may hold values from 0.099609375 to 1.8984375
- ln1_shift: bfloat16 [768], P(('grp', 'seq')), may hold values from -2 to 2
- ln2_gain: bfloat16 [768], P(('grp', 'seq')), may hold values from 0.099609375 to 1.8984375
- ln2_shift: bfloat16 [768], P(('grp', 'seq')), may hold values from -2 to 2
- w_up: bfloat16 [768, 3072], P(('grp', 'seq')), may hold values from -0.21875 to 0.21875
- b_up: bfloat16 [3072], P(('grp', 'seq')), may hold values from -3 to 3
- w_down: bfloat16 [3072, 768], P(('grp', 'seq')), may hold values from -0.109375 to 0.109375
- b_down: bfloat16 [768], P(('grp', 'seq')), may hold values from -2 to 2
Outputs:
- output: bfloat16 [4, 1024, 768], P('grp', 'seq')
- grad_input: bfloat16 [4, 1024, 768], P('grp', 'seq')
- grad_w_query: float32 [768, 768], P(('grp', 'seq'))
- grad_b_query: float32 [768], P(('grp', 'seq'))
- grad_w_key: float32 [768, 768], P(('grp', 'seq'))
- grad_w_value: float32 [768, 768], P(('grp', 'seq'))
- grad_b_value: float32 [768], P(('grp', 'seq'))
- grad_w_out: float32 [768, 768], P(('grp', 'seq'))
- grad_b_out: float32 [768], P(('grp', 'seq'))
- grad_ln1_gain: float32 [768], P(('grp', 'seq'))
- grad_ln1_shift: float32 [768], P(('grp', 'seq'))
- grad_ln2_gain: float32 [768], P(('grp', 'seq'))
- grad_ln2_shift: float32 [768], P(('grp', 'seq'))
- grad_w_up: float32 [768, 3072], P(('grp', 'seq'))
- grad_b_up: float32 [3072], P(('grp', 'seq'))
- grad_w_down: float32 [3072, 768], P(('grp', 'seq'))
- grad_b_down: float32 [768], P(('grp', 'seq'))
Inputs may be any that keep to these rules, and one draw needn't show every extreme that they name: `segment_ids`: per sequence the numbers never fall along the positions; a document spans at most 512 positions.
All inputs are finite; a program needn't handle non-finite values. No bound on the sum of `padding` on one device may be relied on, other than what follows from the above.
Results may differ from a plain program's by a relative error of at most 0.014.
Values may be sent and summed in bfloat16 or wider, within the bound.
No kernel may reach another device: no remote copies, remote signals or barrier semaphores. Data moves between devices by JAX's collectives and lax.ppermute only.
A program may use at most 192 MiB of HBM per device.

v0:
```python
import jax
import jax.numpy as jnp
from jax import lax
from jax.sharding import PartitionSpec as P

HEADS = 12
HEAD_DIM = 64


scaling = 0.125


def product(left, right):
    return jnp.dot(left, right, preferred_element_type=jnp.float32)


def contract_rows(left, right):
    return lax.dot_general(
        left, right, (((0,), (0,)), ((), ())), preferred_element_type=jnp.float32
    )


def contract_cols(left, right):
    return lax.dot_general(
        left, right, (((1,), (1,)), ((), ())), preferred_element_type=jnp.float32
    )


def normalize(values, gain, shift):
    center = values - jnp.mean(values, axis=-1, keepdims=True)
    variance = jnp.mean(center * center, axis=-1, keepdims=True)
    return center * lax.rsqrt(variance + 1e-05) * gain + shift


def exact_gelu(values):
    return jax.nn.gelu(values, approximate=False)


def masked_scores(query_part, key_part, same_doc):
    raw_scores = (
        jnp.einsum("qhe,khe->hqk", query_part, key_part, preferred_element_type=jnp.float32)
        * scaling
    )
    return jnp.where(same_doc[None], raw_scores, -1e30)


def local(
    inputs,
    segment_ids,
    padding,
    cotangent,
    w_query,
    b_query,
    w_key,
    w_value,
    b_value,
    w_out,
    b_out,
    ln1_gain,
    ln1_shift,
    ln2_gain,
    ln2_shift,
    w_up,
    b_up,
    w_down,
    b_down,
):
    weights = (
        lax.all_gather(w_query, ("grp", "seq"), axis=0, tiled=True),
        lax.all_gather(b_query, ("grp", "seq"), axis=0, tiled=True),
        lax.all_gather(w_key, ("grp", "seq"), axis=0, tiled=True),
        lax.all_gather(w_value, ("grp", "seq"), axis=0, tiled=True),
        lax.all_gather(b_value, ("grp", "seq"), axis=0, tiled=True),
        lax.all_gather(w_out, ("grp", "seq"), axis=0, tiled=True),
        lax.all_gather(b_out, ("grp", "seq"), axis=0, tiled=True),
        lax.all_gather(ln1_gain, ("grp", "seq"), axis=0, tiled=True),
        lax.all_gather(ln1_shift, ("grp", "seq"), axis=0, tiled=True),
        lax.all_gather(ln2_gain, ("grp", "seq"), axis=0, tiled=True),
        lax.all_gather(ln2_shift, ("grp", "seq"), axis=0, tiled=True),
        lax.all_gather(w_up, ("grp", "seq"), axis=0, tiled=True),
        lax.all_gather(b_up, ("grp", "seq"), axis=0, tiled=True),
        lax.all_gather(w_down, ("grp", "seq"), axis=0, tiled=True),
        lax.all_gather(b_down, ("grp", "seq"), axis=0, tiled=True),
    )
    local_rows = inputs.shape[1]
    seq_index = lax.axis_index("seq")
    doc_all = segment_ids[0]
    doc_local = lax.dynamic_slice_in_dim(doc_all, seq_index * local_rows, local_rows)
    same_doc = doc_local[:, None] == doc_all[None, :]
    pair_width = 2 * HEAD_DIM
    pairs = HEADS // 2
    x_local = inputs[0].astype(jnp.float32)
    normed_one, pull_one = jax.vjp(
        normalize, x_local, weights[7].astype(jnp.float32), weights[8].astype(jnp.float32)
    )
    normed_low = normed_one.astype(jnp.bfloat16)
    queries = (product(normed_low, weights[0]) + weights[1].astype(jnp.float32)).astype(
        jnp.bfloat16
    )
    keys_local = product(normed_low, weights[2]).astype(jnp.bfloat16)
    values_local = (product(normed_low, weights[3]) + weights[4].astype(jnp.float32)).astype(
        jnp.bfloat16
    )
    keys_all, values_all = (
        lax.all_gather(keys_local, "seq", axis=0, tiled=True),
        lax.all_gather(values_local, "seq", axis=0, tiled=True),
    )
    key_count = keys_all.shape[0]
    mixed_parts = []
    lse_parts = []
    for head_pair in range(pairs):
        first_col = head_pair * pair_width
        query_part = queries[:, first_col : first_col + pair_width].reshape(local_rows, 2, HEAD_DIM)
        key_part = keys_all[:, first_col : first_col + pair_width].reshape(key_count, 2, HEAD_DIM)
        value_part = values_all[:, first_col : first_col + pair_width].reshape(
            key_count, 2, HEAD_DIM
        )
        scores = masked_scores(query_part, key_part, same_doc)
        row_peak = jnp.max(scores, axis=-1, keepdims=True)
        exponent = jnp.exp(scores - row_peak)
        row_total = jnp.sum(exponent, axis=-1, keepdims=True)
        attn_probs = (exponent / row_total).astype(jnp.bfloat16)
        mixed_parts.append(
            jnp.einsum(
                "hqk,khe->qhe", attn_probs, value_part, preferred_element_type=jnp.float32
            ).reshape(local_rows, pair_width)
        )
        lse_parts.append(row_peak + jnp.log(row_total))
    mixed = jnp.concatenate(mixed_parts, axis=1).astype(jnp.bfloat16)
    attended = product(mixed, weights[5]) + weights[6].astype(jnp.float32)
    residual = x_local + attended
    normed_two, pull_two = jax.vjp(
        normalize, residual, weights[9].astype(jnp.float32), weights[10].astype(jnp.float32)
    )
    normed_mlp = normed_two.astype(jnp.bfloat16)
    pre_act = product(normed_mlp, weights[11]) + weights[12].astype(jnp.float32)
    activated, pull_gelu = jax.vjp(exact_gelu, pre_act)
    act_low = activated.astype(jnp.bfloat16)
    output = residual + product(act_low, weights[13]) + weights[14].astype(jnp.float32)
    backing = (
        lax.all_gather(w_query, ("grp", "seq"), axis=0, tiled=True),
        lax.all_gather(b_query, ("grp", "seq"), axis=0, tiled=True),
        lax.all_gather(w_key, ("grp", "seq"), axis=0, tiled=True),
        lax.all_gather(w_value, ("grp", "seq"), axis=0, tiled=True),
        lax.all_gather(b_value, ("grp", "seq"), axis=0, tiled=True),
        lax.all_gather(w_out, ("grp", "seq"), axis=0, tiled=True),
        lax.all_gather(b_out, ("grp", "seq"), axis=0, tiled=True),
        lax.all_gather(ln1_gain, ("grp", "seq"), axis=0, tiled=True),
        lax.all_gather(ln1_shift, ("grp", "seq"), axis=0, tiled=True),
        lax.all_gather(ln2_gain, ("grp", "seq"), axis=0, tiled=True),
        lax.all_gather(ln2_shift, ("grp", "seq"), axis=0, tiled=True),
        lax.all_gather(w_up, ("grp", "seq"), axis=0, tiled=True),
        lax.all_gather(b_up, ("grp", "seq"), axis=0, tiled=True),
        lax.all_gather(w_down, ("grp", "seq"), axis=0, tiled=True),
        lax.all_gather(b_down, ("grp", "seq"), axis=0, tiled=True),
    )
    keys_back, values_back = (
        lax.all_gather(keys_local, "seq", axis=0, tiled=True),
        lax.all_gather(values_local, "seq", axis=0, tiled=True),
    )
    grad_out = cotangent[0].astype(jnp.float32) * padding[0].astype(jnp.float32)[:, None]
    grad_branch = grad_out.astype(jnp.bfloat16)
    grad_w_down = contract_rows(act_low, grad_branch)
    grad_b_down = jnp.sum(grad_out, axis=0)
    grad_act = contract_cols(grad_branch, backing[13])
    grad_pre = pull_gelu(grad_act)[0].astype(jnp.bfloat16)
    grad_w_up = contract_rows(normed_mlp, grad_pre)
    grad_b_up = jnp.sum(grad_pre.astype(jnp.float32), axis=0)
    grad_normed_two = contract_cols(grad_pre, backing[11])
    grad_resid_norm, grad_gain_two, grad_shift_two = pull_two(grad_normed_two)
    grad_resid = grad_out + grad_resid_norm
    grad_attended = grad_resid.astype(jnp.bfloat16)
    grad_w_out = contract_rows(mixed, grad_attended)
    grad_b_out = jnp.sum(grad_attended.astype(jnp.float32), axis=0)
    grad_mixed = contract_cols(grad_attended, backing[5]).astype(jnp.bfloat16)
    query_grads = []
    key_terms = []
    value_terms = []
    delta_parts = []
    for head_pair in range(pairs):
        first_col = head_pair * pair_width
        query_part = queries[:, first_col : first_col + pair_width].reshape(local_rows, 2, HEAD_DIM)
        key_part = keys_back[:, first_col : first_col + pair_width].reshape(key_count, 2, HEAD_DIM)
        value_part = values_back[:, first_col : first_col + pair_width].reshape(
            key_count, 2, HEAD_DIM
        )
        grad_part = grad_mixed[:, first_col : first_col + pair_width].reshape(
            local_rows, 2, HEAD_DIM
        )
        scores = masked_scores(query_part, key_part, same_doc)
        attn_probs = jnp.exp(scores - lse_parts[head_pair])
        grad_probs = jnp.einsum(
            "qhe,khe->hqk", grad_part, value_part, preferred_element_type=jnp.float32
        )
        row_delta = jnp.sum(attn_probs * grad_probs, axis=-1, keepdims=True)
        delta_parts.append(row_delta)
        grad_scores = (attn_probs * (grad_probs - row_delta)).astype(jnp.bfloat16)
        query_grads.append(
            (
                jnp.einsum(
                    "hqk,khe->qhe", grad_scores, key_part, preferred_element_type=jnp.float32
                )
                * scaling
            ).reshape(local_rows, pair_width)
        )
        key_terms.append(
            (
                jnp.einsum(
                    "hqk,qhe->khe", grad_scores, query_part, preferred_element_type=jnp.float32
                )
                * scaling
            ).reshape(key_count, pair_width)
        )
        value_terms.append(
            jnp.einsum(
                "hqk,qhe->khe",
                attn_probs.astype(jnp.bfloat16),
                grad_part,
                preferred_element_type=jnp.float32,
            ).reshape(key_count, pair_width)
        )
    grad_query = jnp.concatenate(query_grads, axis=1).astype(jnp.bfloat16)
    key_sums, value_sums = (
        lax.psum_scatter(
            jnp.concatenate(key_terms, axis=1).astype(jnp.bfloat16),
            "seq",
            scatter_dimension=0,
            tiled=True,
        ).astype(jnp.float32),
        lax.psum_scatter(
            jnp.concatenate(value_terms, axis=1).astype(jnp.bfloat16),
            "seq",
            scatter_dimension=0,
            tiled=True,
        ).astype(jnp.float32),
    )
    grad_keys = key_sums.astype(jnp.bfloat16)
    grad_values = value_sums.astype(jnp.bfloat16)
    grad_w_query = contract_rows(normed_low, grad_query)
    grad_b_query = jnp.sum(grad_query.astype(jnp.float32), axis=0)
    grad_w_key = contract_rows(normed_low, grad_keys)
    grad_w_value = contract_rows(normed_low, grad_values)
    grad_b_value = jnp.sum(grad_values.astype(jnp.float32), axis=0)
    grad_normed_one = (
        contract_cols(grad_query, backing[0])
        + contract_cols(grad_keys, backing[2])
        + contract_cols(grad_values, backing[3])
    )
    grad_x_norm, grad_gain_one, grad_shift_one = pull_one(grad_normed_one)
    grad_input = (grad_resid + grad_x_norm).astype(jnp.bfloat16)
    summed = (
        lax.psum_scatter(grad_w_query, ("grp", "seq"), scatter_dimension=0, tiled=True),
        lax.psum_scatter(grad_b_query, ("grp", "seq"), scatter_dimension=0, tiled=True),
        lax.psum_scatter(grad_w_key, ("grp", "seq"), scatter_dimension=0, tiled=True),
        lax.psum_scatter(grad_w_value, ("grp", "seq"), scatter_dimension=0, tiled=True),
        lax.psum_scatter(grad_b_value, ("grp", "seq"), scatter_dimension=0, tiled=True),
        lax.psum_scatter(grad_w_out, ("grp", "seq"), scatter_dimension=0, tiled=True),
        lax.psum_scatter(grad_b_out, ("grp", "seq"), scatter_dimension=0, tiled=True),
        lax.psum_scatter(grad_gain_one, ("grp", "seq"), scatter_dimension=0, tiled=True),
        lax.psum_scatter(grad_shift_one, ("grp", "seq"), scatter_dimension=0, tiled=True),
        lax.psum_scatter(grad_gain_two, ("grp", "seq"), scatter_dimension=0, tiled=True),
        lax.psum_scatter(grad_shift_two, ("grp", "seq"), scatter_dimension=0, tiled=True),
        lax.psum_scatter(grad_w_up, ("grp", "seq"), scatter_dimension=0, tiled=True),
        lax.psum_scatter(grad_b_up, ("grp", "seq"), scatter_dimension=0, tiled=True),
        lax.psum_scatter(grad_w_down, ("grp", "seq"), scatter_dimension=0, tiled=True),
        lax.psum_scatter(grad_b_down, ("grp", "seq"), scatter_dimension=0, tiled=True),
    )
    return (
        output.astype(jnp.bfloat16)[None],
        grad_input[None],
        summed[0],
        summed[1],
        summed[2],
        summed[3],
        summed[4],
        summed[5],
        summed[6],
        summed[7],
        summed[8],
        summed[9],
        summed[10],
        summed[11],
        summed[12],
        summed[13],
        summed[14],
    )


def solution(mesh):
    return jax.shard_map(
        local,
        mesh=mesh,
        in_specs=(
            P("grp", "seq", None),
            P("grp", None),
            P("grp", "seq"),
            P("grp", "seq", None),
            P(("grp", "seq"), None),
            P(("grp", "seq")),
            P(("grp", "seq"), None),
            P(("grp", "seq"), None),
            P(("grp", "seq")),
            P(("grp", "seq"), None),
            P(("grp", "seq")),
            P(("grp", "seq")),
            P(("grp", "seq")),
            P(("grp", "seq")),
            P(("grp", "seq")),
            P(("grp", "seq"), None),
            P(("grp", "seq")),
            P(("grp", "seq"), None),
            P(("grp", "seq")),
        ),
        out_specs=(
            P("grp", "seq", None),
            P("grp", "seq", None),
            P(("grp", "seq"), None),
            P(("grp", "seq")),
            P(("grp", "seq"), None),
            P(("grp", "seq"), None),
            P(("grp", "seq")),
            P(("grp", "seq"), None),
            P(("grp", "seq")),
            P(("grp", "seq")),
            P(("grp", "seq")),
            P(("grp", "seq")),
            P(("grp", "seq")),
            P(("grp", "seq"), None),
            P(("grp", "seq")),
            P(("grp", "seq"), None),
            P(("grp", "seq")),
        ),
        check_vma=False,
    )
```

profile of v0, /device:TPU:2, one launch (start us, length us, event | category | flops | bytes accessed | tf_op | source)
XLA Modules:
  0.0 1335.2 jit_solution(17881390713222281536)
XLA Ops:
  17.0 42.0 %all-reduce.19 = (bf16[768]{0:T(1024)(128)(2,1)S(1)}, bf16[768]{0:T(1024)(128)(2,1)S(1)}, bf16[768]{0:T(1024)(128)(2,1)S(1)}, bf16[768]{0:T(1024)(128)(2,1)S(1)}...) all-reduce(bf16[768]{0:T(1024)(128)(2,1)S(1)} %dynamic-update-slice, ...), channel_id=1, replica_groups=mesh['grp'=4,'seq'=8] {'grp','seq'}, use_global_device_ids=true, to_apply=%add.2 | all-reduce | flops 9216 | bytes 36864
  61.3 5.0 all-gather.9.cloned.1.call-done
  68.8 53.6 %all-gather.15.cloned.1.call-done = bf16[768,768]{1,0:T(8,128)(2,1)} async-done(((bf16[24,768]{1,0:T(8,128)(2,1)}), bf16[768,768]{1,0:T(8,128)(2,1)}) %all-gather.15.cloned.1.call-update) | async-done | bytes 1179664 | tf_op jit(solution)/shard_map/all_gather | solution.py:71
  128.9 49.5 %all-gather.13.cloned.1.call-done = bf16[768,768]{1,0:T(8,128)(2,1)} async-done(((bf16[24,768]{1,0:T(8,128)(2,1)}), bf16[768,768]{1,0:T(8,128)(2,1)}) %all-gather.13.cloned.1.call-update) | async-done | bytes 1179664 | tf_op jit(solution)/shard_map/all_gather | solution.py:69
  183.2 40.9 %all-gather.11.cloned.1.call-done = bf16[1024,768]{1,0:T(8,128)(2,1)} async-done(((bf16[128,768]{1,0:T(8,128)(2,1)}), bf16[1024,768]{1,0:T(8,128)(2,1)}) %all-gather.11.cloned.1.call-update) | async-done | bytes 1572880 | tf_op jit(solution)/shard_map/all_gather | solution.py:106
  226.5 43.3 %all-gather.17.cloned.1.call-done = bf16[1024,768]{1,0:T(8,128)(2,1)} async-done(((bf16[128,768]{1,0:T(8,128)(2,1)}), bf16[1024,768]{1,0:T(8,128)(2,1)}) %all-gather.17.cloned.1.call-update) | async-done | bytes 1572880 | tf_op jit(solution)/shard_map/all_gather | solution.py:105
  287.3 38.2 %all-gather.19.cloned.1.call-done = bf16[768,768]{1,0:T(8,128)(2,1)} async-done(((bf16[24,768]{1,0:T(8,128)(2,1)}), bf16[768,768]{1,0:T(8,128)(2,1)}) %all-gather.19.cloned.1.call-update) | async-done | bytes 1179664 | tf_op jit(solution)/shard_map/all_gather | solution.py:74
  332.5 58.6 %all-gather.21.cloned.1.call-done = bf16[768,3072]{1,0:T(8,128)(2,1)} async-done(((bf16[24,3072]{1,0:T(8,128)(2,1)}), bf16[768,3072]{1,0:T(8,128)(2,1)}) %all-gather.21.cloned.1.call-update) | async-done | bytes 4718608 | tf_op jit(solution)/shard_map/all_gather | solution.py:80
  391.1 8.7 multiply_convert_fusion
  399.8 56.7 %all-gather.23.cloned.1.call-done = bf16[3072,768]{1,0:T(8,128)(2,1)} async-done(((bf16[96,768]{1,0:T(8,128)(2,1)}), bf16[3072,768]{1,0:T(8,128)(2,1)}) %all-gather.23.cloned.1.call-update) | async-done | bytes 4718608 | tf_op jit(solution)/shard_map/all_gather | solution.py:82
  456.5 5.8 convert_reduce_fusion
  471.1 3.0 multiply_reduce_fusion.3
  522.3 38.5 %reduce-scatter.27.cloned.1.call-done = bf16[128,768]{1,0:T(8,128)(2,1)} async-done(((bf16[1024,768]{1,0:T(8,128)(2,1)}), bf16[128,768]{1,0:T(8,128)(2,1)}) %reduce-scatter.27.cloned.1.call-update) | async-done | bytes 196624
  563.8 64.5 %reduce-scatter.25.cloned.1.call-done = bf16[128,768]{1,0:T(8,128)(2,1)} async-done(((bf16[1024,768]{1,0:T(8,128)(2,1)}), bf16[128,768]{1,0:T(8,128)(2,1)}) %reduce-scatter.25.cloned.1.call-update) | async-done | bytes 196624
  632.5 5.2 fusion.80
  638.8 5.1 fusion.71
  645.7 3.9 fusion.23
  653.0 42.2 %all-reduce.18 = (f32[768]{0:T(1024)S(1)}, f32[768]{0:T(1024)S(1)}, f32[768]{0:T(1024)S(1)}, f32[768]{0:T(1024)S(1)}, f32[768]{0:T(1024)S(1)}, /*index=5*/f32[76...) all-reduce(f32[768]{0:T(1024)S(1)} %convert_reduce_fusion.4, ...), channel_id=5, replica_groups=mesh['grp'=4,'seq'=8] {'grp','seq'}, use_global_device_ids=true, to_apply=%region_30.31.clone | all-reduce | flops 9216 | bytes 73728
  701.4 30.7 %reduce-scatter.13.cloned.1.call-done = f32[24,768]{1,0:T(8,128)} async-done(((f32[768,768]{1,0:T(8,128)}), f32[24,768]{1,0:T(8,128)}) %reduce-scatter.13.cloned.1.call-update) | async-done | bytes 73744 | tf_op jit(solution)/shard_map/reduce_scatter | solution.py:252
  732.1 104.6 %reduce-scatter.19.cloned.1.call-done = f32[24,768]{1,0:T(8,128)} async-done(((f32[768,768]{1,0:T(8,128)}), f32[24,768]{1,0:T(8,128)}) %reduce-scatter.19.cloned.1.call-update) | async-done | bytes 73744 | tf_op jit(solution)/shard_map/reduce_scatter | solution.py:257
  836.7 103.9 %reduce-scatter.17.cloned.1.call-done = f32[24,768]{1,0:T(8,128)} async-done(((f32[768,768]{1,0:T(8,128)}), f32[24,768]{1,0:T(8,128)}) %reduce-scatter.17.cloned.1.call-update) | async-done | bytes 73744 | tf_op jit(solution)/shard_map/reduce_scatter | solution.py:255
  940.6 104.6 %reduce-scatter.15.cloned.1.call-done = f32[24,768]{1,0:T(8,128)} async-done(((f32[768,768]{1,0:T(8,128)}), f32[24,768]{1,0:T(8,128)}) %reduce-scatter.15.cloned.1.call-update) | async-done | bytes 73744 | tf_op jit(solution)/shard_map/reduce_scatter | solution.py:254
  1045.3 141.0 %reduce-scatter.21.cloned.1.call-done = f32[24,3072]{1,0:T(8,128)} async-done(((f32[768,3072]{1,0:T(8,128)}), f32[24,3072]{1,0:T(8,128)}) %reduce-scatter.21.cloned.1.call-update) | async-done | bytes 294928 | tf_op jit(solution)/shard_map/reduce_scatter | solution.py:263
  1186.3 141.9 %reduce-scatter.23.cloned.1.call-done = f32[96,768]{1,0:T(8,128)} async-done(((f32[3072,768]{1,0:T(8,128)}), f32[96,768]{1,0:T(8,128)}) %reduce-scatter.23.cloned.1.call-update) | async-done | bytes 294928 | tf_op jit(solution)/shard_map/reduce_scatter | solution.py:265
  (465 shorter events, 127.7 us)
Async XLA Ops:
  7.2 115.2 %copy-start.7 = (bf16[1,128,768]{2,1,0:T(8,128)(2,1)S(1)}, bf16[1,128,768]{2,1,0:T(8,128)(2,1)}, u32[]{:S(2)}) copy-start(bf16[1,128,768]{2,1,0:T(8,128)(2,1)} %param.19) | copy-start | bytes 589828
  7.2 59.1 %all-gather.9.cloned.1.call-start = ((), (), s32[]{:S(2)}) async-start(), calls=%async_computation.8 | async-start | bytes 1216512 | tf_op jit(solution)/shard_map/all_gather | solution.py:72
  7.9 114.4 %all-gather.15.cloned.1.call-start = ((), (), s32[]{:S(2)}) async-start(), calls=%async_computation.11 | async-start | bytes 1216512 | tf_op jit(solution)/shard_map/all_gather | solution.py:71
  8.7 169.7 %all-gather.13.cloned.1.call-start = ((), (), s32[]{:S(2)}) async-start(), calls=%async_computation.10 | async-start | bytes 1216512 | tf_op jit(solution)/shard_map/all_gather | solution.py:69
  9.4 214.8 %all-gather.11.cloned.1.call-start = ((), (), s32[]{:S(2)}) async-start(), calls=%async_computation.9 | async-start | bytes 1769472 | tf_op jit(solution)/shard_map/all_gather | solution.py:106
  60.1 118.3 %copy-start.72 = (f32[128]{0:T(128)}, f32[128]{0:T(128)S(1)}, u32[]{:S(2)}) copy-start(f32[128]{0:T(128)S(1)} %broadcast_multiply_fusion.1) | copy-start | bytes 1540
  61.3 117.1 %copy-start.86 = (f32[128]{0:T(128)}, f32[128]{0:T(128)S(1)}, u32[]{:S(2)}) copy-start(f32[128]{0:T(128)S(1)} %fusion.77) | copy-start | bytes 1540
  68.7 58.3 %copy-start.127 = (s32[1,128]{1,0:T(1,128)S(1)}, s32[1,128]{1,0:T(1,128)}, u32[]{:S(2)}) copy-start(s32[1,128]{1,0:T(1,128)} %param.21) | copy-start | bytes 1540
  68.7 60.0 %copy-start.109 = (s32[1,1024]{1,0:T(1,128)S(1)}, s32[1,1024]{1,0:T(1,128)}, u32[]{:S(2)}) copy-start(s32[1,1024]{1,0:T(1,128)} %param.20) | copy-start | bytes 12292
  68.8 201.0 %all-gather.17.cloned.1.call-start = ((), (), s32[]{:S(2)}) async-start(), calls=%async_computation.12 | async-start | bytes 1769472 | tf_op jit(solution)/shard_map/all_gather | solution.py:105
  124.7 200.8 %all-gather.19.cloned.1.call-start = ((), (), s32[]{:S(2)}) async-start(), calls=%async_computation.13 | async-start | bytes 1216512 | tf_op jit(solution)/shard_map/all_gather | solution.py:74
  125.3 265.8 %all-gather.21.cloned.1.call-start = ((), (), s32[]{:S(2)}) async-start(), calls=%async_computation.14 | async-start | bytes 4866048 | tf_op jit(solution)/shard_map/all_gather | solution.py:80
  126.0 330.4 %all-gather.23.cloned.1.call-start = ((), (), s32[]{:S(2)}) async-start(), calls=%async_computation.15 | async-start | bytes 4866048 | tf_op jit(solution)/shard_map/all_gather | solution.py:82
  126.8 434.0 %reduce-scatter.27.cloned.1.call-start = ((), (), s32[]{:S(2)}) async-start(), calls=%async_computation.23 | async-start | bytes 1769472
  180.2 105.2 %copy-start.61 = (bf16[128,128]{0,1:T(8,128)(2,1)}, bf16[128,128]{0,1:T(8,128)(2,1)S(1)}, u32[]{:S(2)}) copy-start(bf16[128,128]{0,1:T(8,128)(2,1)S(1)} %copy.124) | copy-start | bytes 98308
  180.3 103.1 %copy-start.63 = (bf16[128,128]{0,1:T(8,128)(2,1)}, bf16[128,128]{0,1:T(8,128)(2,1)S(1)}, u32[]{:S(2)}) copy-start(bf16[128,128]{0,1:T(8,128)(2,1)S(1)} %copy.121) | copy-start | bytes 98308
  332.5 124.0 %copy-start.41 = (bf16[1,128,768]{2,1,0:T(8,128)(2,1)S(1)}, bf16[1,128,768]{2,1,0:T(8,128)(2,1)}, u32[]{:S(2)}) copy-start(bf16[1,128,768]{2,1,0:T(8,128)(2,1)} %param.22) | copy-start | bytes 589828
  496.7 131.6 %reduce-scatter.25.cloned.1.call-start = ((), (), s32[]{:S(2)}) async-start(), calls=%async_computation.22 | async-start | bytes 1769472
  510.4 221.7 %reduce-scatter.13.cloned.1.call-start = ((), (), s32[]{:S(2)}) async-start(), calls=%async_computation.16 | async-start | bytes 2433024 | tf_op jit(solution)/shard_map/reduce_scatter | solution.py:252
  518.5 318.2 %reduce-scatter.19.cloned.1.call-start = ((), (), s32[]{:S(2)}) async-start(), calls=%async_computation.19 | async-start | bytes 2433024 | tf_op jit(solution)/shard_map/reduce_scatter | solution.py:257
  522.2 418.4 %reduce-scatter.17.cloned.1.call-start = ((), (), s32[]{:S(2)}) async-start(), calls=%async_computation.18 | async-start | bytes 2433024 | tf_op jit(solution)/shard_map/reduce_scatter | solution.py:255
  563.7 481.5 %reduce-scatter.15.cloned.1.call-start = ((), (), s32[]{:S(2)}) async-start(), calls=%async_computation.17 | async-start | bytes 2433024 | tf_op jit(solution)/shard_map/reduce_scatter | solution.py:254
  631.3 555.0 %reduce-scatter.21.cloned.1.call-start = ((), (), s32[]{:S(2)}) async-start(), calls=%async_computation.20 | async-start | bytes 9732096 | tf_op jit(solution)/shard_map/reduce_scatter | solution.py:263
  637.7 690.5 %reduce-scatter.23.cloned.1.call-start = ((), (), s32[]{:S(2)}) async-start(), calls=%async_computation.21 | async-start | bytes 9732096 | tf_op jit(solution)/shard_map/reduce_scatter | solution.py:265
  (120 other events, 868.4 us)
Sparse Core Ops, SparseCore 0:
  10.9 55.3 all-gather.8
  69.2 53.1 all-gather.14
  125.3 53.0 all-gather.12
  181.0 43.1 all-gather.10
  226.8 42.9 all-gather.16
  272.6 52.9 all-gather.18
  328.5 62.5 all-gather.20
  394.0 62.4 all-gather.22
  496.8 63.9 reduce-scatter.26
  564.4 63.8 reduce-scatter.24
  634.2 97.8 reduce-scatter.12
  738.7 98.0 reduce-scatter.18
  842.6 97.9 reduce-scatter.16
  947.2 98.0 reduce-scatter.14
  1051.6 134.6 reduce-scatter.20
  1193.6 134.5 reduce-scatter.22
where the time goes:
time: 1340 us
  waiting for transfers between devices  1080 us (81%)
  blocking collectives  84.2 us (6%)
  matrix products  83.6 us (6%)
  local copies, waits for them, and re-layouts  53 us (4%)
  other arithmetic  17.6 us (1%)
  between operations  16 us (1%)
    reduce_scatter x1, waiting for transfers between devices, local(): lax.psum_scatter(grad_w_down, ('grp', 'seq'), scatter_dimension=0, tiled=...  142 us
    reduce_scatter x1, waiting for transfers between devices, local(): lax.psum_scatter(grad_w_up, ('grp', 'seq'), scatter_dimension=0, tiled=True)  141 us
    unnamed x18, waiting for transfers between devices  107 us
    reduce_scatter x1, waiting for transfers between devices, local(): lax.psum_scatter(grad_w_key, ('grp', 'seq'), scatter_dimension=0, tiled=T...  105 us
    reduce_scatter x1, waiting for transfers between devices, local(): lax.psum_scatter(grad_w_out, ('grp', 'seq'), scatter_dimension=0, tiled=T...  105 us
    reduce_scatter x1, waiting for transfers between devices, local(): lax.psum_scatter(grad_w_value, ('grp', 'seq'), scatter_dimension=0, tiled...  104 us
    unnamed x2, blocking collectives  84.2 us
    all_gather x1, waiting for transfers between devices, local(): lax.all_gather(w_up, ('grp', 'seq'), axis=0, tiled=True)  58.6 us
  transfers between devices with their start and end apart: 16, of which 16 were waited for; matrix products, arithmetic and copies ran while one was open for 8% of the time, Pallas kernels for 0%

commit v1 on v0

v1 whole, which is shorter than its diff:
```python
import functools

import jax
import jax.numpy as jnp
from jax import lax
from jax.experimental import pallas as pl
from jax.experimental.pallas import tpu as pltpu
from jax.sharding import Mesh, PartitionSpec as P

HEADS = 12
HEAD_DIM = 64
TP = 4
HEADS_TP = HEADS // TP
EPS = 1e-05
NEG = -1e30
SCALE = 0.125
ALL = ("gx", "c", "sz", "sy")
SAME = ("gx", "sz", "sy")
SMALLS = 64
f32 = jnp.float32
bf16 = jnp.bfloat16


class Plan:
    def __init__(self, groups, blocks):
        if (groups, blocks) == (4, 8):
            self.shape = (2, 2, 4, 2)
            self.tp, self.half, self.rep = ("gx", "sy"), "c", ("c", "sz")
        else:
            self.shape = (groups // 2, 2, blocks // TP, TP)
            self.tp, self.half, self.rep = ("sy",), "sz", ("gx", "c", "sz")
        self.size = dict(zip(ALL, self.shape))
        self.devices = groups * blocks
        self.parts = self.size[self.half]
        self.copies = self.devices // TP
        self.route = []
        for src in range(self.devices):
            seq, block = divmod(src, blocks)
            part, member = divmod(block, TP)
            if self.tp == ("sy",):
                dst = src
            else:
                dst = (((member >> 1) * 2 + part) * 4 + seq) * 2 + (member & 1)
            self.route.append((src, dst))
        self.back = [(dst, src) for src, dst in self.route]

    def move(self, value, table):
        if all(a == b for a, b in table):
            return value
        return lax.ppermute(value, ALL, table)

    def shuffle(self, value, before, after):
        tail = value.shape[1:]
        dims = [self.size[a] for a in before]
        order = [before.index(a) for a in after]
        value = value.reshape(*dims, *tail)
        value = value.transpose(*order, *range(len(dims), len(dims) + len(tail)))
        return value.reshape(-1, *tail)


def dot(left, right, left_dim=1, right_dim=0):
    return lax.dot_general(
        left, right, (((left_dim,), (right_dim,)), ((), ())), preferred_element_type=f32
    )


def unit(values):
    center = values - jnp.mean(values, axis=-1, keepdims=True)
    variance = jnp.mean(center * center, axis=-1, keepdims=True)
    rstd = lax.rsqrt(variance + EPS)
    return center * rstd, rstd


def unit_back(grad_unit, units, rstd):
    first = jnp.mean(grad_unit, axis=-1, keepdims=True)
    second = jnp.mean(grad_unit * units, axis=-1, keepdims=True)
    return rstd * (grad_unit - first - units * second)


def params(limit=60 * 1024 * 1024, axes=1):
    return pltpu.CompilerParams(
        dimension_semantics=("arbitrary",) * axes, vmem_limit_bytes=limit
    )


def cost(flops, nbytes, trans=0):
    return pl.CostEstimate(flops=int(flops), bytes_accessed=int(nbytes), transcendentals=int(trans))


def whole(shape):
    zeros = (0,) * len(shape)
    return pl.BlockSpec(shape, lambda *_: zeros)


def head_lanes(value, head):
    lane = lax.broadcasted_iota(jnp.int32, value.shape, 1)
    keep = (lane >= head * HEAD_DIM) & (lane < (head + 1) * HEAD_DIM)
    return jnp.where(keep, value, jnp.zeros_like(value))


def qkv_kernel(x_ref, w_ref, vec_ref, bias_ref, h_ref, q_ref, kv_ref):
    units, _ = unit(x_ref[...].astype(f32))
    low = (units * vec_ref[3:4, :] + vec_ref[4:5, :]).astype(bf16)
    h_ref[...] = low
    cols = q_ref.shape[1]
    out = dot(low, w_ref[...])
    query = (out[:, :cols] + bias_ref[0:1, :]).astype(bf16)
    q_ref[...] = (query.astype(f32) * SCALE).astype(bf16)
    kv_ref[0] = out[:, cols : 2 * cols].astype(bf16)
    kv_ref[1] = (out[:, 2 * cols : 3 * cols] + bias_ref[1:2, :]).astype(bf16)


def qkv(x_all, w_qkv, vecs, bias):
    rows, width = x_all.shape
    cols = width // TP
    step = rows // TP
    return pl.pallas_call(
        qkv_kernel,
        grid=(TP,),
        in_specs=[
            pl.BlockSpec((step, width), lambda i: (i, 0)),
            whole(w_qkv.shape),
            whole(vecs.shape),
            whole(bias.shape),
        ],
        out_specs=[
            pl.BlockSpec((step, width), lambda i: (i, 0)),
            pl.BlockSpec((step, cols), lambda i: (i, 0)),
            pl.BlockSpec((2, step, cols), lambda i: (0, i, 0)),
        ],
        out_shape=[
            jax.ShapeDtypeStruct((rows, width), bf16),
            jax.ShapeDtypeStruct((rows, cols), bf16),
            jax.ShapeDtypeStruct((2, rows, cols), bf16),
        ],
        compiler_params=params(),
        cost_estimate=cost(2 * rows * width * 3 * cols, rows * width * 8),
        name="qkv",
    )(x_all, w_qkv, vecs, bias)


def fill_docs(ids_ref, part, parts, doc_ref):
    span, width = doc_ref.shape[1:]
    for j in range(parts):
        at = lax.rem(part + j, parts) * span
        row = ids_ref[0:1, pl.ds(pl.multiple_of(at, 512), span)]
        doc_ref[j] = jnp.broadcast_to(row, (width, span)).T


def fwd_kernel(parts, idx_ref, ids_ref, q_ref, *refs):
    kv_refs = refs[:parts]
    o_ref, lse_ref, turned, doc_ref = refs[parts:]
    step = pl.program_id(0)
    part = idx_ref[1]
    span = kv_refs[0].shape[1]
    width = q_ref.shape[0]

    @pl.when(step == 0)
    def _():
        fill_docs(ids_ref, part, parts, doc_ref)
        for j in range(parts):
            turned[j] = kv_refs[j][1].T

    at = part * span + step * width
    own = ids_ref[0:1, pl.ds(pl.multiple_of(at, 128), width)]
    query = q_ref[...]
    outs, lses = [], []
    for head in range(HEADS_TP):
        masked = head_lanes(query, head)
        scores = []
        for j in range(parts):
            raw = dot(kv_refs[j][0], masked, 1, 1)
            scores.append(jnp.where(doc_ref[j] == own, raw, NEG))
        peak = functools.reduce(
            jnp.maximum, [jnp.max(s, axis=0, keepdims=True) for s in scores]
        )
        exps = [jnp.exp(s - peak) for s in scores]
        total = functools.reduce(jnp.add, [jnp.sum(e, axis=0, keepdims=True) for e in exps])
        scale = 1.0 / total
        acc = None
        for j in range(parts):
            probs = (exps[j] * scale).astype(bf16)
            term = dot(turned[j, head * HEAD_DIM : (head + 1) * HEAD_DIM, :], probs)
            acc = term if acc is None else acc + term
        outs.append(acc)
        lses.append(peak + jnp.log(total))
    o_ref[...] = jnp.concatenate(outs, axis=0).T.astype(bf16)
    for head in range(HEADS_TP):
        lse_ref[head : head + 1, :] = lses[head]


def attend(idx, ids, q, kvs, width=256):
    rows, cols = q.shape
    parts = len(kvs)
    span = kvs[0].shape[1]
    return pl.pallas_call(
        functools.partial(fwd_kernel, parts),
        grid_spec=pltpu.PrefetchScalarGridSpec(
            num_scalar_prefetch=1,
            grid=(rows // width,),
            in_specs=[whole(ids.shape), pl.BlockSpec((width, cols), lambda i, *_: (i, 0))]
            + [whole(kv.shape) for kv in kvs],
            out_specs=[
                pl.BlockSpec((width, cols), lambda i, *_: (i, 0)),
                pl.BlockSpec((8, width), lambda i, *_: (0, i)),
            ],
            scratch_shapes=[
                pltpu.VMEM((parts, cols, span), bf16),
                pltpu.VMEM((parts, span, width), f32),
            ],
        ),
        out_shape=[
            jax.ShapeDtypeStruct((rows, cols), bf16),
            jax.ShapeDtypeStruct((8, rows), f32),
        ],
        compiler_params=params(),
        cost_estimate=cost(4 * rows * span * parts * cols, span * parts * cols * 4, rows * span * parts * HEADS_TP),
        name="attend",
    )(idx, ids, q, *kvs)


def bwd_kernel(parts, idx_ref, ids_ref, q_ref, da_ref, w_ref, lse_ref, *refs):
    kv_refs = refs[:parts]
    dq_ref, own_ref = refs[parts : parts + 2]
    other_refs = refs[parts + 2 : 2 * parts + 1]
    turned, doc_ref, key_acc, value_acc = refs[2 * parts + 1 :]
    step = pl.program_id(0)
    part = idx_ref[1]
    span = kv_refs[0].shape[1]
    width, cols = q_ref.shape

    @pl.when(step == 0)
    def _():
        fill_docs(ids_ref, part, parts, doc_ref)
        for j in range(parts):
            turned[j] = kv_refs[j][0].T
        key_acc[...] = jnp.zeros_like(key_acc)
        value_acc[...] = jnp.zeros_like(value_acc)

    at = part * span + step * width
    own = ids_ref[0:1, pl.ds(pl.multiple_of(at, 128), width)]
    query = q_ref[...]
    grad_mixed = dot(da_ref[...], w_ref[0], 1, 1).astype(bf16)
    turned_grads = []
    for head in range(HEADS_TP):
        masked_q = head_lanes(query, head)
        masked_g = head_lanes(grad_mixed, head)
        lse = lse_ref[head : head + 1, :]
        probs, grads = [], []
        for j in range(parts):
            raw = dot(kv_refs[j][0], masked_q, 1, 1)
            probs.append(jnp.exp(jnp.where(doc_ref[j] == own, raw, NEG) - lse))
            grads.append(dot(kv_refs[j][1], masked_g, 1, 1))
        delta = functools.reduce(
            jnp.add,
            [jnp.sum(p * g, axis=0, keepdims=True) for p, g in zip(probs, grads)],
        )
        acc = None
        for j in range(parts):
            grad_scores = (probs[j] * (grads[j] - delta)).astype(bf16)
            value_acc[j] += dot(probs[j].astype(bf16), masked_g)
            key_acc[j] += dot(grad_scores, masked_q)
            term = dot(turned[j, head * HEAD_DIM : (head + 1) * HEAD_DIM, :], grad_scores)
            acc = term if acc is None else acc + term
        turned_grads.append(acc)
    dq_ref[...] = (jnp.concatenate(turned_grads, axis=0).T * SCALE).astype(bf16)

    @pl.when(step == pl.num_programs(0) - 1)
    def _():
        own_ref[0] = key_acc[0]
        own_ref[1] = value_acc[0]
        for j in range(1, parts):
            other_refs[j - 1][0] = key_acc[j].astype(bf16)
            other_refs[j - 1][1] = value_acc[j].astype(bf16)


def attend_back(idx, ids, q, da_all, w_out, lse, kvs, width=256):
    rows, cols = q.shape
    model = da_all.shape[1]
    parts = len(kvs)
    span = kvs[0].shape[1]
    return pl.pallas_call(
        functools.partial(bwd_kernel, parts),
        grid_spec=pltpu.PrefetchScalarGridSpec(
            num_scalar_prefetch=1,
            grid=(rows // width,),
            in_specs=[
                whole(ids.shape),
                pl.BlockSpec((width, cols), lambda i, *_: (i, 0)),
                pl.BlockSpec((width, model), lambda i, *_: (i, 0)),
                pl.BlockSpec((1, cols, model), lambda i, idx: (idx[0], 0, 0)),
                pl.BlockSpec((8, width), lambda i, *_: (0, i)),
            ]
            + [whole(kv.shape) for kv in kvs],
            out_specs=[
                pl.BlockSpec((width, cols), lambda i, *_: (i, 0)),
                whole((2, span, cols)),
            ]
            + [whole((2, span, cols))] * (parts - 1),
            scratch_shapes=[
                pltpu.VMEM((parts, cols, span), bf16),
                pltpu.VMEM((parts, span, width), f32),
                pltpu.VMEM((parts, span, cols), f32),
                pltpu.VMEM((parts, span, cols), f32),
            ],
        ),
        out_shape=[
            jax.ShapeDtypeStruct((rows, cols), bf16),
            jax.ShapeDtypeStruct((2, span, cols), f32),
        ]
        + [jax.ShapeDtypeStruct((2, span, cols), bf16)] * (parts - 1),
        compiler_params=params(),
        cost_estimate=cost(10 * rows * span * parts * cols, span * parts * cols * 12, rows * span * parts * HEADS_TP),
        name="attend_back",
    )(idx, ids, q, da_all, w_out, lse, *kvs)


def mlp_kernel(
    x_ref, o_ref, dm_ref, wo_ref, wu_ref, wd_ref, vec_ref, bup_ref,
    r_ref, h_ref, a_ref, du_ref, out_ref, dh_ref, sum_ref, bsum_ref,
):
    step = pl.program_id(0)

    @pl.when(step == 0)
    def _():
        sum_ref[...] = jnp.zeros_like(sum_ref)
        bsum_ref[...] = jnp.zeros_like(bsum_ref)

    attended = dot(o_ref[0], wo_ref[0])
    for j in range(1, TP):
        attended += dot(o_ref[j], wo_ref[j])
    residual = x_ref[...].astype(f32) + (attended + vec_ref[2:3, :])
    r_ref[...] = residual
    units, _ = unit(residual)
    low = (units * vec_ref[5:6, :] + vec_ref[6:7, :]).astype(bf16)
    h_ref[...] = low
    pre = dot(low, wu_ref[...]) + bup_ref[...]
    normal = 0.5 * (1.0 + lax.erf(pre * 0.7071067811865476))
    act = (pre * normal).astype(bf16)
    a_ref[...] = act
    slope = normal + pre * (0.3989422804014327 * jnp.exp(-0.5 * pre * pre))
    out_ref[...] = dot(act, wd_ref[...]).astype(bf16)
    grad_pre = (dot(dm_ref[...], wd_ref[...], 1, 1) * slope).astype(bf16)
    du_ref[...] = grad_pre
    bsum_ref[0:1, :] += jnp.sum(grad_pre.astype(f32), axis=0, keepdims=True)
    grad = dot(grad_pre, wu_ref[...], 1, 1)
    dh_ref[...] = grad.astype(bf16)
    sum_ref[0:1, :] += jnp.sum(grad * units, axis=0, keepdims=True)
    sum_ref[1:2, :] += jnp.sum(grad, axis=0, keepdims=True)


def mlp(x_all, o_all, dm_all, w_out, w_up, w_down, vecs, b_up):
    rows, width = x_all.shape
    hidden = w_up.shape[1]
    cols = width // TP
    step = 128
    token = pl.BlockSpec((step, width), lambda i: (i, 0))
    inner = pl.BlockSpec((step, hidden), lambda i: (i, 0))
    return pl.pallas_call(
        mlp_kernel,
        grid=(rows // step,),
        in_specs=[
            token,
            pl.BlockSpec((TP, step, cols), lambda i: (0, i, 0)),
            token,
            whole(w_out.shape),
            whole(w_up.shape),
            whole(w_down.shape),
            whole(vecs.shape),
            whole(b_up.shape),
        ],
        out_specs=[token, token, inner, inner, token, token, whole((8, width)), whole((8, hidden))],
        out_shape=[
            jax.ShapeDtypeStruct((rows, width), f32),
            jax.ShapeDtypeStruct((rows, width), bf16),
            jax.ShapeDtypeStruct((rows, hidden), bf16),
            jax.ShapeDtypeStruct((rows, hidden), bf16),
            jax.ShapeDtypeStruct((rows, width), bf16),
            jax.ShapeDtypeStruct((rows, width), bf16),
            jax.ShapeDtypeStruct((8, width), f32),
            jax.ShapeDtypeStruct((8, hidden), f32),
        ],
        compiler_params=params(),
        cost_estimate=cost(2 * rows * width * (width + 4 * hidden), rows * width * 24, rows * hidden * 4),
        name="mlp",
    )(x_all, o_all, dm_all, w_out, w_up, w_down, vecs, b_up)


def pair_kernel(h_ref, du_ref, a_ref, dm_ref, up_ref, down_ref):
    up_ref[...] = dot(h_ref[...], du_ref[...], 0, 0).astype(bf16)
    down_ref[...] = dot(a_ref[...], dm_ref[...], 0, 0).astype(bf16)


def mlp_weight_grads(low, grad_pre, act, dm_all):
    rows, width = low.shape
    hidden = act.shape[1]
    step = 256
    return pl.pallas_call(
        pair_kernel,
        grid=(hidden // step,),
        in_specs=[
            whole((rows, width)),
            pl.BlockSpec((rows, step), lambda i: (0, i)),
            pl.BlockSpec((rows, step), lambda i: (0, i)),
            whole((rows, width)),
        ],
        out_specs=[
            pl.BlockSpec((width, step), lambda i: (0, i)),
            pl.BlockSpec((step, width), lambda i: (i, 0)),
        ],
        out_shape=[
            jax.ShapeDtypeStruct((width, hidden), bf16),
            jax.ShapeDtypeStruct((hidden, width), bf16),
        ],
        compiler_params=params(),
        cost_estimate=cost(4 * rows * width * hidden, width * hidden * 8),
        name="mlp_weight_grads",
    )(low, grad_pre, act, dm_all)


def resid_kernel(idx_ref, parts_ref, r_ref, dm_ref, vec_ref, dr_ref, da_ref, sum_ref):
    total = parts_ref[0].astype(f32)
    for j in range(1, TP):
        total += parts_ref[j].astype(f32)
    units, rstd = unit(r_ref[0])
    dm = dm_ref[...].astype(f32)
    dr = dm + unit_back(total * vec_ref[5:6, :], units, rstd)
    da = dr.astype(bf16)
    dr_ref[...] = dr
    da_ref[...] = da
    sum_ref[...] = jnp.zeros_like(sum_ref)
    sum_ref[0:1, :] = jnp.sum(da.astype(f32), axis=0, keepdims=True)
    sum_ref[1:2, :] = jnp.sum(dm, axis=0, keepdims=True)


def resid_back(idx, parts, r_all, dm, vecs):
    rows, width = dm.shape
    return pl.pallas_call(
        resid_kernel,
        grid_spec=pltpu.PrefetchScalarGridSpec(
            num_scalar_prefetch=1,
            grid=(1,),
            in_specs=[
                whole(parts.shape),
                pl.BlockSpec((1, rows, width), lambda i, idx: (idx[0], 0, 0)),
                whole(dm.shape),
                whole(vecs.shape),
            ],
            out_specs=[whole((rows, width)), whole((rows, width)), whole((8, width))],
        ),
        out_shape=[
            jax.ShapeDtypeStruct((rows, width), f32),
            jax.ShapeDtypeStruct((rows, width), bf16),
            jax.ShapeDtypeStruct((8, width), f32),
        ],
        compiler_params=params(),
        cost_estimate=cost(30 * rows * width, rows * width * 20),
        name="resid_back",
    )(idx, parts, r_all, dm, vecs)


def output_kernel(idx_ref, parts_ref, r_ref, vec_ref, out_ref):
    total = r_ref[0] + vec_ref[7:8, :]
    for j in range(TP):
        total += parts_ref[j].astype(f32)
    out_ref[...] = total.astype(bf16)


def finish_output(idx, parts, r_all, vecs):
    _, rows, width = parts.shape
    return pl.pallas_call(
        output_kernel,
        grid_spec=pltpu.PrefetchScalarGridSpec(
            num_scalar_prefetch=1,
            grid=(1,),
            in_specs=[
                whole(parts.shape),
                pl.BlockSpec((1, rows, width), lambda i, idx: (idx[0], 0, 0)),
                whole(vecs.shape),
            ],
            out_specs=whole((rows, width)),
        ),
        out_shape=jax.ShapeDtypeStruct((rows, width), bf16),
        compiler_params=params(),
        cost_estimate=cost(8 * rows * width, rows * width * 14),
        name="finish_output",
    )(idx, parts, r_all, vecs)


def input_kernel(parts_ref, x_ref, dr_ref, vec_ref, out_ref):
    total = parts_ref[0].astype(f32)
    for j in range(1, TP):
        total += parts_ref[j].astype(f32)
    units, rstd = unit(x_ref[...].astype(f32))
    out_ref[...] = (dr_ref[...] + unit_back(total * vec_ref[3:4, :], units, rstd)).astype(bf16)


def finish_input(parts, x, dr, vecs):
    return pl.pallas_call(
        input_kernel,
        out_shape=jax.ShapeDtypeStruct(x.shape, bf16),
        cost_estimate=cost(30 * x.size, x.size * 16),
        name="finish_input",
    )(parts, x, dr, vecs)


def normed_kernel(n_recv, x_ref, dq_ref, own_ref, *refs):
    recv_refs = refs[:n_recv]
    w_ref, d_ref, dh_ref, sum_ref = refs[n_recv:]
    step = pl.program_id(0)

    @pl.when(step == 0)
    def _():
        sum_ref[...] = jnp.zeros_like(sum_ref)

    cols = dq_ref.shape[1]
    width = x_ref.shape[1]
    grad_k, grad_v = own_ref[0], own_ref[1]
    for ref in recv_refs:
        grad_k += ref[0].astype(f32)
        grad_v += ref[1].astype(f32)
    d_ref[:, :cols] = dq_ref[...]
    d_ref[:, cols : 2 * cols] = grad_k.astype(bf16)
    d_ref[:, 2 * cols : 3 * cols] = grad_v.astype(bf16)
    d_ref[:, 3 * cols :] = jnp.zeros_like(d_ref[:, 3 * cols :])
    low = d_ref[...]
    grad = dot(low, w_ref[...], 1, 1)
    dh_ref[...] = grad.astype(bf16)
    units, _ = unit(x_ref[...].astype(f32))
    sum_ref[0:1, :width] += jnp.sum(grad * units, axis=0, keepdims=True)
    sum_ref[1:2, :width] += jnp.sum(grad, axis=0, keepdims=True)
    sum_ref[2:3, : low.shape[1]] += jnp.sum(low.astype(f32), axis=0, keepdims=True)


def normed_back(x_all, dq, own, recvs, w_qkv):
    rows, width = x_all.shape
    cols = dq.shape[1]
    wide = w_qkv.shape[1]
    step = 128
    pairs = pl.BlockSpec((2, step, cols), lambda i: (0, i, 0))
    return pl.pallas_call(
        functools.partial(normed_kernel, len(recvs)),
        grid=(rows // step,),
        in_specs=[
            pl.BlockSpec((step, width), lambda i: (i, 0)),
            pl.BlockSpec((step, cols), lambda i: (i, 0)),
            pairs,
        ]
        + [pairs] * len(recvs)
        + [whole(w_qkv.shape)],
        out_specs=[
            pl.BlockSpec((step, wide), lambda i: (i, 0)),
            pl.BlockSpec((step, width), lambda i: (i, 0)),
            whole((8, width)),
        ],
        out_shape=[
            jax.ShapeDtypeStruct((rows, wide), bf16),
            jax.ShapeDtypeStruct((rows, width), bf16),
            jax.ShapeDtypeStruct((8, width), f32),
        ],
        compiler_params=params(),
        cost_estimate=cost(2 * rows * width * wide, rows * width * 12),
        name="normed_back",
    )(x_all, dq, own, *recvs, w_qkv)


def proj_grads_kernel(h_ref, d_ref, o_ref, da_ref, v_ref, g_ref):
    wide = d_ref.shape[1]
    cols = da_ref.shape[1]
    g_ref[:, :wide] = dot(h_ref[...], d_ref[...], 0, 0).astype(bf16)
    for j in range(TP):
        at = j * cols
        part = dot(o_ref[j], da_ref[...], 0, 0)
        g_ref[at : at + cols, wide : wide + cols] = part.astype(bf16)
    turned = v_ref[...].T
    g_ref[:, wide + cols :] = turned[:, SMALLS:].astype(bf16)


def proj_grads(low, grads, o_all, da_cols, small):
    rows, width = low.shape
    wide = grads.shape[1] + da_cols.shape[1] + SMALLS
    return pl.pallas_call(
        proj_grads_kernel,
        out_shape=jax.ShapeDtypeStruct((width, wide), bf16),
        compiler_params=pltpu.CompilerParams(vmem_limit_bytes=60 * 1024 * 1024),
        cost_estimate=cost(2 * rows * width * wide, width * wide * 6),
        name="proj_grads",
    )(low, grads, o_all, da_cols, small)


def local(
    plan, inputs, segment_ids, padding, cotangent, w_query, b_query, w_key, w_value, b_value,
    w_out, b_out, ln1_gain, ln1_shift, ln2_gain, ln2_shift, w_up, b_up, w_down, b_down,
):
    x_own = inputs[0]
    rows, width = x_own.shape
    cols = width // TP
    length = segment_ids.shape[1]
    block = w_query.shape[0]
    hidden = w_up.shape[1]
    slab = b_up.shape[0]
    size = plan.size
    member = lax.axis_index(plan.tp)
    part = lax.axis_index(plan.half)
    core = lax.axis_index("c")
    idx = jnp.stack([member, part]).astype(jnp.int32)

    id_rows = jnp.pad(segment_ids[0].astype(bf16), (0, 8 * width - length)).reshape(8, width)
    moved = plan.move(jnp.concatenate([x_own, id_rows], axis=0), plan.route)
    x_mine = moved[:rows]
    ids = moved[rows:].reshape(1, -1)[:, :length].astype(f32)
    dm_own = (cotangent[0].astype(f32) * padding[0].astype(f32)[:, None]).astype(bf16)
    dm_mine = plan.move(dm_own, plan.route)

    small = jnp.stack(
        [b_query, b_value, b_out, ln1_gain, ln1_shift, ln2_gain, ln2_shift, b_down], axis=1
    )
    small = jnp.pad(small, ((0, 0), (0, SMALLS - small.shape[1])))
    split = [w.reshape(block, TP, cols).transpose(1, 0, 2) for w in (w_query, w_key, w_value)]
    chunk = jnp.concatenate(split + [jnp.broadcast_to(small, (TP, block, SMALLS))], axis=2)

    def spread(value):
        dims = [size[a] if a in plan.tp else 1 for a in SAME]
        tail = value.shape[1:]
        value = jnp.broadcast_to(value.reshape(*dims, *tail), (*[size[a] for a in SAME], *tail))
        return value.reshape(-1, *tail)

    got = lax.all_to_all(spread(chunk), SAME, 0, 0, tiled=True)
    both = lax.all_gather(got, "c", axis=0, tiled=True)
    table = plan.shuffle(both, ("c",) + SAME, ALL).reshape(width, -1)
    vecs = table[:, 3 * cols : 3 * cols + 8].T.astype(f32)
    w_qkv = table
    bias = lax.dynamic_slice(vecs, (0, member * cols), (2, cols))

    fields = w_up.reshape(block, plan.devices, slab).transpose(1, 0, 2)
    fields = plan.shuffle(fields, ALL, plan.tp + plan.rep)
    fields = fields.reshape(TP, plan.copies, block, slab).transpose(0, 2, 1, 3)
    fields = fields.reshape(TP, block, -1)
    fields = jnp.concatenate([fields, jnp.broadcast_to(w_out, (TP, block, width))], axis=1)
    fields = lax.all_to_all(fields, plan.tp, 0, 0, tiled=True)
    b_row = jnp.pad(b_up[None], ((0, 7), (0, width - slab)))
    bundle = jnp.concatenate(
        [
            fields[:, :block].reshape(TP * block, -1),
            fields[:, block:].reshape(TP * block, -1),
            w_down,
            b_row,
        ],
        axis=0,
    )
    bundle = lax.all_gather(bundle, plan.rep, axis=0, tiled=False)
    first = TP * block

    def by_row(value):
        value = value.reshape(plan.copies * TP, block, width)
        return plan.shuffle(value, plan.rep + plan.tp, ALL).reshape(width, width)

    up_mine = by_row(bundle[:, :first])
    out_full = by_row(bundle[:, first : 2 * first]).reshape(TP, cols, width)
    down_mine = bundle[:, 2 * first : 2 * first + slab].reshape(-1, width)
    b_up_mine = bundle[:, 2 * first + slab, :slab].reshape(1, -1).astype(f32)

    x_all = lax.all_gather(x_mine, plan.tp, axis=0, tiled=True)
    low_one, query, kv = qkv(x_all, w_qkv, vecs, bias)
    parts = plan.parts

    def turn(value, by):
        table = [(i, (i + by) % parts) for i in range(parts)]
        return lax.ppermute(value, plan.half, table)

    kvs = [kv] + [turn(kv, -j) for j in range(1, parts)]
    mixed, lse = attend(idx, ids, query, kvs)
    o_all = lax.all_gather(mixed, plan.tp, axis=0, tiled=False)
    dm_all = lax.all_gather(dm_mine, plan.tp, axis=0, tiled=True)
    r_all, low_two, act, grad_pre, out_part, dh_two, sum_two, sum_up = mlp(
        x_all, o_all, dm_all, out_full, up_mine, down_mine, vecs, b_up_mine
    )
    r_all = r_all.reshape(TP, rows, width)

    back_two = lax.all_to_all(dh_two.reshape(TP, rows, width), plan.tp, 0, 0, tiled=True)
    grad_up, grad_down = mlp_weight_grads(low_two, grad_pre, act, dm_all)
    dr, da, sum_own = resid_back(idx, back_two, r_all, dm_mine, vecs)
    da_all = lax.all_gather(da, plan.tp, axis=0, tiled=True)
    out_parts = lax.all_to_all(out_part.reshape(TP, rows, width), plan.tp, 0, 0, tiled=True)
    output = plan.move(finish_output(idx, out_parts, r_all, vecs), plan.back)

    grad_up = plan.shuffle(grad_up.reshape(plan.devices, block, -1), ALL, plan.rep + plan.tp)
    up_row = jnp.pad(
        sum_up[0].reshape(plan.copies, 1, slab).astype(bf16), ((0, 0), (0, 7), (0, width - slab))
    )
    summed = jnp.concatenate(
        [
            grad_up.reshape(plan.copies, first, width),
            grad_down.reshape(plan.copies, slab, width),
            up_row,
        ],
        axis=1,
    )
    summed = lax.psum_scatter(summed, plan.rep, scatter_dimension=0, tiled=False)
    g_w_down = summed[first : first + slab].astype(f32)
    g_b_up = summed[first + slab, :slab].astype(f32)
    ups = lax.all_to_all(summed[:first].reshape(TP, block, width), plan.tp, 0, 0, tiled=True)
    ups = ups.reshape(TP, block, plan.copies, slab).transpose(0, 2, 1, 3)
    ups = plan.shuffle(ups.reshape(plan.devices, block, slab), plan.tp + plan.rep, ALL)
    g_w_up = ups.transpose(1, 0, 2).reshape(block, hidden).astype(f32)

    results = attend_back(idx, ids, query, da_all, out_full, lse, kvs)
    grad_query, kv_own, kv_others = results[0], results[1], results[2:]
    recvs = [turn(kv_others[j - 1], j) for j in range(1, parts)]
    grads, dh_one, sum_one = normed_back(x_all, grad_query, kv_own, recvs, w_qkv)
    back_one = lax.all_to_all(dh_one.reshape(TP, rows, width), plan.tp, 0, 0, tiled=True)

    def placed(vector):
        return lax.dynamic_update_slice(jnp.zeros((width,), f32), vector, (member * cols,))

    vectors = [
        placed(sum_one[2, :cols]),
        placed(sum_one[2, 2 * cols : 3 * cols]),
        sum_own[0],
        sum_one[0],
        sum_one[1],
        sum_two[0],
        sum_two[1],
        sum_own[1],
    ]
    vectors = jnp.pad(jnp.stack(vectors), ((SMALLS, 2 * SMALLS - 8 - SMALLS), (0, 0)))
    da_cols = lax.dynamic_slice(da_all, (0, member * cols), (TP * rows, cols))
    chunk = proj_grads(low_one, grads, o_all, da_cols, vectors)
    chunk = chunk.reshape(size["gx"], 2, -1, block, chunk.shape[1])
    keep = lax.dynamic_index_in_dim(chunk, core, 1, keepdims=False)
    send = lax.dynamic_index_in_dim(chunk, 1 - core, 1, keepdims=False)
    other = lax.ppermute(send, "c", [(0, 1), (1, 0)])
    chunk = (keep.astype(f32) + other.astype(f32)).astype(bf16)
    chunk = chunk.reshape(-1, *chunk.shape[2:])
    chunk = lax.all_to_all(chunk, SAME, 0, 0, tiled=True).astype(f32)
    dims = [size[a] for a in SAME]
    chunk = chunk.reshape(*dims, *chunk.shape[1:])
    chunk = jnp.sum(chunk, axis=tuple(i for i, a in enumerate(SAME) if a not in plan.tp))
    chunk = chunk.reshape(TP, block, -1)

    def joined(at):
        return chunk[:, :, at : at + cols].transpose(1, 0, 2).reshape(block, width)

    wide = w_qkv.shape[1]
    vec = jnp.sum(chunk[:, :, wide + cols : wide + cols + 8], axis=0)

    grad_input = plan.move(finish_input(back_one, x_mine, dr, vecs), plan.back)
    return (
        output[None],
        grad_input[None],
        joined(0),
        vec[:, 0],
        joined(cols),
        joined(2 * cols),
        vec[:, 1],
        joined(wide),
        vec[:, 2],
        vec[:, 3],
        vec[:, 4],
        vec[:, 5],
        vec[:, 6],
        g_w_up,
        g_b_up,
        g_w_down,
        vec[:, 7],
    )


def solution(mesh):
    groups, blocks = mesh.shape["grp"], mesh.shape["seq"]
    plan = Plan(groups, blocks)
    fine = Mesh(mesh.devices.reshape(plan.shape), ALL)
    grp, seq = ("gx", "c"), ("sz", "sy")
    matrix, vector = P(ALL, None), P(ALL)
    token = P(grp, seq, None)
    return jax.shard_map(
        functools.partial(local, plan),
        mesh=fine,
        in_specs=(
            token, P(grp, None), P(grp, seq), token,
            matrix, vector, matrix, matrix, vector, matrix, vector,
            vector, vector, vector, vector, matrix, vector, matrix, vector,
        ),
        out_specs=(
            token, token,
            matrix, vector, matrix, matrix, vector, matrix, vector,
            vector, vector, vector, vector, matrix, vector, matrix, vector,
        ),
        check_vma=False,
    )
```

time: 1340 us -> 298 us (0.22)
  waiting for transfers between devices: 1080 us -> 46.3 us
  matrix products: 83.6 us -> 0 us
  Pallas kernels: 0 us -> 55 us
  starting transfers between devices: 1.07 us -> 38.8 us
  local copies, waits for them, and re-layouts: 53 us -> 30.7 us
  blocking collectives: 84.2 us -> 98 us
    reduce_scatter x6 -> x1, waiting for transfers between devices: 627 us -> 0.01 us  [local(): lax.psum_scatter(summed, plan.rep, scatter_dimension=0, tiled=False)]
    all_gather x8 -> x1, waiting for transfers between devices: 346 us -> 0.01 us  [local(): bundle = lax.all_gather(bundle, plan.rep, axis=0, tiled=False)]
    unnamed x18 -> x2, waiting for transfers between devices: 107 us -> 0.03 us
    unnamed x2 -> x0, blocking collectives: 84.2 us -> none
    dot_general x54 -> x0, matrix products: 83.6 us -> none  [the longest x6 20.9 us: contract_rows(): lax.dot_general(left, right, (((0,), (0,)), ((), ())), preferred_element_...]
    all_gather x0 -> x5, blocking collectives: none -> 75 us  [the longest x1 23.3 us: local(): both = lax.all_gather(got, 'c', axis=0, tiled=True)]
    pallas_call x0 -> x10, Pallas kernels: none -> 55 us  [the longest x1 10.8 us: mlp(): pl.pallas_call(mlp_kernel, grid=(rows // step,), in_specs=[token, pl.Bloc...]
    ppermute x0 -> x7, waiting for transfers between devices: none -> 34.9 us  [the longest x4 33.8 us: move(): return lax.ppermute(value, ALL, table)]
  transfers between devices with their start and end apart: 16 -> 14, of which waited for: 16 -> 6; matrix products, arithmetic and copies ran while one was open for 8% -> 7% of each run, Pallas kernels for 0% -> 13%
where the time goes in v1:
time: 298 us; the launch traced here: 294 us
  blocking collectives  98 us (33%)
  Pallas kernels  55 us (18%)
  waiting for transfers between devices  46.3 us (16%)
  starting transfers between devices  38.8 us (13%)
  local copies, waits for them, and re-layouts  30.7 us (10%)
  between operations  14.7 us (5%)
  other arithmetic  10.5 us (4%)
    ppermute x4, waiting for transfers between devices, move(): return lax.ppermute(value, ALL, table)  33.8 us
    all_gather x1, blocking collectives, local(): both = lax.all_gather(got, 'c', axis=0, tiled=True)  23.3 us
    all_gather x1, blocking collectives, local(): o_all = lax.all_gather(mixed, plan.tp, axis=0, tiled=False)  15.9 us
    all_to_all x1, blocking collectives, local(): lax.all_to_all(dh_two.reshape(TP, rows, width), plan.tp, 0, 0, tiled=True)  13.9 us
    all_gather x1, blocking collectives, local(): da_all = lax.all_gather(da, plan.tp, axis=0, tiled=True)  12.5 us
    all_gather x1, blocking collectives, local(): dm_all = lax.all_gather(dm_mine, plan.tp, axis=0, tiled=True)  12.2 us
    ppermute x4, starting transfers between devices, move(): return lax.ppermute(value, ALL, table)  11.5 us
    all_gather x1, blocking collectives, local(): x_all = lax.all_gather(x_mine, plan.tp, axis=0, tiled=True)  11 us
  transfers between devices with their start and end apart: 14, of which 6 were waited for; matrix products, arithmetic and copies ran while one was open for 7% of the time, Pallas kernels for 13%

profile of v1, /device:TPU:2, one launch (start us, length us, event | category | flops | bytes accessed | tf_op | source)
XLA Modules:
  0.0 294.1 jit_solution(2764051447850446192)
XLA Ops:
  9.6 9.1 %all_to_all.35 = bf16[4,48,768]{2,1,0:T(8,128)(2,1)S(1)} all-to-all(bf16[4,48,768]{2,1,0:T(8,128)(2,1)S(1)} %pad_maximum_fusion), channel_id=1, replica_groups=mesh['gx'=2,'c'=2,'sz'=4,'sy'=2] {'gx','sy'}, dimensions={0} | all-to-all | bytes 589824 | tf_op jit(solution)/shard_map/all_to_all | solution.py:640
  21.2 6.4 %all-to-all-start = ((bf16[16,24,640]{2,1,0:T(8,128)(2,1)}), bf16[16,24,640]{2,1,0:T(8,128)(2,1)S(1)}, u32[]{:S(2)}, u32[]{:S(2)}) async-start(bf16[16,24,640]{2,1,0:T(8,128)(2,1)} %bitcast.15), calls=%async_computation | async-start | bytes 983040 | tf_op jit(solution)/shard_map/all_to_all | solution.py:628
  27.8 4.3 %collective-permute-start.2 = (bf16[128,768]{1,0:T(8,128)(2,1)S(1)}, bf16[128,768]{1,0:T(8,128)(2,1)S(1)}, u32[]{:S(2)}, u32[]{:S(2)}) collective-permute-start(bf16[128,768]{1,0:T(8,128)(2,1)S(1)} %fusion.5), channel_id=1, source_target_pairs={{0,0},{1,1},{2,16},{3,17},{4,8},{5,9},{6,24},{7,25},{8,2},{9,3},{1... | collective-permute-start | bytes 589832 | tf_op jit(solution)/shard_map/ppermute | solution.py:50
  34.7 18.1 %collective-permute-done.2.dm_ref = bf16[128,768]{1,0:T(8,128)(2,1)S(1)} collective-permute-done((bf16[128,768]{1,0:T(8,128)(2,1)S(1)}, bf16[128,768]{1,0:T(8,128)(2,1)S(1)}, u32[]{:S(2)}, u32[]{:S(2)}) %collective-permute-start.2) | collective-permute-done | bytes 196640 | tf_op jit(solution)/shard_map/ppermute | solution.py:50
  52.7 12.2 %all_gather.28.dm_ref = bf16[512,768]{1,0:T(8,128)(2,1)} all-gather(bf16[128,768]{1,0:T(8,128)(2,1)S(1)} %collective-permute-done.2.dm_ref), channel_id=1, replica_groups=mesh['gx'=2,'c'=2,'sz'=4,'sy'=2] {'gx','sy'}, dimensions={0}, use_global_device_ids=true | all-gather | bytes 983040 | tf_op jit(solution)/shard_map/all_gather | solution.py:674
  65.0 11.0 %all_gather.24.x_ref = bf16[512,768]{1,0:T(8,128)(2,1)} all-gather(bf16[128,768]{1,0:T(8,128)(2,1)S(1)} %slice.139.x_ref), channel_id=1, replica_groups=mesh['gx'=2,'c'=2,'sz'=4,'sy'=2] {'gx','sy'}, dimensions={0}, use_global_device_ids=true | all-gather | bytes 983040 | tf_op jit(solution)/shard_map/all_gather | solution.py:663
  76.0 23.3 %all_gather.25 = bf16[32,24,640]{2,1,0:T(8,128)(2,1)S(1)} all-gather(bf16[16,24,640]{2,1,0:T(8,128)(2,1)S(1)} %all-to-all-done), channel_id=1, replica_groups=mesh['gx'=2,'c'=2,'sz'=4,'sy'=2] {'c'}, dimensions={0}, use_global_device_ids=true | all-gather | bytes 1474560 | tf_op jit(solution)/shard_map/all_gather | solution.py:629
  101.0 4.6 %qkv.1 = (bf16[512,768]{1,0:T(8,128)(2,1)}, bf16[512,192]{1,0:T(8,128)(2,1)}, bf16[2,512,192]{2,1,0:T(8,128)(2,1)}) custom-call(bf16[512,768]{1,0:T(8,128)(2,1)} %all_gather.24.x_ref, bf16[768,640]{1,0:T(8,128)(2,1)} %bitcast.107, f32[8,768]{1,0:T(8,128)} %get-tuple-element.89.vec_ref, f32[2,192]{1,0:T(2,128)} %dynamic-slice_bitcast_fusion.1.bias_ref), custom_call_target="tpu_custom_call" | custom-call | flops 452984832 | bytes 3145728 | tf_op jit(solution)/shard_map/qkv/pallas_call | solution.py:117
  108.5 7.2 %attend.1 = (bf16[512,192]{1,0:T(8,128)(2,1)}, f32[8,512]{1,0:T(8,128)}) custom-call(s32[2]{0:T(128)} %pad_add_fusion.idx_ref, f32[1,1024]{1,0:T(1,128)} %slice_convert_fusion.1.ids_ref, bf16[512,192]{1,0:T(8,128)(2,1)} %get-tuple-element.41.q_ref, bf16[2,512,192]{2,1,0:T(8,128)(2,1)} %get-tuple-element.42.refs_0_, bf16[2,512,192]{2,1,0:T(8,128)(2,1)} %copy-done.25), custom_call_target="tpu_custom_call" | custom-call | flops 402653184 | bytes 786432 | tf_op jit(solution)/shard_map/attend/pallas_call | solution.py:196
  115.7 15.9 %all-gather = bf16[2048,192]{1,0:T(8,128)(2,1)} all-gather(bf16[512,192]{1,0:T(8,128)(2,1)} %get-tuple-element.43), channel_id=2, replica_groups=mesh['gx'=2,'c'=2,'sz'=4,'sy'=2] {'gx','sy'}, dimensions={0}, use_global_device_ids=true | all-gather | bytes 983040 | tf_op jit(solution)/shard_map/all_gather | solution.py:673
  138.4 10.8 %mlp.1 = (f32[512,768]{1,0:T(8,128)}, bf16[512,768]{1,0:T(8,128)(2,1)}, bf16[512,768]{1,0:T(8,128)(2,1)}, bf16[512,768]{1,0:T(8,128)(2,1)}, bf16[512,768]{1,0:T(...) custom-call(bf16[512,768]{1,0:T(8,128)(2,1)} %all_gather.24.x_ref, ...), custom_call_target="tpu_custom_call" | custom-call | flops 3019898880 | bytes 9437184 | tf_op jit(solution)/shard_map/mlp/pallas_call | solution.py:359
  149.3 5.1 %mlp_weight_grads.1 = (bf16[768,768]{1,0:T(8,128)(2,1)}, bf16[768,768]{1,0:T(8,128)(2,1)}) custom-call(bf16[512,768]{1,0:T(8,128)(2,1)} %get-tuple-element.59.h_ref, bf16[512,768]{1,0:T(8,128)(2,1)} %get-tuple-element.60.du_ref, bf16[512,768]{1,0:T(8,128)(2,1)} %get-tuple-element.61.a_ref, bf16[512,768]{1,0:T(8,128)(2,1)} %all_gather.28.dm_ref), custom_call_target="tpu_custom_call" | custom-call | flops 1207959552 | bytes 4718592 | tf_op jit(solution)/shard_map/mlp_weight_grads/pallas_call | solution.py:398
  159.5 13.9 %all_to_all.36.parts_ref = bf16[4,128,768]{2,1,0:T(8,128)(2,1)} all-to-all(bf16[4,128,768]{2,1,0:T(8,128)(2,1)S(1)} %bitcast.134), channel_id=1, replica_groups=mesh['gx'=2,'c'=2,'sz'=4,'sy'=2] {'gx','sy'}, dimensions={0} | all-to-all | bytes 1572864 | tf_op jit(solution)/shard_map/all_to_all | solution.py:680
  176.6 12.5 %all_gather.31.da_ref = bf16[512,768]{1,0:T(8,128)(2,1)} all-gather(bf16[128,768]{1,0:T(8,128)(2,1)} %get-tuple-element.47), channel_id=1, replica_groups=mesh['gx'=2,'c'=2,'sz'=4,'sy'=2] {'gx','sy'}, dimensions={0}, use_global_device_ids=true | all-gather | bytes 983040 | tf_op jit(solution)/shard_map/all_gather | solution.py:683
  189.1 10.2 %attend_back.1 = (bf16[512,192]{1,0:T(8,128)(2,1)}, f32[2,512,192]{2,1,0:T(8,128)}, bf16[2,512,192]{2,1,0:T(8,128)(2,1)}) custom-call(s32[2]{0:T(128)} %pad_add_fusion.idx_ref, f32[1,1024]{1,0:T(1,128)} %slice_convert_fusion.1.ids_ref, bf16[512,192]{1,0:T(8,128)(2,1)} %get-tuple-element.41.q_ref, bf16[512,768]{1,0:T(8,128)(2,1)} %all_gather.31.da_ref, ...), custom_call_target="tpu_custom_call" | custom-call | flops 1006632960 | bytes 2359296 | tf_op jit(solution)/shard_map/attend_back/pallas_call | solution.py:282
  200.1 4.0 %all-to-all-start.2 = ((bf16[4,128,768]{2,1,0:T(8,128)(2,1)}), bf16[4,128,768]{2,1,0:T(8,128)(2,1)S(1)}, u32[]{:S(2)}, u32[]{:S(2)}) async-start(bf16[4,128,768]{2,1,0:T(8,128)(2,1)} %bitcast.40), calls=%async_computation.2 | async-start | bytes 1572864 | tf_op jit(solution)/shard_map/all_to_all | solution.py:684
  207.6 4.9 %normed_back.1 = (bf16[512,640]{1,0:T(8,128)(2,1)}, bf16[512,768]{1,0:T(8,128)(2,1)}, f32[8,768]{1,0:T(8,128)}) custom-call(bf16[512,768]{1,0:T(8,128)(2,1)} %all_gather.24.x_ref, bf16[512,192]{1,0:T(8,128)(2,1)} %get-tuple-element.49.dq_ref, f32[2,512,192]{2,1,0:T(8,128)} %get-tuple-element.50.own_ref, bf16[2,512,192]{2,1,0:T(8,128)(2,1)} %copy-done.8, ...), custom_call_target="tpu_custom_call" | custom-call | flops 503316480 | bytes 4718592 | tf_op jit(solution)/shard_map/normed_back/pallas_call | solution.py:541
  215.1 4.0 %proj_grads.1 = bf16[768,896]{1,0:T(8,128)(2,1)} custom-call(bf16[512,768]{1,0:T(8,128)(2,1)} %get-tuple-element.54.h_ref, bf16[512,640]{1,0:T(8,128)(2,1)} %get-tuple-element.55.d_ref, bf16[4,512,192]{2,1,0:T(8,128)(2,1)} %bitcast.117, bf16[512,192]{1,0:T(8,128)(2,1)} %constant_dynamic-slice_fusion.da_ref, f32[128,768]{1,0:T(8,128)} %pad.23.v_ref), custom_call_target="tpu_custom_call" | custom-call | flops 704643072 | bytes 4128768 | tf_op jit(solution)/shard_map/proj_grads/pallas_call | solution.py:582
  221.4 4.3 %all-to-all-start.4 = ((bf16[4,128,768]{2,1,0:T(8,128)(2,1)}), bf16[4,128,768]{2,1,0:T(8,128)(2,1)S(1)}, u32[]{:S(2)}, u32[]{:S(2)}) async-start(bf16[4,128,768]{2,1,0:T(8,128)(2,1)} %bitcast.133), calls=%async_computation.4 | async-start | bytes 1572864 | tf_op jit(solution)/shard_map/all_to_all | solution.py:711
  227.8 8.5 %all-to-all-done.4.parts_ref = bf16[4,128,768]{2,1,0:T(8,128)(2,1)S(1)} async-done(((bf16[4,128,768]{2,1,0:T(8,128)(2,1)}), bf16[4,128,768]{2,1,0:T(8,128)(2,1)S(1)}, u32[]{:S(2)}, u32[]{:S(2)}) %all-to-all-start.4) | async-done | bytes 786464 | tf_op jit(solution)/shard_map/all_to_all | solution.py:711
  236.4 7.8 %all-to-all-start.5 = ((bf16[16,24,896]{2,1,0:T(8,128)(2,1)}), bf16[16,24,896]{2,1,0:T(8,128)(2,1)S(1)}, u32[]{:S(2)}, u32[]{:S(2)}) async-start(bf16[16,24,896]{2,1,0:T(8,128)(2,1)} %bitcast.121), calls=%async_computation.5 | async-start | bytes 1376256 | tf_op jit(solution)/shard_map/all_to_all | solution.py:735
  246.9 3.4 %collective-permute-start.3 = (bf16[128,768]{1,0:T(8,128)(2,1)}, bf16[128,768]{1,0:T(8,128)(2,1)S(1)}, u32[]{:S(2)}, u32[]{:S(2)}) collective-permute-start(bf16[128,768]{1,0:T(8,128)(2,1)} %finish_output.1), channel_id=1, source_target_pairs={{0,0},{1,1},{16,2},{17,3},{8,4},{9,5},{24,6},{25,7},{2,8},{3,9},{1... | collective-permute-start | bytes 589832 | tf_op jit(solution)/shard_map/ppermute | solution.py:50
  254.5 13.6 %collective-permute-done.3 = bf16[128,768]{1,0:T(8,128)(2,1)S(1)} collective-permute-done((bf16[128,768]{1,0:T(8,128)(2,1)}, bf16[128,768]{1,0:T(8,128)(2,1)S(1)}, u32[]{:S(2)}, u32[]{:S(2)}) %collective-permute-start.3) | collective-permute-done | bytes 196640 | tf_op jit(solution)/shard_map/ppermute | solution.py:50
  276.2 4.2 %all-to-all-start.6 = ((bf16[4,24,768]{2,1,0:T(8,128)(2,1)}), bf16[4,24,768]{2,1,0:T(8,128)(2,1)S(1)}, u32[]{:S(2)}, u32[]{:S(2)}) async-start(bf16[4,24,768]{2,1,0:T(8,128)(2,1)} %bitcast.60), calls=%async_computation.7 | async-start | bytes 294912 | tf_op jit(solution)/shard_map/all_to_all | solution.py:702
  (151 shorter events, 60.2 us)
Async XLA Ops:
  7.2 124.4 %all-gather.4.cloned.1.call-start = ((), (), s32[]{:S(2)}) async-start(), calls=%async_computation.9 | async-start | bytes 4091904 | tf_op jit(solution)/shard_map/all_gather | solution.py:651
  9.5 10.5 %copy-start.17 = (bf16[24]{0:T(256)(128)(2,1)S(1)}, bf16[24]{0:T(256)(128)(2,1)}, u32[]{:S(2)}) copy-start(bf16[24]{0:T(256)(128)(2,1)} %param.24) | copy-start | bytes 148
  9.5 10.5 %copy-start.18 = (bf16[24]{0:T(256)(128)(2,1)S(1)}, bf16[24]{0:T(256)(128)(2,1)}, u32[]{:S(2)}) copy-start(bf16[24]{0:T(256)(128)(2,1)} %param.27) | copy-start | bytes 148
  9.5 10.5 %copy-start.19 = (bf16[24]{0:T(256)(128)(2,1)S(1)}, bf16[24]{0:T(256)(128)(2,1)}, u32[]{:S(2)}) copy-start(bf16[24]{0:T(256)(128)(2,1)} %param.29) | copy-start | bytes 148
  9.5 10.5 %copy-start.20 = (bf16[24]{0:T(256)(128)(2,1)S(1)}, bf16[24]{0:T(256)(128)(2,1)}, u32[]{:S(2)}) copy-start(bf16[24]{0:T(256)(128)(2,1)} %param.30) | copy-start | bytes 148
  9.5 10.5 %copy-start.21 = (bf16[24]{0:T(256)(128)(2,1)S(1)}, bf16[24]{0:T(256)(128)(2,1)}, u32[]{:S(2)}) copy-start(bf16[24]{0:T(256)(128)(2,1)} %param.31) | copy-start | bytes 148
  9.5 10.5 %copy-start.22 = (bf16[24]{0:T(256)(128)(2,1)S(1)}, bf16[24]{0:T(256)(128)(2,1)}, u32[]{:S(2)}) copy-start(bf16[24]{0:T(256)(128)(2,1)} %param.32) | copy-start | bytes 148
  19.7 12.3 %copy-start.15 = (s32[1,1024]{1,0:T(1,128)S(1)}, s32[1,1024]{1,0:T(1,128)}, u32[]{:S(2)}) copy-start(s32[1,1024]{1,0:T(1,128)} %param.20) | copy-start | bytes 12292
  19.9 12.3 %copy-start.10 = (bf16[1,128,768]{2,1,0:T(8,128)(2,1)S(1)}, bf16[1,128,768]{2,1,0:T(8,128)(2,1)}, u32[]{:S(2)}) copy-start(bf16[1,128,768]{2,1,0:T(8,128)(2,1)} %param.19) | copy-start | bytes 589828
  21.2 54.8 %all-to-all-start = ((bf16[16,24,640]{2,1,0:T(8,128)(2,1)}), bf16[16,24,640]{2,1,0:T(8,128)(2,1)S(1)}, u32[]{:S(2)}, u32[]{:S(2)}) async-start(bf16[16,24,640]{2,1,0:T(8,128)(2,1)} %bitcast.15), calls=%async_computation | async-start | bytes 983040 | tf_op jit(solution)/shard_map/all_to_all | solution.py:628
  27.6 246.9 %reduce-scatter.2.cloned.1.call-start = ((), (), s32[]{:S(2)}) async-start(), calls=%async_computation.8 | async-start | bytes 2764800 | tf_op jit(solution)/shard_map/reduce_scatter | solution.py:699
  27.8 25.0 %collective-permute-start.2 = (bf16[128,768]{1,0:T(8,128)(2,1)S(1)}, bf16[128,768]{1,0:T(8,128)(2,1)S(1)}, u32[]{:S(2)}, u32[]{:S(2)}) collective-permute-start(bf16[128,768]{1,0:T(8,128)(2,1)S(1)} %fusion.5), channel_id=1, source_target_pairs={{0,0},{1,1},{2,16},{3,17},{4,8},{5,9},{6,24},{7,25},{8,2},{9,3},{1... | collective-permute-start | bytes 589832 | tf_op jit(solution)/shard_map/ppermute | solution.py:50
  32.2 32.8 %collective-permute-start = (bf16[136,768]{1,0:T(8,128)(2,1)S(1)}, bf16[136,768]{1,0:T(8,128)(2,1)S(1)}, u32[]{:S(2)}, u32[]{:S(2)}) collective-permute-start(bf16[136,768]{1,0:T(8,128)(2,1)S(1)} %pad_maximum_fusion.1), channel_id=1, source_target_pairs={{0,0},{1,1},{2,16},{3,17},{4,8},{5,9},{6,24},{7,25},{8,2},{9,3},{1... | collective-permute-start | bytes 626696 | tf_op jit(solution)/shard_map/ppermute | solution.py:50
  52.7 46.6 %copy-start.7 = (bf16[128,768]{1,0:T(8,128)(2,1)}, bf16[128,768]{1,0:T(8,128)(2,1)S(1)}, u32[]{:S(2)}) copy-start(bf16[128,768]{1,0:T(8,128)(2,1)S(1)} %collective-permute-done.2.dm_ref) | copy-start | bytes 589828
  64.9 34.5 %copy-start.4 = (bf16[128,768]{1,0:T(8,128)(2,1)}, bf16[128,768]{1,0:T(8,128)(2,1)S(1)}, u32[]{:S(2)}) copy-start(bf16[128,768]{1,0:T(8,128)(2,1)S(1)} %slice.139.x_ref) | copy-start | bytes 589828
  105.6 2.1 collective-permute-start.1
  199.3 7.5 %collective-permute-start.4 = (bf16[2,512,192]{2,1,0:T(8,128)(2,1)}, bf16[2,512,192]{2,1,0:T(8,128)(2,1)S(1)}, u32[]{:S(2)}, u32[]{:S(2)}) collective-permute-start(bf16[2,512,192]{2,1,0:T(8,128)(2,1)} %get-tuple-element.51), channel_id=1, source_target_pairs={{0,8},{8,0},{1,9},{9,1},{2,10},{10,2},{3,11},{11,3},{4,12},{12,4},... | collective-permute-start | bytes 1179656 | tf_op jit(solution)/shard_map/ppermute | solution.py:669
  200.1 21.3 %all-to-all-start.2 = ((bf16[4,128,768]{2,1,0:T(8,128)(2,1)}), bf16[4,128,768]{2,1,0:T(8,128)(2,1)S(1)}, u32[]{:S(2)}, u32[]{:S(2)}) async-start(bf16[4,128,768]{2,1,0:T(8,128)(2,1)} %bitcast.40), calls=%async_computation.2 | async-start | bytes 1572864 | tf_op jit(solution)/shard_map/all_to_all | solution.py:684
  221.2 4.5 %collective-permute-start.6 = (bf16[2,8,24,896]{3,2,1,0:T(8,128)(2,1)}, bf16[2,8,24,896]{3,2,1,0:T(8,128)(2,1)}, u32[]{:S(2)}, u32[]{:S(2)}) collective-permute-start(bf16[2,8,24,896]{3,2,1,0:T(8,128)(2,1)} %dynamic-slice_bitcast_fusion), channel_id=1, source_target_pairs={{0,8},{8,0},{1,9},{9,1},{2,10},{10,2},{3,11},{11,3},{4,12},{12,4},... | collective-permute-start | bytes 2064392 | tf_op jit(solution)/shard_map/ppermute | solution.py:732
  221.4 15.0 %all-to-all-start.4 = ((bf16[4,128,768]{2,1,0:T(8,128)(2,1)}), bf16[4,128,768]{2,1,0:T(8,128)(2,1)S(1)}, u32[]{:S(2)}, u32[]{:S(2)}) async-start(bf16[4,128,768]{2,1,0:T(8,128)(2,1)} %bitcast.133), calls=%async_computation.4 | async-start | bytes 1572864 | tf_op jit(solution)/shard_map/all_to_all | solution.py:711
  236.4 33.9 %all-to-all-start.5 = ((bf16[16,24,896]{2,1,0:T(8,128)(2,1)}), bf16[16,24,896]{2,1,0:T(8,128)(2,1)S(1)}, u32[]{:S(2)}, u32[]{:S(2)}) async-start(bf16[16,24,896]{2,1,0:T(8,128)(2,1)} %bitcast.121), calls=%async_computation.5 | async-start | bytes 1376256 | tf_op jit(solution)/shard_map/all_to_all | solution.py:735
  246.9 21.3 %collective-permute-start.3 = (bf16[128,768]{1,0:T(8,128)(2,1)}, bf16[128,768]{1,0:T(8,128)(2,1)S(1)}, u32[]{:S(2)}, u32[]{:S(2)}) collective-permute-start(bf16[128,768]{1,0:T(8,128)(2,1)} %finish_output.1), channel_id=1, source_target_pairs={{0,0},{1,1},{16,2},{17,3},{8,4},{9,5},{24,6},{25,7},{2,8},{3,9},{1... | collective-permute-start | bytes 589832 | tf_op jit(solution)/shard_map/ppermute | solution.py:50
  252.6 17.6 %collective-permute-start.5 = (bf16[128,768]{1,0:T(8,128)(2,1)}, bf16[128,768]{1,0:T(8,128)(2,1)S(1)}, u32[]{:S(2)}, u32[]{:S(2)}) collective-permute-start(bf16[128,768]{1,0:T(8,128)(2,1)} %finish_input.1), channel_id=1, source_target_pairs={{0,0},{1,1},{16,2},{17,3},{8,4},{9,5},{24,6},{25,7},{2,8},{3,9},{1... | collective-permute-start | bytes 589832 | tf_op jit(solution)/shard_map/ppermute | solution.py:50
  276.2 8.2 %all-to-all-start.6 = ((bf16[4,24,768]{2,1,0:T(8,128)(2,1)}), bf16[4,24,768]{2,1,0:T(8,128)(2,1)S(1)}, u32[]{:S(2)}, u32[]{:S(2)}) async-start(bf16[4,24,768]{2,1,0:T(8,128)(2,1)} %bitcast.60), calls=%async_computation.7 | async-start | bytes 294912 | tf_op jit(solution)/shard_map/all_to_all | solution.py:702
  (17 other events, 118.9 us)
Sparse Core Ops, SparseCore 0:
  19.7 52.9 all-gather.3
  158.5 58.4 reduce-scatter.1

commit v2 on v1

v2 whole, which is shorter than its diff:
```python
import functools

import jax
import jax.numpy as jnp
from jax import lax
from jax.experimental import pallas as pl
from jax.experimental.pallas import tpu as pltpu
from jax.sharding import Mesh, PartitionSpec as P

HEADS = 12
HEAD_DIM = 64
TP = 4
HEADS_TP = HEADS // TP
EPS = 1e-05
NEG = -1e30
SCALE = 0.125
ALL = ("gx", "c", "sz", "sy")
SAME = ("gx", "sz", "sy")
SMALLS = 64
f32 = jnp.float32
bf16 = jnp.bfloat16


class Plan:
    def __init__(self, groups, blocks):
        if (groups, blocks) == (4, 8):
            self.shape = (2, 2, 4, 2)
            self.tp, self.half, self.rep = ("gx", "sy"), "c", ("c", "sz")
            self.fast = True
        else:
            self.shape = (groups // 2, 2, blocks // TP, TP)
            self.tp, self.half, self.rep = ("sy",), "sz", ("gx", "c", "sz")
            self.fast = False
        self.size = dict(zip(ALL, self.shape))
        self.devices = groups * blocks
        self.parts = self.size[self.half]
        self.copies = self.devices // TP
        self.lines = tuple(a for a in self.rep if a != "c")
        self.route = []
        for src in range(self.devices):
            seq, block = divmod(src, blocks)
            part, member = divmod(block, TP)
            if self.tp == ("sy",):
                dst = src
            else:
                dst = (((member >> 1) * 2 + part) * 4 + seq) * 2 + (member & 1)
            self.route.append((src, dst))
        self.back = [(dst, src) for src, dst in self.route]

    def swap(self, value):
        return lax.ppermute(value, "c", [(0, 1), (1, 0)])

    def partner(self, value, j):
        table = [(t, t ^ j) for t in range(TP)]
        return lax.ppermute(value, self.tp, table)

    def partners(self, value):
        return [value] + [self.partner(value, j) for j in range(1, TP)]

    def reduce(self, values):
        return [values[0]] + [self.partner(values[j], j) for j in range(1, TP)]

    def turn(self, value, axis, by):
        count = self.size[axis]
        return lax.ppermute(value, axis, [(i, (i + by) % count) for i in range(count)])

    def place(self, r):
        at, rest = {}, r
        for axis in reversed(ALL):
            rest, at[axis] = divmod(rest, self.size[axis])
        numbers = []
        for axes in (self.tp, self.rep):
            number = 0
            for axis in axes:
                number = number * self.size[axis] + at[axis]
            numbers.append(number)
        return tuple(numbers)

    def same(self, n):
        span = self.devices // 2 // self.size["gx"]
        gx, rest = divmod(n, span)
        return gx * 2 * span + rest

    def move(self, value, table):
        if all(a == b for a, b in table):
            return value
        return lax.ppermute(value, ALL, table)

    def shuffle(self, value, before, after):
        tail = value.shape[1:]
        dims = [self.size[a] for a in before]
        order = [before.index(a) for a in after]
        value = value.reshape(*dims, *tail)
        value = value.transpose(*order, *range(len(dims), len(dims) + len(tail)))
        return value.reshape(-1, *tail)


def dot(left, right, left_dim=1, right_dim=0):
    return lax.dot_general(
        left, right, (((left_dim,), (right_dim,)), ((), ())), preferred_element_type=f32
    )


def unit(values):
    center = values - jnp.mean(values, axis=-1, keepdims=True)
    variance = jnp.mean(center * center, axis=-1, keepdims=True)
    rstd = lax.rsqrt(variance + EPS)
    return center * rstd, rstd


def unit_back(grad_unit, units, rstd):
    first = jnp.mean(grad_unit, axis=-1, keepdims=True)
    second = jnp.mean(grad_unit * units, axis=-1, keepdims=True)
    return rstd * (grad_unit - first - units * second)


def params(limit=60 * 1024 * 1024, axes=1):
    return pltpu.CompilerParams(
        dimension_semantics=("arbitrary",) * axes, vmem_limit_bytes=limit
    )


def cost(flops, nbytes, trans=0):
    return pl.CostEstimate(flops=int(flops), bytes_accessed=int(nbytes), transcendentals=int(trans))


def whole(shape):
    zeros = (0,) * len(shape)
    return pl.BlockSpec(shape, lambda *_: zeros)


def head_lanes(value, head):
    lane = lax.broadcasted_iota(jnp.int32, value.shape, 1)
    keep = (lane >= head * HEAD_DIM) & (lane < (head + 1) * HEAD_DIM)
    return jnp.where(keep, value, jnp.zeros_like(value))


def member_cols(row, member, cols):
    out = jnp.zeros((row.shape[0], cols), row.dtype)
    for j in range(TP):
        out = jnp.where(member == j, row[:, j * cols : (j + 1) * cols], out)
    return out


def prep_kernel(rep_of, idx_ref, q_ref, k_ref, v_ref, small_ref, up_ref, *refs):
    chunk_refs, hold_ref = refs[:-1], refs[-1]
    block, width = q_ref.shape
    cols = width // TP
    wide = 3 * cols + SMALLS
    slab = up_ref.shape[1] // len(rep_of)
    for j in range(TP):
        at = slice(j * cols, (j + 1) * cols)
        hold_ref[j, :, :wide] = jnp.concatenate(
            [r[:, at].astype(f32) for r in (q_ref, k_ref, v_ref)] + [small_ref[...].astype(f32)],
            axis=1,
        )
    for r, (member, copy) in enumerate(rep_of):
        first = wide + copy * slab
        hold_ref[member, :, first : first + slab] = up_ref[:, r * slab : (r + 1) * slab].astype(f32)
    for j, ref in enumerate(chunk_refs):
        ref[...] = hold_ref[idx_ref[0] ^ j].astype(bf16)


def prepare(plan, idx, w_query, w_key, w_value, small, w_up):
    block, width = w_query.shape
    rep_of = [plan.place(r) for r in range(plan.devices)]
    shape = (block, 3 * width // TP + SMALLS + w_up.shape[1] // TP)
    return pl.pallas_call(
        functools.partial(prep_kernel, rep_of),
        in_specs=[pl.BlockSpec(memory_space=pltpu.SMEM)]
        + [pl.BlockSpec(memory_space=pltpu.VMEM)] * 5,
        out_shape=[jax.ShapeDtypeStruct(shape, bf16)] * TP,
        scratch_shapes=[pltpu.VMEM((TP, *shape), f32)],
        cost_estimate=cost(1000, 4 * w_up.size),
        name="prepare",
    )(idx, w_query, w_key, w_value, small, w_up)


def shards_kernel(idx_ref, *refs):
    part_refs, (proj_ref, up_ref, hold_ref) = refs[:TP], refs[TP:]
    for j, ref in enumerate(part_refs):
        hold_ref[idx_ref[0] ^ j] = ref[...].astype(f32)
    wide = proj_ref.shape[1]
    value = hold_ref[...].reshape(proj_ref.shape[0], -1).astype(bf16)
    proj_ref[...] = value[:, :wide]
    up_ref[...] = value[:, wide:]


def shards_of(idx, parts, wide):
    block, both = parts[0].shape
    return pl.pallas_call(
        shards_kernel,
        in_specs=[pl.BlockSpec(memory_space=pltpu.SMEM)]
        + [pl.BlockSpec(memory_space=pltpu.VMEM)] * TP,
        out_shape=[
            jax.ShapeDtypeStruct((TP * block, wide), bf16),
            jax.ShapeDtypeStruct((TP * block, both - wide), bf16),
        ],
        scratch_shapes=[pltpu.VMEM((TP, block, both), f32)],
        cost_estimate=cost(1000, 8 * TP * block * both),
        name="shards_of",
    )(idx, *parts)


def assemble_kernel(plan, idx_ref, *refs):
    lines = plan.copies // 2
    sides = refs[: 2 * (1 + lines + TP)]
    up_ref, out_ref, down_ref, row_ref, wide_ref = refs[2 * (1 + lines + TP) :]
    member, core, line = idx_ref[0], idx_ref[2], idx_ref[3]
    block = up_ref.shape[0] // plan.devices
    slab = down_ref.shape[2]
    pair = plan.size["sy"] * block
    for n, side in ((0, core), (1, 1 - core)):
        mine = sides[n * (1 + lines + TP) : (n + 1) * (1 + lines + TP)]
        raw_ref, up_refs, out_refs = mine[0], mine[1 : 1 + lines], mine[1 + lines :]
        for z in range(lines):
            down_ref[side, z] = raw_ref[z, block : block + slab, :]
            row_ref[side, z] = raw_ref[z, block + slab :, :]
        for j, ref in enumerate(up_refs):
            z = lax.rem(line + j, lines)
            value = ref[...].astype(f32)
            for gx in range(plan.size["gx"]):
                for sy in range(plan.size["sy"]):
                    at = gx * pair + sy * block
                    wide_ref[0, gx * 2 + side, z, sy] = value[at : at + block]
        for j, ref in enumerate(out_refs):
            other = member ^ j
            gx, sy = other // plan.size["sy"], lax.rem(other, plan.size["sy"])
            for z in range(lines):
                wide_ref[1, gx * 2 + side, z, sy] = ref[z].astype(f32)
    for ref, k in ((up_ref, 0), (out_ref, 1)):
        ref[...] = wide_ref[k].reshape(ref.shape).astype(bf16)


def assemble(plan, idx, own, other, block, slab):
    width = own[0].shape[2]
    lines = plan.copies // 2
    hidden = plan.copies * slab
    operands = [*own, *other]
    return pl.pallas_call(
        functools.partial(assemble_kernel, plan),
        in_specs=[pl.BlockSpec(memory_space=pltpu.SMEM)]
        + [pl.BlockSpec(memory_space=pltpu.VMEM)] * len(operands),
        out_shape=[
            jax.ShapeDtypeStruct((width, hidden), bf16),
            jax.ShapeDtypeStruct((width, width), bf16),
            jax.ShapeDtypeStruct((2, lines, slab, width), bf16),
            jax.ShapeDtypeStruct((2, lines, 8, width), bf16),
        ],
        scratch_shapes=[
            pltpu.VMEM((2, 2 * plan.size["gx"], lines, plan.size["sy"], block, width), f32)
        ],
        compiler_params=pltpu.CompilerParams(vmem_limit_bytes=60 * 1024 * 1024),
        cost_estimate=cost(1000, 12 * width * width),
        name="assemble",
    )(idx, *operands)


def qkv_kernel(plan, idx_ref, x_ref, *refs):
    fast = plan.fast
    if fast:
        own_ref, other_ref, h_ref, q_ref, kv_ref, w_ref, vec_ref, wide_ref = refs
    else:
        w_ref, vec_ref, h_ref, q_ref, kv_ref = refs
    cols = q_ref.shape[1]
    if fast:

        @pl.when(pl.program_id(0) == 0)
        def _():
            core = idx_ref[2]
            line = idx_ref[3]
            lines, rows, _ = own_ref.shape
            pair = rows // plan.size["gx"]
            for ref, side in ((own_ref, core), (other_ref, 1 - core)):
                for j in range(lines):
                    z = lax.rem(line + j, lines)
                    value = ref[j].astype(f32)
                    for gx in range(plan.size["gx"]):
                        wide_ref[gx * 2 + side, z] = value[gx * pair : (gx + 1) * pair, :]
            table = wide_ref[...].reshape(w_ref.shape)
            w_ref[...] = table.astype(bf16)
            vec_ref[...] = table[:, 512:640].T[64:72, :]

    units, _ = unit(x_ref[...].astype(f32))
    low = (units * vec_ref[3:4, :] + vec_ref[4:5, :]).astype(bf16)
    h_ref[...] = low
    out = dot(low, w_ref[...])
    bias = member_cols(vec_ref[0:2, :], idx_ref[0], cols)
    query = (out[:, :cols] + bias[0:1, :]).astype(bf16)
    q_ref[...] = (query.astype(f32) * SCALE).astype(bf16)
    kv_ref[0] = out[:, cols : 2 * cols].astype(bf16)
    kv_ref[1] = (out[:, 2 * cols : 3 * cols] + bias[1:2, :]).astype(bf16)


def qkv(plan, idx, x_all, *operands):
    rows, width = x_all.shape
    cols = width // TP
    step = rows // TP
    wide = 3 * cols + SMALLS
    out_specs = [
        pl.BlockSpec((step, width), lambda i, *_: (i, 0)),
        pl.BlockSpec((step, cols), lambda i, *_: (i, 0)),
        pl.BlockSpec((2, step, cols), lambda i, *_: (0, i, 0)),
    ]
    out_shape = [
        jax.ShapeDtypeStruct((rows, width), bf16),
        jax.ShapeDtypeStruct((rows, cols), bf16),
        jax.ShapeDtypeStruct((2, rows, cols), bf16),
    ]
    scratch = []
    if plan.fast:
        out_specs += [whole((width, wide)), whole((8, width))]
        out_shape += [
            jax.ShapeDtypeStruct((width, wide), bf16),
            jax.ShapeDtypeStruct((8, width), f32),
        ]
        lines = plan.copies // 2
        scratch = [pltpu.VMEM((2 * plan.size["gx"], lines, width // (2 * plan.size["gx"] * lines), wide), f32)]
    return pl.pallas_call(
        functools.partial(qkv_kernel, plan),
        grid_spec=pltpu.PrefetchScalarGridSpec(
            num_scalar_prefetch=1,
            grid=(TP,),
            in_specs=[pl.BlockSpec((step, width), lambda i, *_: (i, 0))]
            + [whole(v.shape) for v in operands],
            out_specs=out_specs,
            scratch_shapes=scratch,
        ),
        out_shape=out_shape,
        compiler_params=params(),
        cost_estimate=cost(2 * rows * width * 3 * cols, rows * width * 8),
        name="qkv",
    )(idx, x_all, *operands)


def fill_docs(ids_ref, part, parts, doc_ref):
    span, width = doc_ref.shape[1:]
    for j in range(parts):
        at = lax.rem(part + j, parts) * span
        row = ids_ref[0:1, pl.ds(pl.multiple_of(at, 512), span)]
        doc_ref[j] = jnp.broadcast_to(row, (width, span)).T


def fwd_kernel(parts, idx_ref, ids_ref, q_ref, *refs):
    kv_refs = refs[:parts]
    o_ref, lse_ref, turned, doc_ref = refs[parts:]
    step = pl.program_id(0)
    part = idx_ref[1]
    span = kv_refs[0].shape[1]
    width = q_ref.shape[0]

    @pl.when(step == 0)
    def _():
        fill_docs(ids_ref, part, parts, doc_ref)
        for j in range(parts):
            turned[j] = kv_refs[j][1].T

    at = part * span + step * width
    own = ids_ref[0:1, pl.ds(pl.multiple_of(at, 128), width)]
    query = q_ref[...]
    outs, lses = [], []
    for head in range(HEADS_TP):
        masked = head_lanes(query, head)
        scores = []
        for j in range(parts):
            raw = dot(kv_refs[j][0], masked, 1, 1)
            scores.append(jnp.where(doc_ref[j] == own, raw, NEG))
        peak = functools.reduce(
            jnp.maximum, [jnp.max(s, axis=0, keepdims=True) for s in scores]
        )
        exps = [jnp.exp(s - peak) for s in scores]
        total = functools.reduce(jnp.add, [jnp.sum(e, axis=0, keepdims=True) for e in exps])
        scale = 1.0 / total
        acc = None
        for j in range(parts):
            probs = (exps[j] * scale).astype(bf16)
            term = dot(turned[j, head * HEAD_DIM : (head + 1) * HEAD_DIM, :], probs)
            acc = term if acc is None else acc + term
        outs.append(acc)
        lses.append(peak + jnp.log(total))
    o_ref[...] = jnp.concatenate(outs, axis=0).T.astype(bf16)
    for head in range(HEADS_TP):
        lse_ref[head : head + 1, :] = lses[head]


def attend(idx, ids, q, kvs, width=256):
    rows, cols = q.shape
    parts = len(kvs)
    span = kvs[0].shape[1]
    return pl.pallas_call(
        functools.partial(fwd_kernel, parts),
        grid_spec=pltpu.PrefetchScalarGridSpec(
            num_scalar_prefetch=1,
            grid=(rows // width,),
            in_specs=[whole(ids.shape), pl.BlockSpec((width, cols), lambda i, *_: (i, 0))]
            + [whole(kv.shape) for kv in kvs],
            out_specs=[
                pl.BlockSpec((width, cols), lambda i, *_: (i, 0)),
                pl.BlockSpec((8, width), lambda i, *_: (0, i)),
            ],
            scratch_shapes=[
                pltpu.VMEM((parts, cols, span), bf16),
                pltpu.VMEM((parts, span, width), f32),
            ],
        ),
        out_shape=[
            jax.ShapeDtypeStruct((rows, cols), bf16),
            jax.ShapeDtypeStruct((8, rows), f32),
        ],
        compiler_params=params(),
        cost_estimate=cost(4 * rows * span * parts * cols, span * parts * cols * 4, rows * span * parts * HEADS_TP),
        name="attend",
    )(idx, ids, q, *kvs)


def bwd_kernel(parts, idx_ref, ids_ref, q_ref, w_ref, lse_ref, *refs):
    da_refs, refs = refs[:TP], refs[TP:]
    kv_refs = refs[:parts]
    dq_ref, own_ref, cols_ref = refs[parts : parts + 3]
    other_refs = refs[parts + 3 : 2 * parts + 2]
    turned, doc_ref, key_acc, value_acc, mixed_ref = refs[2 * parts + 2 :]
    step = pl.program_id(0)
    part = idx_ref[1]
    span = kv_refs[0].shape[1]
    width, cols = q_ref.shape

    @pl.when(step == 0)
    def _():
        fill_docs(ids_ref, part, parts, doc_ref)
        for j in range(parts):
            turned[j] = kv_refs[j][0].T
        key_acc[...] = jnp.zeros_like(key_acc)
        value_acc[...] = jnp.zeros_like(value_acc)
        member = idx_ref[0]
        for j in range(TP):
            da = da_refs[j][...]
            mixed_ref[member ^ j] = dot(da, w_ref[0], 1, 1).astype(bf16)
            cols_ref[member ^ j] = member_cols(da, member, cols)

    at = part * span + step * width
    own = ids_ref[0:1, pl.ds(pl.multiple_of(at, 128), width)]
    query = q_ref[...]
    group = width // mixed_ref.shape[1]
    grad_mixed = mixed_ref[pl.ds(step * group, group)].reshape(width, cols)
    turned_grads = []
    for head in range(HEADS_TP):
        masked_q = head_lanes(query, head)
        masked_g = head_lanes(grad_mixed, head)
        lse = lse_ref[head : head + 1, :]
        probs, grads = [], []
        for j in range(parts):
            raw = dot(kv_refs[j][0], masked_q, 1, 1)
            probs.append(jnp.exp(jnp.where(doc_ref[j] == own, raw, NEG) - lse))
            grads.append(dot(kv_refs[j][1], masked_g, 1, 1))
        delta = functools.reduce(
            jnp.add,
            [jnp.sum(p * g, axis=0, keepdims=True) for p, g in zip(probs, grads)],
        )
        acc = None
        for j in range(parts):
            grad_scores = (probs[j] * (grads[j] - delta)).astype(bf16)
            value_acc[j] += dot(probs[j].astype(bf16), masked_g)
            key_acc[j] += dot(grad_scores, masked_q)
            term = dot(turned[j, head * HEAD_DIM : (head + 1) * HEAD_DIM, :], grad_scores)
            acc = term if acc is None else acc + term
        turned_grads.append(acc)
    dq_ref[...] = (jnp.concatenate(turned_grads, axis=0).T * SCALE).astype(bf16)

    @pl.when(step == pl.num_programs(0) - 1)
    def _():
        own_ref[0] = key_acc[0]
        own_ref[1] = value_acc[0]
        for j in range(1, parts):
            other_refs[j - 1][0] = key_acc[j].astype(bf16)
            other_refs[j - 1][1] = value_acc[j].astype(bf16)


def attend_back(idx, ids, q, das, w_out, lse, kvs, width=256):
    rows, cols = q.shape
    step, model = das[0].shape
    parts = len(kvs)
    span = kvs[0].shape[1]
    return pl.pallas_call(
        functools.partial(bwd_kernel, parts),
        grid_spec=pltpu.PrefetchScalarGridSpec(
            num_scalar_prefetch=1,
            grid=(rows // width,),
            in_specs=[
                whole(ids.shape),
                pl.BlockSpec((width, cols), lambda i, *_: (i, 0)),
                pl.BlockSpec((1, cols, model), lambda i, idx: (idx[0], 0, 0)),
                pl.BlockSpec((8, width), lambda i, *_: (0, i)),
            ]
            + [whole((step, model))] * TP
            + [whole(kv.shape) for kv in kvs],
            out_specs=[
                pl.BlockSpec((width, cols), lambda i, *_: (i, 0)),
                whole((2, span, cols)),
                whole((TP, step, cols)),
            ]
            + [whole((2, span, cols))] * (parts - 1),
            scratch_shapes=[
                pltpu.VMEM((parts, cols, span), bf16),
                pltpu.VMEM((parts, span, width), f32),
                pltpu.VMEM((parts, span, cols), f32),
                pltpu.VMEM((parts, span, cols), f32),
                pltpu.VMEM((TP, step, cols), bf16),
            ],
        ),
        out_shape=[
            jax.ShapeDtypeStruct((rows, cols), bf16),
            jax.ShapeDtypeStruct((2, span, cols), f32),
            jax.ShapeDtypeStruct((TP, step, cols), bf16),
        ]
        + [jax.ShapeDtypeStruct((2, span, cols), bf16)] * (parts - 1),
        compiler_params=params(),
        cost_estimate=cost(10 * rows * span * parts * cols, span * parts * cols * 12, rows * span * parts * HEADS_TP),
        name="attend_back",
    )(idx, ids, q, w_out, lse, *das, *kvs)


def mlp_kernel(idx_ref, x_ref, *refs):
    o_refs, dm_refs, refs = refs[:TP], refs[TP : 2 * TP], refs[2 * TP :]
    wo_ref, wu_ref, wd_ref, vec_ref, bup_ref, r_ref, h_ref, a_ref, du_ref, dm_ref, sum_ref = refs[:11]
    dh_refs, dm_now, dh_now = refs[11 : 11 + TP], refs[-2], refs[-1]
    step = pl.program_id(0)
    member = idx_ref[0]

    @pl.when(step == 0)
    def _():
        sum_ref[...] = jnp.zeros_like(sum_ref)

    attended = dot(o_refs[0][...], wo_ref[member])
    for j in range(1, TP):
        attended += dot(o_refs[j][...], wo_ref[member ^ j])
    residual = x_ref[...].astype(f32) + (attended + vec_ref[2:3, :])

    for j in range(TP):

        @pl.when(step == j)
        def _(j=j):
            dm_now[...] = dm_refs[j][...]
            if j == 0:
                r_ref[...] = residual

    units, _ = unit(residual)
    low = (units * vec_ref[5:6, :] + vec_ref[6:7, :]).astype(bf16)
    h_ref[...] = low
    pre = dot(low, wu_ref[...]) + bup_ref[...]
    normal = 0.5 * (1.0 + lax.erf(pre * 0.7071067811865476))
    act = (pre * normal).astype(bf16)
    a_ref[...] = act
    slope = normal + pre * (0.3989422804014327 * jnp.exp(-0.5 * pre * pre))
    dm = dm_now[...]
    dm_ref[...] = dm
    grad_pre = (dot(dm, wd_ref[...], 1, 1) * slope).astype(bf16)
    du_ref[...] = grad_pre
    grad = dot(grad_pre, wu_ref[...], 1, 1)
    sum_ref[0:1, :] += jnp.sum(grad * units, axis=0, keepdims=True)
    sum_ref[1:2, :] += jnp.sum(grad, axis=0, keepdims=True)
    dh_now[...] = grad.astype(bf16)
    for j in range(TP):

        @pl.when(step == j)
        def _(j=j):
            dh_refs[j][...] = dh_now[...]


def mlp(idx, x_all, os, dms, w_out, w_up, w_down, vecs, b_up):
    rows, width = x_all.shape
    hidden = w_up.shape[1]
    cols = width // TP
    step = rows // TP
    token = pl.BlockSpec((step, width), lambda i, idx: (i ^ idx[0], 0))
    inner = pl.BlockSpec((step, hidden), lambda i, idx: (i ^ idx[0], 0))
    head = pl.BlockSpec((step, cols), lambda i, idx: (i ^ idx[0], 0))
    one = whole((step, width))
    return pl.pallas_call(
        mlp_kernel,
        grid_spec=pltpu.PrefetchScalarGridSpec(
            num_scalar_prefetch=1,
            grid=(TP,),
            in_specs=[token]
            + [head] * TP
            + [one] * TP
            + [whole(v.shape) for v in (w_out, w_up, w_down, vecs, b_up)],
            out_specs=[one, token, inner, inner, token, whole((8, width))] + [one] * TP,
            scratch_shapes=[pltpu.VMEM((step, width), bf16), pltpu.VMEM((step, width), bf16)],
        ),
        out_shape=[
            jax.ShapeDtypeStruct((step, width), f32),
            jax.ShapeDtypeStruct((rows, width), bf16),
            jax.ShapeDtypeStruct((rows, hidden), bf16),
            jax.ShapeDtypeStruct((rows, hidden), bf16),
            jax.ShapeDtypeStruct((rows, width), bf16),
            jax.ShapeDtypeStruct((8, width), f32),
        ]
        + [jax.ShapeDtypeStruct((step, width), bf16)] * TP,
        compiler_params=params(),
        cost_estimate=cost(2 * rows * width * (width + 3 * hidden), rows * width * 24, rows * hidden * 4),
        name="mlp",
    )(idx, x_all, *os, *dms, w_out, w_up, w_down, vecs, b_up)


def pair_kernel(plan, idx_ref, h_ref, du_ref, a_ref, dm_ref, wd_ref, near_ref, far_ref, *refs):
    out_refs, acc_ref, wide_ref = refs[:TP], refs[TP], refs[TP + 1]
    lines = plan.copies // 2
    step = pl.program_id(0)
    member, core = idx_ref[0], idx_ref[2]
    half = step ^ core
    grad_pre = du_ref[...]
    act = a_ref[...]
    width = h_ref.shape[1]
    block = width // plan.devices
    size = act.shape[1]
    slab = size // lines
    first = TP * block
    up = dot(h_ref[...], grad_pre, 0, 0)
    down = dot(act, dm_ref[...], 0, 0)
    bias = jnp.sum(grad_pre.astype(f32), axis=0, keepdims=True)
    term = dot(act, wd_ref[...])

    @pl.when(step == 0)
    def _():
        acc_ref[...] = term.reshape(acc_ref.shape)
        wide_ref[:, :size] = up

    @pl.when(step == 1)
    def _():
        acc_ref[...] += term.reshape(acc_ref.shape)
        for j in range(TP):
            out_refs[j][...] = acc_ref[member ^ j].astype(bf16)
        wide_ref[:, size:] = up
        pair = plan.size["sy"] * block
        for ref, owner in ((near_ref, core), (far_ref, 1 - core)):
            for z in range(lines):
                for gx in range(plan.size["gx"]):
                    at = ((gx * 2 + owner) * lines + z) * pair
                    value = wide_ref[pl.ds(pl.multiple_of(at, 16), pair), :]
                    ref[z, gx * pair : (gx + 1) * pair, :] = value.astype(bf16)

    def put(ref):
        for k in range(lines):
            at = k * slab
            row = jnp.concatenate(
                [bias[:, at : at + slab], jnp.zeros((1, width - slab), f32)], axis=1
            )
            ref[k, first : first + slab, :] = down[at : at + slab, :].astype(bf16)
            ref[k, first + slab :, :] = jnp.broadcast_to(row, (8, width)).astype(bf16)

    @pl.when(half == 0)
    def _():
        put(near_ref)

    @pl.when(half == 1)
    def _():
        put(far_ref)


def mlp_weight_grads(plan, idx, low, grad_pre, act, dm_all, w_down):
    rows, width = low.shape
    hidden = act.shape[1]
    step = hidden // 2
    lines = plan.copies // 2
    block = width // plan.devices
    slab = hidden // plan.copies
    bundle = (lines, TP * block + slab + 8, width)
    token = (rows // TP, width)
    return pl.pallas_call(
        functools.partial(pair_kernel, plan),
        grid_spec=pltpu.PrefetchScalarGridSpec(
            num_scalar_prefetch=1,
            grid=(2,),
            in_specs=[
                whole((rows, width)),
                pl.BlockSpec((rows, step), lambda i, idx: (0, i)),
                pl.BlockSpec((rows, step), lambda i, idx: (0, i)),
                whole((rows, width)),
                pl.BlockSpec((step, width), lambda i, idx: (i, 0)),
            ],
            out_specs=[whole(bundle)] * 2 + [whole(token)] * TP,
            scratch_shapes=[
                pltpu.VMEM((TP, *token), f32),
                pltpu.VMEM((width, hidden), f32),
            ],
        ),
        out_shape=[jax.ShapeDtypeStruct(bundle, bf16)] * 2
        + [jax.ShapeDtypeStruct(token, bf16)] * TP,
        compiler_params=params(),
        cost_estimate=cost(6 * rows * width * hidden, width * hidden * 12),
        name="mlp_weight_grads",
    )(idx, low, grad_pre, act, dm_all, w_down)


def add_kernel(*refs):
    *in_refs, out_ref = refs
    total = in_refs[0][...].astype(f32)
    for ref in in_refs[1:]:
        total += ref[...].astype(f32)
    out_ref[...] = total.astype(out_ref.dtype)


def add(*values, dtype=bf16):
    return pl.pallas_call(
        add_kernel,
        out_shape=jax.ShapeDtypeStruct(values[0].shape, dtype),
        compiler_params=pltpu.CompilerParams(vmem_limit_bytes=60 * 1024 * 1024),
        cost_estimate=cost(values[0].size * len(values), 2 * values[0].size * (len(values) + 1)),
        name="add",
    )(*values)


def rows_kernel(plan, idx_ref, *refs):
    term_ref, up_refs = refs[0], refs[1 : 1 + TP]
    down_ref, row_ref, total_ref = refs[1 + TP :]
    member = idx_ref[0]
    total = term_ref[0].astype(f32)
    for z in range(1, term_ref.shape[0]):
        total += term_ref[z].astype(f32)
    block = up_refs[0].shape[0]
    first, slab = TP * block, down_ref.shape[0]
    total_ref[...] = total[:first].reshape(total_ref.shape)
    for j in range(TP):
        up_refs[j][...] = total_ref[member ^ j].astype(bf16)
    down_ref[...] = total[first : first + slab]
    row_ref[...] = total[first + slab : first + slab + 1, :slab]


def sum_rows(plan, idx, terms, block, slab):
    lines, rows, width = terms.shape
    return pl.pallas_call(
        functools.partial(rows_kernel, plan),
        in_specs=[pl.BlockSpec(memory_space=pltpu.SMEM), pl.BlockSpec(memory_space=pltpu.VMEM)],
        out_shape=[jax.ShapeDtypeStruct((block, width), bf16)] * TP
        + [jax.ShapeDtypeStruct((slab, width), f32), jax.ShapeDtypeStruct((1, slab), f32)],
        scratch_shapes=[pltpu.VMEM((TP, block, width), f32)],
        cost_estimate=cost(lines * rows * width, 2 * lines * rows * width),
        name="sum_rows",
    )(idx, terms)


def up_kernel(plan, idx_ref, *refs):
    part_refs, out_ref, hold_ref = refs[:TP], refs[TP], refs[TP + 1]
    member = idx_ref[0]
    for j in range(TP):
        hold_ref[member ^ j] = part_refs[j][...].astype(f32)
    slab = out_ref.shape[1] // plan.devices
    for r in range(plan.devices):
        t, copy = plan.place(r)
        out_ref[:, r * slab : (r + 1) * slab] = hold_ref[t, :, copy * slab : (copy + 1) * slab]


def join_up(plan, idx, parts, hidden):
    block, width = parts[0].shape
    return pl.pallas_call(
        functools.partial(up_kernel, plan),
        in_specs=[pl.BlockSpec(memory_space=pltpu.SMEM)]
        + [pl.BlockSpec(memory_space=pltpu.VMEM)] * TP,
        out_shape=jax.ShapeDtypeStruct((block, hidden), f32),
        scratch_shapes=[pltpu.VMEM((TP, block, width), f32)],
        cost_estimate=cost(block * hidden, 6 * block * hidden),
        name="join_up",
    )(idx, *parts)


def resid_kernel(r_ref, dm_ref, vec_ref, *refs):
    part_refs, (dr_ref, da_ref, sum_ref) = refs[:TP], refs[TP:]
    total = part_refs[0][...].astype(f32)
    for j in range(1, TP):
        total += part_refs[j][...].astype(f32)
    units, rstd = unit(r_ref[...])
    dm = dm_ref[...].astype(f32)
    dr = dm + unit_back(total * vec_ref[5:6, :], units, rstd)
    da = dr.astype(bf16)
    dr_ref[...] = dr
    da_ref[...] = da
    sum_ref[...] = jnp.zeros_like(sum_ref)
    sum_ref[0:1, :] = jnp.sum(da.astype(f32), axis=0, keepdims=True)
    sum_ref[1:2, :] = jnp.sum(dm, axis=0, keepdims=True)


def resid_back(parts, r_own, dm, vecs):
    rows, width = dm.shape
    return pl.pallas_call(
        resid_kernel,
        out_shape=[
            jax.ShapeDtypeStruct((rows, width), f32),
            jax.ShapeDtypeStruct((rows, width), bf16),
            jax.ShapeDtypeStruct((8, width), f32),
        ],
        cost_estimate=cost(30 * rows * width, rows * width * 20),
        name="resid_back",
    )(r_own, dm, vecs, *parts)


def output_kernel(r_ref, vec_ref, *refs):
    total = r_ref[...] + vec_ref[7:8, :]
    for ref in refs[:TP]:
        total += ref[...].astype(f32)
    refs[TP][...] = total.astype(bf16)


def finish_output(parts, r_own, vecs):
    return pl.pallas_call(
        output_kernel,
        out_shape=jax.ShapeDtypeStruct(r_own.shape, bf16),
        cost_estimate=cost(8 * r_own.size, r_own.size * 14),
        name="finish_output",
    )(r_own, vecs, *parts)


def input_kernel(x_ref, dr_ref, vec_ref, *refs):
    total = refs[0][...].astype(f32)
    for ref in refs[1:TP]:
        total += ref[...].astype(f32)
    units, rstd = unit(x_ref[...].astype(f32))
    grad = dr_ref[...] + unit_back(total * vec_ref[3:4, :], units, rstd)
    refs[TP][...] = grad.astype(bf16)


def finish_input(parts, x, dr, vecs):
    return pl.pallas_call(
        input_kernel,
        out_shape=jax.ShapeDtypeStruct(x.shape, bf16),
        cost_estimate=cost(30 * x.size, x.size * 16),
        name="finish_input",
    )(x, dr, vecs, *parts)


def normed_kernel(n_recv, idx_ref, x_ref, dq_ref, own_ref, *refs):
    recv_refs = refs[:n_recv]
    w_ref, d_ref, sum_ref = refs[n_recv : n_recv + 3]
    dh_refs, dh_now = refs[n_recv + 3 : -1], refs[-1]
    step = pl.program_id(0)

    @pl.when(step == 0)
    def _():
        sum_ref[...] = jnp.zeros_like(sum_ref)

    cols = dq_ref.shape[1]
    width = x_ref.shape[1]
    grad_k, grad_v = own_ref[0], own_ref[1]
    for ref in recv_refs:
        grad_k += ref[0].astype(f32)
        grad_v += ref[1].astype(f32)
    d_ref[:, :cols] = dq_ref[...]
    d_ref[:, cols : 2 * cols] = grad_k.astype(bf16)
    d_ref[:, 2 * cols : 3 * cols] = grad_v.astype(bf16)
    d_ref[:, 3 * cols :] = jnp.zeros_like(d_ref[:, 3 * cols :])
    low = d_ref[...]
    grad = dot(low, w_ref[...], 1, 1)
    dh_now[...] = grad.astype(bf16)
    for j in range(TP):

        @pl.when(step == j)
        def _(j=j):
            dh_refs[j][...] = dh_now[...]

    units, _ = unit(x_ref[...].astype(f32))
    sum_ref[0:1, :width] += jnp.sum(grad * units, axis=0, keepdims=True)
    sum_ref[1:2, :width] += jnp.sum(grad, axis=0, keepdims=True)
    sum_ref[2:3, : low.shape[1]] += jnp.sum(low.astype(f32), axis=0, keepdims=True)


def normed_back(idx, x_all, dq, own, recvs, w_qkv):
    rows, width = x_all.shape
    cols = dq.shape[1]
    wide = w_qkv.shape[1]
    step = rows // TP
    pairs = pl.BlockSpec((2, step, cols), lambda i, idx: (0, i ^ idx[0], 0))
    return pl.pallas_call(
        functools.partial(normed_kernel, len(recvs)),
        grid_spec=pltpu.PrefetchScalarGridSpec(
            num_scalar_prefetch=1,
            grid=(TP,),
            in_specs=[
                pl.BlockSpec((step, width), lambda i, idx: (i ^ idx[0], 0)),
                pl.BlockSpec((step, cols), lambda i, idx: (i ^ idx[0], 0)),
                pairs,
            ]
            + [pairs] * len(recvs)
            + [whole(w_qkv.shape)],
            out_specs=[
                pl.BlockSpec((step, wide), lambda i, idx: (i ^ idx[0], 0)),
                whole((8, width)),
            ]
            + [whole((step, width))] * TP,
            scratch_shapes=[pltpu.VMEM((step, width), bf16)],
        ),
        out_shape=[
            jax.ShapeDtypeStruct((rows, wide), bf16),
            jax.ShapeDtypeStruct((8, width), f32),
        ]
        + [jax.ShapeDtypeStruct((step, width), bf16)] * TP,
        compiler_params=params(),
        cost_estimate=cost(2 * rows * width * wide, rows * width * 12),
        name="normed_back",
    )(idx, x_all, dq, own, *recvs, w_qkv)


def proj_grads_kernel(plan, idx_ref, h_ref, d_ref, sum_ref, own_ref, two_ref, da_ref, *refs):
    o_refs, refs = refs[:TP], refs[TP:]
    fast = plan.fast
    acc_ref, out_acc, vec_ref = refs[-3:]
    wide = d_ref.shape[1]
    cols = o_refs[0].shape[1]
    rows, width = h_ref.shape
    member = idx_ref[0]
    acc_ref[:, :wide] = dot(h_ref[...], d_ref[...], 0, 0)
    da = da_ref[...].reshape(rows, cols)
    for j in range(TP):
        out_acc[member ^ j] = dot(o_refs[j][...], da, 0, 0)
    acc_ref[:, wide : wide + cols] = out_acc[...].reshape(width, cols)
    bias_q, bias_v = sum_ref[2:3, :cols], sum_ref[2:3, 2 * cols : 3 * cols]
    zero = jnp.zeros_like(bias_q)
    vec_ref[...] = jnp.zeros_like(vec_ref)
    rows_of = [
        jnp.concatenate([jnp.where(member == j, b, zero) for j in range(TP)], axis=1)
        for b in (bias_q, bias_v)
    ]
    rows_of += [own_ref[0:1, :], sum_ref[0:1, :], sum_ref[1:2, :], two_ref[0:1, :], two_ref[1:2, :], own_ref[1:2, :]]
    for j, row in enumerate(rows_of):
        vec_ref[SMALLS + j : SMALLS + j + 1, :] = row
    acc_ref[:, wide + cols :] = vec_ref[...].T[:, SMALLS:]
    if not fast:
        refs[0][...] = acc_ref[...].astype(bf16)
        return
    core = idx_ref[2]
    keep_ref, send_ref = refs[:2]
    near, block, _ = keep_ref.shape
    span = near // plan.size["gx"]
    for ref, owner in ((keep_ref, core), (send_ref, 1 - core)):
        for n in range(near):
            gx, rest = divmod(n, span)
            at = ((gx * 2 + owner) * span + rest) * block
            ref[n] = acc_ref[pl.ds(pl.multiple_of(at, 8), block), :].astype(bf16)


def proj_grads(plan, idx, low, grads, sums, sum_own, sum_two, da_cols, os):
    rows, width = low.shape
    cols = os[0].shape[1]
    wide = grads.shape[1] + cols + SMALLS
    near = plan.devices // 2
    if plan.fast:
        out_shape = [jax.ShapeDtypeStruct((near, width // plan.devices, wide), bf16)] * 2
    else:
        out_shape = jax.ShapeDtypeStruct((width, wide), bf16)
    operands = (low, grads, sums, sum_own, sum_two, da_cols, *os)
    return pl.pallas_call(
        functools.partial(proj_grads_kernel, plan),
        in_specs=[pl.BlockSpec(memory_space=pltpu.SMEM)]
        + [pl.BlockSpec(memory_space=pltpu.VMEM)] * len(operands),
        out_shape=out_shape,
        scratch_shapes=[
            pltpu.VMEM((width, wide), f32),
            pltpu.VMEM((TP, cols, cols), f32),
            pltpu.VMEM((2 * SMALLS, width), f32),
        ],
        compiler_params=pltpu.CompilerParams(vmem_limit_bytes=60 * 1024 * 1024),
        cost_estimate=cost(2 * rows * width * wide, width * wide * 6),
        name="proj_grads",
    )(idx, *operands)


def join_kernel(keep, cols, wide, in_ref, *out_refs):
    *mats, vec_ref = out_refs
    groups = {}
    for n in range(in_ref.shape[0]):
        value = in_ref[n].astype(f32)
        key = keep[n]
        groups[key] = value if key not in groups else groups[key] + value
    for j in range(TP):
        for ref, at in zip(mats, (0, cols, 2 * cols, wide)):
            ref[:, j * cols : (j + 1) * cols] = groups[j][:, at : at + cols]
    total = functools.reduce(jnp.add, [groups[j] for j in range(TP)])
    vec_ref[...] = total[:, wide + cols :]


def join_grads(plan, got, cols, wide):
    near, block, _ = got.shape
    dims = [plan.size[a] for a in SAME]
    members = []
    for n in range(near):
        place = dict(zip(SAME, (n // (dims[1] * dims[2]), n // dims[2] % dims[1], n % dims[2])))
        member = 0
        for axis in plan.tp:
            member = member * plan.size[axis] + place[axis]
        members.append(member)
    width = cols * TP
    return pl.pallas_call(
        functools.partial(join_kernel, members, cols, wide),
        out_shape=[jax.ShapeDtypeStruct((block, width), f32)] * 4
        + [jax.ShapeDtypeStruct((block, SMALLS), f32)],
        compiler_params=pltpu.CompilerParams(vmem_limit_bytes=60 * 1024 * 1024),
        cost_estimate=cost(got.size, got.size * 2),
        name="join_grads",
    )(got)


def local(
    plan, inputs, segment_ids, padding, cotangent, w_query, b_query, w_key, w_value, b_value,
    w_out, b_out, ln1_gain, ln1_shift, ln2_gain, ln2_shift, w_up, b_up, w_down, b_down,
):
    x_own = inputs[0]
    rows, width = x_own.shape
    cols = width // TP
    length = segment_ids.shape[1]
    block = w_query.shape[0]
    hidden = w_up.shape[1]
    slab = b_up.shape[0]
    size = plan.size
    member = lax.axis_index(plan.tp)
    part = lax.axis_index(plan.half)
    core = lax.axis_index("c")
    idx = jnp.stack([member, part, core, lax.axis_index("sz")]).astype(jnp.int32)
    lines = plan.copies // 2
    fast = plan.fast

    id_rows = jnp.pad(segment_ids[0].astype(bf16), (0, 8 * width - length)).reshape(8, width)
    moved = plan.move(jnp.concatenate([x_own, id_rows], axis=0), plan.route)
    x_mine = moved[:rows]
    ids = moved[rows:].reshape(1, -1)[:, :length].astype(f32)
    dm_own = (cotangent[0].astype(f32) * padding[0].astype(f32)[:, None]).astype(bf16)
    dm_mine = plan.move(dm_own, plan.route)
    x_all = lax.all_gather(x_mine, plan.tp, axis=0, tiled=True)

    small = [b_query, b_value, b_out, ln1_gain, ln1_shift, ln2_gain, ln2_shift, b_down]
    small = jnp.stack(small, axis=1)
    b_row = jnp.pad(b_up[None], ((0, 7), (0, width - slab)))
    if fast:
        small = jnp.pad(small, ((0, 0), (0, SMALLS - small.shape[1])))
        raw = jnp.concatenate([w_out, w_down, b_row], axis=0)
        raw = jnp.broadcast_to(raw, (lines, *raw.shape))
        raw = lax.all_to_all(raw, "sz", 0, 0, tiled=True)
        chunks = prepare(plan, idx, w_query, w_key, w_value, small, w_up)
        proj, up = shards_of(idx, plan.reduce(chunks), 3 * cols + SMALLS)
        projs = [proj] + [plan.turn(proj, "sz", -j) for j in range(1, lines)]
        projs, x_all = lax.optimization_barrier((projs, x_all))
        projs = jnp.stack(projs)
        low_one, query, kv, w_qkv, vecs = qkv(plan, idx, x_all, projs, plan.swap(projs))
        ups = [up] + [plan.turn(up, "sz", -j) for j in range(1, lines)]
        outs = plan.partners(raw[:, :block])
        ups, outs, query = lax.optimization_barrier((ups, outs, query))
    else:
        table = [w_query, w_key, w_value, w_out, small]
        table = lax.all_gather(jnp.concatenate(table, axis=1), ALL, axis=0, tiled=True)
        vecs = table[:, 4 * width :].T.astype(f32)
        split = [lax.dynamic_slice(table, (0, i * width + member * cols), (width, cols)) for i in range(3)]
        w_qkv = jnp.concatenate([*split, jnp.zeros((width, SMALLS), bf16)], axis=1)
        out_full = table[:, 3 * width : 4 * width].reshape(TP, cols, width)
        low_one, query, kv = qkv(plan, idx, x_all, w_qkv, vecs)
        up_mine = lax.all_gather(w_up, ALL, axis=0, tiled=True)
        up_mine = up_mine.reshape(width, plan.devices, slab).transpose(1, 0, 2)
        up_mine = plan.shuffle(up_mine, ALL, plan.tp + plan.rep).reshape(TP, plan.copies, width, slab)
        up_mine = lax.dynamic_index_in_dim(up_mine, member, 0, keepdims=False)
        up_mine = up_mine.transpose(1, 0, 2).reshape(width, -1)
        downs = jnp.concatenate([w_down, b_row], axis=0)
        downs = lax.all_gather(downs, plan.rep, axis=0, tiled=False)
        down_mine = downs[:, :slab].reshape(-1, width)
        b_up_mine = downs[:, slab, :slab].reshape(1, -1).astype(f32)

    parts = plan.parts
    kvs = [kv] + [plan.turn(kv, plan.half, -j) for j in range(1, parts)]
    mixed, lse = attend(idx, ids, query, kvs)
    if fast:
        raw, ups, outs, mixed = lax.optimization_barrier((raw, ups, outs, mixed))
        own = [raw, *ups, *outs]
        other = [plan.swap(v) for v in own]
        up_mine, out_full, down_mine, row = assemble(plan, idx, own, other, block, slab)
        out_full = out_full.reshape(TP, cols, width)
        down_mine = down_mine.reshape(-1, width)
        b_up_mine = row[:, :, 0, :slab].reshape(1, -1).astype(f32)
    os = plan.partners(mixed)
    dms = plan.partners(dm_mine)
    r_own, low_two, act, grad_pre, dm_all, sum_two, *dh_two = mlp(
        idx, x_all, os, dms, out_full, up_mine, down_mine, vecs, b_up_mine
    )

    back_two = plan.reduce(dh_two)
    if fast:
        near_terms, far_terms, *out_terms = mlp_weight_grads(
            plan, idx, low_two, grad_pre, act, dm_all, down_mine
        )
        back_two, out_terms, far_terms = lax.optimization_barrier((back_two, out_terms, far_terms))
    else:
        up_terms = dot(low_two, grad_pre, 0, 0).astype(bf16)
        down_terms = dot(act, dm_all, 0, 0).astype(bf16)
        row = jnp.sum(grad_pre.astype(f32), axis=0).astype(bf16)
        out_terms = dot(act, down_mine).astype(bf16).reshape(TP, rows, width)
        out_terms = [
            lax.dynamic_index_in_dim(out_terms, member ^ j, 0, keepdims=False) for j in range(TP)
        ]
    dr, da, sum_own = resid_back(back_two, r_own, dm_mine, vecs)
    das = plan.partners(da)
    das, out_terms = lax.optimization_barrier((das, out_terms))
    out_parts = plan.reduce(out_terms)
    output = finish_output(out_parts, r_own, vecs)

    if fast:
        terms = add(near_terms, plan.swap(far_terms))
        das, terms = lax.optimization_barrier((das, terms))
        terms = lax.all_to_all(terms, "sz", 0, 0, tiled=True)
        *ups, g_w_down, g_b_up = sum_rows(plan, idx, terms, block, slab)
    else:
        row = jnp.pad(row.reshape(plan.copies, 1, slab), ((0, 0), (0, 7), (0, width - slab)))
        downs = jnp.concatenate([down_terms.reshape(plan.copies, slab, width), row], axis=1)
        downs = lax.psum_scatter(downs, plan.rep, scatter_dimension=0, tiled=False)
        g_w_down = downs[:slab].astype(f32)
        g_b_up = downs[slab, :slab].astype(f32)
        ups = plan.shuffle(up_terms.reshape(plan.devices, block, -1), ALL, plan.rep + plan.tp)
        ups = ups.reshape(plan.copies, TP * block, -1)
        ups = lax.psum_scatter(ups, plan.rep, scatter_dimension=0, tiled=False)
        ups = lax.all_to_all(ups.reshape(TP, block, -1), plan.tp, 0, 0, tiled=True).astype(f32)
    grad_query, kv_own, da_cols, *kv_others = attend_back(idx, ids, query, das, out_full, lse, kvs)
    recvs = [plan.turn(kv_others[j - 1], plan.half, j) for j in range(1, parts)]
    recvs, output = lax.optimization_barrier((recvs, output))
    grads, sum_one, *dh_one = normed_back(idx, x_all, grad_query, kv_own, recvs, w_qkv)
    back_one = plan.reduce(dh_one)
    output, sum_one = lax.optimization_barrier((output, sum_one))
    output = plan.move(output, plan.back)
    terms = proj_grads(plan, idx, low_one, grads, sum_one, sum_own, sum_two, da_cols, os)
    if fast:
        keep, send = terms
        terms = add(keep, plan.swap(send))
        terms, back_one, ups = lax.optimization_barrier((terms, back_one, ups))
        got = lax.all_to_all(terms, SAME, 0, 0, tiled=True)
    else:
        terms = plan.shuffle(terms.reshape(plan.devices, block, -1), ALL, ("c",) + SAME)
        terms = terms.reshape(2, -1, *terms.shape[1:])
        keep, send = jnp.where(core == 0, terms, terms[::-1])
        got = lax.all_to_all(add(keep, plan.swap(send)), SAME, 0, 0, tiled=True)
    if fast:
        g_w_up = join_up(plan, idx, plan.reduce(ups), hidden)
        g_b_up = g_b_up[0]
    else:
        ups = ups.reshape(TP, block, plan.copies, slab).transpose(0, 2, 1, 3)
        ups = plan.shuffle(ups.reshape(plan.devices, block, slab), plan.tp + plan.rep, ALL)
        g_w_up = ups.transpose(1, 0, 2).reshape(block, hidden)
    g_query, g_key, g_value, g_out, vec = join_grads(plan, got, cols, w_qkv.shape[1])

    grad_input = plan.move(finish_input(back_one, x_mine, dr, vecs), plan.back)
    return (
        output[None],
        grad_input[None],
        g_query,
        vec[:, 0],
        g_key,
        g_value,
        vec[:, 1],
        g_out,
        vec[:, 2],
        vec[:, 3],
        vec[:, 4],
        vec[:, 5],
        vec[:, 6],
        g_w_up,
        g_b_up,
        g_w_down,
        vec[:, 7],
    )


def solution(mesh):
    groups, blocks = mesh.shape["grp"], mesh.shape["seq"]
    plan = Plan(groups, blocks)
    fine = Mesh(mesh.devices.reshape(plan.shape), ALL)
    grp, seq = ("gx", "c"), ("sz", "sy")
    matrix, vector = P(ALL, None), P(ALL)
    token = P(grp, seq, None)
    return jax.shard_map(
        functools.partial(local, plan),
        mesh=fine,
        in_specs=(
            token, P(grp, None), P(grp, seq), token,
            matrix, vector, matrix, matrix, vector, matrix, vector,
            vector, vector, vector, vector, matrix, vector, matrix, vector,
        ),
        out_specs=(
            token, token,
            matrix, vector, matrix, matrix, vector, matrix, vector,
            vector, vector, vector, vector, matrix, vector, matrix, vector,
        ),
        check_vma=False,
    )
```

time: 298 us -> 254 us (0.85)
  blocking collectives: 98 us -> 11.7 us
  starting transfers between devices: 38.8 us -> 77.5 us
  Pallas kernels: 55 us -> 80.7 us
  local copies, waits for them, and re-layouts: 30.7 us -> 16.2 us
  waiting for transfers between devices: 46.3 us -> 60 us
  between operations: 14.7 us -> 1.4 us
  other arithmetic: 10.5 us -> 4.7 us
    all_gather x4 -> x0, blocking collectives: 63.9 us -> none  [the longest x1 23.3 us: local(): both = lax.all_gather(got, 'c', axis=0, tiled=True)]
    ppermute x3 -> x47, starting transfers between devices: 0.62 us -> 49.1 us  [the longest x27 31.6 us: partner(): return lax.ppermute(value, self.tp, table)]
    ppermute x3 -> x47, waiting for transfers between devices: 1.12 us -> 40.9 us  [the longest x27 40.3 us: partner(): return lax.ppermute(value, self.tp, table)]
    pallas_call x7 -> x15, Pallas kernels: 35.2 us -> 60.2 us  [the longest x1 12.2 us: mlp(): pl.pallas_call(mlp_kernel, grid_spec=pltpu.PrefetchScalarGridSpec(num_sca...]
    all_to_all x2 -> x0, blocking collectives: 23.1 us -> none  [the longest x1 13.9 us: local(): lax.all_to_all(dh_two.reshape(TP, rows, width), plan.tp, 0, 0, tiled=True)]
    ppermute x4, waiting for transfers between devices: 33.8 us -> 19.2 us  [move(): return lax.ppermute(value, ALL, table)]
    all_to_all x5 -> x3, waiting for transfers between devices: 11.4 us -> 0.01 us  [the longest x1 0.01 us: local(): raw = lax.all_to_all(raw, 'sz', 0, 0, tiled=True)]
    all_to_all x5 -> x3, starting transfers between devices: 26.7 us -> 15.3 us  [the longest x1 7.55 us: local(): got = lax.all_to_all(terms, SAME, 0, 0, tiled=True)]
  transfers between devices with their start and end apart: 14 -> 54, of which waited for: 6 -> 22; matrix products, arithmetic and copies ran while one was open for 7% -> 2% of each run, Pallas kernels for 13% -> 22%
where the time goes in v2:
time: 254 us; the launch traced here: 252 us
  Pallas kernels  80.7 us (32%)
  starting transfers between devices  77.5 us (31%)
  waiting for transfers between devices  60 us (24%)
  local copies, waits for them, and re-layouts  16.2 us (6%)
  blocking collectives  11.7 us (5%)
  other arithmetic  4.7 us (2%)
    ppermute x27, waiting for transfers between devices, partner(): return lax.ppermute(value, self.tp, table)  40.3 us
    ppermute x27, starting transfers between devices, partner(): return lax.ppermute(value, self.tp, table)  31.6 us
    ppermute x4, waiting for transfers between devices, move(): return lax.ppermute(value, ALL, table)  19.2 us
    ppermute x4, starting transfers between devices, move(): return lax.ppermute(value, ALL, table)  13.1 us
    pallas_call x1, Pallas kernels, mlp(): pl.pallas_call(mlp_kernel, grid_spec=pltpu.PrefetchScalarGridSpec(num_sca...  12.2 us
    unnamed x144, local copies, waits for them, and re-layouts  11.9 us
    all_gather x1, blocking collectives, local(): x_all = lax.all_gather(x_mine, plan.tp, axis=0, tiled=True)  11.7 us
    pallas_call x1, Pallas kernels, attend_back(): pl.pallas_call(functools.partial(bwd_kernel, parts), grid_spec=pltpu.Pref...  10.9 us
  transfers between devices with their start and end apart: 54, of which 22 were waited for; matrix products, arithmetic and copies ran while one was open for 2% of the time, Pallas kernels for 22%

profile of v2, /device:TPU:2, one launch (start us, length us, event | category | flops | bytes accessed | tf_op | source)
XLA Modules:
  0.0 252.3 jit_solution(11374438065546796020)
XLA Ops:
  2.4 4.5 %collective-permute-start = (bf16[136,768]{1,0:T(8,128)(2,1)S(1)}, bf16[136,768]{1,0:T(8,128)(2,1)S(1)}, u32[]{:S(2)}, u32[]{:S(2)}) collective-permute-start(bf16[136,768]{1,0:T(8,128)(2,1)S(1)} %pad_maximum_fusion.1), channel_id=1, source_target_pairs={{0,0},{1,1},{2,16},{3,17},{4,8},{5,9},{6,24},{7,25},{8,2},{9,3},{1... | collective-permute-start | bytes 626696 | tf_op jit(solution)/shard_map/ppermute | solution.py:87
  8.8 3.5 %all-to-all-start = ((bf16[4,128,768]{2,1,0:T(8,128)(2,1)}), bf16[4,128,768]{2,1,0:T(8,128)(2,1)S(1)}, u32[]{:S(2)}, u32[]{:S(2)}) async-start(bf16[4,128,768]{2,1,0:T(8,128)(2,1)} %broadcast_in_dim.14), calls=%async_computation | async-start | bytes 1572864 | tf_op jit(solution)/shard_map/all_to_all | solution.py:1034
  31.6 11.7 %all_gather.3.x_ref = bf16[512,768]{1,0:T(8,128)(2,1)} all-gather(bf16[128,768]{1,0:T(8,128)(2,1)S(1)} %slice.55.x_ref), channel_id=1, replica_groups=mesh['gx'=2,'c'=2,'sz'=4,'sy'=2] {'gx','sy'}, dimensions={0}, use_global_device_ids=true | all-gather | bytes 983040 | tf_op jit(solution)/shard_map/all_gather | solution.py:1025
  45.3 3.0 %collective-permute-start.5 = (bf16[96,768]{1,0:T(8,128)(2,1)S(1)}, bf16[96,768]{1,0:T(8,128)(2,1)S(1)}, u32[]{:S(2)}, u32[]{:S(2)}) collective-permute-start(bf16[96,768]{1,0:T(8,128)(2,1)S(1)} %copy-done.26), channel_id=1, source_target_pairs={{0,4},{2,6},{4,0},{6,2},{1,5},{3,7},{5,1},{7,3},{8,12},{10,14},{12... | collective-permute-start | bytes 442376 | tf_op jit(solution)/shard_map/ppermute | solution.py:65
  49.1 5.9 %qkv.1 = (bf16[512,768]{1,0:T(8,128)(2,1)}, bf16[512,192]{1,0:T(8,128)(2,1)}, bf16[2,512,192]{2,1,0:T(8,128)(2,1)}, bf16[768,640]{1,0:T(8,128)(2,1)}, f32[8,768]{1,0:T(8,128)}) custom-call(s32[4]{0:T(128)} %pad_add_fusion.idx_ref, bf16[512,768]{1,0:T(8,128)(2,1)} %all_gather.3.x_ref, bf16[4,96,640]{2,1,0:T(8,128)(2,1)} %copy-done.3, ...), custom_call_target="tpu_custom_call" | custom-call | flops 452984832 | bytes 3145728 | tf_op jit(solution)/shard_map/qkv/pallas_call | solution.py:319
  66.5 7.2 %attend.1 = (bf16[512,192]{1,0:T(8,128)(2,1)}, f32[8,512]{1,0:T(8,128)}) custom-call(s32[4]{0:T(128)} %pad_add_fusion.idx_ref, f32[1,1024]{1,0:T(1,128)} %slice_convert_fusion.ids_ref, bf16[512,192]{1,0:T(8,128)(2,1)} %get-tuple-element.147.q_ref, bf16[2,512,192]{2,1,0:T(8,128)(2,1)} %get-tuple-element.156.refs_0_.refs_4_, bf16[2,512,192]{2,1,0:T(8,128)(2,1)} %copy-done.56), custom_call_target="tpu_custom_call" | custom-call | flops 402653184 | bytes 786432 | tf_op jit(solution)/shard_map/attend/pallas_call | solution.py:390
  73.8 3.3 %collective-permute-start.27 = (bf16[128,768]{1,0:T(8,128)(2,1)S(1)}, bf16[128,768]{1,0:T(8,128)(2,1)S(1)}, u32[]{:S(2)}, u32[]{:S(2)}) collective-permute-start(bf16[128,768]{1,0:T(8,128)(2,1)S(1)} %fusion), channel_id=1, source_target_pairs={{0,0},{1,1},{2,16},{3,17},{4,8},{5,9},{6,24},{7,25},{8,2},{9,3},{1... | collective-permute-start | bytes 589832 | tf_op jit(solution)/shard_map/ppermute | solution.py:87
  77.1 7.2 %collective-permute-done.27.refs_4_.dm_ref = bf16[128,768]{1,0:T(8,128)(2,1)S(1)} collective-permute-done((bf16[128,768]{1,0:T(8,128)(2,1)S(1)}, bf16[128,768]{1,0:T(8,128)(2,1)S(1)}, u32[]{:S(2)}, u32[]{:S(2)}) %collective-permute-start.27) | collective-permute-done | bytes 196640 | tf_op jit(solution)/shard_map/ppermute | solution.py:87
  84.4 4.5 %collective-permute-start.16 = (bf16[96,768]{1,0:T(8,128)(2,1)S(1)}, bf16[96,768]{1,0:T(8,128)(2,1)S(1)}, u32[]{:S(2)}, u32[]{:S(2)}) collective-permute-start(bf16[96,768]{1,0:T(8,128)(2,1)S(1)} %copy-done.26), channel_id=1, source_target_pairs={{0,8},{8,0},{1,9},{9,1},{2,10},{10,2},{3,11},{11,3},{4,12},{12,4},... | collective-permute-start | bytes 442376 | tf_op jit(solution)/shard_map/ppermute | solution.py:51
  100.6 4.4 %assemble.1 = (bf16[768,768]{1,0:T(8,128)(2,1)}, bf16[768,768]{1,0:T(8,128)(2,1)}, bf16[2,4,96,768]{3,2,1,0:T(8,128)(2,1)}, bf16[2,4,8,768]{3,2,1,0:T(8,128)(2,1)}) custom-call(s32[4]{0:T(128)} %pad_add_fusion.idx_ref, bf16[4,128,768]{2,1,0:T(8,128)(2,1)} %copy-done.1, bf16[96,768]{1,0:T(8,128)(2,1)} %get-tuple-element.159.refs_1_, ...), custom_call_target="tpu_custom_call" | custom-call | flops 1000 | bytes 7077888 | tf_op jit(solution)/shard_map/assemble/pallas_call | solution.py:240
  106.4 3.2 %collective-permute-done.28.refs_5_ = bf16[128,768]{1,0:T(8,128)(2,1)} collective-permute-done((bf16[128,768]{1,0:T(8,128)(2,1)S(1)}, bf16[128,768]{1,0:T(8,128)(2,1)}, u32[]{:S(2)}, u32[]{:S(2)}) %collective-permute-start.28) | collective-permute-done | bytes 196640 | tf_op jit(solution)/shard_map/ppermute | solution.py:55
  109.6 3.0 %collective-permute-done.25.refs_2_ = bf16[512,192]{1,0:T(8,128)(2,1)S(1)} collective-permute-done((bf16[512,192]{1,0:T(8,128)(2,1)}, bf16[512,192]{1,0:T(8,128)(2,1)S(1)}, u32[]{:S(2)}, u32[]{:S(2)}) %collective-permute-start.25) | collective-permute-done | bytes 196640 | tf_op jit(solution)/shard_map/ppermute | solution.py:55
  114.7 12.2 %mlp.1 = (f32[128,768]{1,0:T(8,128)}, bf16[512,768]{1,0:T(8,128)(2,1)}, bf16[512,768]{1,0:T(8,128)(2,1)}, bf16[512,768]{1,0:T(8,128)(2,1)}, bf16[512,768]{1,0:T(...) custom-call(s32[4]{0:T(128)} %pad_add_fusion.idx_ref, ...), custom_call_target="tpu_custom_call" | custom-call | flops 2415919104 | bytes 9437184 | tf_op jit(solution)/shard_map/mlp/pallas_call | solution.py:578
  130.5 7.7 %mlp_weight_grads.1 = (bf16[4,200,768]{2,1,0:T(8,128)(2,1)}, bf16[4,200,768]{2,1,0:T(8,128)(2,1)}, bf16[128,768]{1,0:T(8,128)(2,1)}, bf16[128,768]{1,0:T(8,128)(...) custom-call(s32[4]{0:T(128)} %pad_add_fusion.idx_ref, bf16[512,768]{1,0:T(8,128)(2,1)} %get-tuple-element.179.h_ref, ...), custom_call_target="tpu_custom_call" | custom-call | flops 1811939328 | bytes 7077888 | tf_op jit(solution)/shard_map/mlp_weight_grads/pallas_call | solution.py:669
  145.2 5.5 %collective-permute-done.36.refs_3_ = bf16[128,768]{1,0:T(8,128)(2,1)S(1)} collective-permute-done((bf16[128,768]{1,0:T(8,128)(2,1)}, bf16[128,768]{1,0:T(8,128)(2,1)S(1)}, u32[]{:S(2)}, u32[]{:S(2)}) %collective-permute-start.36) | collective-permute-done | bytes 196640 | tf_op jit(solution)/shard_map/ppermute | solution.py:55
  157.8 4.3 %all-to-all-start.1 = ((bf16[4,200,768]{2,1,0:T(8,128)(2,1)}), bf16[4,200,768]{2,1,0:T(8,128)(2,1)S(1)}, u32[]{:S(2)}, u32[]{:S(2)}) async-start(bf16[4,200,768]{2,1,0:T(8,128)(2,1)} %add.30), calls=%async_computation.1 | async-start | bytes 2457600 | tf_op jit(solution)/shard_map/all_to_all | solution.py:1102
  162.1 10.9 %attend_back.1 = (bf16[512,192]{1,0:T(8,128)(2,1)}, f32[2,512,192]{2,1,0:T(8,128)}, bf16[4,128,192]{2,1,0:T(8,128)(2,1)}, bf16[2,512,192]{2,1,0:T(8,128)(2,1)}) custom-call(s32[4]{0:T(128)} %pad_add_fusion.idx_ref, f32[1,1024]{1,0:T(1,128)} %slice_convert_fusion.ids_ref, bf16[512,192]{1,0:T(8,128)(2,1)} %get-tuple-element.147.q_ref, ...), custom_call_target="tpu_custom_call" | custom-call | flops 1006632960 | bytes 2359296 | tf_op jit(solution)/shard_map/attend_back/pallas_call | solution.py:483
  176.6 3.8 %collective-permute-done.39.refs_1_ = bf16[128,768]{1,0:T(8,128)(2,1)S(1)} collective-permute-done((bf16[128,768]{1,0:T(8,128)(2,1)S(1)}, bf16[128,768]{1,0:T(8,128)(2,1)S(1)}, u32[]{:S(2)}, u32[]{:S(2)}) %collective-permute-start.39) | collective-permute-done | bytes 196640 | tf_op jit(solution)/shard_map/ppermute | solution.py:55
  182.3 3.5 %collective-permute-done.41.refs_3_ = bf16[128,768]{1,0:T(8,128)(2,1)S(1)} collective-permute-done((bf16[128,768]{1,0:T(8,128)(2,1)S(1)}, bf16[128,768]{1,0:T(8,128)(2,1)S(1)}, u32[]{:S(2)}, u32[]{:S(2)}) %collective-permute-start.41) | collective-permute-done | bytes 196640 | tf_op jit(solution)/shard_map/ppermute | solution.py:55
  189.3 6.4 %normed_back.1 = (bf16[512,640]{1,0:T(8,128)(2,1)}, f32[8,768]{1,0:T(8,128)}, bf16[128,768]{1,0:T(8,128)(2,1)}, bf16[128,768]{1,0:T(8,128)(2,1)}, bf16[128,768]{1,0:T(8,128)(2,1)}, /*index=5*/bf16[128,768]{1,0:T(8,128)(2,1)}) custom-call(s32[4]{0:T(128)} %pad_add_fusion.idx_ref, bf16[512,768]{1,0:T(8,128)(2,1)} %all_gather.3.x_ref, ...), custom_call_target="tpu_custom_call" | custom-call | flops 503316480 | bytes 4718592 | tf_op jit(solution)/shard_map/normed_back/pallas_call | solution.py:871
  195.7 4.1 %proj_grads.1 = (bf16[16,24,896]{2,1,0:T(8,128)(2,1)}, bf16[16,24,896]{2,1,0:T(8,128)(2,1)}) custom-call(s32[4]{0:T(128)} %pad_add_fusion.idx_ref, bf16[512,768]{1,0:T(8,128)(2,1)} %get-tuple-element.220.h_ref, bf16[512,640]{1,0:T(8,128)(2,1)} %get-tuple-element.221.d_ref, f32[8,768]{1,0:T(8,128)} %get-tuple-element.222.sum_ref, ...), custom_call_target="tpu_custom_call" | custom-call | flops 704643072 | bytes 4128768 | tf_op jit(solution)/shard_map/proj_grads/pallas_call | solution.py:949
  212.5 7.6 %all-to-all-start.2 = ((bf16[16,24,896]{2,1,0:T(8,128)(2,1)}), bf16[16,24,896]{2,1,0:T(8,128)(2,1)S(1)}, u32[]{:S(2)}, u32[]{:S(2)}) async-start(bf16[16,24,896]{2,1,0:T(8,128)(2,1)} %add.31), calls=%async_computation.2 | async-start | bytes 1376256 | tf_op jit(solution)/shard_map/all_to_all | solution.py:1126
  220.1 3.4 %collective-permute-start.42 = (bf16[128,768]{1,0:T(8,128)(2,1)S(1)}, bf16[128,768]{1,0:T(8,128)(2,1)S(1)}, u32[]{:S(2)}, u32[]{:S(2)}) collective-permute-start(bf16[128,768]{1,0:T(8,128)(2,1)S(1)} %copy-done.19), channel_id=1, source_target_pairs={{0,0},{1,1},{16,2},{17,3},{8,4},{9,5},{24,6},{25,7},{2,8},{3,9},{1... | collective-permute-start | bytes 589832 | tf_op jit(solution)/shard_map/ppermute | solution.py:87
  231.4 11.9 %collective-permute-done.42 = bf16[128,768]{1,0:T(8,128)(2,1)S(1)} collective-permute-done((bf16[128,768]{1,0:T(8,128)(2,1)S(1)}, bf16[128,768]{1,0:T(8,128)(2,1)S(1)}, u32[]{:S(2)}, u32[]{:S(2)}) %collective-permute-start.42) | collective-permute-done | bytes 196640 | tf_op jit(solution)/shard_map/ppermute | solution.py:87
  (266 shorter events, 108.4 us)
Async XLA Ops:
  2.4 29.2 %collective-permute-start = (bf16[136,768]{1,0:T(8,128)(2,1)S(1)}, bf16[136,768]{1,0:T(8,128)(2,1)S(1)}, u32[]{:S(2)}, u32[]{:S(2)}) collective-permute-start(bf16[136,768]{1,0:T(8,128)(2,1)S(1)} %pad_maximum_fusion.1), channel_id=1, source_target_pairs={{0,0},{1,1},{2,16},{3,17},{4,8},{5,9},{6,24},{7,25},{8,2},{9,3},{1... | collective-permute-start | bytes 626696 | tf_op jit(solution)/shard_map/ppermute | solution.py:87
  8.8 46.3 %all-to-all-start = ((bf16[4,128,768]{2,1,0:T(8,128)(2,1)}), bf16[4,128,768]{2,1,0:T(8,128)(2,1)S(1)}, u32[]{:S(2)}, u32[]{:S(2)}) async-start(bf16[4,128,768]{2,1,0:T(8,128)(2,1)} %broadcast_in_dim.14), calls=%async_computation | async-start | bytes 1572864 | tf_op jit(solution)/shard_map/all_to_all | solution.py:1034
  26.0 17.3 %collective-permute-start.12 = (bf16[96,640]{1,0:T(8,128)(2,1)}, bf16[96,640]{1,0:T(8,128)(2,1)S(1)}, u32[]{:S(2)}, u32[]{:S(2)}) collective-permute-start(bf16[96,640]{1,0:T(8,128)(2,1)} %get-tuple-element.142), channel_id=1, source_target_pairs={{0,2},{2,4},{4,6},{6,0},{1,3},{3,5},{5,7},{7,1},{8,10},{10,12},{12... | collective-permute-start | bytes 368648 | tf_op jit(solution)/shard_map/ppermute | solution.py:65
  27.7 15.6 %collective-permute-start.11 = (bf16[96,640]{1,0:T(8,128)(2,1)}, bf16[96,640]{1,0:T(8,128)(2,1)S(1)}, u32[]{:S(2)}, u32[]{:S(2)}) collective-permute-start(bf16[96,640]{1,0:T(8,128)(2,1)} %get-tuple-element.142), channel_id=1, source_target_pairs={{0,4},{2,6},{4,0},{6,2},{1,5},{3,7},{5,1},{7,3},{8,12},{10,14},{12... | collective-permute-start | bytes 368648 | tf_op jit(solution)/shard_map/ppermute | solution.py:65
  30.1 13.2 %collective-permute-start.10 = (bf16[96,640]{1,0:T(8,128)(2,1)}, bf16[96,640]{1,0:T(8,128)(2,1)S(1)}, u32[]{:S(2)}, u32[]{:S(2)}) collective-permute-start(bf16[96,640]{1,0:T(8,128)(2,1)} %get-tuple-element.142), channel_id=1, source_target_pairs={{0,6},{2,0},{4,2},{6,4},{1,7},{3,1},{5,3},{7,5},{8,14},{10,8},{12,... | collective-permute-start | bytes 368648 | tf_op jit(solution)/shard_map/ppermute | solution.py:65
  43.6 12.3 %collective-permute-start.6 = (bf16[96,768]{1,0:T(8,128)(2,1)S(1)}, bf16[96,768]{1,0:T(8,128)(2,1)S(1)}, u32[]{:S(2)}, u32[]{:S(2)}) collective-permute-start(bf16[96,768]{1,0:T(8,128)(2,1)S(1)} %copy-done.26), channel_id=1, source_target_pairs={{0,2},{2,4},{4,6},{6,0},{1,3},{3,5},{5,7},{7,1},{8,10},{10,12},{12... | collective-permute-start | bytes 442376 | tf_op jit(solution)/shard_map/ppermute | solution.py:65
  45.3 13.1 %collective-permute-start.5 = (bf16[96,768]{1,0:T(8,128)(2,1)S(1)}, bf16[96,768]{1,0:T(8,128)(2,1)S(1)}, u32[]{:S(2)}, u32[]{:S(2)}) collective-permute-start(bf16[96,768]{1,0:T(8,128)(2,1)S(1)} %copy-done.26), channel_id=1, source_target_pairs={{0,4},{2,6},{4,0},{6,2},{1,5},{3,7},{5,1},{7,3},{8,12},{10,14},{12... | collective-permute-start | bytes 442376 | tf_op jit(solution)/shard_map/ppermute | solution.py:65
  48.3 12.3 %collective-permute-start.4 = (bf16[96,768]{1,0:T(8,128)(2,1)S(1)}, bf16[96,768]{1,0:T(8,128)(2,1)S(1)}, u32[]{:S(2)}, u32[]{:S(2)}) collective-permute-start(bf16[96,768]{1,0:T(8,128)(2,1)S(1)} %copy-done.26), channel_id=1, source_target_pairs={{0,6},{2,0},{4,2},{6,4},{1,7},{3,1},{5,3},{7,5},{8,14},{10,8},{12,... | collective-permute-start | bytes 442376 | tf_op jit(solution)/shard_map/ppermute | solution.py:65
  73.7 26.0 %collective-permute-start.15 = (bf16[4,128,768]{2,1,0:T(8,128)(2,1)S(1)}, bf16[4,128,768]{2,1,0:T(8,128)(2,1)S(1)}, u32[]{:S(2)}, u32[]{:S(2)}) collective-permute-start(bf16[4,128,768]{2,1,0:T(8,128)(2,1)S(1)} %all-to-all-done.refs_0_), channel_id=1, source_target_pairs={{0,8},{8,0},{1,9},{9,1},{2,10},{10,2},{3,11},{11,3},{4,12},{12,4},... | collective-permute-start | bytes 2359304 | tf_op jit(solution)/shard_map/ppermute | solution.py:51
  94.4 12.0 %collective-permute-start.29 = (bf16[128,768]{1,0:T(8,128)(2,1)S(1)}, bf16[128,768]{1,0:T(8,128)(2,1)}, u32[]{:S(2)}, u32[]{:S(2)}) collective-permute-start(bf16[128,768]{1,0:T(8,128)(2,1)S(1)} %collective-permute-done.27.refs_4_.dm_ref), channel_id=1, source_target_pairs={{0,16},{1,17},{16,0},{17,1},{2,18},{3,19},{18,2},{19,3},{4,20},{5,... | collective-permute-start | bytes 589832 | tf_op jit(solution)/shard_map/ppermute | solution.py:55
  96.1 13.5 %collective-permute-start.28 = (bf16[128,768]{1,0:T(8,128)(2,1)S(1)}, bf16[128,768]{1,0:T(8,128)(2,1)}, u32[]{:S(2)}, u32[]{:S(2)}) collective-permute-start(bf16[128,768]{1,0:T(8,128)(2,1)S(1)} %collective-permute-done.27.refs_4_.dm_ref), channel_id=1, source_target_pairs={{0,1},{1,0},{16,17},{17,16},{2,3},{3,2},{18,19},{19,18},{4,5},{5,4... | collective-permute-start | bytes 589832 | tf_op jit(solution)/shard_map/ppermute | solution.py:55
  96.7 12.9 %collective-permute-start.26 = (bf16[512,192]{1,0:T(8,128)(2,1)}, bf16[512,192]{1,0:T(8,128)(2,1)S(1)}, u32[]{:S(2)}, u32[]{:S(2)}) collective-permute-start(bf16[512,192]{1,0:T(8,128)(2,1)} %get-tuple-element.169.refs_0_), channel_id=1, source_target_pairs={{0,17},{1,16},{16,1},{17,0},{2,19},{3,18},{18,3},{19,2},{4,21},{5,... | collective-permute-start | bytes 589832 | tf_op jit(solution)/shard_map/ppermute | solution.py:55
  98.0 14.7 %collective-permute-start.25 = (bf16[512,192]{1,0:T(8,128)(2,1)}, bf16[512,192]{1,0:T(8,128)(2,1)S(1)}, u32[]{:S(2)}, u32[]{:S(2)}) collective-permute-start(bf16[512,192]{1,0:T(8,128)(2,1)} %get-tuple-element.169.refs_0_), channel_id=1, source_target_pairs={{0,16},{1,17},{16,0},{17,1},{2,18},{3,19},{18,2},{19,3},{4,20},{5,... | collective-permute-start | bytes 589832 | tf_op jit(solution)/shard_map/ppermute | solution.py:55
  99.7 14.3 %collective-permute-start.24 = (bf16[512,192]{1,0:T(8,128)(2,1)}, bf16[512,192]{1,0:T(8,128)(2,1)S(1)}, u32[]{:S(2)}, u32[]{:S(2)}) collective-permute-start(bf16[512,192]{1,0:T(8,128)(2,1)} %get-tuple-element.169.refs_0_), channel_id=1, source_target_pairs={{0,1},{1,0},{16,17},{17,16},{2,3},{3,2},{18,19},{19,18},{4,5},{5,4... | collective-permute-start | bytes 589832 | tf_op jit(solution)/shard_map/ppermute | solution.py:55
  126.9 11.2 %collective-permute-start.31 = (bf16[128,768]{1,0:T(8,128)(2,1)}, bf16[128,768]{1,0:T(8,128)(2,1)S(1)}, u32[]{:S(2)}, u32[]{:S(2)}) collective-permute-start(bf16[128,768]{1,0:T(8,128)(2,1)} %get-tuple-element.176), channel_id=1, source_target_pairs={{0,1},{1,0},{16,17},{17,16},{2,3},{3,2},{18,19},{19,18},{4,5},{5,4... | collective-permute-start | bytes 589832 | tf_op jit(solution)/shard_map/ppermute | solution.py:55
  138.4 15.3 %collective-permute-start.37 = (bf16[4,200,768]{2,1,0:T(8,128)(2,1)}, bf16[4,200,768]{2,1,0:T(8,128)(2,1)S(1)}, u32[]{:S(2)}, u32[]{:S(2)}) collective-permute-start(bf16[4,200,768]{2,1,0:T(8,128)(2,1)} %get-tuple-element.202), channel_id=1, source_target_pairs={{0,8},{8,0},{1,9},{9,1},{2,10},{10,2},{3,11},{11,3},{4,12},{12,4},... | collective-permute-start | bytes 3686408 | tf_op jit(solution)/shard_map/ppermute | solution.py:51
  157.8 48.8 %all-to-all-start.1 = ((bf16[4,200,768]{2,1,0:T(8,128)(2,1)}), bf16[4,200,768]{2,1,0:T(8,128)(2,1)S(1)}, u32[]{:S(2)}, u32[]{:S(2)}) async-start(bf16[4,200,768]{2,1,0:T(8,128)(2,1)} %add.30), calls=%async_computation.1 | async-start | bytes 2457600 | tf_op jit(solution)/shard_map/all_to_all | solution.py:1102
  173.0 15.6 %collective-permute-start.38 = (bf16[2,512,192]{2,1,0:T(8,128)(2,1)}, bf16[2,512,192]{2,1,0:T(8,128)(2,1)S(1)}, u32[]{:S(2)}, u32[]{:S(2)}) collective-permute-start(bf16[2,512,192]{2,1,0:T(8,128)(2,1)} %get-tuple-element.207), channel_id=1, source_target_pairs={{0,8},{8,0},{1,9},{9,1},{2,10},{10,2},{3,11},{11,3},{4,12},{12,4},... | collective-permute-start | bytes 1179656 | tf_op jit(solution)/shard_map/ppermute | solution.py:65
  212.5 33.8 %all-to-all-start.2 = ((bf16[16,24,896]{2,1,0:T(8,128)(2,1)}), bf16[16,24,896]{2,1,0:T(8,128)(2,1)S(1)}, u32[]{:S(2)}, u32[]{:S(2)}) async-start(bf16[16,24,896]{2,1,0:T(8,128)(2,1)} %add.31), calls=%async_computation.2 | async-start | bytes 1376256 | tf_op jit(solution)/shard_map/all_to_all | solution.py:1126
  220.1 23.2 %collective-permute-start.42 = (bf16[128,768]{1,0:T(8,128)(2,1)S(1)}, bf16[128,768]{1,0:T(8,128)(2,1)S(1)}, u32[]{:S(2)}, u32[]{:S(2)}) collective-permute-start(bf16[128,768]{1,0:T(8,128)(2,1)S(1)} %copy-done.19), channel_id=1, source_target_pairs={{0,0},{1,1},{16,2},{17,3},{8,4},{9,5},{24,6},{25,7},{2,8},{3,9},{1... | collective-permute-start | bytes 589832 | tf_op jit(solution)/shard_map/ppermute | solution.py:87
  225.9 20.4 %collective-permute-start.47 = (bf16[128,768]{1,0:T(8,128)(2,1)}, bf16[128,768]{1,0:T(8,128)(2,1)S(1)}, u32[]{:S(2)}, u32[]{:S(2)}) collective-permute-start(bf16[128,768]{1,0:T(8,128)(2,1)} %finish_input.1), channel_id=1, source_target_pairs={{0,0},{1,1},{16,2},{17,3},{8,4},{9,5},{24,6},{25,7},{2,8},{3,9},{1... | collective-permute-start | bytes 589832 | tf_op jit(solution)/shard_map/ppermute | solution.py:87
  227.8 15.5 %collective-permute-start.48 = (bf16[24,768]{1,0:T(8,128)(2,1)S(1)}, bf16[24,768]{1,0:T(8,128)(2,1)S(1)}, u32[]{:S(2)}, u32[]{:S(2)}) collective-permute-start(bf16[24,768]{1,0:T(8,128)(2,1)S(1)} %copy-done.68), channel_id=1, source_target_pairs={{0,1},{1,0},{16,17},{17,16},{2,3},{3,2},{18,19},{19,18},{4,5},{5,4... | collective-permute-start | bytes 110600 | tf_op jit(solution)/shard_map/ppermute | solution.py:55
  229.4 14.0 %collective-permute-start.49 = (bf16[24,768]{1,0:T(8,128)(2,1)S(1)}, bf16[24,768]{1,0:T(8,128)(2,1)S(1)}, u32[]{:S(2)}, u32[]{:S(2)}) collective-permute-start(bf16[24,768]{1,0:T(8,128)(2,1)S(1)} %copy-done.67), channel_id=1, source_target_pairs={{0,16},{1,17},{16,0},{17,1},{2,18},{3,19},{18,2},{19,3},{4,20},{5,... | collective-permute-start | bytes 110600 | tf_op jit(solution)/shard_map/ppermute | solution.py:55
  229.4 14.0 %collective-permute-start.50 = (bf16[24,768]{1,0:T(8,128)(2,1)S(1)}, bf16[24,768]{1,0:T(8,128)(2,1)S(1)}, u32[]{:S(2)}, u32[]{:S(2)}) collective-permute-start(bf16[24,768]{1,0:T(8,128)(2,1)S(1)} %copy-done.66), channel_id=1, source_target_pairs={{0,17},{1,16},{16,1},{17,0},{2,19},{3,18},{18,3},{19,2},{4,21},{5,... | collective-permute-start | bytes 110600 | tf_op jit(solution)/shard_map/ppermute | solution.py:55
  (100 other events, 859.8 us)

commit v3 on v2

--- a/solution.py
+++ b/solution.py
@@ -50,6 +50,11 @@
     def swap(self, value):
         return lax.ppermute(value, "c", [(0, 1), (1, 0)])
 
+    def gather(self, value):
+        return lax.all_to_all(
+            jnp.broadcast_to(value, (TP, *value.shape)), self.tp, 0, 0, tiled=True
+        )
+
     def partner(self, value, j):
         table = [(t, t ^ j) for t in range(TP)]
         return lax.ppermute(value, self.tp, table)
@@ -142,118 +147,108 @@
     return out
 
 
-def prep_kernel(rep_of, idx_ref, q_ref, k_ref, v_ref, small_ref, up_ref, *refs):
-    chunk_refs, hold_ref = refs[:-1], refs[-1]
+def prep_kernel(rep_of, q_ref, k_ref, v_ref, small_ref, up_ref, out_ref, chunk_ref, turn_ref):
     block, width = q_ref.shape
     cols = width // TP
     wide = 3 * cols + SMALLS
     slab = up_ref.shape[1] // len(rep_of)
+    turn_ref[...] = jnp.zeros_like(turn_ref)
+    turn_ref[: small_ref.shape[0], :block] = small_ref[...].astype(f32)
+    small = turn_ref[...].T[:block, :SMALLS]
     for j in range(TP):
         at = slice(j * cols, (j + 1) * cols)
-        hold_ref[j, :, :wide] = jnp.concatenate(
-            [r[:, at].astype(f32) for r in (q_ref, k_ref, v_ref)] + [small_ref[...].astype(f32)],
-            axis=1,
-        )
+        chunk_ref[j, :, :wide] = jnp.concatenate(
+            [r[:, at].astype(f32) for r in (q_ref, k_ref, v_ref)] + [small], axis=1
+        ).astype(bf16)
+        chunk_ref[j, :, wide + width :] = out_ref[...]
     for r, (member, copy) in enumerate(rep_of):
         first = wide + copy * slab
-        hold_ref[member, :, first : first + slab] = up_ref[:, r * slab : (r + 1) * slab].astype(f32)
-    for j, ref in enumerate(chunk_refs):
-        ref[...] = hold_ref[idx_ref[0] ^ j].astype(bf16)
-
-
-def prepare(plan, idx, w_query, w_key, w_value, small, w_up):
+        chunk_ref[member, :, first : first + slab] = up_ref[:, r * slab : (r + 1) * slab]
+
+
+def prepare(plan, w_query, w_key, w_value, small, w_up, w_out):
     block, width = w_query.shape
     rep_of = [plan.place(r) for r in range(plan.devices)]
-    shape = (block, 3 * width // TP + SMALLS + w_up.shape[1] // TP)
+    wide = 3 * width // TP + SMALLS
     return pl.pallas_call(
         functools.partial(prep_kernel, rep_of),
-        in_specs=[pl.BlockSpec(memory_space=pltpu.SMEM)]
-        + [pl.BlockSpec(memory_space=pltpu.VMEM)] * 5,
-        out_shape=[jax.ShapeDtypeStruct(shape, bf16)] * TP,
-        scratch_shapes=[pltpu.VMEM((TP, *shape), f32)],
+        out_shape=jax.ShapeDtypeStruct((TP, block, wide + w_up.shape[1] // TP + width), bf16),
+        scratch_shapes=[pltpu.VMEM((128, 128), f32)],
         cost_estimate=cost(1000, 4 * w_up.size),
         name="prepare",
-    )(idx, w_query, w_key, w_value, small, w_up)
-
-
-def shards_kernel(idx_ref, *refs):
-    part_refs, (proj_ref, up_ref, hold_ref) = refs[:TP], refs[TP:]
-    for j, ref in enumerate(part_refs):
-        hold_ref[idx_ref[0] ^ j] = ref[...].astype(f32)
-    wide = proj_ref.shape[1]
-    value = hold_ref[...].reshape(proj_ref.shape[0], -1).astype(bf16)
-    proj_ref[...] = value[:, :wide]
-    up_ref[...] = value[:, wide:]
-
-
-def shards_of(idx, parts, wide):
-    block, both = parts[0].shape
-    return pl.pallas_call(
-        shards_kernel,
-        in_specs=[pl.BlockSpec(memory_space=pltpu.SMEM)]
-        + [pl.BlockSpec(memory_space=pltpu.VMEM)] * TP,
+    )(w_query, w_key, w_value, small, w_up, w_out)
+
+
+def shards_kernel(wide, got_ref, down_ref, row_ref, proj_ref, shard_ref):
+    block = got_ref.shape[1]
+    slab, width = down_ref.shape
+    first = TP * block
+    for t in range(TP):
+        at = t * block
+        proj_ref[at : at + block, :] = got_ref[t, :, :wide]
+        up = got_ref[t, :, wide : wide + width]
+        out = got_ref[t, :, wide + width :]
+        for n in range(shard_ref.shape[0]):
+            shard_ref[n, at : at + block, :] = up
+            shard_ref[n, first + at : first + at + block, :] = out
+    row = jnp.concatenate([row_ref[...].astype(f32), jnp.zeros((1, width - slab), f32)], axis=1)
+    row = jnp.broadcast_to(row, (8, width)).astype(bf16)
+    for n in range(shard_ref.shape[0]):
+        shard_ref[n, 2 * first : 2 * first + slab, :] = down_ref[...]
+        shard_ref[n, 2 * first + slab :, :] = row
+
+
+def shards_of(got, w_down, b_row, wide, lines):
+    _, block, _ = got.shape
+    slab, width = w_down.shape
+    return pl.pallas_call(
+        functools.partial(shards_kernel, wide),
         out_shape=[
             jax.ShapeDtypeStruct((TP * block, wide), bf16),
-            jax.ShapeDtypeStruct((TP * block, both - wide), bf16),
+            jax.ShapeDtypeStruct((lines, 2 * TP * block + slab + 8, width), bf16),
         ],
-        scratch_shapes=[pltpu.VMEM((TP, block, both), f32)],
-        cost_estimate=cost(1000, 8 * TP * block * both),
+        cost_estimate=cost(1000, 4 * lines * slab * width),
         name="shards_of",
-    )(idx, *parts)
-
-
-def assemble_kernel(plan, idx_ref, *refs):
-    lines = plan.copies // 2
-    sides = refs[: 2 * (1 + lines + TP)]
-    up_ref, out_ref, down_ref, row_ref, wide_ref = refs[2 * (1 + lines + TP) :]
-    member, core, line = idx_ref[0], idx_ref[2], idx_ref[3]
-    block = up_ref.shape[0] // plan.devices
+    )(got, w_down, b_row)
+
+
+def assemble_kernel(plan, idx_ref, own_ref, other_ref, up_ref, out_ref, down_ref, row_ref, wide_ref):
+    core = idx_ref[2]
     slab = down_ref.shape[2]
-    pair = plan.size["sy"] * block
-    for n, side in ((0, core), (1, 1 - core)):
-        mine = sides[n * (1 + lines + TP) : (n + 1) * (1 + lines + TP)]
-        raw_ref, up_refs, out_refs = mine[0], mine[1 : 1 + lines], mine[1 + lines :]
-        for z in range(lines):
-            down_ref[side, z] = raw_ref[z, block : block + slab, :]
-            row_ref[side, z] = raw_ref[z, block + slab :, :]
-        for j, ref in enumerate(up_refs):
-            z = lax.rem(line + j, lines)
-            value = ref[...].astype(f32)
+    first = TP * up_ref.shape[0] // plan.devices
+    pair = first // plan.size["gx"]
+    for ref, side in ((own_ref, core), (other_ref, 1 - core)):
+        for z in range(ref.shape[0]):
+            value = ref[z, : 2 * first, :].astype(f32)
             for gx in range(plan.size["gx"]):
-                for sy in range(plan.size["sy"]):
-                    at = gx * pair + sy * block
-                    wide_ref[0, gx * 2 + side, z, sy] = value[at : at + block]
-        for j, ref in enumerate(out_refs):
-            other = member ^ j
-            gx, sy = other // plan.size["sy"], lax.rem(other, plan.size["sy"])
-            for z in range(lines):
-                wide_ref[1, gx * 2 + side, z, sy] = ref[z].astype(f32)
+                at = gx * pair
+                wide_ref[0, gx * 2 + side, z] = value[at : at + pair]
+                wide_ref[1, gx * 2 + side, z] = value[first + at : first + at + pair]
+            down_ref[side, z] = ref[z, 2 * first : 2 * first + slab, :]
+            row_ref[side, z] = ref[z, 2 * first + slab :, :]
     for ref, k in ((up_ref, 0), (out_ref, 1)):
         ref[...] = wide_ref[k].reshape(ref.shape).astype(bf16)
 
 
-def assemble(plan, idx, own, other, block, slab):
-    width = own[0].shape[2]
-    lines = plan.copies // 2
+def assemble(plan, idx, own, other, slab):
+    lines, _, width = own.shape
     hidden = plan.copies * slab
-    operands = [*own, *other]
+    pair = plan.size["sy"] * width // plan.devices
     return pl.pallas_call(
         functools.partial(assemble_kernel, plan),
         in_specs=[pl.BlockSpec(memory_space=pltpu.SMEM)]
-        + [pl.BlockSpec(memory_space=pltpu.VMEM)] * len(operands),
+        + [pl.BlockSpec(memory_space=pltpu.VMEM)] * 2,
         out_shape=[
             jax.ShapeDtypeStruct((width, hidden), bf16),
             jax.ShapeDtypeStruct((width, width), bf16),
             jax.ShapeDtypeStruct((2, lines, slab, width), bf16),
             jax.ShapeDtypeStruct((2, lines, 8, width), bf16),
         ],
-        scratch_shapes=[
-            pltpu.VMEM((2, 2 * plan.size["gx"], lines, plan.size["sy"], block, width), f32)
-        ],
+        scratch_shapes=[pltpu.VMEM((2, 2 * plan.size["gx"], lines, pair, width), f32)],
         compiler_params=pltpu.CompilerParams(vmem_limit_bytes=60 * 1024 * 1024),
         cost_estimate=cost(1000, 12 * width * width),
         name="assemble",
-    )(idx, *operands)
+    )(idx, own, other)
 
 
 def qkv_kernel(plan, idx_ref, x_ref, *refs):
@@ -295,7 +290,7 @@
 def qkv(plan, idx, x_all, *operands):
     rows, width = x_all.shape
     cols = width // TP
-    step = rows // TP
+    step = rows // 2
     wide = 3 * cols + SMALLS
     out_specs = [
         pl.BlockSpec((step, width), lambda i, *_: (i, 0)),
@@ -320,7 +315,7 @@
         functools.partial(qkv_kernel, plan),
         grid_spec=pltpu.PrefetchScalarGridSpec(
             num_scalar_prefetch=1,
-            grid=(TP,),
+            grid=(2,),
             in_specs=[pl.BlockSpec((step, width), lambda i, *_: (i, 0))]
             + [whole(v.shape) for v in operands],
             out_specs=out_specs,
@@ -519,29 +514,31 @@
     )(idx, ids, q, w_out, lse, *das, *kvs)
 
 
-def mlp_kernel(idx_ref, x_ref, *refs):
-    o_refs, dm_refs, refs = refs[:TP], refs[TP : 2 * TP], refs[2 * TP :]
+def mlp_kernel(idx_ref, x_ref, o_ref, *refs):
+    dm_refs, refs = refs[:TP], refs[TP:]
     wo_ref, wu_ref, wd_ref, vec_ref, bup_ref, r_ref, h_ref, a_ref, du_ref, dm_ref, sum_ref = refs[:11]
-    dh_refs, dm_now, dh_now = refs[11 : 11 + TP], refs[-2], refs[-1]
+    dh_refs, dm_now, r_now, dh_now = refs[11 : 11 + TP], refs[-3], refs[-2], refs[-1]
     step = pl.program_id(0)
-    member = idx_ref[0]
+    side = lax.rem(idx_ref[0], 2)
 
     @pl.when(step == 0)
     def _():
         sum_ref[...] = jnp.zeros_like(sum_ref)
 
-    attended = dot(o_refs[0][...], wo_ref[member])
+    attended = dot(o_ref[0], wo_ref[0])
     for j in range(1, TP):
-        attended += dot(o_refs[j][...], wo_ref[member ^ j])
+        attended += dot(o_ref[j], wo_ref[j])
     residual = x_ref[...].astype(f32) + (attended + vec_ref[2:3, :])
 
-    for j in range(TP):
-
-        @pl.when(step == j)
-        def _(j=j):
-            dm_now[...] = dm_refs[j][...]
-            if j == 0:
-                r_ref[...] = residual
+    for i in range(2):
+
+        @pl.when(step == i)
+        def _(i=i):
+            for b in range(2):
+                dm_now[side ^ b] = dm_refs[2 * i + b][...]
+            if i == 0:
+                r_now[...] = residual.reshape(r_now.shape)
+                r_ref[...] = r_now[side]
 
     units, _ = unit(residual)
     low = (units * vec_ref[5:6, :] + vec_ref[6:7, :]).astype(bf16)
@@ -551,55 +548,59 @@
     act = (pre * normal).astype(bf16)
     a_ref[...] = act
     slope = normal + pre * (0.3989422804014327 * jnp.exp(-0.5 * pre * pre))
-    dm = dm_now[...]
+    dm = dm_now[...].reshape(x_ref.shape)
     dm_ref[...] = dm
     grad_pre = (dot(dm, wd_ref[...], 1, 1) * slope).astype(bf16)
     du_ref[...] = grad_pre
     grad = dot(grad_pre, wu_ref[...], 1, 1)
     sum_ref[0:1, :] += jnp.sum(grad * units, axis=0, keepdims=True)
     sum_ref[1:2, :] += jnp.sum(grad, axis=0, keepdims=True)
-    dh_now[...] = grad.astype(bf16)
-    for j in range(TP):
-
-        @pl.when(step == j)
-        def _(j=j):
-            dh_refs[j][...] = dh_now[...]
-
-
-def mlp(idx, x_all, os, dms, w_out, w_up, w_down, vecs, b_up):
+    dh_now[...] = grad.astype(bf16).reshape(dh_now.shape)
+    for i in range(2):
+
+        @pl.when(step == i)
+        def _(i=i):
+            for b in range(2):
+                dh_refs[2 * i + b][...] = dh_now[side ^ b]
+
+
+def mlp(idx, x_all, o_all, dms, w_out, w_up, w_down, vecs, b_up):
     rows, width = x_all.shape
     hidden = w_up.shape[1]
     cols = width // TP
-    step = rows // TP
-    token = pl.BlockSpec((step, width), lambda i, idx: (i ^ idx[0], 0))
-    inner = pl.BlockSpec((step, hidden), lambda i, idx: (i ^ idx[0], 0))
-    head = pl.BlockSpec((step, cols), lambda i, idx: (i ^ idx[0], 0))
-    one = whole((step, width))
+    step = rows // 2
+
+    def block(i, idx):
+        return (i ^ (idx[0] // 2), 0)
+
+    token = pl.BlockSpec((step, width), block)
+    inner = pl.BlockSpec((step, hidden), block)
+    one = whole((rows // TP, width))
+    now = (2, rows // TP, width)
     return pl.pallas_call(
         mlp_kernel,
         grid_spec=pltpu.PrefetchScalarGridSpec(
             num_scalar_prefetch=1,
-            grid=(TP,),
-            in_specs=[token]
-            + [head] * TP
+            grid=(2,),
+            in_specs=[token, pl.BlockSpec((TP, step, cols), lambda i, idx: (0, i ^ (idx[0] // 2), 0))]
             + [one] * TP
             + [whole(v.shape) for v in (w_out, w_up, w_down, vecs, b_up)],
             out_specs=[one, token, inner, inner, token, whole((8, width))] + [one] * TP,
-            scratch_shapes=[pltpu.VMEM((step, width), bf16), pltpu.VMEM((step, width), bf16)],
+            scratch_shapes=[pltpu.VMEM(now, bf16), pltpu.VMEM(now, f32), pltpu.VMEM(now, bf16)],
         ),
         out_shape=[
-            jax.ShapeDtypeStruct((step, width), f32),
+            jax.ShapeDtypeStruct((rows // TP, width), f32),
             jax.ShapeDtypeStruct((rows, width), bf16),
             jax.ShapeDtypeStruct((rows, hidden), bf16),
             jax.ShapeDtypeStruct((rows, hidden), bf16),
             jax.ShapeDtypeStruct((rows, width), bf16),
             jax.ShapeDtypeStruct((8, width), f32),
         ]
-        + [jax.ShapeDtypeStruct((step, width), bf16)] * TP,
+        + [jax.ShapeDtypeStruct((rows // TP, width), bf16)] * TP,
         compiler_params=params(),
         cost_estimate=cost(2 * rows * width * (width + 3 * hidden), rows * width * 24, rows * hidden * 4),
         name="mlp",
-    )(idx, x_all, *os, *dms, w_out, w_up, w_down, vecs, b_up)
+    )(idx, x_all, o_all, *dms, w_out, w_up, w_down, vecs, b_up)
 
 
 def pair_kernel(plan, idx_ref, h_ref, du_ref, a_ref, dm_ref, wd_ref, near_ref, far_ref, *refs):
@@ -793,41 +794,29 @@
     )(r_own, dm, vecs, *parts)
 
 
-def output_kernel(r_ref, vec_ref, *refs):
-    total = r_ref[...] + vec_ref[7:8, :]
-    for ref in refs[:TP]:
-        total += ref[...].astype(f32)
-    refs[TP][...] = total.astype(bf16)
-
-
-def finish_output(parts, r_own, vecs):
-    return pl.pallas_call(
-        output_kernel,
-        out_shape=jax.ShapeDtypeStruct(r_own.shape, bf16),
-        cost_estimate=cost(8 * r_own.size, r_own.size * 14),
-        name="finish_output",
-    )(r_own, vecs, *parts)
-
-
-def input_kernel(x_ref, dr_ref, vec_ref, *refs):
+def finish_kernel(r_ref, x_ref, dr_ref, vec_ref, *refs):
+    rows = r_ref.shape[0]
     total = refs[0][...].astype(f32)
     for ref in refs[1:TP]:
         total += ref[...].astype(f32)
     units, rstd = unit(x_ref[...].astype(f32))
-    grad = dr_ref[...] + unit_back(total * vec_ref[3:4, :], units, rstd)
-    refs[TP][...] = grad.astype(bf16)
-
-
-def finish_input(parts, x, dr, vecs):
-    return pl.pallas_call(
-        input_kernel,
-        out_shape=jax.ShapeDtypeStruct(x.shape, bf16),
-        cost_estimate=cost(30 * x.size, x.size * 16),
-        name="finish_input",
-    )(x, dr, vecs, *parts)
+    grad = dr_ref[...] + unit_back(total[:rows] * vec_ref[3:4, :], units, rstd)
+    refs[TP][:rows, :] = (r_ref[...] + vec_ref[7:8, :] + total[rows:]).astype(bf16)
+    refs[TP][rows:, :] = grad.astype(bf16)
+
+
+def finish(parts, r_own, x, dr, vecs):
+    rows, width = x.shape
+    return pl.pallas_call(
+        finish_kernel,
+        out_shape=jax.ShapeDtypeStruct((2 * rows, width), bf16),
+        cost_estimate=cost(40 * x.size, x.size * 30),
+        name="finish",
+    )(r_own, x, dr, vecs, *parts)
 
 
 def normed_kernel(n_recv, idx_ref, x_ref, dq_ref, own_ref, *refs):
+    out_refs, refs = refs[:TP], refs[TP:]
     recv_refs = refs[:n_recv]
     w_ref, d_ref, sum_ref = refs[n_recv : n_recv + 3]
     dh_refs, dh_now = refs[n_recv + 3 : -1], refs[-1]
@@ -849,12 +838,16 @@
     d_ref[:, 3 * cols :] = jnp.zeros_like(d_ref[:, 3 * cols :])
     low = d_ref[...]
     grad = dot(low, w_ref[...], 1, 1)
-    dh_now[...] = grad.astype(bf16)
-    for j in range(TP):
-
-        @pl.when(step == j)
-        def _(j=j):
-            dh_refs[j][...] = dh_now[...]
+    dh_now[...] = grad.astype(bf16).reshape(dh_now.shape)
+    side = lax.rem(idx_ref[0], 2)
+    for i in range(2):
+
+        @pl.when(step == i)
+        def _(i=i):
+            for b in range(2):
+                rows = dh_now.shape[1]
+                dh_refs[2 * i + b][:rows, :] = dh_now[side ^ b]
+                dh_refs[2 * i + b][rows:, :] = out_refs[2 * i + b][...]
 
     units, _ = unit(x_ref[...].astype(f32))
     sum_ref[0:1, :width] += jnp.sum(grad * units, axis=0, keepdims=True)
@@ -862,55 +855,56 @@
     sum_ref[2:3, : low.shape[1]] += jnp.sum(low.astype(f32), axis=0, keepdims=True)
 
 
-def normed_back(idx, x_all, dq, own, recvs, w_qkv):
+def normed_back(idx, x_all, dq, own, recvs, w_qkv, out_terms):
     rows, width = x_all.shape
     cols = dq.shape[1]
     wide = w_qkv.shape[1]
-    step = rows // TP
-    pairs = pl.BlockSpec((2, step, cols), lambda i, idx: (0, i ^ idx[0], 0))
+    step = rows // 2
+    one = (rows // TP, width)
+    pairs = pl.BlockSpec((2, step, cols), lambda i, idx: (0, i ^ (idx[0] // 2), 0))
     return pl.pallas_call(
         functools.partial(normed_kernel, len(recvs)),
         grid_spec=pltpu.PrefetchScalarGridSpec(
             num_scalar_prefetch=1,
-            grid=(TP,),
+            grid=(2,),
             in_specs=[
-                pl.BlockSpec((step, width), lambda i, idx: (i ^ idx[0], 0)),
-                pl.BlockSpec((step, cols), lambda i, idx: (i ^ idx[0], 0)),
+                pl.BlockSpec((step, width), lambda i, idx: (i ^ (idx[0] // 2), 0)),
+                pl.BlockSpec((step, cols), lambda i, idx: (i ^ (idx[0] // 2), 0)),
                 pairs,
             ]
+            + [whole(one)] * TP
             + [pairs] * len(recvs)
             + [whole(w_qkv.shape)],
             out_specs=[
-                pl.BlockSpec((step, wide), lambda i, idx: (i ^ idx[0], 0)),
+                pl.BlockSpec((step, wide), lambda i, idx: (i ^ (idx[0] // 2), 0)),
                 whole((8, width)),
             ]
-            + [whole((step, width))] * TP,
-            scratch_shapes=[pltpu.VMEM((step, width), bf16)],
+            + [whole((2 * one[0], width))] * TP,
+            scratch_shapes=[pltpu.VMEM((2, *one), bf16)],
         ),
         out_shape=[
             jax.ShapeDtypeStruct((rows, wide), bf16),
             jax.ShapeDtypeStruct((8, width), f32),
         ]
-        + [jax.ShapeDtypeStruct((step, width), bf16)] * TP,
+        + [jax.ShapeDtypeStruct((2 * one[0], width), bf16)] * TP,
         compiler_params=params(),
         cost_estimate=cost(2 * rows * width * wide, rows * width * 12),
         name="normed_back",
-    )(idx, x_all, dq, own, *recvs, w_qkv)
-
-
-def proj_grads_kernel(plan, idx_ref, h_ref, d_ref, sum_ref, own_ref, two_ref, da_ref, *refs):
-    o_refs, refs = refs[:TP], refs[TP:]
+    )(idx, x_all, dq, own, *out_terms, *recvs, w_qkv)
+
+
+def proj_grads_kernel(plan, idx_ref, h_ref, d_ref, sum_ref, own_ref, two_ref, da_ref, o_ref, *refs):
     fast = plan.fast
-    acc_ref, out_acc, vec_ref = refs[-3:]
+    acc_ref, vec_ref = refs[-2:]
     wide = d_ref.shape[1]
-    cols = o_refs[0].shape[1]
+    cols = o_ref.shape[2]
     rows, width = h_ref.shape
     member = idx_ref[0]
     acc_ref[:, :wide] = dot(h_ref[...], d_ref[...], 0, 0)
     da = da_ref[...].reshape(rows, cols)
     for j in range(TP):
-        out_acc[member ^ j] = dot(o_refs[j][...], da, 0, 0)
-    acc_ref[:, wide : wide + cols] = out_acc[...].reshape(width, cols)
+        at = j * cols
+        acc_ref[at : at + cols, wide : wide + cols] = dot(o_ref[j], da, 0, 0)
     bias_q, bias_v = sum_ref[2:3, :cols], sum_ref[2:3, 2 * cols : 3 * cols]
     zero = jnp.zeros_like(bias_q)
     vec_ref[...] = jnp.zeros_like(vec_ref)
@@ -936,16 +930,16 @@
             ref[n] = acc_ref[pl.ds(pl.multiple_of(at, 8), block), :].astype(bf16)
 
 
-def proj_grads(plan, idx, low, grads, sums, sum_own, sum_two, da_cols, os):
+def proj_grads(plan, idx, low, grads, sums, sum_own, sum_two, da_cols, o_all):
     rows, width = low.shape
-    cols = os[0].shape[1]
+    cols = o_all.shape[2]
     wide = grads.shape[1] + cols + SMALLS
     near = plan.devices // 2
     if plan.fast:
         out_shape = [jax.ShapeDtypeStruct((near, width // plan.devices, wide), bf16)] * 2
     else:
         out_shape = jax.ShapeDtypeStruct((width, wide), bf16)
-    operands = (low, grads, sums, sum_own, sum_two, da_cols, *os)
+    operands = (low, grads, sums, sum_own, sum_two, da_cols, o_all)
     return pl.pallas_call(
         functools.partial(proj_grads_kernel, plan),
         in_specs=[pl.BlockSpec(memory_space=pltpu.SMEM)]
@@ -953,7 +947,6 @@
         out_shape=out_shape,
         scratch_shapes=[
             pltpu.VMEM((width, wide), f32),
-            pltpu.VMEM((TP, cols, cols), f32),
             pltpu.VMEM((2 * SMALLS, width), f32),
         ],
         compiler_params=pltpu.CompilerParams(vmem_limit_bytes=60 * 1024 * 1024),
@@ -962,8 +955,12 @@
     )(idx, *operands)
 
 
-def join_kernel(keep, cols, wide, in_ref, *out_refs):
-    *mats, vec_ref = out_refs
+def join_kernel(keep, cols, wide, in_ref, both_ref, *refs):
+    mats, vec_refs = refs[:4], refs[4:12]
+    output_ref, input_ref, turn_ref = refs[12:]
+    rows = output_ref.shape[0]
+    output_ref[...] = both_ref[:rows, :]
+    input_ref[...] = both_ref[rows:, :]
     groups = {}
     for n in range(in_ref.shape[0]):
         value = in_ref[n].astype(f32)
@@ -973,28 +970,28 @@
         for ref, at in zip(mats, (0, cols, 2 * cols, wide)):
             ref[:, j * cols : (j + 1) * cols] = groups[j][:, at : at + cols]
     total = functools.reduce(jnp.add, [groups[j] for j in range(TP)])
-    vec_ref[...] = total[:, wide + cols :]
-
-
-def join_grads(plan, got, cols, wide):
+    block = in_ref.shape[1]
+    turn_ref[...] = jnp.zeros_like(turn_ref)
+    turn_ref[:block, :SMALLS] = total[:, wide + cols :]
+    turned = turn_ref[...].T
+    for j, ref in enumerate(vec_refs):
+        ref[...] = turned[j : j + 1, :block]
+
+
+def join_grads(plan, got, both, cols, wide):
     near, block, _ = got.shape
-    dims = [plan.size[a] for a in SAME]
-    members = []
-    for n in range(near):
-        place = dict(zip(SAME, (n // (dims[1] * dims[2]), n // dims[2] % dims[1], n % dims[2])))
-        member = 0
-        for axis in plan.tp:
-            member = member * plan.size[axis] + place[axis]
-        members.append(member)
+    members = [plan.place(plan.same(n))[0] for n in range(near)]
     width = cols * TP
     return pl.pallas_call(
         functools.partial(join_kernel, members, cols, wide),
         out_shape=[jax.ShapeDtypeStruct((block, width), f32)] * 4
-        + [jax.ShapeDtypeStruct((block, SMALLS), f32)],
+        + [jax.ShapeDtypeStruct((1, block), f32)] * 8
+        + [jax.ShapeDtypeStruct((both.shape[0] // 2, both.shape[1]), bf16)] * 2,
+        scratch_shapes=[pltpu.VMEM((128, 128), f32)],
         compiler_params=pltpu.CompilerParams(vmem_limit_bytes=60 * 1024 * 1024),
         cost_estimate=cost(got.size, got.size * 2),
         name="join_grads",
-    )(got)
+    )(got, both)
 
 
 def local(
@@ -1022,26 +1019,24 @@
     ids = moved[rows:].reshape(1, -1)[:, :length].astype(f32)
     dm_own = (cotangent[0].astype(f32) * padding[0].astype(f32)[:, None]).astype(bf16)
     dm_mine = plan.move(dm_own, plan.route)
-    x_all = lax.all_gather(x_mine, plan.tp, axis=0, tiled=True)
 
     small = [b_query, b_value, b_out, ln1_gain, ln1_shift, ln2_gain, ln2_shift, b_down]
-    small = jnp.stack(small, axis=1)
-    b_row = jnp.pad(b_up[None], ((0, 7), (0, width - slab)))
     if fast:
-        small = jnp.pad(small, ((0, 0), (0, SMALLS - small.shape[1])))
-        raw = jnp.concatenate([w_out, w_down, b_row], axis=0)
-        raw = jnp.broadcast_to(raw, (lines, *raw.shape))
-        raw = lax.all_to_all(raw, "sz", 0, 0, tiled=True)
-        chunks = prepare(plan, idx, w_query, w_key, w_value, small, w_up)
-        proj, up = shards_of(idx, plan.reduce(chunks), 3 * cols + SMALLS)
+        small = jnp.stack(small, axis=0)
+        chunk = prepare(plan, w_query, w_key, w_value, small, w_up, w_out)
+        got = lax.all_to_all(chunk, plan.tp, 0, 0, tiled=True)
+        got, x_mine = lax.optimization_barrier((got, x_mine))
+        x_all = lax.all_gather(x_mine, plan.tp, axis=0, tiled=True)
+        proj, shard = shards_of(got, w_down, b_up[None], 3 * cols + SMALLS, lines)
         projs = [proj] + [plan.turn(proj, "sz", -j) for j in range(1, lines)]
-        projs, x_all = lax.optimization_barrier((projs, x_all))
+        projs, x_all, shard, dm_mine = lax.optimization_barrier((projs, x_all, shard, dm_mine))
+        shard = lax.all_to_all(shard, "sz", 0, 0, tiled=True)
         projs = jnp.stack(projs)
         low_one, query, kv, w_qkv, vecs = qkv(plan, idx, x_all, projs, plan.swap(projs))
-        ups = [up] + [plan.turn(up, "sz", -j) for j in range(1, lines)]
-        outs = plan.partners(raw[:, :block])
-        ups, outs, query = lax.optimization_barrier((ups, outs, query))
     else:
+        small = jnp.stack(small, axis=1)
+        x_all = lax.all_gather(x_mine, plan.tp, axis=0, tiled=True)
+        b_row = jnp.pad(b_up[None], ((0, 7), (0, width - slab)))
         table = [w_query, w_key, w_value, w_out, small]
         table = lax.all_gather(jnp.concatenate(table, axis=1), ALL, axis=0, tiled=True)
         vecs = table[:, 4 * width :].T.astype(f32)
@@ -1062,18 +1057,16 @@
     parts = plan.parts
     kvs = [kv] + [plan.turn(kv, plan.half, -j) for j in range(1, parts)]
     mixed, lse = attend(idx, ids, query, kvs)
+    o_all = lax.all_gather(mixed, plan.tp, axis=0, tiled=False)
+    dms = plan.partners(dm_mine)
     if fast:
-        raw, ups, outs, mixed = lax.optimization_barrier((raw, ups, outs, mixed))
-        own = [raw, *ups, *outs]
-        other = [plan.swap(v) for v in own]
-        up_mine, out_full, down_mine, row = assemble(plan, idx, own, other, block, slab)
+        shard, o_all, dms = lax.optimization_barrier((shard, o_all, dms))
+        up_mine, out_full, down_mine, row = assemble(plan, idx, shard, plan.swap(shard), slab)
         out_full = out_full.reshape(TP, cols, width)
         down_mine = down_mine.reshape(-1, width)
         b_up_mine = row[:, :, 0, :slab].reshape(1, -1).astype(f32)
-    os = plan.partners(mixed)
-    dms = plan.partners(dm_mine)
     r_own, low_two, act, grad_pre, dm_all, sum_two, *dh_two = mlp(
-        idx, x_all, os, dms, out_full, up_mine, down_mine, vecs, b_up_mine
+        idx, x_all, o_all, dms, out_full, up_mine, down_mine, vecs, b_up_mine
     )
 
     back_two = plan.reduce(dh_two)
@@ -1091,17 +1084,15 @@
             lax.dynamic_index_in_dim(out_terms, member ^ j, 0, keepdims=False) for j in range(TP)
         ]
     dr, da, sum_own = resid_back(back_two, r_own, dm_mine, vecs)
-    das = plan.partners(da)
-    das, out_terms = lax.optimization_barrier((das, out_terms))
-    out_parts = plan.reduce(out_terms)
-    output = finish_output(out_parts, r_own, vecs)
-
     if fast:
         terms = add(near_terms, plan.swap(far_terms))
-        das, terms = lax.optimization_barrier((das, terms))
+        das = [da, plan.partner(da, 1), plan.partner(da, 2)]
+        terms, da = lax.optimization_barrier((terms, da))
+        das += [plan.partner(da, 3)]
         terms = lax.all_to_all(terms, "sz", 0, 0, tiled=True)
         *ups, g_w_down, g_b_up = sum_rows(plan, idx, terms, block, slab)
     else:
+        das = plan.partners(da)
         row = jnp.pad(row.reshape(plan.copies, 1, slab), ((0, 0), (0, 7), (0, width - slab)))
         downs = jnp.concatenate([down_terms.reshape(plan.copies, slab, width), row], axis=1)
         downs = lax.psum_scatter(downs, plan.rep, scatter_dimension=0, tiled=False)
@@ -1113,16 +1104,13 @@
         ups = lax.all_to_all(ups.reshape(TP, block, -1), plan.tp, 0, 0, tiled=True).astype(f32)
     grad_query, kv_own, da_cols, *kv_others = attend_back(idx, ids, query, das, out_full, lse, kvs)
     recvs = [plan.turn(kv_others[j - 1], plan.half, j) for j in range(1, parts)]
-    recvs, output = lax.optimization_barrier((recvs, output))
-    grads, sum_one, *dh_one = normed_back(idx, x_all, grad_query, kv_own, recvs, w_qkv)
-    back_one = plan.reduce(dh_one)
-    output, sum_one = lax.optimization_barrier((output, sum_one))
-    output = plan.move(output, plan.back)
-    terms = proj_grads(plan, idx, low_one, grads, sum_one, sum_own, sum_two, da_cols, os)
+    grads, sum_one, *both = normed_back(idx, x_all, grad_query, kv_own, recvs, w_qkv, out_terms)
+    both = plan.reduce(both)
+    terms = proj_grads(plan, idx, low_one, grads, sum_one, sum_own, sum_two, da_cols, o_all)
     if fast:
         keep, send = terms
         terms = add(keep, plan.swap(send))
-        terms, back_one, ups = lax.optimization_barrier((terms, back_one, ups))
+        terms, ups, both = lax.optimization_barrier((terms, ups, both))
         got = lax.all_to_all(terms, SAME, 0, 0, tiled=True)
     else:
         terms = plan.shuffle(terms.reshape(plan.devices, block, -1), ALL, ("c",) + SAME)
@@ -1136,27 +1124,28 @@
         ups = ups.reshape(TP, block, plan.copies, slab).transpose(0, 2, 1, 3)
         ups = plan.shuffle(ups.reshape(plan.devices, block, slab), plan.tp + plan.rep, ALL)
         g_w_up = ups.transpose(1, 0, 2).reshape(block, hidden)
-    g_query, g_key, g_value, g_out, vec = join_grads(plan, got, cols, w_qkv.shape[1])
-
-    grad_input = plan.move(finish_input(back_one, x_mine, dr, vecs), plan.back)
+    both = plan.move(finish(both, r_own, x_mine, dr, vecs), plan.back)
+    joined = join_grads(plan, got, both, cols, w_qkv.shape[1])
+    g_query, g_key, g_value, g_out, *vec, output, grad_input = joined
+    vec = [v[0] for v in vec]
     return (
         output[None],
         grad_input[None],
         g_query,
-        vec[:, 0],
+        vec[0],
         g_key,
         g_value,
-        vec[:, 1],
+        vec[1],
         g_out,
-        vec[:, 2],
-        vec[:, 3],
-        vec[:, 4],
-        vec[:, 5],
-        vec[:, 6],
+        vec[2],
+        vec[3],
+        vec[4],
+        vec[5],
+        vec[6],
         g_w_up,
         g_b_up,
         g_w_down,
-        vec[:, 7],
+        vec[7],
     )
 
 

time: 254 us -> 222 us (0.87)
  starting transfers between devices: 77.5 us -> 50.5 us
  blocking collectives: 11.7 us -> 26.6 us
  waiting for transfers between devices: 60 us -> 51 us
  Pallas kernels: 80.7 us -> 75.7 us
  local copies, waits for them, and re-layouts: 16.2 us -> 11.9 us
    ppermute x27 -> x15, waiting for transfers between devices: 40.3 us -> 24.6 us  [partner(): return lax.ppermute(value, self.tp, table)]
    all_gather x0 -> x1, blocking collectives: none -> 14.2 us  [local(): o_all = lax.all_gather(mixed, plan.tp, axis=0, tiled=False)]
    ppermute x27 -> x15, starting transfers between devices: 31.6 us -> 17.7 us  [partner(): return lax.ppermute(value, self.tp, table)]
    all_to_all x1 -> x2, waiting for transfers between devices: 0.01 us -> 10.1 us  [the longest x1 5.47 us: local(): got = lax.all_to_all(chunk, plan.tp, 0, 0, tiled=True)]
    ppermute x4 -> x3, waiting for transfers between devices: 19.2 us -> 9.05 us  [move(): return lax.ppermute(value, ALL, table)]
    ppermute x12 -> x4, starting transfers between devices: 7.18 us -> 0.22 us  [swap(): return lax.ppermute(value, 'c', [(0, 1), (1, 0)])]
    ppermute x8 -> x5, starting transfers between devices: 10.4 us -> 4.1 us  [turn(): lax.ppermute(value, axis, [(i, (i + by) % count) for i in range(count)])]
    all_to_all x1 -> x2, starting transfers between devices: 3.49 us -> 8.38 us  [the longest x1 4.25 us: local(): got = lax.all_to_all(chunk, plan.tp, 0, 0, tiled=True)]
  transfers between devices with their start and end apart: 54 -> 31, of which waited for: 22 -> 15; matrix products, arithmetic and copies ran while one was open for 2% -> 1% of each run, Pallas kernels for 22% -> 26%
where the time goes in v3:
time: 222 us; the launch traced here: 221 us
  Pallas kernels  75.7 us (34%)
  waiting for transfers between devices  51 us (23%)
  starting transfers between devices  50.5 us (23%)
  blocking collectives  26.6 us (12%)
  local copies, waits for them, and re-layouts  11.9 us (5%)
  other arithmetic  3.79 us (2%)
    ppermute x15, waiting for transfers between devices, partner(): return lax.ppermute(value, self.tp, table)  24.6 us
    ppermute x15, starting transfers between devices, partner(): return lax.ppermute(value, self.tp, table)  17.7 us
    all_gather x1, blocking collectives, local(): o_all = lax.all_gather(mixed, plan.tp, axis=0, tiled=False)  14.2 us
    all_gather x1, blocking collectives, local(): x_all = lax.all_gather(x_mine, plan.tp, axis=0, tiled=True)  12.4 us
    pallas_call x1, Pallas kernels, attend_back(): pl.pallas_call(functools.partial(bwd_kernel, parts), grid_spec=pltpu.Pref...  10.8 us
    unnamed x74, local copies, waits for them, and re-layouts  9.85 us
    ppermute x3, starting transfers between devices, move(): return lax.ppermute(value, ALL, table)  9.74 us
    pallas_call x1, Pallas kernels, mlp(): pl.pallas_call(mlp_kernel, grid_spec=pltpu.PrefetchScalarGridSpec(num_sca...  9.61 us
  transfers between devices with their start and end apart: 31, of which 15 were waited for; matrix products, arithmetic and copies ran while one was open for 1% of the time, Pallas kernels for 26%

profile of v3, /device:TPU:2, one launch (start us, length us, event | category | flops | bytes accessed | tf_op | source)
XLA Modules:
  0.0 220.7 jit_solution(9383806082443812780)
XLA Ops:
  2.4 4.5 %collective-permute-start = (bf16[136,768]{1,0:T(8,128)(2,1)S(1)}, bf16[136,768]{1,0:T(8,128)(2,1)S(1)}, u32[]{:S(2)}, u32[]{:S(2)}) collective-permute-start(bf16[136,768]{1,0:T(8,128)(2,1)S(1)} %pad_maximum_fusion.1), channel_id=1, source_target_pairs={{0,0},{1,1},{2,16},{3,17},{4,8},{5,9},{6,24},{7,25},{8,2},{9,3},{1... | collective-permute-start | bytes 626696 | tf_op jit(solution)/shard_map/ppermute | solution.py:92
  10.2 4.2 %all-to-all-start = ((bf16[4,24,2176]{2,1,0:T(8,128)(2,1)}), bf16[4,24,2176]{2,1,0:T(8,128)(2,1)S(1)}, u32[]{:S(2)}, u32[]{:S(2)}) async-start(bf16[4,24,2176]{2,1,0:T(8,128)(2,1)} %prepare.1), calls=%async_computation | async-start | bytes 835584 | tf_op jit(solution)/shard_map/all_to_all | solution.py:1027
  16.6 5.5 %all-to-all-done.got_ref = bf16[4,24,2176]{2,1,0:T(8,128)(2,1)S(1)} async-done(((bf16[4,24,2176]{2,1,0:T(8,128)(2,1)}), bf16[4,24,2176]{2,1,0:T(8,128)(2,1)S(1)}, u32[]{:S(2)}, u32[]{:S(2)}) %all-to-all-start) | async-done | bytes 417824 | tf_op jit(solution)/shard_map/all_to_all | solution.py:1027
  29.1 12.4 %all_gather.9.x_ref = bf16[512,768]{1,0:T(8,128)(2,1)} all-gather(bf16[128,768]{1,0:T(8,128)(2,1)S(1)} %slice.16.x_ref), channel_id=1, replica_groups=mesh['gx'=2,'c'=2,'sz'=4,'sy'=2] {'gx','sy'}, dimensions={0}, use_global_device_ids=true | all-gather | bytes 983040 | tf_op jit(solution)/shard_map/all_gather | solution.py:1029
  41.6 4.1 %all-to-all-start.1 = ((bf16[4,296,768]{2,1,0:T(8,128)(2,1)}), bf16[4,296,768]{2,1,0:T(8,128)(2,1)S(1)}, u32[]{:S(2)}, u32[]{:S(2)}) async-start(bf16[4,296,768]{2,1,0:T(8,128)(2,1)} %get-tuple-element.127), calls=%async_computation.1 | async-start | bytes 3637248 | tf_op jit(solution)/shard_map/all_to_all | solution.py:1033
  48.6 4.8 %qkv.1 = (bf16[512,768]{1,0:T(8,128)(2,1)}, bf16[512,192]{1,0:T(8,128)(2,1)}, bf16[2,512,192]{2,1,0:T(8,128)(2,1)}, bf16[768,640]{1,0:T(8,128)(2,1)}, f32[8,768]{1,0:T(8,128)}) custom-call(s32[4]{0:T(128)} %pad_add_fusion.idx_ref, bf16[512,768]{1,0:T(8,128)(2,1)} %all_gather.9.x_ref, bf16[4,96,640]{2,1,0:T(8,128)(2,1)} %copy-done.3, ...), custom_call_target="tpu_custom_call" | custom-call | flops 452984832 | bytes 3145728 | tf_op jit(solution)/shard_map/qkv/pallas_call | solution.py:314
  58.6 7.2 %attend.1 = (bf16[512,192]{1,0:T(8,128)(2,1)}, f32[8,512]{1,0:T(8,128)}) custom-call(s32[4]{0:T(128)} %pad_add_fusion.idx_ref, f32[1,1024]{1,0:T(1,128)} %slice_convert_fusion.ids_ref, bf16[512,192]{1,0:T(8,128)(2,1)} %get-tuple-element.126.q_ref, bf16[2,512,192]{2,1,0:T(8,128)(2,1)} %get-tuple-element.128.refs_0_.refs_4_, bf16[2,512,192]{2,1,0:T(8,128)(2,1)} %copy-done.23), custom_call_target="tpu_custom_call" | custom-call | flops 402653184 | bytes 786432 | tf_op jit(solution)/shard_map/attend/pallas_call | solution.py:385
  65.8 14.2 %all-gather = bf16[2048,192]{1,0:T(8,128)(2,1)} all-gather(bf16[512,192]{1,0:T(8,128)(2,1)} %get-tuple-element.129), channel_id=2, replica_groups=mesh['gx'=2,'c'=2,'sz'=4,'sy'=2] {'gx','sy'}, dimensions={0}, use_global_device_ids=true | all-gather | bytes 983040 | tf_op jit(solution)/shard_map/all_gather | solution.py:1060
  80.0 4.7 %all-to-all-done.1.own_ref = bf16[4,296,768]{2,1,0:T(8,128)(2,1)S(1)} async-done(((bf16[4,296,768]{2,1,0:T(8,128)(2,1)}), bf16[4,296,768]{2,1,0:T(8,128)(2,1)S(1)}, u32[]{:S(2)}, u32[]{:S(2)}) %all-to-all-start.1) | async-done | bytes 1818656 | tf_op jit(solution)/shard_map/all_to_all | solution.py:1033
  84.7 3.9 %collective-permute-done.10.other_ref = bf16[4,296,768]{2,1,0:T(8,128)(2,1)} collective-permute-done((bf16[4,296,768]{2,1,0:T(8,128)(2,1)S(1)}, bf16[4,296,768]{2,1,0:T(8,128)(2,1)}, u32[]{:S(2)}, u32[]{:S(2)}) %collective-permute-start.10) | collective-permute-done | bytes 1818656 | tf_op jit(solution)/shard_map/ppermute | solution.py:51
  88.6 4.3 %assemble.1 = (bf16[768,768]{1,0:T(8,128)(2,1)}, bf16[768,768]{1,0:T(8,128)(2,1)}, bf16[2,4,96,768]{3,2,1,0:T(8,128)(2,1)}, bf16[2,4,8,768]{3,2,1,0:T(8,128)(2,1)}) custom-call(s32[4]{0:T(128)} %pad_add_fusion.idx_ref, bf16[4,296,768]{2,1,0:T(8,128)(2,1)} %copy-done, bf16[4,296,768]{2,1,0:T(8,128)(2,1)} %collective-permute-done.10.other_ref), custom_call_target="tpu_custom_call" | custom-call | flops 1000 | bytes 7077888 | tf_op jit(solution)/shard_map/assemble/pallas_call | solution.py:237
  94.3 9.6 %mlp.1 = (f32[128,768]{1,0:T(8,128)}, bf16[512,768]{1,0:T(8,128)(2,1)}, bf16[512,768]{1,0:T(8,128)(2,1)}, bf16[512,768]{1,0:T(8,128)(2,1)}, bf16[512,768]{1,0:T(...) custom-call(s32[4]{0:T(128)} %pad_add_fusion.idx_ref, ...), custom_call_target="tpu_custom_call" | custom-call | flops 2415919104 | bytes 9437184 | tf_op jit(solution)/shard_map/mlp/pallas_call | solution.py:580
  107.5 7.7 %mlp_weight_grads.1 = (bf16[4,200,768]{2,1,0:T(8,128)(2,1)}, bf16[4,200,768]{2,1,0:T(8,128)(2,1)}, bf16[128,768]{1,0:T(8,128)(2,1)}, bf16[128,768]{1,0:T(8,128)(...) custom-call(s32[4]{0:T(128)} %pad_add_fusion.idx_ref, bf16[512,768]{1,0:T(8,128)(2,1)} %get-tuple-element.148.h_ref, ...), custom_call_target="tpu_custom_call" | custom-call | flops 1811939328 | bytes 7077888 | tf_op jit(solution)/shard_map/mlp_weight_grads/pallas_call | solution.py:670
  124.0 3.8 %all-to-all-start.2 = ((bf16[4,200,768]{2,1,0:T(8,128)(2,1)}), bf16[4,200,768]{2,1,0:T(8,128)(2,1)S(1)}, u32[]{:S(2)}, u32[]{:S(2)}) async-start(bf16[4,200,768]{2,1,0:T(8,128)(2,1)} %add.18), calls=%async_computation.2 | async-start | bytes 2457600 | tf_op jit(solution)/shard_map/all_to_all | solution.py:1092
  131.4 4.3 %collective-permute-done.15.refs_2_ = bf16[128,768]{1,0:T(8,128)(2,1)S(1)} collective-permute-done((bf16[128,768]{1,0:T(8,128)(2,1)S(1)}, bf16[128,768]{1,0:T(8,128)(2,1)S(1)}, u32[]{:S(2)}, u32[]{:S(2)}) %collective-permute-start.15) | collective-permute-done | bytes 196640 | tf_op jit(solution)/shard_map/ppermute | solution.py:60
  135.7 3.8 %collective-permute-done.14.refs_1_ = bf16[128,768]{1,0:T(8,128)(2,1)S(1)} collective-permute-done((bf16[128,768]{1,0:T(8,128)(2,1)S(1)}, bf16[128,768]{1,0:T(8,128)(2,1)S(1)}, u32[]{:S(2)}, u32[]{:S(2)}) %collective-permute-start.14) | collective-permute-done | bytes 196640 | tf_op jit(solution)/shard_map/ppermute | solution.py:60
  140.3 10.8 %attend_back.1 = (bf16[512,192]{1,0:T(8,128)(2,1)}, f32[2,512,192]{2,1,0:T(8,128)}, bf16[4,128,192]{2,1,0:T(8,128)(2,1)}, bf16[2,512,192]{2,1,0:T(8,128)(2,1)}) custom-call(s32[4]{0:T(128)} %pad_add_fusion.idx_ref, f32[1,1024]{1,0:T(1,128)} %slice_convert_fusion.ids_ref, bf16[512,192]{1,0:T(8,128)(2,1)} %get-tuple-element.126.q_ref, ...), custom_call_target="tpu_custom_call" | custom-call | flops 1006632960 | bytes 2359296 | tf_op jit(solution)/shard_map/attend_back/pallas_call | solution.py:478
  154.1 5.6 %normed_back.1 = (bf16[512,640]{1,0:T(8,128)(2,1)}, f32[8,768]{1,0:T(8,128)}, bf16[256,768]{1,0:T(8,128)(2,1)}, bf16[256,768]{1,0:T(8,128)(2,1)}, bf16[256,768]{1,0:T(8,128)(2,1)}, /*index=5*/bf16[256,768]{1,0:T(8,128)(2,1)}) custom-call(s32[4]{0:T(128)} %pad_add_fusion.idx_ref, bf16[512,768]{1,0:T(8,128)(2,1)} %all_gather.9.x_ref, ...), custom_call_target="tpu_custom_call" | custom-call | flops 503316480 | bytes 4718592 | tf_op jit(solution)/shard_map/normed_back/pallas_call | solution.py:865
  159.7 4.1 %proj_grads.1 = (bf16[16,24,896]{2,1,0:T(8,128)(2,1)}, bf16[16,24,896]{2,1,0:T(8,128)(2,1)}) custom-call(s32[4]{0:T(128)} %pad_add_fusion.idx_ref, bf16[512,768]{1,0:T(8,128)(2,1)} %get-tuple-element.125.h_ref, bf16[512,640]{1,0:T(8,128)(2,1)} %get-tuple-element.173.d_ref, f32[8,768]{1,0:T(8,128)} %get-tuple-element.174.sum_ref, ...), custom_call_target="tpu_custom_call" | custom-call | flops 704643072 | bytes 4128768 | tf_op jit(solution)/shard_map/proj_grads/pallas_call | solution.py:943
  177.1 8.0 %collective-permute-done.22.refs_3_ = bf16[256,768]{1,0:T(8,128)(2,1)S(1)} collective-permute-done((bf16[256,768]{1,0:T(8,128)(2,1)S(1)}, bf16[256,768]{1,0:T(8,128)(2,1)S(1)}, u32[]{:S(2)}, u32[]{:S(2)}) %collective-permute-start.22) | collective-permute-done | bytes 393248 | tf_op jit(solution)/shard_map/ppermute | solution.py:60
  185.1 6.5 %all-to-all-start.3 = ((bf16[16,24,896]{2,1,0:T(8,128)(2,1)}), bf16[16,24,896]{2,1,0:T(8,128)(2,1)S(1)}, u32[]{:S(2)}, u32[]{:S(2)}) async-start(bf16[16,24,896]{2,1,0:T(8,128)(2,1)} %add.19), calls=%async_computation.3 | async-start | bytes 1376256 | tf_op jit(solution)/shard_map/all_to_all | solution.py:1114
  191.6 3.0 %finish.1 = bf16[256,768]{1,0:T(8,128)(2,1)} custom-call(f32[128,768]{1,0:T(8,128)} %get-tuple-element.143.r_ref, bf16[128,768]{1,0:T(8,128)(2,1)} %copy-done.4, f32[128,768]{1,0:T(8,128)} %get-tuple-element.190.dr_ref, f32[8,768]{1,0:T(8,128)} %get-tuple-element.141.refs_7_.vec_ref, bf16[256,768]{1,0:T(8,128)(2,1)} %get-tuple-element.191.refs_0_, ...), custom_call_target="tpu_custom_call" | custom-call | flops 3932160 | bytes 2949120 | tf_op jit(solution)/shard_map/finish/pallas_call | solution.py:810
  194.6 3.4 %collective-permute-start.23 = (bf16[256,768]{1,0:T(8,128)(2,1)}, bf16[256,768]{1,0:T(8,128)(2,1)S(1)}, u32[]{:S(2)}, u32[]{:S(2)}) collective-permute-start(bf16[256,768]{1,0:T(8,128)(2,1)} %finish.1), channel_id=1, source_target_pairs={{0,0},{1,1},{16,2},{17,3},{8,4},{9,5},{24,6},{25,7},{2,8},{3,9},{1... | collective-permute-start | bytes 1179656 | tf_op jit(solution)/shard_map/ppermute | solution.py:92
  207.8 9.0 %collective-permute-done.23.both_ref = bf16[256,768]{1,0:T(8,128)(2,1)S(1)} collective-permute-done((bf16[256,768]{1,0:T(8,128)(2,1)}, bf16[256,768]{1,0:T(8,128)(2,1)S(1)}, u32[]{:S(2)}, u32[]{:S(2)}) %collective-permute-start.23) | collective-permute-done | bytes 393248 | tf_op jit(solution)/shard_map/ppermute | solution.py:92
  (144 shorter events, 70.1 us)
Async XLA Ops:
  2.4 14.1 %collective-permute-start = (bf16[136,768]{1,0:T(8,128)(2,1)S(1)}, bf16[136,768]{1,0:T(8,128)(2,1)S(1)}, u32[]{:S(2)}, u32[]{:S(2)}) collective-permute-start(bf16[136,768]{1,0:T(8,128)(2,1)S(1)} %pad_maximum_fusion.1), channel_id=1, source_target_pairs={{0,0},{1,1},{2,16},{3,17},{4,8},{5,9},{6,24},{7,25},{8,2},{9,3},{1... | collective-permute-start | bytes 626696 | tf_op jit(solution)/shard_map/ppermute | solution.py:92
  10.2 11.8 %all-to-all-start = ((bf16[4,24,2176]{2,1,0:T(8,128)(2,1)}), bf16[4,24,2176]{2,1,0:T(8,128)(2,1)S(1)}, u32[]{:S(2)}, u32[]{:S(2)}) async-start(bf16[4,24,2176]{2,1,0:T(8,128)(2,1)} %prepare.1), calls=%async_computation | async-start | bytes 835584 | tf_op jit(solution)/shard_map/all_to_all | solution.py:1027
  14.6 27.0 %collective-permute-start.4 = (bf16[128,768]{1,0:T(8,128)(2,1)S(1)}, bf16[128,768]{1,0:T(8,128)(2,1)S(1)}, u32[]{:S(2)}, u32[]{:S(2)}) collective-permute-start(bf16[128,768]{1,0:T(8,128)(2,1)S(1)} %fusion), channel_id=1, source_target_pairs={{0,0},{1,1},{2,16},{3,17},{4,8},{5,9},{6,24},{7,25},{8,2},{9,3},{1... | collective-permute-start | bytes 589832 | tf_op jit(solution)/shard_map/ppermute | solution.py:92
  25.3 16.3 %collective-permute-start.3 = (bf16[96,640]{1,0:T(8,128)(2,1)}, bf16[96,640]{1,0:T(8,128)(2,1)S(1)}, u32[]{:S(2)}, u32[]{:S(2)}) collective-permute-start(bf16[96,640]{1,0:T(8,128)(2,1)} %get-tuple-element.121), channel_id=1, source_target_pairs={{0,2},{2,4},{4,6},{6,0},{1,3},{3,5},{5,7},{7,1},{8,10},{10,12},{12... | collective-permute-start | bytes 368648 | tf_op jit(solution)/shard_map/ppermute | solution.py:70
  25.9 15.7 %collective-permute-start.2 = (bf16[96,640]{1,0:T(8,128)(2,1)}, bf16[96,640]{1,0:T(8,128)(2,1)S(1)}, u32[]{:S(2)}, u32[]{:S(2)}) collective-permute-start(bf16[96,640]{1,0:T(8,128)(2,1)} %get-tuple-element.121), channel_id=1, source_target_pairs={{0,4},{2,6},{4,0},{6,2},{1,5},{3,7},{5,1},{7,3},{8,12},{10,14},{12... | collective-permute-start | bytes 368648 | tf_op jit(solution)/shard_map/ppermute | solution.py:70
  28.6 13.0 %collective-permute-start.1 = (bf16[96,640]{1,0:T(8,128)(2,1)}, bf16[96,640]{1,0:T(8,128)(2,1)S(1)}, u32[]{:S(2)}, u32[]{:S(2)}) collective-permute-start(bf16[96,640]{1,0:T(8,128)(2,1)} %get-tuple-element.121), channel_id=1, source_target_pairs={{0,6},{2,0},{4,2},{6,4},{1,7},{3,1},{5,3},{7,5},{8,14},{10,8},{12,... | collective-permute-start | bytes 368648 | tf_op jit(solution)/shard_map/ppermute | solution.py:70
  41.6 43.1 %all-to-all-start.1 = ((bf16[4,296,768]{2,1,0:T(8,128)(2,1)}), bf16[4,296,768]{2,1,0:T(8,128)(2,1)S(1)}, u32[]{:S(2)}, u32[]{:S(2)}) async-start(bf16[4,296,768]{2,1,0:T(8,128)(2,1)} %get-tuple-element.127), calls=%async_computation.1 | async-start | bytes 3637248 | tf_op jit(solution)/shard_map/all_to_all | solution.py:1033
  53.4 4.4 %collective-permute-start.6 = (bf16[2,512,192]{2,1,0:T(8,128)(2,1)}, bf16[2,512,192]{2,1,0:T(8,128)(2,1)S(1)}, u32[]{:S(2)}, u32[]{:S(2)}) collective-permute-start(bf16[2,512,192]{2,1,0:T(8,128)(2,1)} %get-tuple-element.128.refs_0_.refs_4_), channel_id=1, source_target_pairs={{0,8},{8,0},{1,9},{9,1},{2,10},{10,2},{3,11},{11,3},{4,12},{12,4},... | collective-permute-start | bytes 1179656 | tf_op jit(solution)/shard_map/ppermute | solution.py:70
  53.6 26.3 %collective-permute-start.9 = (bf16[128,768]{1,0:T(8,128)(2,1)S(1)}, bf16[128,768]{1,0:T(8,128)(2,1)S(1)}, u32[]{:S(2)}, u32[]{:S(2)}) collective-permute-start(bf16[128,768]{1,0:T(8,128)(2,1)S(1)} %collective-permute-done.4.refs_0_.dm_ref), channel_id=1, source_target_pairs={{0,17},{1,16},{16,1},{17,0},{2,19},{3,18},{18,3},{19,2},{4,21},{5,... | collective-permute-start | bytes 589832 | tf_op jit(solution)/shard_map/ppermute | solution.py:60
  55.2 24.8 %collective-permute-start.8 = (bf16[128,768]{1,0:T(8,128)(2,1)S(1)}, bf16[128,768]{1,0:T(8,128)(2,1)S(1)}, u32[]{:S(2)}, u32[]{:S(2)}) collective-permute-start(bf16[128,768]{1,0:T(8,128)(2,1)S(1)} %collective-permute-done.4.refs_0_.dm_ref), channel_id=1, source_target_pairs={{0,16},{1,17},{16,0},{17,1},{2,18},{3,19},{18,2},{19,3},{4,20},{5,... | collective-permute-start | bytes 589832 | tf_op jit(solution)/shard_map/ppermute | solution.py:60
  56.2 23.8 %collective-permute-start.7 = (bf16[128,768]{1,0:T(8,128)(2,1)S(1)}, bf16[128,768]{1,0:T(8,128)(2,1)S(1)}, u32[]{:S(2)}, u32[]{:S(2)}) collective-permute-start(bf16[128,768]{1,0:T(8,128)(2,1)S(1)} %collective-permute-done.4.refs_0_.dm_ref), channel_id=1, source_target_pairs={{0,1},{1,0},{16,17},{17,16},{2,3},{3,2},{18,19},{19,18},{4,5},{5,4... | collective-permute-start | bytes 589832 | tf_op jit(solution)/shard_map/ppermute | solution.py:60
  103.9 11.2 %collective-permute-start.11 = (bf16[128,768]{1,0:T(8,128)(2,1)}, bf16[128,768]{1,0:T(8,128)(2,1)S(1)}, u32[]{:S(2)}, u32[]{:S(2)}) collective-permute-start(bf16[128,768]{1,0:T(8,128)(2,1)} %get-tuple-element.145), channel_id=1, source_target_pairs={{0,1},{1,0},{16,17},{17,16},{2,3},{3,2},{18,19},{19,18},{4,5},{5,4... | collective-permute-start | bytes 589832 | tf_op jit(solution)/shard_map/ppermute | solution.py:60
  105.0 10.2 %collective-permute-start.12 = (bf16[128,768]{1,0:T(8,128)(2,1)}, bf16[128,768]{1,0:T(8,128)(2,1)S(1)}, u32[]{:S(2)}, u32[]{:S(2)}) collective-permute-start(bf16[128,768]{1,0:T(8,128)(2,1)} %get-tuple-element.146), channel_id=1, source_target_pairs={{0,16},{1,17},{16,0},{17,1},{2,18},{3,19},{18,2},{19,3},{4,20},{5,... | collective-permute-start | bytes 589832 | tf_op jit(solution)/shard_map/ppermute | solution.py:60
  106.0 10.5 %collective-permute-start.13 = (bf16[128,768]{1,0:T(8,128)(2,1)}, bf16[128,768]{1,0:T(8,128)(2,1)S(1)}, u32[]{:S(2)}, u32[]{:S(2)}) collective-permute-start(bf16[128,768]{1,0:T(8,128)(2,1)} %get-tuple-element.147), channel_id=1, source_target_pairs={{0,17},{1,16},{16,1},{17,0},{2,19},{3,18},{18,3},{19,2},{4,21},{5,... | collective-permute-start | bytes 589832 | tf_op jit(solution)/shard_map/ppermute | solution.py:60
  124.0 46.5 %all-to-all-start.2 = ((bf16[4,200,768]{2,1,0:T(8,128)(2,1)}), bf16[4,200,768]{2,1,0:T(8,128)(2,1)S(1)}, u32[]{:S(2)}, u32[]{:S(2)}) async-start(bf16[4,200,768]{2,1,0:T(8,128)(2,1)} %add.18), calls=%async_computation.2 | async-start | bytes 2457600 | tf_op jit(solution)/shard_map/all_to_all | solution.py:1092
  127.9 7.9 %collective-permute-start.15 = (bf16[128,768]{1,0:T(8,128)(2,1)S(1)}, bf16[128,768]{1,0:T(8,128)(2,1)S(1)}, u32[]{:S(2)}, u32[]{:S(2)}) collective-permute-start(bf16[128,768]{1,0:T(8,128)(2,1)S(1)} %copy-done.28), channel_id=1, source_target_pairs={{0,16},{1,17},{16,0},{17,1},{2,18},{3,19},{18,2},{19,3},{4,20},{5,... | collective-permute-start | bytes 589832 | tf_op jit(solution)/shard_map/ppermute | solution.py:60
  128.9 10.6 %collective-permute-start.14 = (bf16[128,768]{1,0:T(8,128)(2,1)S(1)}, bf16[128,768]{1,0:T(8,128)(2,1)S(1)}, u32[]{:S(2)}, u32[]{:S(2)}) collective-permute-start(bf16[128,768]{1,0:T(8,128)(2,1)S(1)} %copy-done.28), channel_id=1, source_target_pairs={{0,1},{1,0},{16,17},{17,16},{2,3},{3,2},{18,19},{19,18},{4,5},{5,4... | collective-permute-start | bytes 589832 | tf_op jit(solution)/shard_map/ppermute | solution.py:60
  129.9 9.6 %collective-permute-start.17 = (bf16[128,768]{1,0:T(8,128)(2,1)S(1)}, bf16[128,768]{1,0:T(8,128)(2,1)S(1)}, u32[]{:S(2)}, u32[]{:S(2)}) collective-permute-start(bf16[128,768]{1,0:T(8,128)(2,1)S(1)} %copy-done.28), channel_id=1, source_target_pairs={{0,17},{1,16},{16,1},{17,0},{2,19},{3,18},{18,3},{19,2},{4,21},{5,... | collective-permute-start | bytes 589832 | tf_op jit(solution)/shard_map/ppermute | solution.py:60
  163.9 11.6 %collective-permute-start.20 = (bf16[256,768]{1,0:T(8,128)(2,1)}, bf16[256,768]{1,0:T(8,128)(2,1)S(1)}, u32[]{:S(2)}, u32[]{:S(2)}) collective-permute-start(bf16[256,768]{1,0:T(8,128)(2,1)} %get-tuple-element.186), channel_id=1, source_target_pairs={{0,1},{1,0},{16,17},{17,16},{2,3},{3,2},{18,19},{19,18},{4,5},{5,4... | collective-permute-start | bytes 1179656 | tf_op jit(solution)/shard_map/ppermute | solution.py:60
  164.9 12.2 %collective-permute-start.21 = (bf16[256,768]{1,0:T(8,128)(2,1)}, bf16[256,768]{1,0:T(8,128)(2,1)S(1)}, u32[]{:S(2)}, u32[]{:S(2)}) collective-permute-start(bf16[256,768]{1,0:T(8,128)(2,1)} %get-tuple-element.187), channel_id=1, source_target_pairs={{0,16},{1,17},{16,0},{17,1},{2,18},{3,19},{18,2},{19,3},{4,20},{5,... | collective-permute-start | bytes 1179656 | tf_op jit(solution)/shard_map/ppermute | solution.py:60
  165.9 19.2 %collective-permute-start.22 = (bf16[256,768]{1,0:T(8,128)(2,1)S(1)}, bf16[256,768]{1,0:T(8,128)(2,1)S(1)}, u32[]{:S(2)}, u32[]{:S(2)}) collective-permute-start(bf16[256,768]{1,0:T(8,128)(2,1)S(1)} %copy-done.24), channel_id=1, source_target_pairs={{0,17},{1,16},{16,1},{17,0},{2,19},{3,18},{18,3},{19,2},{4,21},{5,... | collective-permute-start | bytes 1179656 | tf_op jit(solution)/shard_map/ppermute | solution.py:60
  185.1 31.7 %all-to-all-start.3 = ((bf16[16,24,896]{2,1,0:T(8,128)(2,1)}), bf16[16,24,896]{2,1,0:T(8,128)(2,1)S(1)}, u32[]{:S(2)}, u32[]{:S(2)}) async-start(bf16[16,24,896]{2,1,0:T(8,128)(2,1)} %add.19), calls=%async_computation.3 | async-start | bytes 1376256 | tf_op jit(solution)/shard_map/all_to_all | solution.py:1114
  194.6 22.2 %collective-permute-start.23 = (bf16[256,768]{1,0:T(8,128)(2,1)}, bf16[256,768]{1,0:T(8,128)(2,1)S(1)}, u32[]{:S(2)}, u32[]{:S(2)}) collective-permute-start(bf16[256,768]{1,0:T(8,128)(2,1)} %finish.1), channel_id=1, source_target_pairs={{0,0},{1,1},{16,2},{17,3},{8,4},{9,5},{24,6},{25,7},{2,8},{3,9},{1... | collective-permute-start | bytes 1179656 | tf_op jit(solution)/shard_map/ppermute | solution.py:92
  199.5 5.8 %collective-permute-start.26 = (bf16[24,768]{1,0:T(8,128)(2,1)S(1)}, bf16[24,768]{1,0:T(8,128)(2,1)S(1)}, u32[]{:S(2)}, u32[]{:S(2)}) collective-permute-start(bf16[24,768]{1,0:T(8,128)(2,1)S(1)} %copy-done.32), channel_id=1, source_target_pairs={{0,17},{1,16},{16,1},{17,0},{2,19},{3,18},{18,3},{19,2},{4,21},{5,... | collective-permute-start | bytes 110600 | tf_op jit(solution)/shard_map/ppermute | solution.py:60
  (43 other events, 235.0 us)

commit v4 on v3

--- a/solution.py
+++ b/solution.py
@@ -17,6 +17,7 @@
 ALL = ("gx", "c", "sz", "sy")
 SAME = ("gx", "sz", "sy")
 SMALLS = 64
+NORMED = 13.0
 f32 = jnp.float32
 bf16 = jnp.bfloat16
 
@@ -125,8 +126,10 @@
     )
 
 
-def cost(flops, nbytes, trans=0):
-    return pl.CostEstimate(flops=int(flops), bytes_accessed=int(nbytes), transcendentals=int(trans))
+def takes(microseconds):
+    return pl.CostEstimate(
+        flops=0, bytes_accessed=int(microseconds * 3.69e6), transcendentals=0
+    )
 
 
 def whole(shape):
@@ -147,13 +150,15 @@
     return out
 
 
-def prep_kernel(rep_of, q_ref, k_ref, v_ref, small_ref, up_ref, out_ref, chunk_ref, turn_ref):
+def prep_kernel(rep_of, q_ref, k_ref, v_ref, up_ref, out_ref, *refs):
+    small_refs, chunk_ref, turn_ref = refs[:-2], refs[-2], refs[-1]
     block, width = q_ref.shape
     cols = width // TP
     wide = 3 * cols + SMALLS
     slab = up_ref.shape[1] // len(rep_of)
     turn_ref[...] = jnp.zeros_like(turn_ref)
-    turn_ref[: small_ref.shape[0], :block] = small_ref[...].astype(f32)
+    for j, ref in enumerate(small_refs):
+        turn_ref[j : j + 1, :block] = ref[...].astype(f32)
     small = turn_ref[...].T[:block, :SMALLS]
     for j in range(TP):
         at = slice(j * cols, (j + 1) * cols)
@@ -174,9 +179,9 @@
         functools.partial(prep_kernel, rep_of),
         out_shape=jax.ShapeDtypeStruct((TP, block, wide + w_up.shape[1] // TP + width), bf16),
         scratch_shapes=[pltpu.VMEM((128, 128), f32)],
-        cost_estimate=cost(1000, 4 * w_up.size),
+        cost_estimate=takes(1.9),
         name="prepare",
-    )(w_query, w_key, w_value, small, w_up, w_out)
+    )(w_query, w_key, w_value, w_up, w_out, *[v[None] for v in small])
 
 
 def shards_kernel(wide, got_ref, down_ref, row_ref, proj_ref, shard_ref):
@@ -207,48 +212,9 @@
             jax.ShapeDtypeStruct((TP * block, wide), bf16),
             jax.ShapeDtypeStruct((lines, 2 * TP * block + slab + 8, width), bf16),
         ],
-        cost_estimate=cost(1000, 4 * lines * slab * width),
+        cost_estimate=takes(2.4),
         name="shards_of",
     )(got, w_down, b_row)
-
-
-def assemble_kernel(plan, idx_ref, own_ref, other_ref, up_ref, out_ref, down_ref, row_ref, wide_ref):
-    core = idx_ref[2]
-    slab = down_ref.shape[2]
-    first = TP * up_ref.shape[0] // plan.devices
-    pair = first // plan.size["gx"]
-    for ref, side in ((own_ref, core), (other_ref, 1 - core)):
-        for z in range(ref.shape[0]):
-            value = ref[z, : 2 * first, :].astype(f32)
-            for gx in range(plan.size["gx"]):
-                at = gx * pair
-                wide_ref[0, gx * 2 + side, z] = value[at : at + pair]
-                wide_ref[1, gx * 2 + side, z] = value[first + at : first + at + pair]
-            down_ref[side, z] = ref[z, 2 * first : 2 * first + slab, :]
-            row_ref[side, z] = ref[z, 2 * first + slab :, :]
-    for ref, k in ((up_ref, 0), (out_ref, 1)):
-        ref[...] = wide_ref[k].reshape(ref.shape).astype(bf16)
-
-
-def assemble(plan, idx, own, other, slab):
-    lines, _, width = own.shape
-    hidden = plan.copies * slab
-    pair = plan.size["sy"] * width // plan.devices
-    return pl.pallas_call(
-        functools.partial(assemble_kernel, plan),
-        in_specs=[pl.BlockSpec(memory_space=pltpu.SMEM)]
-        + [pl.BlockSpec(memory_space=pltpu.VMEM)] * 2,
-        out_shape=[
-            jax.ShapeDtypeStruct((width, hidden), bf16),
-            jax.ShapeDtypeStruct((width, width), bf16),
-            jax.ShapeDtypeStruct((2, lines, slab, width), bf16),
-            jax.ShapeDtypeStruct((2, lines, 8, width), bf16),
-        ],
-        scratch_shapes=[pltpu.VMEM((2, 2 * plan.size["gx"], lines, pair, width), f32)],
-        compiler_params=pltpu.CompilerParams(vmem_limit_bytes=60 * 1024 * 1024),
-        cost_estimate=cost(1000, 12 * width * width),
-        name="assemble",
-    )(idx, own, other)
 
 
 def qkv_kernel(plan, idx_ref, x_ref, *refs):
@@ -323,7 +289,7 @@
         ),
         out_shape=out_shape,
         compiler_params=params(),
-        cost_estimate=cost(2 * rows * width * 3 * cols, rows * width * 8),
+        cost_estimate=takes(4.8),
         name="qkv",
     )(idx, x_all, *operands)
 
@@ -403,13 +369,13 @@
             jax.ShapeDtypeStruct((8, rows), f32),
         ],
         compiler_params=params(),
-        cost_estimate=cost(4 * rows * span * parts * cols, span * parts * cols * 4, rows * span * parts * HEADS_TP),
+        cost_estimate=takes(7.1),
         name="attend",
     )(idx, ids, q, *kvs)
 
 
-def bwd_kernel(parts, idx_ref, ids_ref, q_ref, w_ref, lse_ref, *refs):
-    da_refs, refs = refs[:TP], refs[TP:]
+def bwd_kernel(parts, waits, idx_ref, ids_ref, q_ref, w_ref, lse_ref, *refs):
+    da_refs, refs = refs[:TP], refs[TP + waits :]
     kv_refs = refs[:parts]
     dq_ref, own_ref, cols_ref = refs[parts : parts + 3]
     other_refs = refs[parts + 3 : 2 * parts + 2]
@@ -429,7 +395,7 @@
         member = idx_ref[0]
         for j in range(TP):
             da = da_refs[j][...]
-            mixed_ref[member ^ j] = dot(da, w_ref[0], 1, 1).astype(bf16)
+            mixed_ref[member ^ j] = dot(da, w_ref[...], 1, 1).astype(bf16)
             cols_ref[member ^ j] = member_cols(da, member, cols)
 
     at = part * span + step * width
@@ -470,23 +436,24 @@
             other_refs[j - 1][1] = value_acc[j].astype(bf16)
 
 
-def attend_back(idx, ids, q, das, w_out, lse, kvs, width=256):
+def attend_back(idx, ids, q, das, after, w_out, lse, kvs, width=256):
     rows, cols = q.shape
     step, model = das[0].shape
     parts = len(kvs)
     span = kvs[0].shape[1]
     return pl.pallas_call(
-        functools.partial(bwd_kernel, parts),
+        functools.partial(bwd_kernel, parts, len(after)),
         grid_spec=pltpu.PrefetchScalarGridSpec(
             num_scalar_prefetch=1,
             grid=(rows // width,),
             in_specs=[
                 whole(ids.shape),
                 pl.BlockSpec((width, cols), lambda i, *_: (i, 0)),
-                pl.BlockSpec((1, cols, model), lambda i, idx: (idx[0], 0, 0)),
+                whole((cols, model)),
                 pl.BlockSpec((8, width), lambda i, *_: (0, i)),
             ]
             + [whole((step, model))] * TP
+            + [pl.BlockSpec(memory_space=pl.ANY)] * len(after)
             + [whole(kv.shape) for kv in kvs],
             out_specs=[
                 pl.BlockSpec((width, cols), lambda i, *_: (i, 0)),
@@ -509,25 +476,66 @@
         ]
         + [jax.ShapeDtypeStruct((2, span, cols), bf16)] * (parts - 1),
         compiler_params=params(),
-        cost_estimate=cost(10 * rows * span * parts * cols, span * parts * cols * 12, rows * span * parts * HEADS_TP),
+        cost_estimate=takes(10.7),
         name="attend_back",
-    )(idx, ids, q, w_out, lse, *das, *kvs)
-
-
-def mlp_kernel(idx_ref, x_ref, o_ref, *refs):
+    )(idx, ids, q, w_out, lse, *das, *after, *kvs)
+
+
+def mlp_kernel(plan, idx_ref, x_ref, o_ref, vec_ref, *refs):
     dm_refs, refs = refs[:TP], refs[TP:]
-    wo_ref, wu_ref, wd_ref, vec_ref, bup_ref, r_ref, h_ref, a_ref, du_ref, dm_ref, sum_ref = refs[:11]
-    dh_refs, dm_now, r_now, dh_now = refs[11 : 11 + TP], refs[-3], refs[-2], refs[-1]
     step = pl.program_id(0)
     side = lax.rem(idx_ref[0], 2)
+    if plan.fast:
+        own_ref, other_ref, r_ref, h_ref, a_ref, du_ref, dm_ref, sum_ref = refs[:8]
+        dh_refs = refs[8 : 8 + TP]
+        out_ref, down_ref, dm_now, r_now, dh_now, held, held_down, held_row = refs[8 + TP :]
+
+        @pl.when(step == 0)
+        def _():
+            core = idx_ref[2]
+            first = held.shape[3] * plan.size["gx"]
+            pair = held.shape[3]
+            slab = held_down.shape[2]
+            rows = []
+            for z in range(held.shape[2]):
+                for ref, owner in ((own_ref, core), (other_ref, 1 - core)):
+                    for gx in range(plan.size["gx"]):
+                        at = gx * pair
+                        held[0, gx * 2 + owner, z] = ref[z, at : at + pair, :]
+                        held[1, gx * 2 + owner, z] = ref[z, first + at : first + at + pair, :]
+                    held_down[owner, z] = ref[z, 2 * first : 2 * first + slab, :]
+            for owner in range(2):
+                for z in range(held.shape[2]):
+                    at = 2 * first + slab
+                    row = jnp.where(
+                        core == owner,
+                        own_ref[z, at : at + 8, :].astype(f32),
+                        other_ref[z, at : at + 8, :].astype(f32),
+                    )
+                    rows.append(row[0:1, :slab])
+            held_row[...] = jnp.concatenate(rows, axis=1)
+            out = held[1, idx_ref[0]]
+            out_ref[...] = out.reshape(out_ref.shape)
+            down_ref[...] = held_down[...].reshape(down_ref.shape)
+
+        width = held.shape[-1]
+        w_up = held[0].reshape(-1, width)
+        outs = [held[1, j].reshape(-1, width) for j in range(TP)]
+        w_down = held_down[...].reshape(-1, width)
+        b_up = held_row[...]
+    else:
+        wo_ref, wu_ref, wd_ref, bup_ref, r_ref, h_ref, a_ref, du_ref, dm_ref, sum_ref = refs[:10]
+        dh_refs, dm_now, r_now, dh_now = refs[10 : 10 + TP], refs[-3], refs[-2], refs[-1]
+        w_up, w_down, b_up = wu_ref[...], wd_ref[...], bup_ref[...]
+        outs = [wo_ref[j] for j in range(TP)]
 
     @pl.when(step == 0)
     def _():
         sum_ref[...] = jnp.zeros_like(sum_ref)
 
-    attended = dot(o_ref[0], wo_ref[0])
+    attended = dot(o_ref[0], outs[0])
     for j in range(1, TP):
-        attended += dot(o_ref[j], wo_ref[j])
+        attended += dot(o_ref[j], outs[j])
     residual = x_ref[...].astype(f32) + (attended + vec_ref[2:3, :])
 
     for i in range(2):
@@ -543,16 +551,16 @@
     units, _ = unit(residual)
     low = (units * vec_ref[5:6, :] + vec_ref[6:7, :]).astype(bf16)
     h_ref[...] = low
-    pre = dot(low, wu_ref[...]) + bup_ref[...]
+    pre = dot(low, w_up) + b_up
     normal = 0.5 * (1.0 + lax.erf(pre * 0.7071067811865476))
     act = (pre * normal).astype(bf16)
     a_ref[...] = act
     slope = normal + pre * (0.3989422804014327 * jnp.exp(-0.5 * pre * pre))
     dm = dm_now[...].reshape(x_ref.shape)
     dm_ref[...] = dm
-    grad_pre = (dot(dm, wd_ref[...], 1, 1) * slope).astype(bf16)
+    grad_pre = (dot(dm, w_down, 1, 1) * slope).astype(bf16)
     du_ref[...] = grad_pre
-    grad = dot(grad_pre, wu_ref[...], 1, 1)
+    grad = dot(grad_pre, w_up, 1, 1)
     sum_ref[0:1, :] += jnp.sum(grad * units, axis=0, keepdims=True)
     sum_ref[1:2, :] += jnp.sum(grad, axis=0, keepdims=True)
     dh_now[...] = grad.astype(bf16).reshape(dh_now.shape)
@@ -564,9 +572,9 @@
                 dh_refs[2 * i + b][...] = dh_now[side ^ b]
 
 
-def mlp(idx, x_all, o_all, dms, w_out, w_up, w_down, vecs, b_up):
+def mlp(plan, idx, x_all, o_all, vecs, dms, weights, slab):
     rows, width = x_all.shape
-    hidden = w_up.shape[1]
+    hidden = plan.copies * slab
     cols = width // TP
     step = rows // 2
 
@@ -577,30 +585,49 @@
     inner = pl.BlockSpec((step, hidden), block)
     one = whole((rows // TP, width))
     now = (2, rows // TP, width)
-    return pl.pallas_call(
-        mlp_kernel,
+    out_specs = [one, token, inner, inner, token, whole((8, width))] + [one] * TP
+    out_shape = [
+        jax.ShapeDtypeStruct((rows // TP, width), f32),
+        jax.ShapeDtypeStruct((rows, width), bf16),
+        jax.ShapeDtypeStruct((rows, hidden), bf16),
+        jax.ShapeDtypeStruct((rows, hidden), bf16),
+        jax.ShapeDtypeStruct((rows, width), bf16),
+        jax.ShapeDtypeStruct((8, width), f32),
+    ] + [jax.ShapeDtypeStruct((rows // TP, width), bf16)] * TP
+    scratch = [pltpu.VMEM(now, bf16), pltpu.VMEM(now, f32), pltpu.VMEM(now, bf16)]
+    if plan.fast:
+        lines = plan.copies // 2
+        gx = plan.size["gx"]
+        out_specs += [whole((cols, width)), whole((hidden, width))]
+        out_shape += [
+            jax.ShapeDtypeStruct((cols, width), bf16),
+            jax.ShapeDtypeStruct((hidden, width), bf16),
+        ]
+        scratch += [
+            pltpu.VMEM((2, 2 * gx, lines, width // (2 * gx * lines), width), bf16),
+            pltpu.VMEM((2, lines, slab, width), bf16),
+            pltpu.VMEM((1, hidden), f32),
+        ]
+    return pl.pallas_call(
+        functools.partial(mlp_kernel, plan),
         grid_spec=pltpu.PrefetchScalarGridSpec(
             num_scalar_prefetch=1,
             grid=(2,),
-            in_specs=[token, pl.BlockSpec((TP, step, cols), lambda i, idx: (0, i ^ (idx[0] // 2), 0))]
+            in_specs=[
+                token,
+                pl.BlockSpec((TP, step, cols), lambda i, idx: (0, i ^ (idx[0] // 2), 0)),
+                whole(vecs.shape),
+            ]
             + [one] * TP
-            + [whole(v.shape) for v in (w_out, w_up, w_down, vecs, b_up)],
-            out_specs=[one, token, inner, inner, token, whole((8, width))] + [one] * TP,
-            scratch_shapes=[pltpu.VMEM(now, bf16), pltpu.VMEM(now, f32), pltpu.VMEM(now, bf16)],
+            + [whole(v.shape) for v in weights],
+            out_specs=out_specs,
+            scratch_shapes=scratch,
         ),
-        out_shape=[
-            jax.ShapeDtypeStruct((rows // TP, width), f32),
-            jax.ShapeDtypeStruct((rows, width), bf16),
-            jax.ShapeDtypeStruct((rows, hidden), bf16),
-            jax.ShapeDtypeStruct((rows, hidden), bf16),
-            jax.ShapeDtypeStruct((rows, width), bf16),
-            jax.ShapeDtypeStruct((8, width), f32),
-        ]
-        + [jax.ShapeDtypeStruct((rows // TP, width), bf16)] * TP,
+        out_shape=out_shape,
         compiler_params=params(),
-        cost_estimate=cost(2 * rows * width * (width + 3 * hidden), rows * width * 24, rows * hidden * 4),
+        cost_estimate=takes(10.5),
         name="mlp",
-    )(idx, x_all, o_all, *dms, w_out, w_up, w_down, vecs, b_up)
+    )(idx, x_all, o_all, vecs, *dms, *weights)
 
 
 def pair_kernel(plan, idx_ref, h_ref, du_ref, a_ref, dm_ref, wd_ref, near_ref, far_ref, *refs):
@@ -688,27 +715,28 @@
         out_shape=[jax.ShapeDtypeStruct(bundle, bf16)] * 2
         + [jax.ShapeDtypeStruct(token, bf16)] * TP,
         compiler_params=params(),
-        cost_estimate=cost(6 * rows * width * hidden, width * hidden * 12),
+        cost_estimate=takes(7.6),
         name="mlp_weight_grads",
     )(idx, low, grad_pre, act, dm_all, w_down)
 
 
-def add_kernel(*refs):
-    *in_refs, out_ref = refs
-    total = in_refs[0][...].astype(f32)
-    for ref in in_refs[1:]:
+def add_kernel(count, *refs):
+    total = refs[0][...].astype(f32)
+    for ref in refs[1:count]:
         total += ref[...].astype(f32)
-    out_ref[...] = total.astype(out_ref.dtype)
-
-
-def add(*values, dtype=bf16):
-    return pl.pallas_call(
-        add_kernel,
-        out_shape=jax.ShapeDtypeStruct(values[0].shape, dtype),
+    refs[-1][...] = total.astype(bf16)
+
+
+def add(*values, after=()):
+    return pl.pallas_call(
+        functools.partial(add_kernel, len(values)),
+        in_specs=[pl.BlockSpec(memory_space=pltpu.VMEM)] * len(values)
+        + [pl.BlockSpec(memory_space=pl.ANY)] * len(after),
+        out_shape=jax.ShapeDtypeStruct(values[0].shape, bf16),
         compiler_params=pltpu.CompilerParams(vmem_limit_bytes=60 * 1024 * 1024),
-        cost_estimate=cost(values[0].size * len(values), 2 * values[0].size * (len(values) + 1)),
+        cost_estimate=takes(2.6),
         name="add",
-    )(*values)
+    )(*values, *after)
 
 
 def rows_kernel(plan, idx_ref, *refs):
@@ -735,7 +763,7 @@
         out_shape=[jax.ShapeDtypeStruct((block, width), bf16)] * TP
         + [jax.ShapeDtypeStruct((slab, width), f32), jax.ShapeDtypeStruct((1, slab), f32)],
         scratch_shapes=[pltpu.VMEM((TP, block, width), f32)],
-        cost_estimate=cost(lines * rows * width, 2 * lines * rows * width),
+        cost_estimate=takes(2.2),
         name="sum_rows",
     )(idx, terms)
 
@@ -759,7 +787,7 @@
         + [pl.BlockSpec(memory_space=pltpu.VMEM)] * TP,
         out_shape=jax.ShapeDtypeStruct((block, hidden), f32),
         scratch_shapes=[pltpu.VMEM((TP, block, width), f32)],
-        cost_estimate=cost(block * hidden, 6 * block * hidden),
+        cost_estimate=takes(1.7),
         name="join_up",
     )(idx, *parts)
 
@@ -789,178 +817,170 @@
             jax.ShapeDtypeStruct((rows, width), bf16),
             jax.ShapeDtypeStruct((8, width), f32),
         ],
-        cost_estimate=cost(30 * rows * width, rows * width * 20),
+        cost_estimate=takes(2.7),
         name="resid_back",
     )(r_own, dm, vecs, *parts)
 
 
-def finish_kernel(r_ref, x_ref, dr_ref, vec_ref, *refs):
-    rows = r_ref.shape[0]
+def output_kernel(r_ref, vec_ref, *refs):
+    total = r_ref[...] + vec_ref[7:8, :]
+    for ref in refs[:TP]:
+        total += ref[...].astype(f32)
+    refs[TP][...] = total.astype(bf16)
+
+
+def finish_output(parts, r_own, vecs):
+    return pl.pallas_call(
+        output_kernel,
+        out_shape=jax.ShapeDtypeStruct(r_own.shape, bf16),
+        cost_estimate=takes(2.1),
+        name="finish_output",
+    )(r_own, vecs, *parts)
+
+
+def input_kernel(x_ref, dr_ref, vec_ref, *refs):
     total = refs[0][...].astype(f32)
     for ref in refs[1:TP]:
         total += ref[...].astype(f32)
     units, rstd = unit(x_ref[...].astype(f32))
-    grad = dr_ref[...] + unit_back(total[:rows] * vec_ref[3:4, :], units, rstd)
-    refs[TP][:rows, :] = (r_ref[...] + vec_ref[7:8, :] + total[rows:]).astype(bf16)
-    refs[TP][rows:, :] = grad.astype(bf16)
-
-
-def finish(parts, r_own, x, dr, vecs):
-    rows, width = x.shape
-    return pl.pallas_call(
-        finish_kernel,
-        out_shape=jax.ShapeDtypeStruct((2 * rows, width), bf16),
-        cost_estimate=cost(40 * x.size, x.size * 30),
-        name="finish",
-    )(r_own, x, dr, vecs, *parts)
-
-
-def normed_kernel(n_recv, idx_ref, x_ref, dq_ref, own_ref, *refs):
-    out_refs, refs = refs[:TP], refs[TP:]
-    recv_refs = refs[:n_recv]
-    w_ref, d_ref, sum_ref = refs[n_recv : n_recv + 3]
-    dh_refs, dh_now = refs[n_recv + 3 : -1], refs[-1]
+    grad = dr_ref[...] + unit_back(total * vec_ref[3:4, :], units, rstd)
+    refs[TP][...] = grad.astype(bf16)
+
+
+def finish_input(parts, x, dr, vecs):
+    return pl.pallas_call(
+        input_kernel,
+        out_shape=jax.ShapeDtypeStruct(x.shape, bf16),
+        cost_estimate=takes(2.4),
+        name="finish_input",
+    )(x, dr, vecs, *parts)
+
+
+def normed_kernel(plan, n_recv, idx_ref, x_ref, dq_ref, own_ref, *refs):
+    recv_refs, refs = refs[:n_recv], refs[n_recv:]
+    w_ref, h_ref, o_ref, da_ref, own_sum_ref, two_ref = refs[:6]
+    dh_refs, refs = refs[6 : 6 + TP], refs[6 + TP :]
+    g_refs, (dh_now, low_ref, sum_ref, acc_ref, vec_ref) = refs[:-5], refs[-5:]
     step = pl.program_id(0)
+    member, core = idx_ref[0], idx_ref[2]
+    side = lax.rem(member, 2)
+    cols = dq_ref.shape[1]
+    rows, width = x_ref.shape
 
     @pl.when(step == 0)
     def _():
         sum_ref[...] = jnp.zeros_like(sum_ref)
 
-    cols = dq_ref.shape[1]
-    width = x_ref.shape[1]
     grad_k, grad_v = own_ref[0], own_ref[1]
     for ref in recv_refs:
         grad_k += ref[0].astype(f32)
         grad_v += ref[1].astype(f32)
-    d_ref[:, :cols] = dq_ref[...]
-    d_ref[:, cols : 2 * cols] = grad_k.astype(bf16)
-    d_ref[:, 2 * cols : 3 * cols] = grad_v.astype(bf16)
-    d_ref[:, 3 * cols :] = jnp.zeros_like(d_ref[:, 3 * cols :])
-    low = d_ref[...]
+    place = step ^ (member // 2)
+    low_ref[place, :, :cols] = dq_ref[...]
+    low_ref[place, :, cols : 2 * cols] = grad_k.astype(bf16)
+    low_ref[place, :, 2 * cols : 3 * cols] = grad_v.astype(bf16)
+    low_ref[place, :, 3 * cols :] = jnp.zeros((rows, SMALLS), bf16)
+    low = low_ref[place]
     grad = dot(low, w_ref[...], 1, 1)
     dh_now[...] = grad.astype(bf16).reshape(dh_now.shape)
-    side = lax.rem(idx_ref[0], 2)
     for i in range(2):
 
         @pl.when(step == i)
         def _(i=i):
             for b in range(2):
-                rows = dh_now.shape[1]
-                dh_refs[2 * i + b][:rows, :] = dh_now[side ^ b]
-                dh_refs[2 * i + b][rows:, :] = out_refs[2 * i + b][...]
+                dh_refs[2 * i + b][...] = dh_now[side ^ b]
 
     units, _ = unit(x_ref[...].astype(f32))
     sum_ref[0:1, :width] += jnp.sum(grad * units, axis=0, keepdims=True)
     sum_ref[1:2, :width] += jnp.sum(grad, axis=0, keepdims=True)
     sum_ref[2:3, : low.shape[1]] += jnp.sum(low.astype(f32), axis=0, keepdims=True)
 
-
-def normed_back(idx, x_all, dq, own, recvs, w_qkv, out_terms):
+    @pl.when(step == 1)
+    def _():
+        wide = low_ref.shape[2]
+        acc_ref[:, :wide] = dot(h_ref[...], low_ref[...].reshape(2 * rows, wide), 0, 0)
+        da = da_ref[...].reshape(2 * rows, cols)
+        for j in range(TP):
+            at = j * cols
+            acc_ref[at : at + cols, wide : wide + cols] = dot(o_ref[j], da, 0, 0)
+        bias_q, bias_v = sum_ref[2:3, :cols], sum_ref[2:3, 2 * cols : 3 * cols]
+        zero = jnp.zeros_like(bias_q)
+        vec_ref[...] = jnp.zeros_like(vec_ref)
+        vectors = [
+            jnp.concatenate([jnp.where(member == j, b, zero) for j in range(TP)], axis=1)
+            for b in (bias_q, bias_v)
+        ]
+        vectors += [
+            own_sum_ref[0:1, :],
+            sum_ref[0:1, :],
+            sum_ref[1:2, :],
+            two_ref[0:1, :],
+            two_ref[1:2, :],
+            own_sum_ref[1:2, :],
+        ]
+        for j, row in enumerate(vectors):
+            vec_ref[SMALLS + j : SMALLS + j + 1, :] = row
+        acc_ref[:, wide + cols :] = vec_ref[...].T[:, SMALLS:]
+        if not plan.fast:
+            g_refs[0][...] = acc_ref[...].astype(bf16)
+            return
+        near, block, _ = g_refs[0].shape
+        span = near // plan.size["gx"]
+        for ref, owner in ((g_refs[0], core), (g_refs[1], 1 - core)):
+            for n in range(near):
+                gx, rest = divmod(n, span)
+                at = ((gx * 2 + owner) * span + rest) * block
+                ref[n] = acc_ref[pl.ds(pl.multiple_of(at, 8), block), :].astype(bf16)
+
+
+def normed_back(plan, idx, x_all, dq, own, recvs, w_qkv, low, o_all, da_cols, sum_own, sum_two):
     rows, width = x_all.shape
     cols = dq.shape[1]
     wide = w_qkv.shape[1]
+    total = wide + cols + SMALLS
     step = rows // 2
     one = (rows // TP, width)
+    near = plan.devices // 2
+
+    def block(i, idx):
+        return (i ^ (idx[0] // 2), 0)
+
     pairs = pl.BlockSpec((2, step, cols), lambda i, idx: (0, i ^ (idx[0] // 2), 0))
-    return pl.pallas_call(
-        functools.partial(normed_kernel, len(recvs)),
+    if plan.fast:
+        sums = [(near, width // plan.devices, total)] * 2
+    else:
+        sums = [(width, total)]
+    constants = (w_qkv, low, o_all, da_cols, sum_own, sum_two)
+    return pl.pallas_call(
+        functools.partial(normed_kernel, plan, len(recvs)),
         grid_spec=pltpu.PrefetchScalarGridSpec(
             num_scalar_prefetch=1,
             grid=(2,),
-            in_specs=[
-                pl.BlockSpec((step, width), lambda i, idx: (i ^ (idx[0] // 2), 0)),
-                pl.BlockSpec((step, cols), lambda i, idx: (i ^ (idx[0] // 2), 0)),
-                pairs,
-            ]
-            + [whole(one)] * TP
+            in_specs=[pl.BlockSpec((step, width), block), pl.BlockSpec((step, cols), block), pairs]
             + [pairs] * len(recvs)
-            + [whole(w_qkv.shape)],
-            out_specs=[
-                pl.BlockSpec((step, wide), lambda i, idx: (i ^ (idx[0] // 2), 0)),
-                whole((8, width)),
-            ]
-            + [whole((2 * one[0], width))] * TP,
-            scratch_shapes=[pltpu.VMEM((2, *one), bf16)],
+            + [whole(v.shape) for v in constants],
+            out_specs=[whole(one)] * TP + [whole(shape) for shape in sums],
+            scratch_shapes=[
+                pltpu.VMEM((2, *one), bf16),
+                pltpu.VMEM((2, step, wide), bf16),
+                pltpu.VMEM((8, width), f32),
+                pltpu.VMEM((width, total), f32),
+                pltpu.VMEM((2 * SMALLS, width), f32),
+            ],
         ),
-        out_shape=[
-            jax.ShapeDtypeStruct((rows, wide), bf16),
-            jax.ShapeDtypeStruct((8, width), f32),
-        ]
-        + [jax.ShapeDtypeStruct((2 * one[0], width), bf16)] * TP,
+        out_shape=[jax.ShapeDtypeStruct(one, bf16)] * TP
+        + [jax.ShapeDtypeStruct(shape, bf16) for shape in sums],
         compiler_params=params(),
-        cost_estimate=cost(2 * rows * width * wide, rows * width * 12),
+        cost_estimate=takes(NORMED),
         name="normed_back",
-    )(idx, x_all, dq, own, *out_terms, *recvs, w_qkv)
-
-
-def proj_grads_kernel(plan, idx_ref, h_ref, d_ref, sum_ref, own_ref, two_ref, da_ref, o_ref, *refs):
-    fast = plan.fast
-    acc_ref, vec_ref = refs[-2:]
-    wide = d_ref.shape[1]
-    cols = o_ref.shape[2]
-    rows, width = h_ref.shape
-    member = idx_ref[0]
-    acc_ref[:, :wide] = dot(h_ref[...], d_ref[...], 0, 0)
-    da = da_ref[...].reshape(rows, cols)
-    for j in range(TP):
-        at = j * cols
-        acc_ref[at : at + cols, wide : wide + cols] = dot(o_ref[j], da, 0, 0)
-    bias_q, bias_v = sum_ref[2:3, :cols], sum_ref[2:3, 2 * cols : 3 * cols]
-    zero = jnp.zeros_like(bias_q)
-    vec_ref[...] = jnp.zeros_like(vec_ref)
-    rows_of = [
-        jnp.concatenate([jnp.where(member == j, b, zero) for j in range(TP)], axis=1)
-        for b in (bias_q, bias_v)
-    ]
-    rows_of += [own_ref[0:1, :], sum_ref[0:1, :], sum_ref[1:2, :], two_ref[0:1, :], two_ref[1:2, :], own_ref[1:2, :]]
-    for j, row in enumerate(rows_of):
-        vec_ref[SMALLS + j : SMALLS + j + 1, :] = row
-    acc_ref[:, wide + cols :] = vec_ref[...].T[:, SMALLS:]
-    if not fast:
-        refs[0][...] = acc_ref[...].astype(bf16)
-        return
-    core = idx_ref[2]
-    keep_ref, send_ref = refs[:2]
-    near, block, _ = keep_ref.shape
-    span = near // plan.size["gx"]
-    for ref, owner in ((keep_ref, core), (send_ref, 1 - core)):
-        for n in range(near):
-            gx, rest = divmod(n, span)
-            at = ((gx * 2 + owner) * span + rest) * block
-            ref[n] = acc_ref[pl.ds(pl.multiple_of(at, 8), block), :].astype(bf16)
-
-
-def proj_grads(plan, idx, low, grads, sums, sum_own, sum_two, da_cols, o_all):
-    rows, width = low.shape
-    cols = o_all.shape[2]
-    wide = grads.shape[1] + cols + SMALLS
-    near = plan.devices // 2
-    if plan.fast:
-        out_shape = [jax.ShapeDtypeStruct((near, width // plan.devices, wide), bf16)] * 2
-    else:
-        out_shape = jax.ShapeDtypeStruct((width, wide), bf16)
-    operands = (low, grads, sums, sum_own, sum_two, da_cols, o_all)
-    return pl.pallas_call(
-        functools.partial(proj_grads_kernel, plan),
-        in_specs=[pl.BlockSpec(memory_space=pltpu.SMEM)]
-        + [pl.BlockSpec(memory_space=pltpu.VMEM)] * len(operands),
-        out_shape=out_shape,
-        scratch_shapes=[
-            pltpu.VMEM((width, wide), f32),
-            pltpu.VMEM((2 * SMALLS, width), f32),
-        ],
-        compiler_params=pltpu.CompilerParams(vmem_limit_bytes=60 * 1024 * 1024),
-        cost_estimate=cost(2 * rows * width * wide, width * wide * 6),
-        name="proj_grads",
-    )(idx, *operands)
-
-
-def join_kernel(keep, cols, wide, in_ref, both_ref, *refs):
+    )(idx, x_all, dq, own, *recvs, *constants)
+
+
+def join_kernel(keep, cols, wide, in_ref, first_ref, second_ref, *refs):
     mats, vec_refs = refs[:4], refs[4:12]
     output_ref, input_ref, turn_ref = refs[12:]
-    rows = output_ref.shape[0]
-    output_ref[...] = both_ref[:rows, :]
-    input_ref[...] = both_ref[rows:, :]
+    output_ref[...] = first_ref[...]
+    input_ref[...] = second_ref[...]
     groups = {}
     for n in range(in_ref.shape[0]):
         value = in_ref[n].astype(f32)
@@ -978,7 +998,7 @@
         ref[...] = turned[j : j + 1, :block]
 
 
-def join_grads(plan, got, both, cols, wide):
+def join_grads(plan, got, first, second, cols, wide):
     near, block, _ = got.shape
     members = [plan.place(plan.same(n))[0] for n in range(near)]
     width = cols * TP
@@ -986,12 +1006,12 @@
         functools.partial(join_kernel, members, cols, wide),
         out_shape=[jax.ShapeDtypeStruct((block, width), f32)] * 4
         + [jax.ShapeDtypeStruct((1, block), f32)] * 8
-        + [jax.ShapeDtypeStruct((both.shape[0] // 2, both.shape[1]), bf16)] * 2,
+        + [jax.ShapeDtypeStruct(first.shape, bf16)] * 2,
         scratch_shapes=[pltpu.VMEM((128, 128), f32)],
         compiler_params=pltpu.CompilerParams(vmem_limit_bytes=60 * 1024 * 1024),
-        cost_estimate=cost(got.size, got.size * 2),
+        cost_estimate=takes(2.2),
         name="join_grads",
-    )(got, both)
+    )(got, first, second)
 
 
 def local(
@@ -1014,18 +1034,17 @@
     fast = plan.fast
 
     id_rows = jnp.pad(segment_ids[0].astype(bf16), (0, 8 * width - length)).reshape(8, width)
-    moved = plan.move(jnp.concatenate([x_own, id_rows], axis=0), plan.route)
-    x_mine = moved[:rows]
-    ids = moved[rows:].reshape(1, -1)[:, :length].astype(f32)
+    packed = jnp.concatenate([x_own, id_rows], axis=0)
     dm_own = (cotangent[0].astype(f32) * padding[0].astype(f32)[:, None]).astype(bf16)
     dm_mine = plan.move(dm_own, plan.route)
 
     small = [b_query, b_value, b_out, ln1_gain, ln1_shift, ln2_gain, ln2_shift, b_down]
     if fast:
-        small = jnp.stack(small, axis=0)
         chunk = prepare(plan, w_query, w_key, w_value, small, w_up, w_out)
         got = lax.all_to_all(chunk, plan.tp, 0, 0, tiled=True)
-        got, x_mine = lax.optimization_barrier((got, x_mine))
+        moved = plan.move(packed, plan.route)
+        got, moved = lax.optimization_barrier((got, moved))
+        x_mine = moved[:rows]
         x_all = lax.all_gather(x_mine, plan.tp, axis=0, tiled=True)
         proj, shard = shards_of(got, w_down, b_up[None], 3 * cols + SMALLS, lines)
         projs = [proj] + [plan.turn(proj, "sz", -j) for j in range(1, lines)]
@@ -1035,6 +1054,8 @@
         low_one, query, kv, w_qkv, vecs = qkv(plan, idx, x_all, projs, plan.swap(projs))
     else:
         small = jnp.stack(small, axis=1)
+        moved = plan.move(packed, plan.route)
+        x_mine = moved[:rows]
         x_all = lax.all_gather(x_mine, plan.tp, axis=0, tiled=True)
         b_row = jnp.pad(b_up[None], ((0, 7), (0, width - slab)))
         table = [w_query, w_key, w_value, w_out, small]
@@ -1054,6 +1075,8 @@
         down_mine = downs[:, :slab].reshape(-1, width)
         b_up_mine = downs[:, slab, :slab].reshape(1, -1).astype(f32)
 
+    ids = moved[rows:].reshape(1, -1)[:, :length].astype(f32)
+
     parts = plan.parts
     kvs = [kv] + [plan.turn(kv, plan.half, -j) for j in range(1, parts)]
     mixed, lse = attend(idx, ids, query, kvs)
@@ -1061,13 +1084,16 @@
     dms = plan.partners(dm_mine)
     if fast:
         shard, o_all, dms = lax.optimization_barrier((shard, o_all, dms))
-        up_mine, out_full, down_mine, row = assemble(plan, idx, shard, plan.swap(shard), slab)
-        out_full = out_full.reshape(TP, cols, width)
-        down_mine = down_mine.reshape(-1, width)
-        b_up_mine = row[:, :, 0, :slab].reshape(1, -1).astype(f32)
-    r_own, low_two, act, grad_pre, dm_all, sum_two, *dh_two = mlp(
-        idx, x_all, o_all, dms, out_full, up_mine, down_mine, vecs, b_up_mine
-    )
+        weights = [shard, plan.swap(shard)]
+    else:
+        weights = [out_full, up_mine, down_mine, b_up_mine]
+    results = mlp(plan, idx, x_all, o_all, vecs, dms, weights, slab)
+    r_own, low_two, act, grad_pre, dm_all, sum_two = results[:6]
+    dh_two = results[6 : 6 + TP]
+    if fast:
+        out_mine, down_mine = results[6 + TP :]
+    else:
+        out_mine = lax.dynamic_index_in_dim(out_full, member, 0, keepdims=False)
 
     back_two = plan.reduce(dh_two)
     if fast:
@@ -1085,14 +1111,14 @@
         ]
     dr, da, sum_own = resid_back(back_two, r_own, dm_mine, vecs)
     if fast:
-        terms = add(near_terms, plan.swap(far_terms))
-        das = [da, plan.partner(da, 1), plan.partner(da, 2)]
-        terms, da = lax.optimization_barrier((terms, da))
-        das += [plan.partner(da, 3)]
+        terms = add(near_terms, plan.swap(far_terms), after=(da,))
+        das = plan.partners(da)
+        after = [terms]
         terms = lax.all_to_all(terms, "sz", 0, 0, tiled=True)
         *ups, g_w_down, g_b_up = sum_rows(plan, idx, terms, block, slab)
     else:
         das = plan.partners(da)
+        after = []
         row = jnp.pad(row.reshape(plan.copies, 1, slab), ((0, 0), (0, 7), (0, width - slab)))
         downs = jnp.concatenate([down_terms.reshape(plan.copies, slab, width), row], axis=1)
         downs = lax.psum_scatter(downs, plan.rep, scatter_dimension=0, tiled=False)
@@ -1102,18 +1128,23 @@
         ups = ups.reshape(plan.copies, TP * block, -1)
         ups = lax.psum_scatter(ups, plan.rep, scatter_dimension=0, tiled=False)
         ups = lax.all_to_all(ups.reshape(TP, block, -1), plan.tp, 0, 0, tiled=True).astype(f32)
-    grad_query, kv_own, da_cols, *kv_others = attend_back(idx, ids, query, das, out_full, lse, kvs)
+    grad_query, kv_own, da_cols, *kv_others = attend_back(
+        idx, ids, query, das, after, out_mine, lse, kvs
+    )
+    kv_others, out_parts = lax.optimization_barrier((kv_others, plan.reduce(out_terms)))
     recvs = [plan.turn(kv_others[j - 1], plan.half, j) for j in range(1, parts)]
-    grads, sum_one, *both = normed_back(idx, x_all, grad_query, kv_own, recvs, w_qkv, out_terms)
-    both = plan.reduce(both)
-    terms = proj_grads(plan, idx, low_one, grads, sum_one, sum_own, sum_two, da_cols, o_all)
+    results = normed_back(
+        plan, idx, x_all, grad_query, kv_own, recvs, w_qkv, low_one, o_all, da_cols, sum_own, sum_two
+    )
+    back_one, terms = plan.reduce(results[:TP]), results[TP:]
+    output = plan.move(finish_output(out_parts, r_own, vecs), plan.back)
     if fast:
         keep, send = terms
         terms = add(keep, plan.swap(send))
-        terms, ups, both = lax.optimization_barrier((terms, ups, both))
+        terms, ups, back_one = lax.optimization_barrier((terms, ups, back_one))
         got = lax.all_to_all(terms, SAME, 0, 0, tiled=True)
     else:
-        terms = plan.shuffle(terms.reshape(plan.devices, block, -1), ALL, ("c",) + SAME)
+        terms = plan.shuffle(terms[0].reshape(plan.devices, block, -1), ALL, ("c",) + SAME)
         terms = terms.reshape(2, -1, *terms.shape[1:])
         keep, send = jnp.where(core == 0, terms, terms[::-1])
         got = lax.all_to_all(add(keep, plan.swap(send)), SAME, 0, 0, tiled=True)
@@ -1124,8 +1155,8 @@
         ups = ups.reshape(TP, block, plan.copies, slab).transpose(0, 2, 1, 3)
         ups = plan.shuffle(ups.reshape(plan.devices, block, slab), plan.tp + plan.rep, ALL)
         g_w_up = ups.transpose(1, 0, 2).reshape(block, hidden)
-    both = plan.move(finish(both, r_own, x_mine, dr, vecs), plan.back)
-    joined = join_grads(plan, got, both, cols, w_qkv.shape[1])
+    grad_input = plan.move(finish_input(back_one, x_mine, dr, vecs), plan.back)
+    joined = join_grads(plan, got, output, grad_input, cols, w_qkv.shape[1])
     g_query, g_key, g_value, g_out, *vec, output, grad_input = joined
     vec = [v[0] for v in vec]
     return (

time: 222 us -> 212 us (0.955); the launches traced: 221 us -> 208 us
  waiting for transfers between devices: 51 us -> 37.3 us
  starting transfers between devices: 50.5 us -> 57.2 us
  Pallas kernels: 75.7 us -> 72 us
    ppermute x15 -> x18, waiting for transfers between devices: 24.6 us -> 12.7 us  [partner(): return lax.ppermute(value, self.tp, table)]
    ppermute x15 -> x18, starting transfers between devices: 17.7 us -> 21.8 us  [partner(): return lax.ppermute(value, self.tp, table)]
    pallas_call x8 -> x7, Pallas kernels: 42.7 us -> 38.9 us  [the longest x1 10.8 us: mlp(): pl.pallas_call(functools.partial(mlp_kernel, plan), grid_spec=pltpu.Prefe...]
    ppermute x3 -> x4, waiting for transfers between devices: 9.05 us -> 5.95 us  [move(): return lax.ppermute(value, ALL, table)]
    ppermute x3 -> x4, starting transfers between devices: 9.74 us -> 11.7 us  [move(): return lax.ppermute(value, ALL, table)]
    unnamed x74 -> x88, local copies, waits for them, and re-layouts: 9.85 us -> 11 us
  transfers between devices with their start and end apart: 31 -> 35, of which waited for: 15 -> 14; matrix products, arithmetic and copies ran while one was open for 1% -> 1% of each run, Pallas kernels for 26% -> 27%
where the time goes in v4:
time: 212 us; the launch traced here: 208 us
  Pallas kernels  72 us (34%)
  starting transfers between devices  57.2 us (27%)
  waiting for transfers between devices  37.3 us (18%)
  blocking collectives  26.4 us (12%)
  local copies, waits for them, and re-layouts  11.1 us (5%)
  other arithmetic  3.06 us (1%)
    ppermute x18, starting transfers between devices, partner(): return lax.ppermute(value, self.tp, table)  21.8 us
    all_gather x1, blocking collectives, local(): o_all = lax.all_gather(mixed, plan.tp, axis=0, tiled=False)  14.2 us
    ppermute x18, waiting for transfers between devices, partner(): return lax.ppermute(value, self.tp, table)  12.7 us
    all_gather x1, blocking collectives, local(): x_all = lax.all_gather(x_mine, plan.tp, axis=0, tiled=True)  12.2 us
    ppermute x4, starting transfers between devices, move(): return lax.ppermute(value, ALL, table)  11.7 us
    unnamed x88, local copies, waits for them, and re-layouts  11 us
    pallas_call x1, Pallas kernels, mlp(): pl.pallas_call(functools.partial(mlp_kernel, plan), grid_spec=pltpu.Prefe...  10.8 us
    pallas_call x1, Pallas kernels, attend_back(): pl.pallas_call(functools.partial(bwd_kernel, parts, len(after)), grid_spe...  10.8 us
  transfers between devices with their start and end apart: 35, of which 14 were waited for; matrix products, arithmetic and copies ran while one was open for 1% of the time, Pallas kernels for 27%

profile of v4, /device:TPU:2, one launch (start us, length us, event | category | flops | bytes accessed | tf_op | source)
XLA Modules:
  0.0 208.3 jit_solution(8429853257404972555)
XLA Ops:
  2.4 4.5 %collective-permute-start = (bf16[136,768]{1,0:T(8,128)(2,1)S(1)}, bf16[136,768]{1,0:T(8,128)(2,1)S(1)}, u32[]{:S(2)}, u32[]{:S(2)}) collective-permute-start(bf16[136,768]{1,0:T(8,128)(2,1)S(1)} %pad_maximum_fusion.1), channel_id=1, source_target_pairs={{0,0},{1,1},{2,16},{3,17},{4,8},{5,9},{6,24},{7,25},{8,2},{9,3},{1... | collective-permute-start | bytes 626696 | tf_op jit(solution)/shard_map/ppermute | solution.py:93
  8.8 4.2 %all-to-all-start = ((bf16[4,24,2176]{2,1,0:T(8,128)(2,1)}), bf16[4,24,2176]{2,1,0:T(8,128)(2,1)S(1)}, u32[]{:S(2)}, u32[]{:S(2)}) async-start(bf16[4,24,2176]{2,1,0:T(8,128)(2,1)} %prepare.1), calls=%async_computation | async-start | bytes 835584 | tf_op jit(solution)/shard_map/all_to_all | solution.py:1044
  15.1 5.5 %all-to-all-done.got_ref = bf16[4,24,2176]{2,1,0:T(8,128)(2,1)S(1)} async-done(((bf16[4,24,2176]{2,1,0:T(8,128)(2,1)}), bf16[4,24,2176]{2,1,0:T(8,128)(2,1)S(1)}, u32[]{:S(2)}, u32[]{:S(2)}) %all-to-all-start) | async-done | bytes 417824 | tf_op jit(solution)/shard_map/all_to_all | solution.py:1044
  21.4 2.4 %shards_of.1 = (bf16[96,640]{1,0:T(8,128)(2,1)}, bf16[4,296,768]{2,1,0:T(8,128)(2,1)}) custom-call(bf16[4,24,2176]{2,1,0:T(8,128)(2,1)} %copy-done.7, bf16[96,768]{1,0:T(8,128)(2,1)} %down_ref.1, bf16[1,96]{1,0:T(2,128)(2,1)} %bitcast.46), custom_call_target="tpu_custom_call" | custom-call | bytes 8856000 | tf_op jit(solution)/shard_map/shards_of/pallas_call | solution.py:209
  24.4 4.2 %collective-permute-start.2 = (bf16[96,640]{1,0:T(8,128)(2,1)}, bf16[96,640]{1,0:T(8,128)(2,1)S(1)}, u32[]{:S(2)}, u32[]{:S(2)}) collective-permute-start(bf16[96,640]{1,0:T(8,128)(2,1)} %get-tuple-element.120), channel_id=1, source_target_pairs={{0,4},{2,6},{4,0},{6,2},{1,5},{3,7},{5,1},{7,3},{8,12},{10,14},{12... | collective-permute-start | bytes 368648 | tf_op jit(solution)/shard_map/ppermute | solution.py:71
  28.7 12.2 %all_gather.9.x_ref = bf16[512,768]{1,0:T(8,128)(2,1)} all-gather(bf16[128,768]{1,0:T(8,128)(2,1)S(1)} %slice.9.x_ref), channel_id=1, replica_groups=mesh['gx'=2,'c'=2,'sz'=4,'sy'=2] {'gx','sy'}, dimensions={0}, use_global_device_ids=true | all-gather | bytes 983040 | tf_op jit(solution)/shard_map/all_gather | solution.py:1048
  41.0 3.7 %all-to-all-start.1 = ((bf16[4,296,768]{2,1,0:T(8,128)(2,1)}), bf16[4,296,768]{2,1,0:T(8,128)(2,1)S(1)}, u32[]{:S(2)}, u32[]{:S(2)}) async-start(bf16[4,296,768]{2,1,0:T(8,128)(2,1)} %get-tuple-element.125), calls=%async_computation.1 | async-start | bytes 3637248 | tf_op jit(solution)/shard_map/all_to_all | solution.py:1052
  47.5 4.8 %qkv.1 = (bf16[512,768]{1,0:T(8,128)(2,1)}, bf16[512,192]{1,0:T(8,128)(2,1)}, bf16[2,512,192]{2,1,0:T(8,128)(2,1)}, bf16[768,640]{1,0:T(8,128)(2,1)}, f32[8,768]{1,0:T(8,128)}) custom-call(s32[4]{0:T(128)} %pad_add_fusion.idx_ref, bf16[512,768]{1,0:T(8,128)(2,1)} %all_gather.9.x_ref, bf16[4,96,640]{2,1,0:T(8,128)(2,1)} %copy-done.4, ...), custom_call_target="tpu_custom_call" | custom-call | bytes 17712000 | tf_op jit(solution)/shard_map/qkv/pallas_call | solution.py:280
  57.6 7.2 %attend.1 = (bf16[512,192]{1,0:T(8,128)(2,1)}, f32[8,512]{1,0:T(8,128)}) custom-call(s32[4]{0:T(128)} %pad_add_fusion.idx_ref, f32[1,1024]{1,0:T(1,128)} %slice_convert_fusion.ids_ref, bf16[512,192]{1,0:T(8,128)(2,1)} %get-tuple-element.124.q_ref, bf16[2,512,192]{2,1,0:T(8,128)(2,1)} %get-tuple-element.126.refs_0_.refs_5_, bf16[2,512,192]{2,1,0:T(8,128)(2,1)} %copy-done.3), custom_call_target="tpu_custom_call" | custom-call | bytes 26199000 | tf_op jit(solution)/shard_map/attend/pallas_call | solution.py:351
  64.8 14.2 %all-gather = bf16[2048,192]{1,0:T(8,128)(2,1)} all-gather(bf16[512,192]{1,0:T(8,128)(2,1)} %get-tuple-element.127), channel_id=2, replica_groups=mesh['gx'=2,'c'=2,'sz'=4,'sy'=2] {'gx','sy'}, dimensions={0}, use_global_device_ids=true | all-gather | bytes 983040 | tf_op jit(solution)/shard_map/all_gather | solution.py:1083
  79.0 6.0 %all-to-all-done.1.refs_4_ = bf16[4,296,768]{2,1,0:T(8,128)(2,1)S(1)} async-done(((bf16[4,296,768]{2,1,0:T(8,128)(2,1)}), bf16[4,296,768]{2,1,0:T(8,128)(2,1)S(1)}, u32[]{:S(2)}, u32[]{:S(2)}) %all-to-all-start.1) | async-done | bytes 1818656 | tf_op jit(solution)/shard_map/all_to_all | solution.py:1052
  85.0 3.8 %collective-permute-done.10.refs_5_ = bf16[4,296,768]{2,1,0:T(8,128)(2,1)S(1)} collective-permute-done((bf16[4,296,768]{2,1,0:T(8,128)(2,1)S(1)}, bf16[4,296,768]{2,1,0:T(8,128)(2,1)S(1)}, u32[]{:S(2)}, u32[]{:S(2)}) %collective-permute-start.10) | collective-permute-done | bytes 1818656 | tf_op jit(solution)/shard_map/ppermute | solution.py:52
  90.0 10.8 %mlp.1 = (f32[128,768]{1,0:T(8,128)}, bf16[512,768]{1,0:T(8,128)(2,1)}, bf16[512,768]{1,0:T(8,128)(2,1)}, bf16[512,768]{1,0:T(8,128)(2,1)}, bf16[512,768]{1,0:T(...) custom-call(s32[4]{0:T(128)} %pad_add_fusion.idx_ref, ...), custom_call_target="tpu_custom_call" | custom-call | bytes 38745000 | tf_op jit(solution)/shard_map/mlp/pallas_call | solution.py:611
  104.5 7.7 %mlp_weight_grads.1 = (bf16[4,200,768]{2,1,0:T(8,128)(2,1)}, bf16[4,200,768]{2,1,0:T(8,128)(2,1)}, bf16[128,768]{1,0:T(8,128)(2,1)}, bf16[128,768]{1,0:T(8,128)(...) custom-call(s32[4]{0:T(128)} %pad_add_fusion.idx_ref, bf16[512,768]{1,0:T(8,128)(2,1)} %get-tuple-element.143.h_ref, ...), custom_call_target="tpu_custom_call" | custom-call | bytes 28044000 | tf_op jit(solution)/shard_map/mlp_weight_grads/pallas_call | solution.py:697
  114.2 2.7 %resid_back.1 = (f32[128,768]{1,0:T(8,128)}, bf16[128,768]{1,0:T(8,128)(2,1)}, f32[8,768]{1,0:T(8,128)}) custom-call(f32[128,768]{1,0:T(8,128)} %get-tuple-element.138.r_ref, bf16[128,768]{1,0:T(8,128)(2,1)} %copy-done.9, f32[8,768]{1,0:T(8,128)} %get-tuple-element.130.vec_ref, bf16[128,768]{1,0:T(8,128)(2,1)} %get-tuple-element.153.refs_0_, ...), custom_call_target="tpu_custom_call" | custom-call | bytes 9963000 | tf_op jit(solution)/shard_map/resid_back/pallas_call | solution.py:813
  117.9 3.0 %add.15.refs_4_ = bf16[4,200,768]{2,1,0:T(8,128)(2,1)} custom-call(bf16[4,200,768]{2,1,0:T(8,128)(2,1)} %get-tuple-element.158.refs_0_, bf16[4,200,768]{2,1,0:T(8,128)(2,1)} %copy-done.8, bf16[128,768]{1,0:T(8,128)(2,1)} %get-tuple-element.157.refs_2_.refs_0_), custom_call_target="tpu_custom_call" | custom-call | bytes 9594000 | tf_op jit(solution)/shard_map/add/pallas_call | solution.py:731
  120.9 3.9 %all-to-all-start.2 = ((bf16[4,200,768]{2,1,0:T(8,128)(2,1)}), bf16[4,200,768]{2,1,0:T(8,128)(2,1)S(1)}, u32[]{:S(2)}, u32[]{:S(2)}) async-start(bf16[4,200,768]{2,1,0:T(8,128)(2,1)} %add.15.refs_4_), calls=%async_computation.2 | async-start | bytes 2457600 | tf_op jit(solution)/shard_map/all_to_all | solution.py:1117
  130.6 2.9 %collective-permute-done.16.refs_3_ = bf16[128,768]{1,0:T(8,128)(2,1)S(1)} collective-permute-done((bf16[128,768]{1,0:T(8,128)(2,1)S(1)}, bf16[128,768]{1,0:T(8,128)(2,1)S(1)}, u32[]{:S(2)}, u32[]{:S(2)}) %collective-permute-start.16) | collective-permute-done | bytes 196640 | tf_op jit(solution)/shard_map/ppermute | solution.py:61
  138.1 10.8 %attend_back.1 = (bf16[512,192]{1,0:T(8,128)(2,1)}, f32[2,512,192]{2,1,0:T(8,128)}, bf16[4,128,192]{2,1,0:T(8,128)(2,1)}, bf16[2,512,192]{2,1,0:T(8,128)(2,1)}) custom-call(s32[4]{0:T(128)} %pad_add_fusion.idx_ref, f32[1,1024]{1,0:T(1,128)} %slice_convert_fusion.ids_ref, bf16[512,192]{1,0:T(8,128)(2,1)} %get-tuple-element.124.q_ref, ...), custom_call_target="tpu_custom_call" | custom-call | bytes 39483000 | tf_op jit(solution)/shard_map/attend_back/pallas_call | solution.py:444
  152.0 7.5 %normed_back.1 = (bf16[128,768]{1,0:T(8,128)(2,1)}, bf16[128,768]{1,0:T(8,128)(2,1)}, bf16[128,768]{1,0:T(8,128)(2,1)}, bf16[128,768]{1,0:T(8,128)(2,1)}, bf16[1...) custom-call(s32[4]{0:T(128)} %pad_add_fusion.idx_ref, bf16[512,768]{1,0:T(8,128)(2,1)} %all_gather.9.x_ref, ...), custom_call_target="tpu_custom_call" | custom-call | bytes 47970000 | tf_op jit(solution)/shard_map/normed_back/pallas_call | solution.py:954
  169.6 2.8 %collective-permute-done.25.refs_3_ = bf16[128,768]{1,0:T(8,128)(2,1)S(1)} collective-permute-done((bf16[128,768]{1,0:T(8,128)(2,1)}, bf16[128,768]{1,0:T(8,128)(2,1)S(1)}, u32[]{:S(2)}, u32[]{:S(2)}) %collective-permute-start.25) | collective-permute-done | bytes 196640 | tf_op jit(solution)/shard_map/ppermute | solution.py:61
  172.4 6.7 %all-to-all-start.3 = ((bf16[16,24,896]{2,1,0:T(8,128)(2,1)}), bf16[16,24,896]{2,1,0:T(8,128)(2,1)S(1)}, u32[]{:S(2)}, u32[]{:S(2)}) async-start(bf16[16,24,896]{2,1,0:T(8,128)(2,1)} %add.16), calls=%async_computation.3 | async-start | bytes 1376256 | tf_op jit(solution)/shard_map/all_to_all | solution.py:1145
  181.2 3.4 %collective-permute-start.26 = (bf16[128,768]{1,0:T(8,128)(2,1)}, bf16[128,768]{1,0:T(8,128)(2,1)S(1)}, u32[]{:S(2)}, u32[]{:S(2)}) collective-permute-start(bf16[128,768]{1,0:T(8,128)(2,1)} %finish_output.1), channel_id=1, source_target_pairs={{0,0},{1,1},{16,2},{17,3},{8,4},{9,5},{24,6},{25,7},{2,8},{3,9},{1... | collective-permute-start | bytes 589832 | tf_op jit(solution)/shard_map/ppermute | solution.py:93
  198.4 3.8 %collective-permute-done.26.first_ref = bf16[128,768]{1,0:T(8,128)(2,1)S(1)} collective-permute-done((bf16[128,768]{1,0:T(8,128)(2,1)}, bf16[128,768]{1,0:T(8,128)(2,1)S(1)}, u32[]{:S(2)}, u32[]{:S(2)}) %collective-permute-start.26) | collective-permute-done | bytes 196640 | tf_op jit(solution)/shard_map/ppermute | solution.py:93
  (162 shorter events, 68.3 us)
Async XLA Ops:
  2.4 12.7 %collective-permute-start = (bf16[136,768]{1,0:T(8,128)(2,1)S(1)}, bf16[136,768]{1,0:T(8,128)(2,1)S(1)}, u32[]{:S(2)}, u32[]{:S(2)}) collective-permute-start(bf16[136,768]{1,0:T(8,128)(2,1)S(1)} %pad_maximum_fusion.1), channel_id=1, source_target_pairs={{0,0},{1,1},{2,16},{3,17},{4,8},{5,9},{6,24},{7,25},{8,2},{9,3},{1... | collective-permute-start | bytes 626696 | tf_op jit(solution)/shard_map/ppermute | solution.py:93
  8.8 11.8 %all-to-all-start = ((bf16[4,24,2176]{2,1,0:T(8,128)(2,1)}), bf16[4,24,2176]{2,1,0:T(8,128)(2,1)S(1)}, u32[]{:S(2)}, u32[]{:S(2)}) async-start(bf16[4,24,2176]{2,1,0:T(8,128)(2,1)} %prepare.1), calls=%async_computation | async-start | bytes 835584 | tf_op jit(solution)/shard_map/all_to_all | solution.py:1044
  13.2 27.7 %collective-permute-start.4 = (bf16[128,768]{1,0:T(8,128)(2,1)S(1)}, bf16[128,768]{1,0:T(8,128)(2,1)S(1)}, u32[]{:S(2)}, u32[]{:S(2)}) collective-permute-start(bf16[128,768]{1,0:T(8,128)(2,1)S(1)} %fusion), channel_id=1, source_target_pairs={{0,0},{1,1},{2,16},{3,17},{4,8},{5,9},{6,24},{7,25},{8,2},{9,3},{1... | collective-permute-start | bytes 589832 | tf_op jit(solution)/shard_map/ppermute | solution.py:93
  23.9 17.1 %collective-permute-start.3 = (bf16[96,640]{1,0:T(8,128)(2,1)}, bf16[96,640]{1,0:T(8,128)(2,1)S(1)}, u32[]{:S(2)}, u32[]{:S(2)}) collective-permute-start(bf16[96,640]{1,0:T(8,128)(2,1)} %get-tuple-element.120), channel_id=1, source_target_pairs={{0,2},{2,4},{4,6},{6,0},{1,3},{3,5},{5,7},{7,1},{8,10},{10,12},{12... | collective-permute-start | bytes 368648 | tf_op jit(solution)/shard_map/ppermute | solution.py:71
  24.4 16.5 %collective-permute-start.2 = (bf16[96,640]{1,0:T(8,128)(2,1)}, bf16[96,640]{1,0:T(8,128)(2,1)S(1)}, u32[]{:S(2)}, u32[]{:S(2)}) collective-permute-start(bf16[96,640]{1,0:T(8,128)(2,1)} %get-tuple-element.120), channel_id=1, source_target_pairs={{0,4},{2,6},{4,0},{6,2},{1,5},{3,7},{5,1},{7,3},{8,12},{10,14},{12... | collective-permute-start | bytes 368648 | tf_op jit(solution)/shard_map/ppermute | solution.py:71
  28.7 12.3 %collective-permute-start.1 = (bf16[96,640]{1,0:T(8,128)(2,1)}, bf16[96,640]{1,0:T(8,128)(2,1)S(1)}, u32[]{:S(2)}, u32[]{:S(2)}) collective-permute-start(bf16[96,640]{1,0:T(8,128)(2,1)} %get-tuple-element.120), channel_id=1, source_target_pairs={{0,6},{2,0},{4,2},{6,4},{1,7},{3,1},{5,3},{7,5},{8,14},{10,8},{12,... | collective-permute-start | bytes 368648 | tf_op jit(solution)/shard_map/ppermute | solution.py:71
  41.0 44.1 %all-to-all-start.1 = ((bf16[4,296,768]{2,1,0:T(8,128)(2,1)}), bf16[4,296,768]{2,1,0:T(8,128)(2,1)S(1)}, u32[]{:S(2)}, u32[]{:S(2)}) async-start(bf16[4,296,768]{2,1,0:T(8,128)(2,1)} %get-tuple-element.125), calls=%async_computation.1 | async-start | bytes 3637248 | tf_op jit(solution)/shard_map/all_to_all | solution.py:1052
  52.6 26.3 %collective-permute-start.9 = (bf16[128,768]{1,0:T(8,128)(2,1)S(1)}, bf16[128,768]{1,0:T(8,128)(2,1)S(1)}, u32[]{:S(2)}, u32[]{:S(2)}) collective-permute-start(bf16[128,768]{1,0:T(8,128)(2,1)S(1)} %collective-permute-done.4.refs_0_.dm_ref), channel_id=1, source_target_pairs={{0,17},{1,16},{16,1},{17,0},{2,19},{3,18},{18,3},{19,2},{4,21},{5,... | collective-permute-start | bytes 589832 | tf_op jit(solution)/shard_map/ppermute | solution.py:61
  54.2 24.8 %collective-permute-start.8 = (bf16[128,768]{1,0:T(8,128)(2,1)S(1)}, bf16[128,768]{1,0:T(8,128)(2,1)S(1)}, u32[]{:S(2)}, u32[]{:S(2)}) collective-permute-start(bf16[128,768]{1,0:T(8,128)(2,1)S(1)} %collective-permute-done.4.refs_0_.dm_ref), channel_id=1, source_target_pairs={{0,16},{1,17},{16,0},{17,1},{2,18},{3,19},{18,2},{19,3},{4,20},{5,... | collective-permute-start | bytes 589832 | tf_op jit(solution)/shard_map/ppermute | solution.py:61
  55.5 23.5 %collective-permute-start.7 = (bf16[128,768]{1,0:T(8,128)(2,1)S(1)}, bf16[128,768]{1,0:T(8,128)(2,1)S(1)}, u32[]{:S(2)}, u32[]{:S(2)}) collective-permute-start(bf16[128,768]{1,0:T(8,128)(2,1)S(1)} %collective-permute-done.4.refs_0_.dm_ref), channel_id=1, source_target_pairs={{0,1},{1,0},{16,17},{17,16},{2,3},{3,2},{18,19},{19,18},{4,5},{5,4... | collective-permute-start | bytes 589832 | tf_op jit(solution)/shard_map/ppermute | solution.py:61
  100.9 11.3 %collective-permute-start.11 = (bf16[128,768]{1,0:T(8,128)(2,1)}, bf16[128,768]{1,0:T(8,128)(2,1)S(1)}, u32[]{:S(2)}, u32[]{:S(2)}) collective-permute-start(bf16[128,768]{1,0:T(8,128)(2,1)} %get-tuple-element.140), channel_id=1, source_target_pairs={{0,1},{1,0},{16,17},{17,16},{2,3},{3,2},{18,19},{19,18},{4,5},{5,4... | collective-permute-start | bytes 589832 | tf_op jit(solution)/shard_map/ppermute | solution.py:61
  102.1 10.1 %collective-permute-start.12 = (bf16[128,768]{1,0:T(8,128)(2,1)}, bf16[128,768]{1,0:T(8,128)(2,1)S(1)}, u32[]{:S(2)}, u32[]{:S(2)}) collective-permute-start(bf16[128,768]{1,0:T(8,128)(2,1)} %get-tuple-element.141), channel_id=1, source_target_pairs={{0,16},{1,17},{16,0},{17,1},{2,18},{3,19},{18,2},{19,3},{4,20},{5,... | collective-permute-start | bytes 589832 | tf_op jit(solution)/shard_map/ppermute | solution.py:61
  103.3 10.3 %collective-permute-start.13 = (bf16[128,768]{1,0:T(8,128)(2,1)}, bf16[128,768]{1,0:T(8,128)(2,1)S(1)}, u32[]{:S(2)}, u32[]{:S(2)}) collective-permute-start(bf16[128,768]{1,0:T(8,128)(2,1)} %get-tuple-element.142), channel_id=1, source_target_pairs={{0,17},{1,16},{16,1},{17,0},{2,19},{3,18},{18,3},{19,2},{4,21},{5,... | collective-permute-start | bytes 589832 | tf_op jit(solution)/shard_map/ppermute | solution.py:61
  120.9 45.4 %all-to-all-start.2 = ((bf16[4,200,768]{2,1,0:T(8,128)(2,1)}), bf16[4,200,768]{2,1,0:T(8,128)(2,1)S(1)}, u32[]{:S(2)}, u32[]{:S(2)}) async-start(bf16[4,200,768]{2,1,0:T(8,128)(2,1)} %add.15.refs_4_), calls=%async_computation.2 | async-start | bytes 2457600 | tf_op jit(solution)/shard_map/all_to_all | solution.py:1117
  126.6 10.8 %collective-permute-start.15 = (bf16[128,768]{1,0:T(8,128)(2,1)S(1)}, bf16[128,768]{1,0:T(8,128)(2,1)S(1)}, u32[]{:S(2)}, u32[]{:S(2)}) collective-permute-start(bf16[128,768]{1,0:T(8,128)(2,1)S(1)} %copy-done.10), channel_id=1, source_target_pairs={{0,16},{1,17},{16,0},{17,1},{2,18},{3,19},{18,2},{19,3},{4,20},{5,... | collective-permute-start | bytes 589832 | tf_op jit(solution)/shard_map/ppermute | solution.py:61
  127.4 10.0 %collective-permute-start.14 = (bf16[128,768]{1,0:T(8,128)(2,1)S(1)}, bf16[128,768]{1,0:T(8,128)(2,1)S(1)}, u32[]{:S(2)}, u32[]{:S(2)}) collective-permute-start(bf16[128,768]{1,0:T(8,128)(2,1)S(1)} %copy-done.10), channel_id=1, source_target_pairs={{0,1},{1,0},{16,17},{17,16},{2,3},{3,2},{18,19},{19,18},{4,5},{5,4... | collective-permute-start | bytes 589832 | tf_op jit(solution)/shard_map/ppermute | solution.py:61
  128.3 20.6 %collective-permute-start.18 = (bf16[128,768]{1,0:T(8,128)(2,1)S(1)}, bf16[128,768]{1,0:T(8,128)(2,1)S(1)}, u32[]{:S(2)}, u32[]{:S(2)}) collective-permute-start(bf16[128,768]{1,0:T(8,128)(2,1)S(1)} %copy-done.38), channel_id=1, source_target_pairs={{0,1},{1,0},{16,17},{17,16},{2,3},{3,2},{18,19},{19,18},{4,5},{5,4... | collective-permute-start | bytes 589832 | tf_op jit(solution)/shard_map/ppermute | solution.py:61
  129.4 19.5 %collective-permute-start.19 = (bf16[128,768]{1,0:T(8,128)(2,1)S(1)}, bf16[128,768]{1,0:T(8,128)(2,1)S(1)}, u32[]{:S(2)}, u32[]{:S(2)}) collective-permute-start(bf16[128,768]{1,0:T(8,128)(2,1)S(1)} %copy-done.37), channel_id=1, source_target_pairs={{0,16},{1,17},{16,0},{17,1},{2,18},{3,19},{18,2},{19,3},{4,20},{5,... | collective-permute-start | bytes 589832 | tf_op jit(solution)/shard_map/ppermute | solution.py:61
  133.6 15.4 %collective-permute-start.20 = (bf16[128,768]{1,0:T(8,128)(2,1)S(1)}, bf16[128,768]{1,0:T(8,128)(2,1)S(1)}, u32[]{:S(2)}, u32[]{:S(2)}) collective-permute-start(bf16[128,768]{1,0:T(8,128)(2,1)S(1)} %copy-done.36), channel_id=1, source_target_pairs={{0,17},{1,16},{16,1},{17,0},{2,19},{3,18},{18,3},{19,2},{4,21},{5,... | collective-permute-start | bytes 589832 | tf_op jit(solution)/shard_map/ppermute | solution.py:61
  159.6 10.0 %collective-permute-start.23 = (bf16[128,768]{1,0:T(8,128)(2,1)}, bf16[128,768]{1,0:T(8,128)(2,1)S(1)}, u32[]{:S(2)}, u32[]{:S(2)}) collective-permute-start(bf16[128,768]{1,0:T(8,128)(2,1)} %get-tuple-element.180), channel_id=1, source_target_pairs={{0,1},{1,0},{16,17},{17,16},{2,3},{3,2},{18,19},{19,18},{4,5},{5,4... | collective-permute-start | bytes 589832 | tf_op jit(solution)/shard_map/ppermute | solution.py:61
  161.6 10.8 %collective-permute-start.25 = (bf16[128,768]{1,0:T(8,128)(2,1)}, bf16[128,768]{1,0:T(8,128)(2,1)S(1)}, u32[]{:S(2)}, u32[]{:S(2)}) collective-permute-start(bf16[128,768]{1,0:T(8,128)(2,1)} %get-tuple-element.182), channel_id=1, source_target_pairs={{0,17},{1,16},{16,1},{17,0},{2,19},{3,18},{18,3},{19,2},{4,21},{5,... | collective-permute-start | bytes 589832 | tf_op jit(solution)/shard_map/ppermute | solution.py:61
  172.4 32.0 %all-to-all-start.3 = ((bf16[16,24,896]{2,1,0:T(8,128)(2,1)}), bf16[16,24,896]{2,1,0:T(8,128)(2,1)S(1)}, u32[]{:S(2)}, u32[]{:S(2)}) async-start(bf16[16,24,896]{2,1,0:T(8,128)(2,1)} %add.16), calls=%async_computation.3 | async-start | bytes 1376256 | tf_op jit(solution)/shard_map/all_to_all | solution.py:1145
  181.2 21.1 %collective-permute-start.26 = (bf16[128,768]{1,0:T(8,128)(2,1)}, bf16[128,768]{1,0:T(8,128)(2,1)S(1)}, u32[]{:S(2)}, u32[]{:S(2)}) collective-permute-start(bf16[128,768]{1,0:T(8,128)(2,1)} %finish_output.1), channel_id=1, source_target_pairs={{0,0},{1,1},{16,2},{17,3},{8,4},{9,5},{24,6},{25,7},{2,8},{3,9},{1... | collective-permute-start | bytes 589832 | tf_op jit(solution)/shard_map/ppermute | solution.py:93
  187.0 17.4 %collective-permute-start.27 = (bf16[128,768]{1,0:T(8,128)(2,1)}, bf16[128,768]{1,0:T(8,128)(2,1)S(1)}, u32[]{:S(2)}, u32[]{:S(2)}) collective-permute-start(bf16[128,768]{1,0:T(8,128)(2,1)} %finish_input.1), channel_id=1, source_target_pairs={{0,0},{1,1},{16,2},{17,3},{8,4},{9,5},{24,6},{25,7},{2,8},{3,9},{1... | collective-permute-start | bytes 589832 | tf_op jit(solution)/shard_map/ppermute | solution.py:93
  (54 other events, 320.6 us)

commit v5 on v4

--- a/solution.py
+++ b/solution.py
@@ -120,10 +120,14 @@
     return rstd * (grad_unit - first - units * second)
 
 
-def params(limit=60 * 1024 * 1024, axes=1):
+def params(limit=14 * 1024 * 1024, axes=1):
     return pltpu.CompilerParams(
         dimension_semantics=("arbitrary",) * axes, vmem_limit_bytes=limit
     )
+
+
+def small_params():
+    return pltpu.CompilerParams(vmem_limit_bytes=8 * 1024 * 1024)
 
 
 def takes(microseconds):
@@ -135,6 +139,10 @@
 def whole(shape):
     zeros = (0,) * len(shape)
     return pl.BlockSpec(shape, lambda *_: zeros)
+
+
+def here(shape):
+    return pl.BlockSpec(memory_space=pltpu.VMEM)
 
 
 def head_lanes(value, head):
@@ -212,6 +220,7 @@
             jax.ShapeDtypeStruct((TP * block, wide), bf16),
             jax.ShapeDtypeStruct((lines, 2 * TP * block + slab + 8, width), bf16),
         ],
+        compiler_params=small_params(),
         cost_estimate=takes(2.4),
         name="shards_of",
     )(got, w_down, b_row)
@@ -270,7 +279,7 @@
     ]
     scratch = []
     if plan.fast:
-        out_specs += [whole((width, wide)), whole((8, width))]
+        out_specs += [here((width, wide)), here((8, width))]
         out_shape += [
             jax.ShapeDtypeStruct((width, wide), bf16),
             jax.ShapeDtypeStruct((8, width), f32),
@@ -283,7 +292,7 @@
             num_scalar_prefetch=1,
             grid=(2,),
             in_specs=[pl.BlockSpec((step, width), lambda i, *_: (i, 0))]
-            + [whole(v.shape) for v in operands],
+            + [here(v.shape) for v in operands],
             out_specs=out_specs,
             scratch_shapes=scratch,
         ),
@@ -353,8 +362,8 @@
         grid_spec=pltpu.PrefetchScalarGridSpec(
             num_scalar_prefetch=1,
             grid=(rows // width,),
-            in_specs=[whole(ids.shape), pl.BlockSpec((width, cols), lambda i, *_: (i, 0))]
-            + [whole(kv.shape) for kv in kvs],
+            in_specs=[here(ids.shape), pl.BlockSpec((width, cols), lambda i, *_: (i, 0))]
+            + [here(kv.shape) for kv in kvs],
             out_specs=[
                 pl.BlockSpec((width, cols), lambda i, *_: (i, 0)),
                 pl.BlockSpec((8, width), lambda i, *_: (0, i)),
@@ -452,15 +461,15 @@
                 whole((cols, model)),
                 pl.BlockSpec((8, width), lambda i, *_: (0, i)),
             ]
-            + [whole((step, model))] * TP
+            + [here((step, model))] * TP
             + [pl.BlockSpec(memory_space=pl.ANY)] * len(after)
             + [whole(kv.shape) for kv in kvs],
             out_specs=[
                 pl.BlockSpec((width, cols), lambda i, *_: (i, 0)),
-                whole((2, span, cols)),
-                whole((TP, step, cols)),
+                here((2, span, cols)),
+                here((TP, step, cols)),
             ]
-            + [whole((2, span, cols))] * (parts - 1),
+            + [here((2, span, cols))] * (parts - 1),
             scratch_shapes=[
                 pltpu.VMEM((parts, cols, span), bf16),
                 pltpu.VMEM((parts, span, width), f32),
@@ -583,9 +592,9 @@
 
     token = pl.BlockSpec((step, width), block)
     inner = pl.BlockSpec((step, hidden), block)
-    one = whole((rows // TP, width))
+    one = here((rows // TP, width))
     now = (2, rows // TP, width)
-    out_specs = [one, token, inner, inner, token, whole((8, width))] + [one] * TP
+    out_specs = [one, token, inner, inner, token, here((8, width))] + [one] * TP
     out_shape = [
         jax.ShapeDtypeStruct((rows // TP, width), f32),
         jax.ShapeDtypeStruct((rows, width), bf16),
@@ -598,7 +607,7 @@
     if plan.fast:
         lines = plan.copies // 2
         gx = plan.size["gx"]
-        out_specs += [whole((cols, width)), whole((hidden, width))]
+        out_specs += [here((cols, width)), here((hidden, width))]
         out_shape += [
             jax.ShapeDtypeStruct((cols, width), bf16),
             jax.ShapeDtypeStruct((hidden, width), bf16),
@@ -616,10 +625,10 @@
             in_specs=[
                 token,
                 pl.BlockSpec((TP, step, cols), lambda i, idx: (0, i ^ (idx[0] // 2), 0)),
-                whole(vecs.shape),
+                here(vecs.shape),
             ]
-            + [one] * TP
-            + [whole(v.shape) for v in weights],
+            + [here(dms[0].shape)] * TP
+            + [here(v.shape) for v in weights],
             out_specs=out_specs,
             scratch_shapes=scratch,
         ),
@@ -700,13 +709,13 @@
             num_scalar_prefetch=1,
             grid=(2,),
             in_specs=[
-                whole((rows, width)),
+                here((rows, width)),
                 pl.BlockSpec((rows, step), lambda i, idx: (0, i)),
                 pl.BlockSpec((rows, step), lambda i, idx: (0, i)),
-                whole((rows, width)),
+                here((rows, width)),
                 pl.BlockSpec((step, width), lambda i, idx: (i, 0)),
             ],
-            out_specs=[whole(bundle)] * 2 + [whole(token)] * TP,
+            out_specs=[here(bundle)] * 2 + [here(token)] * TP,
             scratch_shapes=[
                 pltpu.VMEM((TP, *token), f32),
                 pltpu.VMEM((width, hidden), f32),
@@ -733,7 +742,7 @@
         in_specs=[pl.BlockSpec(memory_space=pltpu.VMEM)] * len(values)
         + [pl.BlockSpec(memory_space=pl.ANY)] * len(after),
         out_shape=jax.ShapeDtypeStruct(values[0].shape, bf16),
-        compiler_params=pltpu.CompilerParams(vmem_limit_bytes=60 * 1024 * 1024),
+        compiler_params=small_params(),
         cost_estimate=takes(2.6),
         name="add",
     )(*values, *after)
@@ -763,6 +772,7 @@
         out_shape=[jax.ShapeDtypeStruct((block, width), bf16)] * TP
         + [jax.ShapeDtypeStruct((slab, width), f32), jax.ShapeDtypeStruct((1, slab), f32)],
         scratch_shapes=[pltpu.VMEM((TP, block, width), f32)],
+        compiler_params=small_params(),
         cost_estimate=takes(2.2),
         name="sum_rows",
     )(idx, terms)
@@ -787,6 +797,7 @@
         + [pl.BlockSpec(memory_space=pltpu.VMEM)] * TP,
         out_shape=jax.ShapeDtypeStruct((block, hidden), f32),
         scratch_shapes=[pltpu.VMEM((TP, block, width), f32)],
+        compiler_params=small_params(),
         cost_estimate=takes(1.7),
         name="join_up",
     )(idx, *parts)
@@ -817,6 +828,7 @@
             jax.ShapeDtypeStruct((rows, width), bf16),
             jax.ShapeDtypeStruct((8, width), f32),
         ],
+        compiler_params=small_params(),
         cost_estimate=takes(2.7),
         name="resid_back",
     )(r_own, dm, vecs, *parts)
@@ -851,6 +863,7 @@
     return pl.pallas_call(
         input_kernel,
         out_shape=jax.ShapeDtypeStruct(x.shape, bf16),
+        compiler_params=small_params(),
         cost_estimate=takes(2.4),
         name="finish_input",
     )(x, dr, vecs, *parts)
@@ -958,8 +971,8 @@
             grid=(2,),
             in_specs=[pl.BlockSpec((step, width), block), pl.BlockSpec((step, cols), block), pairs]
             + [pairs] * len(recvs)
-            + [whole(v.shape) for v in constants],
-            out_specs=[whole(one)] * TP + [whole(shape) for shape in sums],
+            + [here(v.shape) for v in constants],
+            out_specs=[here(one)] * TP + [here(shape) for shape in sums],
             scratch_shapes=[
                 pltpu.VMEM((2, *one), bf16),
                 pltpu.VMEM((2, step, wide), bf16),
@@ -1008,7 +1021,7 @@
         + [jax.ShapeDtypeStruct((1, block), f32)] * 8
         + [jax.ShapeDtypeStruct(first.shape, bf16)] * 2,
         scratch_shapes=[pltpu.VMEM((128, 128), f32)],
-        compiler_params=pltpu.CompilerParams(vmem_limit_bytes=60 * 1024 * 1024),
+        compiler_params=small_params(),
         cost_estimate=takes(2.2),
         name="join_grads",
     )(got, first, second)
@@ -1043,10 +1056,10 @@
         chunk = prepare(plan, w_query, w_key, w_value, small, w_up, w_out)
         got = lax.all_to_all(chunk, plan.tp, 0, 0, tiled=True)
         moved = plan.move(packed, plan.route)
-        got, moved = lax.optimization_barrier((got, moved))
+        proj, shard = shards_of(got, w_down, b_up[None], 3 * cols + SMALLS, lines)
+        moved, shard = lax.optimization_barrier((moved, shard))
         x_mine = moved[:rows]
         x_all = lax.all_gather(x_mine, plan.tp, axis=0, tiled=True)
-        proj, shard = shards_of(got, w_down, b_up[None], 3 * cols + SMALLS, lines)
         projs = [proj] + [plan.turn(proj, "sz", -j) for j in range(1, lines)]
         projs, x_all, shard, dm_mine = lax.optimization_barrier((projs, x_all, shard, dm_mine))
         shard = lax.all_to_all(shard, "sz", 0, 0, tiled=True)

time: 212 us -> 195 us (0.920); the launches traced: 208 us -> 194 us
  Pallas kernels: 72 us -> 44.6 us
  waiting for transfers between devices: 37.3 us -> 56.3 us
  local copies, waits for them, and re-layouts: 11.1 us -> 7.29 us
    ppermute x18, waiting for transfers between devices: 12.7 us -> 19.9 us  [partner(): return lax.ppermute(value, self.tp, table)]
    all_to_all x1, waiting for transfers between devices: 6.01 us -> 12.3 us  [local(): shard = lax.all_to_all(shard, 'sz', 0, 0, tiled=True)]
    unnamed x88 -> x80, local copies, waits for them, and re-layouts: 11 us -> 7.23 us
    pallas_call x1, Pallas kernels: 7.73 us -> 4.1 us  [mlp_weight_grads(): pl.pallas_call(functools.partial(pair_kernel, plan), grid_spec=pltpu.Pref...]
    ppermute x4, waiting for transfers between devices: 5.95 us -> 9.27 us  [move(): return lax.ppermute(value, ALL, table)]
    pallas_call x1, Pallas kernels: 10.8 us -> 7.86 us  [mlp(): pl.pallas_call(functools.partial(mlp_kernel, plan), grid_spec=pltpu.Prefe...]
    pallas_call x1, Pallas kernels: 10.8 us -> 7.8 us  [attend_back(): pl.pallas_call(functools.partial(bwd_kernel, parts, len(after)), grid_spe...]
    pallas_call x2, Pallas kernels: 5.28 us -> 2.36 us  [add(): pl.pallas_call(functools.partial(add_kernel, len(values)), in_specs=[pl.B...]
  transfers between devices with their start and end apart: 35 -> 35, of which waited for: 14 -> 18; matrix products, arithmetic and copies ran while one was open for 1% -> 1% of each run, Pallas kernels for 27% -> 18%
where the time goes in v5:
time: 195 us; the launch traced here: 194 us
  starting transfers between devices  57.2 us (29%)
  waiting for transfers between devices  56.3 us (29%)
  Pallas kernels  44.6 us (23%)
  blocking collectives  25.5 us (13%)
  local copies, waits for them, and re-layouts  7.29 us (4%)
  other arithmetic  1.96 us (1%)
    ppermute x18, starting transfers between devices, partner(): return lax.ppermute(value, self.tp, table)  21.5 us
    ppermute x18, waiting for transfers between devices, partner(): return lax.ppermute(value, self.tp, table)  19.9 us
    all_gather x1, blocking collectives, local(): o_all = lax.all_gather(mixed, plan.tp, axis=0, tiled=False)  13.5 us
    all_to_all x1, waiting for transfers between devices, local(): shard = lax.all_to_all(shard, 'sz', 0, 0, tiled=True)  12.3 us
    all_gather x1, blocking collectives, local(): x_all = lax.all_gather(x_mine, plan.tp, axis=0, tiled=True)  12 us
    ppermute x4, starting transfers between devices, move(): return lax.ppermute(value, ALL, table)  11.7 us
    ppermute x4, waiting for transfers between devices, move(): return lax.ppermute(value, ALL, table)  9.27 us
    pallas_call x1, Pallas kernels, mlp(): pl.pallas_call(functools.partial(mlp_kernel, plan), grid_spec=pltpu.Prefe...  7.86 us
  transfers between devices with their start and end apart: 35, of which 18 were waited for; matrix products, arithmetic and copies ran while one was open for 1% of the time, Pallas kernels for 18%

profile of v5, /device:TPU:2, one launch (start us, length us, event | category | flops | bytes accessed | tf_op | source)
XLA Modules:
  0.0 194.1 jit_solution(15506310071104339792)
XLA Ops:
  2.5 4.5 %collective-permute-start.3 = (bf16[136,768]{1,0:T(8,128)(2,1)S(1)}, bf16[136,768]{1,0:T(8,128)(2,1)S(1)}, u32[]{:S(2)}, u32[]{:S(2)}) collective-permute-start(bf16[136,768]{1,0:T(8,128)(2,1)S(1)} %pad_maximum_fusion.1), channel_id=1, source_target_pairs={{0,0},{1,1},{2,16},{3,17},{4,8},{5,9},{6,24},{7,25},{8,2},{9,3},{1... | collective-permute-start | bytes 626696 | tf_op jit(solution)/shard_map/ppermute | solution.py:93
  8.9 4.2 %all-to-all-start = ((bf16[4,24,2176]{2,1,0:T(8,128)(2,1)}), bf16[4,24,2176]{2,1,0:T(8,128)(2,1)S(1)}, u32[]{:S(2)}, u32[]{:S(2)}) async-start(bf16[4,24,2176]{2,1,0:T(8,128)(2,1)} %prepare.1), calls=%async_computation | async-start | bytes 835584 | tf_op jit(solution)/shard_map/all_to_all | solution.py:1057
  15.2 5.5 %all-to-all-done.got_ref = bf16[4,24,2176]{2,1,0:T(8,128)(2,1)S(1)} async-done(((bf16[4,24,2176]{2,1,0:T(8,128)(2,1)}), bf16[4,24,2176]{2,1,0:T(8,128)(2,1)S(1)}, u32[]{:S(2)}, u32[]{:S(2)}) %all-to-all-start) | async-done | bytes 417824 | tf_op jit(solution)/shard_map/all_to_all | solution.py:1057
  22.7 3.7 %collective-permute-start.1 = (bf16[96,640]{1,0:T(8,128)(2,1)S(1)}, bf16[96,640]{1,0:T(8,128)(2,1)S(1)}, u32[]{:S(2)}, u32[]{:S(2)}) collective-permute-start(bf16[96,640]{1,0:T(8,128)(2,1)S(1)} %get-tuple-element.120), channel_id=1, source_target_pairs={{0,4},{2,6},{4,0},{6,2},{1,5},{3,7},{5,1},{7,3},{8,12},{10,14},{12... | collective-permute-start | bytes 368648 | tf_op jit(solution)/shard_map/ppermute | solution.py:71
  26.4 12.0 %all_gather.9.x_ref = bf16[512,768]{1,0:T(8,128)(2,1)S(1)} all-gather(bf16[128,768]{1,0:T(8,128)(2,1)S(1)} %slice.9.x_ref), channel_id=1, replica_groups=mesh['gx'=2,'c'=2,'sz'=4,'sy'=2] {'gx','sy'}, dimensions={0}, use_global_device_ids=true | all-gather | bytes 983040 | tf_op jit(solution)/shard_map/all_gather | solution.py:1062
  38.4 4.4 %all-to-all-start.1 = ((bf16[4,296,768]{2,1,0:T(8,128)(2,1)}), bf16[4,296,768]{2,1,0:T(8,128)(2,1)}, u32[]{:S(2)}, u32[]{:S(2)}) async-start(bf16[4,296,768]{2,1,0:T(8,128)(2,1)} %get-tuple-element.125), calls=%async_computation.1 | async-start | bytes 3637248 | tf_op jit(solution)/shard_map/all_to_all | solution.py:1065
  44.9 2.3 %qkv.1 = (bf16[512,768]{1,0:T(8,128)(2,1)S(1)}, bf16[512,192]{1,0:T(8,128)(2,1)S(1)}, bf16[2,512,192]{2,1,0:T(8,128)(2,1)S(1)}, bf16[768,640]{1,0:T(8,128)(2,1)S(1)}, f32[8,768]{1,0:T(8,128)S(1)}) custom-call(s32[4]{0:T(128)S(1)} %pad_add_fusion.idx_ref, bf16[512,768]{1,0:T(8,128)(2,1)S(1)} %all_gather.9.x_ref, ...), custom_call_target="tpu_custom_call" | custom-call | bytes 17712000 | tf_op jit(solution)/shard_map/qkv/pallas_call | solution.py:289
  52.6 5.1 %attend.1 = (bf16[512,192]{1,0:T(8,128)(2,1)S(1)}, f32[8,512]{1,0:T(8,128)S(1)}) custom-call(s32[4]{0:T(128)S(1)} %pad_add_fusion.idx_ref, f32[1,1024]{1,0:T(1,128)S(1)} %slice_convert_fusion.ids_ref, bf16[512,192]{1,0:T(8,128)(2,1)S(1)} %get-tuple-element.124.q_ref, bf16[2,512,192]{2,1,0:T(8,128)(2,1)S(1)} %get-tuple-element.126.refs_0_.refs_5_, ...), custom_call_target="tpu_custom_call" | custom-call | bytes 26199000 | tf_op jit(solution)/shard_map/attend/pallas_call | solution.py:360
  57.8 13.5 %all-gather = bf16[2048,192]{1,0:T(8,128)(2,1)S(1)} all-gather(bf16[512,192]{1,0:T(8,128)(2,1)S(1)} %get-tuple-element.127), channel_id=2, replica_groups=mesh['gx'=2,'c'=2,'sz'=4,'sy'=2] {'gx','sy'}, dimensions={0}, use_global_device_ids=true | all-gather | bytes 983040 | tf_op jit(solution)/shard_map/all_gather | solution.py:1096
  71.3 12.3 %all-to-all-done.1.refs_4_ = bf16[4,296,768]{2,1,0:T(8,128)(2,1)} async-done(((bf16[4,296,768]{2,1,0:T(8,128)(2,1)}), bf16[4,296,768]{2,1,0:T(8,128)(2,1)}, u32[]{:S(2)}, u32[]{:S(2)}) %all-to-all-start.1) | async-done | bytes 1818656 | tf_op jit(solution)/shard_map/all_to_all | solution.py:1065
  83.6 4.0 %collective-permute-done.10.refs_5_ = bf16[4,296,768]{2,1,0:T(8,128)(2,1)S(1)} collective-permute-done((bf16[4,296,768]{2,1,0:T(8,128)(2,1)}, bf16[4,296,768]{2,1,0:T(8,128)(2,1)S(1)}, u32[]{:S(2)}, u32[]{:S(2)}) %collective-permute-start.10) | collective-permute-done | bytes 1818656 | tf_op jit(solution)/shard_map/ppermute | solution.py:52
  87.6 7.9 %mlp.1 = (f32[128,768]{1,0:T(8,128)S(1)}, bf16[512,768]{1,0:T(8,128)(2,1)S(1)}, bf16[512,768]{1,0:T(8,128)(2,1)S(1)}, bf16[512,768]{1,0:T(8,128)(2,1)S(1)}, bf16...) custom-call(s32[4]{0:T(128)S(1)} %pad_add_fusion.idx_ref, ...), custom_call_target="tpu_custom_call" | custom-call | bytes 38745000 | tf_op jit(solution)/shard_map/mlp/pallas_call | solution.py:620
  99.0 4.1 %mlp_weight_grads.1 = (bf16[4,200,768]{2,1,0:T(8,128)(2,1)S(1)}, bf16[4,200,768]{2,1,0:T(8,128)(2,1)S(1)}, bf16[128,768]{1,0:T(8,128)(2,1)S(1)}, bf16[128,768]{1...) custom-call(s32[4]{0:T(128)S(1)} %pad_add_fusion.idx_ref, ...), custom_call_target="tpu_custom_call" | custom-call | bytes 28044000 | tf_op jit(solution)/shard_map/mlp_weight_grads/pallas_call | solution.py:706
  104.3 3.6 %collective-permute-done.13.refs_3_ = bf16[128,768]{1,0:T(8,128)(2,1)S(1)} collective-permute-done((bf16[128,768]{1,0:T(8,128)(2,1)S(1)}, bf16[128,768]{1,0:T(8,128)(2,1)S(1)}, u32[]{:S(2)}, u32[]{:S(2)}) %collective-permute-start.13) | collective-permute-done | bytes 196640 | tf_op jit(solution)/shard_map/ppermute | solution.py:61
  112.2 3.7 %all-to-all-start.2 = ((bf16[4,200,768]{2,1,0:T(8,128)(2,1)}), bf16[4,200,768]{2,1,0:T(8,128)(2,1)S(1)}, u32[]{:S(2)}, u32[]{:S(2)}) async-start(bf16[4,200,768]{2,1,0:T(8,128)(2,1)} %add.15.refs_4_), calls=%async_computation.2 | async-start | bytes 2457600 | tf_op jit(solution)/shard_map/all_to_all | solution.py:1130
  121.6 3.3 %collective-permute-done.16.refs_3_ = bf16[128,768]{1,0:T(8,128)(2,1)S(1)} collective-permute-done((bf16[128,768]{1,0:T(8,128)(2,1)}, bf16[128,768]{1,0:T(8,128)(2,1)S(1)}, u32[]{:S(2)}, u32[]{:S(2)}) %collective-permute-start.16) | collective-permute-done | bytes 196640 | tf_op jit(solution)/shard_map/ppermute | solution.py:61
  133.2 7.8 %attend_back.1 = (bf16[512,192]{1,0:T(8,128)(2,1)S(1)}, f32[2,512,192]{2,1,0:T(8,128)S(1)}, bf16[4,128,192]{2,1,0:T(8,128)(2,1)S(1)}, bf16[2,512,192]{2,1,0:T(8,128)(2,1)S(1)}) custom-call(s32[4]{0:T(128)S(1)} %pad_add_fusion.idx_ref, f32[1,1024]{1,0:T(1,128)S(1)} %slice_convert_fusion.ids_ref, bf16[512,192]{1,0:T(8,128)(2,1)S(1)} %get-tuple-element.124.q_ref, ...), custom_call_target="tpu_custom_call" | custom-call | bytes 39483000 | tf_op jit(solution)/shard_map/attend_back/pallas_call | solution.py:453
  143.1 4.7 %normed_back.1 = (bf16[128,768]{1,0:T(8,128)(2,1)S(1)}, bf16[128,768]{1,0:T(8,128)(2,1)}, bf16[128,768]{1,0:T(8,128)(2,1)}, bf16[128,768]{1,0:T(8,128)(2,1)}, bf...) custom-call(s32[4]{0:T(128)S(1)} %pad_add_fusion.idx_ref, bf16[512,768]{1,0:T(8,128)(2,1)S(1)} %all_gather.9.x_ref, ...), custom_call_target="tpu_custom_call" | custom-call | bytes 47970000 | tf_op jit(solution)/shard_map/normed_back/pallas_call | solution.py:967
  157.1 3.7 %collective-permute-done.25.refs_3_ = bf16[128,768]{1,0:T(8,128)(2,1)S(1)} collective-permute-done((bf16[128,768]{1,0:T(8,128)(2,1)}, bf16[128,768]{1,0:T(8,128)(2,1)S(1)}, u32[]{:S(2)}, u32[]{:S(2)}) %collective-permute-start.25) | collective-permute-done | bytes 196640 | tf_op jit(solution)/shard_map/ppermute | solution.py:61
  160.8 7.0 %all-to-all-start.3 = ((bf16[16,24,896]{2,1,0:T(8,128)(2,1)}), bf16[16,24,896]{2,1,0:T(8,128)(2,1)S(1)}, u32[]{:S(2)}, u32[]{:S(2)}) async-start(bf16[16,24,896]{2,1,0:T(8,128)(2,1)} %add.16), calls=%async_computation.3 | async-start | bytes 1376256 | tf_op jit(solution)/shard_map/all_to_all | solution.py:1158
  167.8 2.1 %finish_output.1 = bf16[128,768]{1,0:T(8,128)(2,1)} custom-call(f32[128,768]{1,0:T(8,128)} %copy-done.4, f32[8,768]{1,0:T(8,128)} %copy-done.11, bf16[128,768]{1,0:T(8,128)(2,1)} %copy-done.17, bf16[128,768]{1,0:T(8,128)(2,1)} %copy-done.35, bf16[128,768]{1,0:T(8,128)(2,1)} %copy-done.36, bf16[128,768]{1,0:T(8,128)(2,1)} %copy-done.37), custom_call_target="tpu_custom_call" | custom-call | bytes 7749000 | tf_op jit(solution)/shard_map/finish_output/pallas_call | solution.py:845
  169.9 3.4 %collective-permute-start.26 = (bf16[128,768]{1,0:T(8,128)(2,1)}, bf16[128,768]{1,0:T(8,128)(2,1)S(1)}, u32[]{:S(2)}, u32[]{:S(2)}) collective-permute-start(bf16[128,768]{1,0:T(8,128)(2,1)} %finish_output.1), channel_id=1, source_target_pairs={{0,0},{1,1},{16,2},{17,3},{8,4},{9,5},{24,6},{25,7},{2,8},{3,9},{1... | collective-permute-start | bytes 589832 | tf_op jit(solution)/shard_map/ppermute | solution.py:93
  183.8 7.2 %collective-permute-done.26.first_ref = bf16[128,768]{1,0:T(8,128)(2,1)S(1)} collective-permute-done((bf16[128,768]{1,0:T(8,128)(2,1)}, bf16[128,768]{1,0:T(8,128)(2,1)S(1)}, u32[]{:S(2)}, u32[]{:S(2)}) %collective-permute-start.26) | collective-permute-done | bytes 196640 | tf_op jit(solution)/shard_map/ppermute | solution.py:93
  191.0 2.1 %collective-permute-done.27.second_ref = bf16[128,768]{1,0:T(8,128)(2,1)S(1)} collective-permute-done((bf16[128,768]{1,0:T(8,128)(2,1)S(1)}, bf16[128,768]{1,0:T(8,128)(2,1)S(1)}, u32[]{:S(2)}, u32[]{:S(2)}) %collective-permute-start.27) | collective-permute-done | bytes 196640 | tf_op jit(solution)/shard_map/ppermute | solution.py:93
  (154 shorter events, 60.8 us)
Async XLA Ops:
  2.5 23.9 %collective-permute-start.3 = (bf16[136,768]{1,0:T(8,128)(2,1)S(1)}, bf16[136,768]{1,0:T(8,128)(2,1)S(1)}, u32[]{:S(2)}, u32[]{:S(2)}) collective-permute-start(bf16[136,768]{1,0:T(8,128)(2,1)S(1)} %pad_maximum_fusion.1), channel_id=1, source_target_pairs={{0,0},{1,1},{2,16},{3,17},{4,8},{5,9},{6,24},{7,25},{8,2},{9,3},{1... | collective-permute-start | bytes 626696 | tf_op jit(solution)/shard_map/ppermute | solution.py:93
  8.9 11.8 %all-to-all-start = ((bf16[4,24,2176]{2,1,0:T(8,128)(2,1)}), bf16[4,24,2176]{2,1,0:T(8,128)(2,1)S(1)}, u32[]{:S(2)}, u32[]{:S(2)}) async-start(bf16[4,24,2176]{2,1,0:T(8,128)(2,1)} %prepare.1), calls=%async_computation | async-start | bytes 835584 | tf_op jit(solution)/shard_map/all_to_all | solution.py:1057
  13.3 25.1 %collective-permute-start.4 = (bf16[128,768]{1,0:T(8,128)(2,1)S(1)}, bf16[128,768]{1,0:T(8,128)(2,1)S(1)}, u32[]{:S(2)}, u32[]{:S(2)}) collective-permute-start(bf16[128,768]{1,0:T(8,128)(2,1)S(1)} %fusion), channel_id=1, source_target_pairs={{0,0},{1,1},{2,16},{3,17},{4,8},{5,9},{6,24},{7,25},{8,2},{9,3},{1... | collective-permute-start | bytes 589832 | tf_op jit(solution)/shard_map/ppermute | solution.py:93
  22.1 16.3 %collective-permute-start.2 = (bf16[96,640]{1,0:T(8,128)(2,1)S(1)}, bf16[96,640]{1,0:T(8,128)(2,1)S(1)}, u32[]{:S(2)}, u32[]{:S(2)}) collective-permute-start(bf16[96,640]{1,0:T(8,128)(2,1)S(1)} %get-tuple-element.120), channel_id=1, source_target_pairs={{0,2},{2,4},{4,6},{6,0},{1,3},{3,5},{5,7},{7,1},{8,10},{10,12},{12... | collective-permute-start | bytes 368648 | tf_op jit(solution)/shard_map/ppermute | solution.py:71
  22.7 15.7 %collective-permute-start.1 = (bf16[96,640]{1,0:T(8,128)(2,1)S(1)}, bf16[96,640]{1,0:T(8,128)(2,1)S(1)}, u32[]{:S(2)}, u32[]{:S(2)}) collective-permute-start(bf16[96,640]{1,0:T(8,128)(2,1)S(1)} %get-tuple-element.120), channel_id=1, source_target_pairs={{0,4},{2,6},{4,0},{6,2},{1,5},{3,7},{5,1},{7,3},{8,12},{10,14},{12... | collective-permute-start | bytes 368648 | tf_op jit(solution)/shard_map/ppermute | solution.py:71
  26.4 12.0 %collective-permute-start = (bf16[96,640]{1,0:T(8,128)(2,1)S(1)}, bf16[96,640]{1,0:T(8,128)(2,1)S(1)}, u32[]{:S(2)}, u32[]{:S(2)}) collective-permute-start(bf16[96,640]{1,0:T(8,128)(2,1)S(1)} %get-tuple-element.120), channel_id=1, source_target_pairs={{0,6},{2,0},{4,2},{6,4},{1,7},{3,1},{5,3},{7,5},{8,14},{10,8},{12,... | collective-permute-start | bytes 368648 | tf_op jit(solution)/shard_map/ppermute | solution.py:71
  38.4 45.2 %all-to-all-start.1 = ((bf16[4,296,768]{2,1,0:T(8,128)(2,1)}), bf16[4,296,768]{2,1,0:T(8,128)(2,1)}, u32[]{:S(2)}, u32[]{:S(2)}) async-start(bf16[4,296,768]{2,1,0:T(8,128)(2,1)} %get-tuple-element.125), calls=%async_computation.1 | async-start | bytes 3637248 | tf_op jit(solution)/shard_map/all_to_all | solution.py:1065
  49.0 22.3 %collective-permute-start.9 = (bf16[128,768]{1,0:T(8,128)(2,1)S(1)}, bf16[128,768]{1,0:T(8,128)(2,1)S(1)}, u32[]{:S(2)}, u32[]{:S(2)}) collective-permute-start(bf16[128,768]{1,0:T(8,128)(2,1)S(1)} %collective-permute-done.4.refs_0_.dm_ref), channel_id=1, source_target_pairs={{0,17},{1,16},{16,1},{17,0},{2,19},{3,18},{18,3},{19,2},{4,21},{5,... | collective-permute-start | bytes 589832 | tf_op jit(solution)/shard_map/ppermute | solution.py:61
  50.6 20.7 %collective-permute-start.8 = (bf16[128,768]{1,0:T(8,128)(2,1)S(1)}, bf16[128,768]{1,0:T(8,128)(2,1)S(1)}, u32[]{:S(2)}, u32[]{:S(2)}) collective-permute-start(bf16[128,768]{1,0:T(8,128)(2,1)S(1)} %collective-permute-done.4.refs_0_.dm_ref), channel_id=1, source_target_pairs={{0,16},{1,17},{16,0},{17,1},{2,18},{3,19},{18,2},{19,3},{4,20},{5,... | collective-permute-start | bytes 589832 | tf_op jit(solution)/shard_map/ppermute | solution.py:61
  52.3 19.0 %collective-permute-start.7 = (bf16[128,768]{1,0:T(8,128)(2,1)S(1)}, bf16[128,768]{1,0:T(8,128)(2,1)S(1)}, u32[]{:S(2)}, u32[]{:S(2)}) collective-permute-start(bf16[128,768]{1,0:T(8,128)(2,1)S(1)} %collective-permute-done.4.refs_0_.dm_ref), channel_id=1, source_target_pairs={{0,1},{1,0},{16,17},{17,16},{2,3},{3,2},{18,19},{19,18},{4,5},{5,4... | collective-permute-start | bytes 589832 | tf_op jit(solution)/shard_map/ppermute | solution.py:61
  96.5 7.8 %collective-permute-start.12 = (bf16[128,768]{1,0:T(8,128)(2,1)S(1)}, bf16[128,768]{1,0:T(8,128)(2,1)S(1)}, u32[]{:S(2)}, u32[]{:S(2)}) collective-permute-start(bf16[128,768]{1,0:T(8,128)(2,1)S(1)} %get-tuple-element.141), channel_id=1, source_target_pairs={{0,16},{1,17},{16,0},{17,1},{2,18},{3,19},{18,2},{19,3},{4,20},{5,... | collective-permute-start | bytes 589832 | tf_op jit(solution)/shard_map/ppermute | solution.py:61
  97.6 10.3 %collective-permute-start.13 = (bf16[128,768]{1,0:T(8,128)(2,1)S(1)}, bf16[128,768]{1,0:T(8,128)(2,1)S(1)}, u32[]{:S(2)}, u32[]{:S(2)}) collective-permute-start(bf16[128,768]{1,0:T(8,128)(2,1)S(1)} %get-tuple-element.142), channel_id=1, source_target_pairs={{0,17},{1,16},{16,1},{17,0},{2,19},{3,18},{18,3},{19,2},{4,21},{5,... | collective-permute-start | bytes 589832 | tf_op jit(solution)/shard_map/ppermute | solution.py:61
  112.2 40.4 %all-to-all-start.2 = ((bf16[4,200,768]{2,1,0:T(8,128)(2,1)}), bf16[4,200,768]{2,1,0:T(8,128)(2,1)S(1)}, u32[]{:S(2)}, u32[]{:S(2)}) async-start(bf16[4,200,768]{2,1,0:T(8,128)(2,1)} %add.15.refs_4_), calls=%async_computation.2 | async-start | bytes 2457600 | tf_op jit(solution)/shard_map/all_to_all | solution.py:1130
  115.9 9.0 %collective-permute-start.16 = (bf16[128,768]{1,0:T(8,128)(2,1)}, bf16[128,768]{1,0:T(8,128)(2,1)S(1)}, u32[]{:S(2)}, u32[]{:S(2)}) collective-permute-start(bf16[128,768]{1,0:T(8,128)(2,1)} %copy-done.9), channel_id=1, source_target_pairs={{0,17},{1,16},{16,1},{17,0},{2,19},{3,18},{18,3},{19,2},{4,21},{5,... | collective-permute-start | bytes 589832 | tf_op jit(solution)/shard_map/ppermute | solution.py:61
  117.5 11.0 %collective-permute-start.15 = (bf16[128,768]{1,0:T(8,128)(2,1)}, bf16[128,768]{1,0:T(8,128)(2,1)S(1)}, u32[]{:S(2)}, u32[]{:S(2)}) collective-permute-start(bf16[128,768]{1,0:T(8,128)(2,1)} %copy-done.9), channel_id=1, source_target_pairs={{0,16},{1,17},{16,0},{17,1},{2,18},{3,19},{18,2},{19,3},{4,20},{5,... | collective-permute-start | bytes 589832 | tf_op jit(solution)/shard_map/ppermute | solution.py:61
  118.3 10.2 %collective-permute-start.14 = (bf16[128,768]{1,0:T(8,128)(2,1)}, bf16[128,768]{1,0:T(8,128)(2,1)S(1)}, u32[]{:S(2)}, u32[]{:S(2)}) collective-permute-start(bf16[128,768]{1,0:T(8,128)(2,1)} %copy-done.9), channel_id=1, source_target_pairs={{0,1},{1,0},{16,17},{17,16},{2,3},{3,2},{18,19},{19,18},{4,5},{5,4... | collective-permute-start | bytes 589832 | tf_op jit(solution)/shard_map/ppermute | solution.py:61
  119.4 21.6 %collective-permute-start.18 = (bf16[128,768]{1,0:T(8,128)(2,1)}, bf16[128,768]{1,0:T(8,128)(2,1)S(1)}, u32[]{:S(2)}, u32[]{:S(2)}) collective-permute-start(bf16[128,768]{1,0:T(8,128)(2,1)} %copy-done.28), channel_id=1, source_target_pairs={{0,1},{1,0},{16,17},{17,16},{2,3},{3,2},{18,19},{19,18},{4,5},{5,4... | collective-permute-start | bytes 589832 | tf_op jit(solution)/shard_map/ppermute | solution.py:61
  120.4 20.7 %collective-permute-start.19 = (bf16[128,768]{1,0:T(8,128)(2,1)}, bf16[128,768]{1,0:T(8,128)(2,1)S(1)}, u32[]{:S(2)}, u32[]{:S(2)}) collective-permute-start(bf16[128,768]{1,0:T(8,128)(2,1)} %copy-done.27), channel_id=1, source_target_pairs={{0,16},{1,17},{16,0},{17,1},{2,18},{3,19},{18,2},{19,3},{4,20},{5,... | collective-permute-start | bytes 589832 | tf_op jit(solution)/shard_map/ppermute | solution.py:61
  124.9 16.2 %collective-permute-start.20 = (bf16[128,768]{1,0:T(8,128)(2,1)}, bf16[128,768]{1,0:T(8,128)(2,1)S(1)}, u32[]{:S(2)}, u32[]{:S(2)}) collective-permute-start(bf16[128,768]{1,0:T(8,128)(2,1)} %copy-done.26), channel_id=1, source_target_pairs={{0,17},{1,16},{16,1},{17,0},{2,19},{3,18},{18,3},{19,2},{4,21},{5,... | collective-permute-start | bytes 589832 | tf_op jit(solution)/shard_map/ppermute | solution.py:61
  149.1 8.0 %collective-permute-start.24 = (bf16[128,768]{1,0:T(8,128)(2,1)}, bf16[128,768]{1,0:T(8,128)(2,1)S(1)}, u32[]{:S(2)}, u32[]{:S(2)}) collective-permute-start(bf16[128,768]{1,0:T(8,128)(2,1)} %get-tuple-element.181), channel_id=1, source_target_pairs={{0,16},{1,17},{16,0},{17,1},{2,18},{3,19},{18,2},{19,3},{4,20},{5,... | collective-permute-start | bytes 589832 | tf_op jit(solution)/shard_map/ppermute | solution.py:61
  150.1 10.8 %collective-permute-start.25 = (bf16[128,768]{1,0:T(8,128)(2,1)}, bf16[128,768]{1,0:T(8,128)(2,1)S(1)}, u32[]{:S(2)}, u32[]{:S(2)}) collective-permute-start(bf16[128,768]{1,0:T(8,128)(2,1)} %get-tuple-element.182), channel_id=1, source_target_pairs={{0,17},{1,16},{16,1},{17,0},{2,19},{3,18},{18,3},{19,2},{4,21},{5,... | collective-permute-start | bytes 589832 | tf_op jit(solution)/shard_map/ppermute | solution.py:61
  160.8 32.3 %all-to-all-start.3 = ((bf16[16,24,896]{2,1,0:T(8,128)(2,1)}), bf16[16,24,896]{2,1,0:T(8,128)(2,1)S(1)}, u32[]{:S(2)}, u32[]{:S(2)}) async-start(bf16[16,24,896]{2,1,0:T(8,128)(2,1)} %add.16), calls=%async_computation.3 | async-start | bytes 1376256 | tf_op jit(solution)/shard_map/all_to_all | solution.py:1158
  169.9 21.1 %collective-permute-start.26 = (bf16[128,768]{1,0:T(8,128)(2,1)}, bf16[128,768]{1,0:T(8,128)(2,1)S(1)}, u32[]{:S(2)}, u32[]{:S(2)}) collective-permute-start(bf16[128,768]{1,0:T(8,128)(2,1)} %finish_output.1), channel_id=1, source_target_pairs={{0,0},{1,1},{16,2},{17,3},{8,4},{9,5},{24,6},{25,7},{2,8},{3,9},{1... | collective-permute-start | bytes 589832 | tf_op jit(solution)/shard_map/ppermute | solution.py:93
  173.7 19.3 %collective-permute-start.27 = (bf16[128,768]{1,0:T(8,128)(2,1)S(1)}, bf16[128,768]{1,0:T(8,128)(2,1)S(1)}, u32[]{:S(2)}, u32[]{:S(2)}) collective-permute-start(bf16[128,768]{1,0:T(8,128)(2,1)S(1)} %finish_input.1), channel_id=1, source_target_pairs={{0,0},{1,1},{16,2},{17,3},{8,4},{9,5},{24,6},{25,7},{2,8},{3,9},{1... | collective-permute-start | bytes 589832 | tf_op jit(solution)/shard_map/ppermute | solution.py:93
  (50 other events, 474.1 us)

commit v6 on v5

--- a/solution.py
+++ b/solution.py
@@ -132,7 +132,9 @@
 
 def takes(microseconds):
     return pl.CostEstimate(
-        flops=0, bytes_accessed=int(microseconds * 3.69e6), transcendentals=0
+        flops=int(microseconds * 0.2 * 1.15e9),
+        bytes_accessed=int(microseconds * 3.69e6),
+        transcendentals=0,
     )
 
 
@@ -798,7 +800,7 @@
         out_shape=jax.ShapeDtypeStruct((block, hidden), f32),
         scratch_shapes=[pltpu.VMEM((TP, block, width), f32)],
         compiler_params=small_params(),
-        cost_estimate=takes(1.7),
+        cost_estimate=takes(40),
         name="join_up",
     )(idx, *parts)
 
@@ -864,7 +866,7 @@
         input_kernel,
         out_shape=jax.ShapeDtypeStruct(x.shape, bf16),
         compiler_params=small_params(),
-        cost_estimate=takes(2.4),
+        cost_estimate=takes(40),
         name="finish_input",
     )(x, dr, vecs, *parts)
 
@@ -1057,11 +1059,10 @@
         got = lax.all_to_all(chunk, plan.tp, 0, 0, tiled=True)
         moved = plan.move(packed, plan.route)
         proj, shard = shards_of(got, w_down, b_up[None], 3 * cols + SMALLS, lines)
-        moved, shard = lax.optimization_barrier((moved, shard))
+        projs = [proj] + [plan.turn(proj, "sz", -j) for j in range(1, lines)]
+        projs, moved, shard, dm_mine = lax.optimization_barrier((projs, moved, shard, dm_mine))
         x_mine = moved[:rows]
         x_all = lax.all_gather(x_mine, plan.tp, axis=0, tiled=True)
-        projs = [proj] + [plan.turn(proj, "sz", -j) for j in range(1, lines)]
-        projs, x_all, shard, dm_mine = lax.optimization_barrier((projs, x_all, shard, dm_mine))
         shard = lax.all_to_all(shard, "sz", 0, 0, tiled=True)
         projs = jnp.stack(projs)
         low_one, query, kv, w_qkv, vecs = qkv(plan, idx, x_all, projs, plan.swap(projs))
@@ -1091,10 +1092,11 @@
     ids = moved[rows:].reshape(1, -1)[:, :length].astype(f32)
 
     parts = plan.parts
+    kv, dm_late = lax.optimization_barrier((kv, dm_mine))
     kvs = [kv] + [plan.turn(kv, plan.half, -j) for j in range(1, parts)]
     mixed, lse = attend(idx, ids, query, kvs)
     o_all = lax.all_gather(mixed, plan.tp, axis=0, tiled=False)
-    dms = plan.partners(dm_mine)
+    dms = plan.partners(dm_late)
     if fast:
         shard, o_all, dms = lax.optimization_barrier((shard, o_all, dms))
         weights = [shard, plan.swap(shard)]
@@ -1150,11 +1152,10 @@
         plan, idx, x_all, grad_query, kv_own, recvs, w_qkv, low_one, o_all, da_cols, sum_own, sum_two
     )
     back_one, terms = plan.reduce(results[:TP]), results[TP:]
-    output = plan.move(finish_output(out_parts, r_own, vecs), plan.back)
     if fast:
         keep, send = terms
         terms = add(keep, plan.swap(send))
-        terms, ups, back_one = lax.optimization_barrier((terms, ups, back_one))
+        terms, ups = lax.optimization_barrier((terms, ups))
         got = lax.all_to_all(terms, SAME, 0, 0, tiled=True)
     else:
         terms = plan.shuffle(terms[0].reshape(plan.devices, block, -1), ALL, ("c",) + SAME)
@@ -1168,6 +1169,8 @@
         ups = ups.reshape(TP, block, plan.copies, slab).transpose(0, 2, 1, 3)
         ups = plan.shuffle(ups.reshape(plan.devices, block, slab), plan.tp + plan.rep, ALL)
         g_w_up = ups.transpose(1, 0, 2).reshape(block, hidden)
+    g_w_down, out_parts = lax.optimization_barrier((g_w_down, out_parts))
+    output = plan.move(finish_output(out_parts, r_own, vecs), plan.back)
     grad_input = plan.move(finish_input(back_one, x_mine, dr, vecs), plan.back)
     joined = join_grads(plan, got, output, grad_input, cols, w_qkv.shape[1])
     g_query, g_key, g_value, g_out, *vec, output, grad_input = joined

time: 195 us -> 185 us (0.949); the launches traced: 194 us -> 182 us
  waiting for transfers between devices: 56.3 us -> 40.4 us
  local copies, waits for them, and re-layouts: 7.29 us -> 11.6 us
    ppermute x18, waiting for transfers between devices: 19.9 us -> 5.85 us  [partner(): return lax.ppermute(value, self.tp, table)]
    all_to_all x1, waiting for transfers between devices: 12.3 us -> 2.36 us  [local(): shard = lax.all_to_all(shard, 'sz', 0, 0, tiled=True)]
    ppermute x5, waiting for transfers between devices: 1.91 us -> 10.2 us  [turn(): lax.ppermute(value, axis, [(i, (i + by) % count) for i in range(count)])]
    unnamed x80 -> x70, local copies, waits for them, and re-layouts: 7.23 us -> 11.6 us
    ppermute x4, waiting for transfers between devices: 7.43 us -> 3.77 us  [swap(): return lax.ppermute(value, 'c', [(0, 1), (1, 0)])]
    ppermute x4, waiting for transfers between devices: 9.27 us -> 12.7 us  [move(): return lax.ppermute(value, ALL, table)]
  transfers between devices with their start and end apart: 35 -> 35, of which waited for: 18 -> 12; matrix products, arithmetic and copies ran while one was open for 1% -> 1% of each run, Pallas kernels for 18% -> 20%
where the time goes in v6:
time: 185 us; the launch traced here: 182 us
  starting transfers between devices  57.1 us (31%)
  Pallas kernels  44.2 us (24%)
  waiting for transfers between devices  40.4 us (22%)
  blocking collectives  25.6 us (14%)
  local copies, waits for them, and re-layouts  11.6 us (6%)
  other arithmetic  1.91 us (1%)
    ppermute x18, starting transfers between devices, partner(): return lax.ppermute(value, self.tp, table)  21.2 us
    all_gather x1, blocking collectives, local(): o_all = lax.all_gather(mixed, plan.tp, axis=0, tiled=False)  12.8 us
    all_gather x1, blocking collectives, local(): x_all = lax.all_gather(x_mine, plan.tp, axis=0, tiled=True)  12.8 us
    ppermute x4, waiting for transfers between devices, move(): return lax.ppermute(value, ALL, table)  12.7 us
    unnamed x70, local copies, waits for them, and re-layouts  11.6 us
    ppermute x4, starting transfers between devices, move(): return lax.ppermute(value, ALL, table)  11.5 us
    ppermute x5, waiting for transfers between devices, turn(): lax.ppermute(value, axis, [(i, (i + by) % count) for i in range(count)])  10.2 us
    pallas_call x1, Pallas kernels, attend_back(): pl.pallas_call(functools.partial(bwd_kernel, parts, len(after)), grid_spe...  9 us
  transfers between devices with their start and end apart: 35, of which 12 were waited for; matrix products, arithmetic and copies ran while one was open for 1% of the time, Pallas kernels for 20%

profile of v6, /device:TPU:2, one launch (start us, length us, event | category | flops | bytes accessed | tf_op | source)
XLA Modules:
  0.0 182.1 jit_solution(11350875882276998680)
XLA Ops:
  2.4 4.5 %collective-permute-start.3 = (bf16[136,768]{1,0:T(8,128)(2,1)S(1)}, bf16[136,768]{1,0:T(8,128)(2,1)S(1)}, u32[]{:S(2)}, u32[]{:S(2)}) collective-permute-start(bf16[136,768]{1,0:T(8,128)(2,1)S(1)} %pad_maximum_fusion.1), channel_id=1, source_target_pairs={{0,0},{1,1},{2,16},{3,17},{4,8},{5,9},{6,24},{7,25},{8,2},{9,3},{1... | collective-permute-start | bytes 626696 | tf_op jit(solution)/shard_map/ppermute | solution.py:93
  8.9 4.2 %all-to-all-start = ((bf16[4,24,2176]{2,1,0:T(8,128)(2,1)}), bf16[4,24,2176]{2,1,0:T(8,128)(2,1)S(1)}, u32[]{:S(2)}, u32[]{:S(2)}) async-start(bf16[4,24,2176]{2,1,0:T(8,128)(2,1)} %prepare.1), calls=%async_computation | async-start | bytes 835584 | tf_op jit(solution)/shard_map/all_to_all | solution.py:1059
  15.2 5.5 %all-to-all-done.got_ref = bf16[4,24,2176]{2,1,0:T(8,128)(2,1)S(1)} async-done(((bf16[4,24,2176]{2,1,0:T(8,128)(2,1)}), bf16[4,24,2176]{2,1,0:T(8,128)(2,1)S(1)}, u32[]{:S(2)}, u32[]{:S(2)}) %all-to-all-start) | async-done | bytes 417824 | tf_op jit(solution)/shard_map/all_to_all | solution.py:1059
  22.7 3.7 %collective-permute-start.1 = (bf16[96,640]{1,0:T(8,128)(2,1)S(1)}, bf16[96,640]{1,0:T(8,128)(2,1)S(1)}, u32[]{:S(2)}, u32[]{:S(2)}) collective-permute-start(bf16[96,640]{1,0:T(8,128)(2,1)S(1)} %get-tuple-element.119), channel_id=1, source_target_pairs={{0,4},{2,6},{4,0},{6,2},{1,5},{3,7},{5,1},{7,3},{8,12},{10,14},{12... | collective-permute-start | bytes 368648 | tf_op jit(solution)/shard_map/ppermute | solution.py:71
  26.4 3.8 %collective-permute-done.2 = bf16[96,640]{1,0:T(8,128)(2,1)S(1)} collective-permute-done((bf16[96,640]{1,0:T(8,128)(2,1)S(1)}, bf16[96,640]{1,0:T(8,128)(2,1)S(1)}, u32[]{:S(2)}, u32[]{:S(2)}) %collective-permute-start.2) | collective-permute-done | bytes 122912 | tf_op jit(solution)/shard_map/ppermute | solution.py:71
  30.1 4.5 %collective-permute-done.1 = bf16[96,640]{1,0:T(8,128)(2,1)S(1)} collective-permute-done((bf16[96,640]{1,0:T(8,128)(2,1)S(1)}, bf16[96,640]{1,0:T(8,128)(2,1)S(1)}, u32[]{:S(2)}, u32[]{:S(2)}) %collective-permute-start.1) | collective-permute-done | bytes 122912 | tf_op jit(solution)/shard_map/ppermute | solution.py:71
  34.6 5.5 %all-to-all-start.1 = ((bf16[4,296,768]{2,1,0:T(8,128)(2,1)}), bf16[4,296,768]{2,1,0:T(8,128)(2,1)S(1)}, u32[]{:S(2)}, u32[]{:S(2)}) async-start(bf16[4,296,768]{2,1,0:T(8,128)(2,1)} %get-tuple-element.124), calls=%async_computation.1 | async-start | bytes 3637248 | tf_op jit(solution)/shard_map/all_to_all | solution.py:1066
  40.4 12.8 %all_gather.9.x_ref = bf16[512,768]{1,0:T(8,128)(2,1)S(1)} all-gather(bf16[128,768]{1,0:T(8,128)(2,1)S(1)} %slice.9.x_ref), channel_id=1, replica_groups=mesh['gx'=2,'c'=2,'sz'=4,'sy'=2] {'gx','sy'}, dimensions={0}, use_global_device_ids=true | all-gather | bytes 983040 | tf_op jit(solution)/shard_map/all_gather | solution.py:1065
  53.2 2.3 %qkv.1 = (bf16[512,768]{1,0:T(8,128)(2,1)S(1)}, bf16[512,192]{1,0:T(8,128)(2,1)S(1)}, bf16[2,512,192]{2,1,0:T(8,128)(2,1)S(1)}, bf16[768,640]{1,0:T(8,128)(2,1)S(1)}, f32[8,768]{1,0:T(8,128)S(1)}) custom-call(s32[4]{0:T(128)S(1)} %pad_add_fusion.idx_ref, bf16[512,768]{1,0:T(8,128)(2,1)S(1)} %all_gather.9.x_ref, ...), custom_call_target="tpu_custom_call" | custom-call | flops 1104000000 | bytes 17712000 | tf_op jit(solution)/shard_map/qkv/pallas_call | solution.py:291
  61.0 5.1 %attend.1 = (bf16[512,192]{1,0:T(8,128)(2,1)S(1)}, f32[8,512]{1,0:T(8,128)S(1)}) custom-call(s32[4]{0:T(128)S(1)} %pad_add_fusion.idx_ref, f32[1,1024]{1,0:T(1,128)S(1)} %slice_convert_fusion.ids_ref, bf16[512,192]{1,0:T(8,128)(2,1)S(1)} %get-tuple-element.123.q_ref, bf16[2,512,192]{2,1,0:T(8,128)(2,1)S(1)} %get-tuple-element.127.refs_0_.refs_5_, ...), custom_call_target="tpu_custom_call" | custom-call | flops 1632999936 | bytes 26199000 | tf_op jit(solution)/shard_map/attend/pallas_call | solution.py:362
  66.2 12.8 %all-gather = bf16[2048,192]{1,0:T(8,128)(2,1)S(1)} all-gather(bf16[512,192]{1,0:T(8,128)(2,1)S(1)} %get-tuple-element.128), channel_id=2, replica_groups=mesh['gx'=2,'c'=2,'sz'=4,'sy'=2] {'gx','sy'}, dimensions={0}, use_global_device_ids=true | all-gather | bytes 983040 | tf_op jit(solution)/shard_map/all_gather | solution.py:1098
  80.3 2.4 %all-to-all-done.1.refs_4_ = bf16[4,296,768]{2,1,0:T(8,128)(2,1)S(1)} async-done(((bf16[4,296,768]{2,1,0:T(8,128)(2,1)}), bf16[4,296,768]{2,1,0:T(8,128)(2,1)S(1)}, u32[]{:S(2)}, u32[]{:S(2)}) %all-to-all-start.1) | async-done | bytes 1818656 | tf_op jit(solution)/shard_map/all_to_all | solution.py:1066
  82.7 3.8 %collective-permute-done.10.refs_5_ = bf16[4,296,768]{2,1,0:T(8,128)(2,1)S(1)} collective-permute-done((bf16[4,296,768]{2,1,0:T(8,128)(2,1)S(1)}, bf16[4,296,768]{2,1,0:T(8,128)(2,1)S(1)}, u32[]{:S(2)}, u32[]{:S(2)}) %collective-permute-start.10) | collective-permute-done | bytes 1818656 | tf_op jit(solution)/shard_map/ppermute | solution.py:52
  89.5 6.4 %mlp.1 = (f32[128,768]{1,0:T(8,128)S(1)}, bf16[512,768]{1,0:T(8,128)(2,1)S(1)}, bf16[512,768]{1,0:T(8,128)(2,1)S(1)}, bf16[512,768]{1,0:T(8,128)(2,1)S(1)}, bf16...) custom-call(s32[4]{0:T(128)S(1)} %pad_add_fusion.idx_ref, ...), custom_call_target="tpu_custom_call" | custom-call | flops 2415000064 | bytes 38745000 | tf_op jit(solution)/shard_map/mlp/pallas_call | solution.py:622
  99.5 4.1 %mlp_weight_grads.1 = (bf16[4,200,768]{2,1,0:T(8,128)(2,1)S(1)}, bf16[4,200,768]{2,1,0:T(8,128)(2,1)S(1)}, bf16[128,768]{1,0:T(8,128)(2,1)S(1)}, bf16[128,768]{1...) custom-call(s32[4]{0:T(128)S(1)} %pad_add_fusion.idx_ref, ...), custom_call_target="tpu_custom_call" | custom-call | flops 1748000000 | bytes 28044000 | tf_op jit(solution)/shard_map/mlp_weight_grads/pallas_call | solution.py:708
  105.3 3.0 %collective-permute-done.13.refs_3_ = bf16[128,768]{1,0:T(8,128)(2,1)S(1)} collective-permute-done((bf16[128,768]{1,0:T(8,128)(2,1)S(1)}, bf16[128,768]{1,0:T(8,128)(2,1)S(1)}, u32[]{:S(2)}, u32[]{:S(2)}) %collective-permute-start.13) | collective-permute-done | bytes 196640 | tf_op jit(solution)/shard_map/ppermute | solution.py:61
  114.4 3.7 %all-to-all-start.2 = ((bf16[4,200,768]{2,1,0:T(8,128)(2,1)}), bf16[4,200,768]{2,1,0:T(8,128)(2,1)S(1)}, u32[]{:S(2)}, u32[]{:S(2)}) async-start(bf16[4,200,768]{2,1,0:T(8,128)(2,1)} %add.15.refs_4_), calls=%async_computation.2 | async-start | bytes 2457600 | tf_op jit(solution)/shard_map/all_to_all | solution.py:1132
  126.6 9.0 %attend_back.1 = (bf16[512,192]{1,0:T(8,128)(2,1)S(1)}, f32[2,512,192]{2,1,0:T(8,128)S(1)}, bf16[4,128,192]{2,1,0:T(8,128)(2,1)S(1)}, bf16[2,512,192]{2,1,0:T(8,128)(2,1)S(1)}) custom-call(s32[4]{0:T(128)S(1)} %pad_add_fusion.idx_ref, f32[1,1024]{1,0:T(1,128)S(1)} %slice_convert_fusion.ids_ref, bf16[512,192]{1,0:T(8,128)(2,1)S(1)} %copy-done.23, ...), custom_call_target="tpu_custom_call" | custom-call | flops 2460999936 | bytes 39483000 | tf_op jit(solution)/shard_map/attend_back/pallas_call | solution.py:455
  137.7 4.6 %normed_back.1 = (bf16[128,768]{1,0:T(8,128)(2,1)S(1)}, bf16[128,768]{1,0:T(8,128)(2,1)}, bf16[128,768]{1,0:T(8,128)(2,1)S(1)}, bf16[128,768]{1,0:T(8,128)(2,1)S...) custom-call(s32[4]{0:T(128)S(1)} %pad_add_fusion.idx_ref, bf16[512,768]{1,0:T(8,128)(2,1)S(1)} %copy-done.2, ...), custom_call_target="tpu_custom_call" | custom-call | flops 2990000128 | bytes 47970000 | tf_op jit(solution)/shard_map/normed_back/pallas_call | solution.py:969
  149.1 6.3 %all-to-all-start.3 = ((bf16[16,24,896]{2,1,0:T(8,128)(2,1)}), bf16[16,24,896]{2,1,0:T(8,128)(2,1)S(1)}, u32[]{:S(2)}, u32[]{:S(2)}) async-start(bf16[16,24,896]{2,1,0:T(8,128)(2,1)} %add.16), calls=%async_computation.3 | async-start | bytes 1376256 | tf_op jit(solution)/shard_map/all_to_all | solution.py:1159
  156.1 3.2 %collective-permute-start.27 = (bf16[128,768]{1,0:T(8,128)(2,1)S(1)}, bf16[128,768]{1,0:T(8,128)(2,1)S(1)}, u32[]{:S(2)}, u32[]{:S(2)}) collective-permute-start(bf16[128,768]{1,0:T(8,128)(2,1)S(1)} %finish_input.1), channel_id=1, source_target_pairs={{0,0},{1,1},{16,2},{17,3},{8,4},{9,5},{24,6},{25,7},{2,8},{3,9},{1... | collective-permute-start | bytes 589832 | tf_op jit(solution)/shard_map/ppermute | solution.py:93
  162.9 2.1 %finish_output.1 = bf16[128,768]{1,0:T(8,128)(2,1)} custom-call(f32[128,768]{1,0:T(8,128)} %copy-done.13, f32[8,768]{1,0:T(8,128)} %copy-done.19, bf16[128,768]{1,0:T(8,128)(2,1)} %copy-done.14, bf16[128,768]{1,0:T(8,128)(2,1)} %copy-done.30, bf16[128,768]{1,0:T(8,128)(2,1)} %copy-done.31, bf16[128,768]{1,0:T(8,128)(2,1)} %copy-done.32), custom_call_target="tpu_custom_call" | custom-call | flops 483000000 | bytes 7749000 | tf_op jit(solution)/shard_map/finish_output/pallas_call | solution.py:847
  168.4 10.6 %collective-permute-done.27.second_ref = bf16[128,768]{1,0:T(8,128)(2,1)S(1)} collective-permute-done((bf16[128,768]{1,0:T(8,128)(2,1)S(1)}, bf16[128,768]{1,0:T(8,128)(2,1)S(1)}, u32[]{:S(2)}, u32[]{:S(2)}) %collective-permute-start.27) | collective-permute-done | bytes 196640 | tf_op jit(solution)/shard_map/ppermute | solution.py:93
  179.0 2.1 %collective-permute-done.23.first_ref = bf16[128,768]{1,0:T(8,128)(2,1)S(1)} collective-permute-done((bf16[128,768]{1,0:T(8,128)(2,1)}, bf16[128,768]{1,0:T(8,128)(2,1)S(1)}, u32[]{:S(2)}, u32[]{:S(2)}) %collective-permute-start.23) | collective-permute-done | bytes 196640 | tf_op jit(solution)/shard_map/ppermute | solution.py:93
  (144 shorter events, 54.8 us)
Async XLA Ops:
  2.4 24.0 %collective-permute-start.3 = (bf16[136,768]{1,0:T(8,128)(2,1)S(1)}, bf16[136,768]{1,0:T(8,128)(2,1)S(1)}, u32[]{:S(2)}, u32[]{:S(2)}) collective-permute-start(bf16[136,768]{1,0:T(8,128)(2,1)S(1)} %pad_maximum_fusion.1), channel_id=1, source_target_pairs={{0,0},{1,1},{2,16},{3,17},{4,8},{5,9},{6,24},{7,25},{8,2},{9,3},{1... | collective-permute-start | bytes 626696 | tf_op jit(solution)/shard_map/ppermute | solution.py:93
  8.9 11.8 %all-to-all-start = ((bf16[4,24,2176]{2,1,0:T(8,128)(2,1)}), bf16[4,24,2176]{2,1,0:T(8,128)(2,1)S(1)}, u32[]{:S(2)}, u32[]{:S(2)}) async-start(bf16[4,24,2176]{2,1,0:T(8,128)(2,1)} %prepare.1), calls=%async_computation | async-start | bytes 835584 | tf_op jit(solution)/shard_map/all_to_all | solution.py:1059
  13.2 13.1 %collective-permute-start.4 = (bf16[128,768]{1,0:T(8,128)(2,1)S(1)}, bf16[128,768]{1,0:T(8,128)(2,1)S(1)}, u32[]{:S(2)}, u32[]{:S(2)}) collective-permute-start(bf16[128,768]{1,0:T(8,128)(2,1)S(1)} %fusion), channel_id=1, source_target_pairs={{0,0},{1,1},{2,16},{3,17},{4,8},{5,9},{6,24},{7,25},{8,2},{9,3},{1... | collective-permute-start | bytes 589832 | tf_op jit(solution)/shard_map/ppermute | solution.py:93
  22.7 12.0 %collective-permute-start.1 = (bf16[96,640]{1,0:T(8,128)(2,1)S(1)}, bf16[96,640]{1,0:T(8,128)(2,1)S(1)}, u32[]{:S(2)}, u32[]{:S(2)}) collective-permute-start(bf16[96,640]{1,0:T(8,128)(2,1)S(1)} %get-tuple-element.119), channel_id=1, source_target_pairs={{0,4},{2,6},{4,0},{6,2},{1,5},{3,7},{5,1},{7,3},{8,12},{10,14},{12... | collective-permute-start | bytes 368648 | tf_op jit(solution)/shard_map/ppermute | solution.py:71
  26.3 8.3 %collective-permute-start = (bf16[96,640]{1,0:T(8,128)(2,1)S(1)}, bf16[96,640]{1,0:T(8,128)(2,1)S(1)}, u32[]{:S(2)}, u32[]{:S(2)}) collective-permute-start(bf16[96,640]{1,0:T(8,128)(2,1)S(1)} %get-tuple-element.119), channel_id=1, source_target_pairs={{0,6},{2,0},{4,2},{6,4},{1,7},{3,1},{5,3},{7,5},{8,14},{10,8},{12,... | collective-permute-start | bytes 368648 | tf_op jit(solution)/shard_map/ppermute | solution.py:71
  34.6 48.1 %all-to-all-start.1 = ((bf16[4,296,768]{2,1,0:T(8,128)(2,1)}), bf16[4,296,768]{2,1,0:T(8,128)(2,1)S(1)}, u32[]{:S(2)}, u32[]{:S(2)}) async-start(bf16[4,296,768]{2,1,0:T(8,128)(2,1)} %get-tuple-element.124), calls=%async_computation.1 | async-start | bytes 3637248 | tf_op jit(solution)/shard_map/all_to_all | solution.py:1066
  40.2 13.0 %collective-permute-start.5 = (bf16[4,96,640]{2,1,0:T(8,128)(2,1)S(1)}, bf16[4,96,640]{2,1,0:T(8,128)(2,1)S(1)}, u32[]{:S(2)}, u32[]{:S(2)}) collective-permute-start(bf16[4,96,640]{2,1,0:T(8,128)(2,1)S(1)} %pad_maximum_fusion.refs_0_), channel_id=1, source_target_pairs={{0,8},{8,0},{1,9},{9,1},{2,10},{10,2},{3,11},{11,3},{4,12},{12,4},... | collective-permute-start | bytes 1474568 | tf_op jit(solution)/shard_map/ppermute | solution.py:52
  57.4 21.6 %collective-permute-start.9 = (bf16[128,768]{1,0:T(8,128)(2,1)S(1)}, bf16[128,768]{1,0:T(8,128)(2,1)S(1)}, u32[]{:S(2)}, u32[]{:S(2)}) collective-permute-start(bf16[128,768]{1,0:T(8,128)(2,1)S(1)} %collective-permute-done.4.refs_0_.dm_ref), channel_id=1, source_target_pairs={{0,17},{1,16},{16,1},{17,0},{2,19},{3,18},{18,3},{19,2},{4,21},{5,... | collective-permute-start | bytes 589832 | tf_op jit(solution)/shard_map/ppermute | solution.py:61
  58.9 20.0 %collective-permute-start.8 = (bf16[128,768]{1,0:T(8,128)(2,1)S(1)}, bf16[128,768]{1,0:T(8,128)(2,1)S(1)}, u32[]{:S(2)}, u32[]{:S(2)}) collective-permute-start(bf16[128,768]{1,0:T(8,128)(2,1)S(1)} %collective-permute-done.4.refs_0_.dm_ref), channel_id=1, source_target_pairs={{0,16},{1,17},{16,0},{17,1},{2,18},{3,19},{18,2},{19,3},{4,20},{5,... | collective-permute-start | bytes 589832 | tf_op jit(solution)/shard_map/ppermute | solution.py:61
  59.9 19.8 %collective-permute-start.7 = (bf16[128,768]{1,0:T(8,128)(2,1)S(1)}, bf16[128,768]{1,0:T(8,128)(2,1)S(1)}, u32[]{:S(2)}, u32[]{:S(2)}) collective-permute-start(bf16[128,768]{1,0:T(8,128)(2,1)S(1)} %collective-permute-done.4.refs_0_.dm_ref), channel_id=1, source_target_pairs={{0,1},{1,0},{16,17},{17,16},{2,3},{3,2},{18,19},{19,18},{4,5},{5,4... | collective-permute-start | bytes 589832 | tf_op jit(solution)/shard_map/ppermute | solution.py:61
  98.3 10.0 %collective-permute-start.13 = (bf16[128,768]{1,0:T(8,128)(2,1)S(1)}, bf16[128,768]{1,0:T(8,128)(2,1)S(1)}, u32[]{:S(2)}, u32[]{:S(2)}) collective-permute-start(bf16[128,768]{1,0:T(8,128)(2,1)S(1)} %get-tuple-element.143), channel_id=1, source_target_pairs={{0,17},{1,16},{16,1},{17,0},{2,19},{3,18},{18,3},{19,2},{4,21},{5,... | collective-permute-start | bytes 589832 | tf_op jit(solution)/shard_map/ppermute | solution.py:61
  109.6 10.9 %collective-permute-start.16 = (bf16[128,768]{1,0:T(8,128)(2,1)S(1)}, bf16[128,768]{1,0:T(8,128)(2,1)S(1)}, u32[]{:S(2)}, u32[]{:S(2)}) collective-permute-start(bf16[128,768]{1,0:T(8,128)(2,1)S(1)} %get-tuple-element.158.refs_2_.refs_0_), channel_id=1, source_target_pairs={{0,17},{1,16},{16,1},{17,0},{2,19},{3,18},{18,3},{19,2},{4,21},{5,... | collective-permute-start | bytes 589832 | tf_op jit(solution)/shard_map/ppermute | solution.py:61
  111.3 11.2 %collective-permute-start.15 = (bf16[128,768]{1,0:T(8,128)(2,1)S(1)}, bf16[128,768]{1,0:T(8,128)(2,1)}, u32[]{:S(2)}, u32[]{:S(2)}) collective-permute-start(bf16[128,768]{1,0:T(8,128)(2,1)S(1)} %get-tuple-element.158.refs_2_.refs_0_), channel_id=1, source_target_pairs={{0,16},{1,17},{16,0},{17,1},{2,18},{3,19},{18,2},{19,3},{4,20},{5,... | collective-permute-start | bytes 589832 | tf_op jit(solution)/shard_map/ppermute | solution.py:61
  112.5 10.0 %collective-permute-start.14 = (bf16[128,768]{1,0:T(8,128)(2,1)S(1)}, bf16[128,768]{1,0:T(8,128)(2,1)}, u32[]{:S(2)}, u32[]{:S(2)}) collective-permute-start(bf16[128,768]{1,0:T(8,128)(2,1)S(1)} %get-tuple-element.158.refs_2_.refs_0_), channel_id=1, source_target_pairs={{0,1},{1,0},{16,17},{17,16},{2,3},{3,2},{18,19},{19,18},{4,5},{5,4... | collective-permute-start | bytes 589832 | tf_op jit(solution)/shard_map/ppermute | solution.py:61
  114.4 33.3 %all-to-all-start.2 = ((bf16[4,200,768]{2,1,0:T(8,128)(2,1)}), bf16[4,200,768]{2,1,0:T(8,128)(2,1)S(1)}, u32[]{:S(2)}, u32[]{:S(2)}) async-start(bf16[4,200,768]{2,1,0:T(8,128)(2,1)} %add.15.refs_4_), calls=%async_computation.2 | async-start | bytes 2457600 | tf_op jit(solution)/shard_map/all_to_all | solution.py:1132
  118.1 17.5 %collective-permute-start.18 = (bf16[128,768]{1,0:T(8,128)(2,1)S(1)}, bf16[128,768]{1,0:T(8,128)(2,1)S(1)}, u32[]{:S(2)}, u32[]{:S(2)}) collective-permute-start(bf16[128,768]{1,0:T(8,128)(2,1)S(1)} %get-tuple-element.165), channel_id=1, source_target_pairs={{0,1},{1,0},{16,17},{17,16},{2,3},{3,2},{18,19},{19,18},{4,5},{5,4... | collective-permute-start | bytes 589832 | tf_op jit(solution)/shard_map/ppermute | solution.py:61
  119.7 15.9 %collective-permute-start.19 = (bf16[128,768]{1,0:T(8,128)(2,1)S(1)}, bf16[128,768]{1,0:T(8,128)(2,1)S(1)}, u32[]{:S(2)}, u32[]{:S(2)}) collective-permute-start(bf16[128,768]{1,0:T(8,128)(2,1)S(1)} %get-tuple-element.166), channel_id=1, source_target_pairs={{0,16},{1,17},{16,0},{17,1},{2,18},{3,19},{18,2},{19,3},{4,20},{5,... | collective-permute-start | bytes 589832 | tf_op jit(solution)/shard_map/ppermute | solution.py:61
  120.5 15.1 %collective-permute-start.20 = (bf16[128,768]{1,0:T(8,128)(2,1)S(1)}, bf16[128,768]{1,0:T(8,128)(2,1)S(1)}, u32[]{:S(2)}, u32[]{:S(2)}) collective-permute-start(bf16[128,768]{1,0:T(8,128)(2,1)S(1)} %get-tuple-element.167), channel_id=1, source_target_pairs={{0,17},{1,16},{16,1},{17,0},{2,19},{3,18},{18,3},{19,2},{4,21},{5,... | collective-permute-start | bytes 589832 | tf_op jit(solution)/shard_map/ppermute | solution.py:61
  143.1 12.4 %collective-permute-start.24 = (bf16[128,768]{1,0:T(8,128)(2,1)}, bf16[128,768]{1,0:T(8,128)(2,1)S(1)}, u32[]{:S(2)}, u32[]{:S(2)}) collective-permute-start(bf16[128,768]{1,0:T(8,128)(2,1)} %get-tuple-element.192), channel_id=1, source_target_pairs={{0,1},{1,0},{16,17},{17,16},{2,3},{3,2},{18,19},{19,18},{4,5},{5,4... | collective-permute-start | bytes 589832 | tf_op jit(solution)/shard_map/ppermute | solution.py:61
  144.2 11.2 %collective-permute-start.25 = (bf16[128,768]{1,0:T(8,128)(2,1)S(1)}, bf16[128,768]{1,0:T(8,128)(2,1)S(1)}, u32[]{:S(2)}, u32[]{:S(2)}) collective-permute-start(bf16[128,768]{1,0:T(8,128)(2,1)S(1)} %get-tuple-element.193), channel_id=1, source_target_pairs={{0,16},{1,17},{16,0},{17,1},{2,18},{3,19},{18,2},{19,3},{4,20},{5,... | collective-permute-start | bytes 589832 | tf_op jit(solution)/shard_map/ppermute | solution.py:61
  145.1 10.6 %collective-permute-start.26 = (bf16[128,768]{1,0:T(8,128)(2,1)S(1)}, bf16[128,768]{1,0:T(8,128)(2,1)S(1)}, u32[]{:S(2)}, u32[]{:S(2)}) collective-permute-start(bf16[128,768]{1,0:T(8,128)(2,1)S(1)} %get-tuple-element.194), channel_id=1, source_target_pairs={{0,17},{1,16},{16,1},{17,0},{2,19},{3,18},{18,3},{19,2},{4,21},{5,... | collective-permute-start | bytes 589832 | tf_op jit(solution)/shard_map/ppermute | solution.py:61
  149.1 31.9 %all-to-all-start.3 = ((bf16[16,24,896]{2,1,0:T(8,128)(2,1)}), bf16[16,24,896]{2,1,0:T(8,128)(2,1)S(1)}, u32[]{:S(2)}, u32[]{:S(2)}) async-start(bf16[16,24,896]{2,1,0:T(8,128)(2,1)} %add.16), calls=%async_computation.3 | async-start | bytes 1376256 | tf_op jit(solution)/shard_map/all_to_all | solution.py:1159
  156.1 22.9 %collective-permute-start.27 = (bf16[128,768]{1,0:T(8,128)(2,1)S(1)}, bf16[128,768]{1,0:T(8,128)(2,1)S(1)}, u32[]{:S(2)}, u32[]{:S(2)}) collective-permute-start(bf16[128,768]{1,0:T(8,128)(2,1)S(1)} %finish_input.1), channel_id=1, source_target_pairs={{0,0},{1,1},{16,2},{17,3},{8,4},{9,5},{24,6},{25,7},{2,8},{3,9},{1... | collective-permute-start | bytes 589832 | tf_op jit(solution)/shard_map/ppermute | solution.py:93
  164.9 16.1 %collective-permute-start.23 = (bf16[128,768]{1,0:T(8,128)(2,1)}, bf16[128,768]{1,0:T(8,128)(2,1)S(1)}, u32[]{:S(2)}, u32[]{:S(2)}) collective-permute-start(bf16[128,768]{1,0:T(8,128)(2,1)} %finish_output.1), channel_id=1, source_target_pairs={{0,0},{1,1},{16,2},{17,3},{8,4},{9,5},{24,6},{25,7},{2,8},{3,9},{1... | collective-permute-start | bytes 589832 | tf_op jit(solution)/shard_map/ppermute | solution.py:93
  (45 other events, 351.7 us)

commit v7 on v6

--- a/solution.py
+++ b/solution.py
@@ -379,7 +379,7 @@
             jax.ShapeDtypeStruct((rows, cols), bf16),
             jax.ShapeDtypeStruct((8, rows), f32),
         ],
-        compiler_params=params(),
+        compiler_params=params(parts * 7 * 1024 * 1024),
         cost_estimate=takes(7.1),
         name="attend",
     )(idx, ids, q, *kvs)
@@ -486,20 +486,41 @@
             jax.ShapeDtypeStruct((TP, step, cols), bf16),
         ]
         + [jax.ShapeDtypeStruct((2, span, cols), bf16)] * (parts - 1),
-        compiler_params=params(),
+        compiler_params=params(parts * 7 * 1024 * 1024),
         cost_estimate=takes(10.7),
         name="attend_back",
     )(idx, ids, q, w_out, lse, *das, *after, *kvs)
 
 
-def mlp_kernel(plan, idx_ref, x_ref, o_ref, vec_ref, *refs):
-    dm_refs, refs = refs[:TP], refs[TP:]
+def stage_kernel(idx_ref, x_ref, *refs):
+    same_ref, dm_ref = refs[TP:]
+    same_ref[...] = x_ref[...]
+    for j in range(TP):
+        dm_ref[idx_ref[0] ^ j] = refs[j][...]
+
+
+def stage(idx, x_all, dms):
+    return pl.pallas_call(
+        stage_kernel,
+        in_specs=[pl.BlockSpec(memory_space=pltpu.SMEM)]
+        + [pl.BlockSpec(memory_space=pltpu.VMEM)] * (1 + TP),
+        out_shape=[
+            jax.ShapeDtypeStruct(x_all.shape, bf16),
+            jax.ShapeDtypeStruct((TP, *dms[0].shape), bf16),
+        ],
+        compiler_params=small_params(),
+        cost_estimate=takes(1.5),
+        name="stage",
+    )(idx, x_all, *dms)
+
+
+def mlp_kernel(plan, idx_ref, x_ref, o_ref, vec_ref, dm_ref, *refs):
     step = pl.program_id(0)
     side = lax.rem(idx_ref[0], 2)
     if plan.fast:
-        own_ref, other_ref, r_ref, h_ref, a_ref, du_ref, dm_ref, sum_ref = refs[:8]
-        dh_refs = refs[8 : 8 + TP]
-        out_ref, down_ref, dm_now, r_now, dh_now, held, held_down, held_row = refs[8 + TP :]
+        own_ref, other_ref, r_ref, h_ref, a_ref, du_ref, sum_ref = refs[:7]
+        dh_refs = refs[7 : 7 + TP]
+        out_ref, down_ref, r_now, dh_now, held, held_down, held_row = refs[7 + TP :]
 
         @pl.when(step == 0)
         def _():
@@ -535,8 +556,8 @@
         w_down = held_down[...].reshape(-1, width)
         b_up = held_row[...]
     else:
-        wo_ref, wu_ref, wd_ref, bup_ref, r_ref, h_ref, a_ref, du_ref, dm_ref, sum_ref = refs[:10]
-        dh_refs, dm_now, r_now, dh_now = refs[10 : 10 + TP], refs[-3], refs[-2], refs[-1]
+        wo_ref, wu_ref, wd_ref, bup_ref, r_ref, h_ref, a_ref, du_ref, sum_ref = refs[:9]
+        dh_refs, r_now, dh_now = refs[9 : 9 + TP], refs[-2], refs[-1]
         w_up, w_down, b_up = wu_ref[...], wd_ref[...], bup_ref[...]
         outs = [wo_ref[j] for j in range(TP)]
 
@@ -549,15 +570,10 @@
         attended += dot(o_ref[j], outs[j])
     residual = x_ref[...].astype(f32) + (attended + vec_ref[2:3, :])
 
-    for i in range(2):
-
-        @pl.when(step == i)
-        def _(i=i):
-            for b in range(2):
-                dm_now[side ^ b] = dm_refs[2 * i + b][...]
-            if i == 0:
-                r_now[...] = residual.reshape(r_now.shape)
-                r_ref[...] = r_now[side]
+    @pl.when(step == 0)
+    def _():
+        r_now[...] = residual.reshape(r_now.shape)
+        r_ref[...] = r_now[side]
 
     units, _ = unit(residual)
     low = (units * vec_ref[5:6, :] + vec_ref[6:7, :]).astype(bf16)
@@ -567,8 +583,7 @@
     act = (pre * normal).astype(bf16)
     a_ref[...] = act
     slope = normal + pre * (0.3989422804014327 * jnp.exp(-0.5 * pre * pre))
-    dm = dm_now[...].reshape(x_ref.shape)
-    dm_ref[...] = dm
+    dm = dm_ref[...]
     grad_pre = (dot(dm, w_down, 1, 1) * slope).astype(bf16)
     du_ref[...] = grad_pre
     grad = dot(grad_pre, w_up, 1, 1)
@@ -583,7 +598,7 @@
                 dh_refs[2 * i + b][...] = dh_now[side ^ b]
 
 
-def mlp(plan, idx, x_all, o_all, vecs, dms, weights, slab):
+def mlp(plan, idx, x_all, o_all, vecs, dm_all, weights, slab):
     rows, width = x_all.shape
     hidden = plan.copies * slab
     cols = width // TP
@@ -596,16 +611,15 @@
     inner = pl.BlockSpec((step, hidden), block)
     one = here((rows // TP, width))
     now = (2, rows // TP, width)
-    out_specs = [one, token, inner, inner, token, here((8, width))] + [one] * TP
+    out_specs = [one, token, inner, inner, here((8, width))] + [one] * TP
     out_shape = [
         jax.ShapeDtypeStruct((rows // TP, width), f32),
         jax.ShapeDtypeStruct((rows, width), bf16),
         jax.ShapeDtypeStruct((rows, hidden), bf16),
         jax.ShapeDtypeStruct((rows, hidden), bf16),
-        jax.ShapeDtypeStruct((rows, width), bf16),
         jax.ShapeDtypeStruct((8, width), f32),
     ] + [jax.ShapeDtypeStruct((rows // TP, width), bf16)] * TP
-    scratch = [pltpu.VMEM(now, bf16), pltpu.VMEM(now, f32), pltpu.VMEM(now, bf16)]
+    scratch = [pltpu.VMEM(now, f32), pltpu.VMEM(now, bf16)]
     if plan.fast:
         lines = plan.copies // 2
         gx = plan.size["gx"]
@@ -628,8 +642,8 @@
                 token,
                 pl.BlockSpec((TP, step, cols), lambda i, idx: (0, i ^ (idx[0] // 2), 0)),
                 here(vecs.shape),
+                token,
             ]
-            + [here(dms[0].shape)] * TP
             + [here(v.shape) for v in weights],
             out_specs=out_specs,
             scratch_shapes=scratch,
@@ -638,7 +652,7 @@
         compiler_params=params(),
         cost_estimate=takes(10.5),
         name="mlp",
-    )(idx, x_all, o_all, vecs, *dms, *weights)
+    )(idx, x_all, o_all, vecs, dm_all, *weights)
 
 
 def pair_kernel(plan, idx_ref, h_ref, du_ref, a_ref, dm_ref, wd_ref, near_ref, far_ref, *refs):
@@ -1102,11 +1116,13 @@
         weights = [shard, plan.swap(shard)]
     else:
         weights = [out_full, up_mine, down_mine, b_up_mine]
-    results = mlp(plan, idx, x_all, o_all, vecs, dms, weights, slab)
-    r_own, low_two, act, grad_pre, dm_all, sum_two = results[:6]
-    dh_two = results[6 : 6 + TP]
+    x_same, dm_all = stage(idx, x_all, dms)
+    dm_all = dm_all.reshape(TP * rows, width)
+    results = mlp(plan, idx, x_same, o_all, vecs, dm_all, weights, slab)
+    r_own, low_two, act, grad_pre, sum_two = results[:5]
+    dh_two = results[5 : 5 + TP]
     if fast:
-        out_mine, down_mine = results[6 + TP :]
+        out_mine, down_mine = results[5 + TP :]
     else:
         out_mine = lax.dynamic_index_in_dim(out_full, member, 0, keepdims=False)
 

time: 185 us -> 183 us (0.989)
  waiting for transfers between devices: 40.4 us -> 34.9 us
    ppermute x4, waiting for transfers between devices: 12.7 us -> 10.3 us  [move(): return lax.ppermute(value, ALL, table)]
    unnamed x70 -> x84, local copies, waits for them, and re-layouts: 11.6 us -> 13.3 us
  transfers between devices with their start and end apart: 35 -> 35, of which waited for: 12 -> 12; matrix products, arithmetic and copies ran while one was open for 1% -> 1% of each run, Pallas kernels for 20% -> 21%
where the time goes in v7:
time: 183 us; the launch traced here: 180 us
  starting transfers between devices  57.1 us (31%)
  Pallas kernels  45.1 us (25%)
  waiting for transfers between devices  34.9 us (19%)
  blocking collectives  25.9 us (14%)
  local copies, waits for them, and re-layouts  13.4 us (7%)
  other arithmetic  1.91 us (1%)
    ppermute x18, starting transfers between devices, partner(): return lax.ppermute(value, self.tp, table)  21.1 us
    unnamed x84, local copies, waits for them, and re-layouts  13.3 us
    all_gather x1, blocking collectives, local(): o_all = lax.all_gather(mixed, plan.tp, axis=0, tiled=False)  13.1 us
    all_gather x1, blocking collectives, local(): x_all = lax.all_gather(x_mine, plan.tp, axis=0, tiled=True)  12.8 us
    ppermute x4, starting transfers between devices, move(): return lax.ppermute(value, ALL, table)  12.2 us
    ppermute x4, waiting for transfers between devices, move(): return lax.ppermute(value, ALL, table)  10.3 us
    ppermute x5, waiting for transfers between devices, turn(): lax.ppermute(value, axis, [(i, (i + by) % count) for i in range(count)])  10.2 us
    pallas_call x1, Pallas kernels, attend_back(): pl.pallas_call(functools.partial(bwd_kernel, parts, len(after)), grid_spe...  9.08 us
  transfers between devices with their start and end apart: 35, of which 12 were waited for; matrix products, arithmetic and copies ran while one was open for 1% of the time, Pallas kernels for 21%

profile of v7, /device:TPU:2, one launch (start us, length us, event | category | flops | bytes accessed | tf_op | source)
XLA Modules:
  0.0 179.6 jit_solution(14997306785963264818)
XLA Ops:
  2.4 4.5 %collective-permute-start.3 = (bf16[136,768]{1,0:T(8,128)(2,1)S(1)}, bf16[136,768]{1,0:T(8,128)(2,1)S(1)}, u32[]{:S(2)}, u32[]{:S(2)}) collective-permute-start(bf16[136,768]{1,0:T(8,128)(2,1)S(1)} %pad_maximum_fusion.1), channel_id=1, source_target_pairs={{0,0},{1,1},{2,16},{3,17},{4,8},{5,9},{6,24},{7,25},{8,2},{9,3},{1... | collective-permute-start | bytes 626696 | tf_op jit(solution)/shard_map/ppermute | solution.py:93
  8.9 4.2 %all-to-all-start = ((bf16[4,24,2176]{2,1,0:T(8,128)(2,1)}), bf16[4,24,2176]{2,1,0:T(8,128)(2,1)S(1)}, u32[]{:S(2)}, u32[]{:S(2)}) async-start(bf16[4,24,2176]{2,1,0:T(8,128)(2,1)} %prepare.1), calls=%async_computation | async-start | bytes 835584 | tf_op jit(solution)/shard_map/all_to_all | solution.py:1073
  15.2 5.5 %all-to-all-done.got_ref = bf16[4,24,2176]{2,1,0:T(8,128)(2,1)S(1)} async-done(((bf16[4,24,2176]{2,1,0:T(8,128)(2,1)}), bf16[4,24,2176]{2,1,0:T(8,128)(2,1)S(1)}, u32[]{:S(2)}, u32[]{:S(2)}) %all-to-all-start) | async-done | bytes 417824 | tf_op jit(solution)/shard_map/all_to_all | solution.py:1073
  22.6 3.7 %collective-permute-start.1 = (bf16[96,640]{1,0:T(8,128)(2,1)S(1)}, bf16[96,640]{1,0:T(8,128)(2,1)S(1)}, u32[]{:S(2)}, u32[]{:S(2)}) collective-permute-start(bf16[96,640]{1,0:T(8,128)(2,1)S(1)} %get-tuple-element.120), channel_id=1, source_target_pairs={{0,4},{2,6},{4,0},{6,2},{1,5},{3,7},{5,1},{7,3},{8,12},{10,14},{12... | collective-permute-start | bytes 368648 | tf_op jit(solution)/shard_map/ppermute | solution.py:71
  26.3 3.8 %collective-permute-done.2 = bf16[96,640]{1,0:T(8,128)(2,1)S(1)} collective-permute-done((bf16[96,640]{1,0:T(8,128)(2,1)S(1)}, bf16[96,640]{1,0:T(8,128)(2,1)S(1)}, u32[]{:S(2)}, u32[]{:S(2)}) %collective-permute-start.2) | collective-permute-done | bytes 122912 | tf_op jit(solution)/shard_map/ppermute | solution.py:71
  30.1 4.5 %collective-permute-done.1 = bf16[96,640]{1,0:T(8,128)(2,1)S(1)} collective-permute-done((bf16[96,640]{1,0:T(8,128)(2,1)S(1)}, bf16[96,640]{1,0:T(8,128)(2,1)S(1)}, u32[]{:S(2)}, u32[]{:S(2)}) %collective-permute-start.1) | collective-permute-done | bytes 122912 | tf_op jit(solution)/shard_map/ppermute | solution.py:71
  34.6 5.5 %all-to-all-start.1 = ((bf16[4,296,768]{2,1,0:T(8,128)(2,1)}), bf16[4,296,768]{2,1,0:T(8,128)(2,1)S(1)}, u32[]{:S(2)}, u32[]{:S(2)}) async-start(bf16[4,296,768]{2,1,0:T(8,128)(2,1)} %get-tuple-element.125), calls=%async_computation.1 | async-start | bytes 3637248 | tf_op jit(solution)/shard_map/all_to_all | solution.py:1080
  40.4 12.8 %all_gather.9.x_ref = bf16[512,768]{1,0:T(8,128)(2,1)S(1)} all-gather(bf16[128,768]{1,0:T(8,128)(2,1)S(1)} %slice.9.x_ref), channel_id=1, replica_groups=mesh['gx'=2,'c'=2,'sz'=4,'sy'=2] {'gx','sy'}, dimensions={0}, use_global_device_ids=true | all-gather | bytes 983040 | tf_op jit(solution)/shard_map/all_gather | solution.py:1079
  53.2 3.3 %qkv.1 = (bf16[512,768]{1,0:T(8,128)(2,1)S(1)}, bf16[512,192]{1,0:T(8,128)(2,1)S(1)}, bf16[2,512,192]{2,1,0:T(8,128)(2,1)S(1)}, bf16[768,640]{1,0:T(8,128)(2,1)S(1)}, f32[8,768]{1,0:T(8,128)S(1)}) custom-call(s32[4]{0:T(128)S(1)} %pad_add_fusion.idx_ref, bf16[512,768]{1,0:T(8,128)(2,1)S(1)} %all_gather.9.x_ref, ...), custom_call_target="tpu_custom_call" | custom-call | flops 1104000000 | bytes 17712000 | tf_op jit(solution)/shard_map/qkv/pallas_call | solution.py:291
  62.8 5.1 %attend.1 = (bf16[512,192]{1,0:T(8,128)(2,1)S(1)}, f32[8,512]{1,0:T(8,128)S(1)}) custom-call(s32[4]{0:T(128)S(1)} %pad_add_fusion.idx_ref, f32[1,1024]{1,0:T(1,128)S(1)} %slice_convert_fusion.ids_ref, bf16[512,192]{1,0:T(8,128)(2,1)S(1)} %get-tuple-element.124.q_ref, bf16[2,512,192]{2,1,0:T(8,128)(2,1)S(1)} %get-tuple-element.128.refs_0_.refs_5_, ...), custom_call_target="tpu_custom_call" | custom-call | flops 1632999936 | bytes 26199000 | tf_op jit(solution)/shard_map/attend/pallas_call | solution.py:362
  67.9 13.1 %all-gather = bf16[2048,192]{1,0:T(8,128)(2,1)} all-gather(bf16[512,192]{1,0:T(8,128)(2,1)S(1)} %get-tuple-element.129), channel_id=2, replica_groups=mesh['gx'=2,'c'=2,'sz'=4,'sy'=2] {'gx','sy'}, dimensions={0}, use_global_device_ids=true | all-gather | bytes 983040 | tf_op jit(solution)/shard_map/all_gather | solution.py:1112
  84.4 2.1 %collective-permute-done.10.refs_1_ = bf16[4,296,768]{2,1,0:T(8,128)(2,1)S(1)} collective-permute-done((bf16[4,296,768]{2,1,0:T(8,128)(2,1)S(1)}, bf16[4,296,768]{2,1,0:T(8,128)(2,1)S(1)}, u32[]{:S(2)}, u32[]{:S(2)}) %collective-permute-start.10) | collective-permute-done | bytes 1818656 | tf_op jit(solution)/shard_map/ppermute | solution.py:52
  86.5 6.4 %mlp.1 = (f32[128,768]{1,0:T(8,128)S(1)}, bf16[512,768]{1,0:T(8,128)(2,1)S(1)}, bf16[512,768]{1,0:T(8,128)(2,1)S(1)}, bf16[512,768]{1,0:T(8,128)(2,1)S(1)}, f32[...) custom-call(s32[4]{0:T(128)S(1)} %pad_add_fusion.idx_ref, ...), custom_call_target="tpu_custom_call" | custom-call | flops 2415000064 | bytes 38745000 | tf_op jit(solution)/shard_map/mlp/pallas_call | solution.py:636
  97.0 4.1 %mlp_weight_grads.1 = (bf16[4,200,768]{2,1,0:T(8,128)(2,1)S(1)}, bf16[4,200,768]{2,1,0:T(8,128)(2,1)S(1)}, bf16[128,768]{1,0:T(8,128)(2,1)S(1)}, bf16[128,768]{1...) custom-call(s32[4]{0:T(128)S(1)} %pad_add_fusion.idx_ref, ...), custom_call_target="tpu_custom_call" | custom-call | flops 1748000000 | bytes 28044000 | tf_op jit(solution)/shard_map/mlp_weight_grads/pallas_call | solution.py:722
  102.8 3.0 %collective-permute-done.13.refs_3_ = bf16[128,768]{1,0:T(8,128)(2,1)S(1)} collective-permute-done((bf16[128,768]{1,0:T(8,128)(2,1)S(1)}, bf16[128,768]{1,0:T(8,128)(2,1)S(1)}, u32[]{:S(2)}, u32[]{:S(2)}) %collective-permute-start.13) | collective-permute-done | bytes 196640 | tf_op jit(solution)/shard_map/ppermute | solution.py:61
  112.4 4.3 %all-to-all-start.2 = ((bf16[4,200,768]{2,1,0:T(8,128)(2,1)}), bf16[4,200,768]{2,1,0:T(8,128)(2,1)S(1)}, u32[]{:S(2)}, u32[]{:S(2)}) async-start(bf16[4,200,768]{2,1,0:T(8,128)(2,1)} %add.15.refs_4_), calls=%async_computation.2 | async-start | bytes 2457600 | tf_op jit(solution)/shard_map/all_to_all | solution.py:1148
  124.2 9.1 %attend_back.1 = (bf16[512,192]{1,0:T(8,128)(2,1)S(1)}, f32[2,512,192]{2,1,0:T(8,128)S(1)}, bf16[4,128,192]{2,1,0:T(8,128)(2,1)S(1)}, bf16[2,512,192]{2,1,0:T(8,128)(2,1)S(1)}) custom-call(s32[4]{0:T(128)S(1)} %pad_add_fusion.idx_ref, f32[1,1024]{1,0:T(1,128)S(1)} %slice_convert_fusion.ids_ref, bf16[512,192]{1,0:T(8,128)(2,1)S(1)} %copy-done.24, ...), custom_call_target="tpu_custom_call" | custom-call | flops 2460999936 | bytes 39483000 | tf_op jit(solution)/shard_map/attend_back/pallas_call | solution.py:455
  135.4 3.9 %normed_back.1 = (bf16[128,768]{1,0:T(8,128)(2,1)S(1)}, bf16[128,768]{1,0:T(8,128)(2,1)S(1)}, bf16[128,768]{1,0:T(8,128)(2,1)S(1)}, bf16[128,768]{1,0:T(8,128)(2...) custom-call(s32[4]{0:T(128)S(1)} %pad_add_fusion.idx_ref, ...), custom_call_target="tpu_custom_call" | custom-call | flops 2990000128 | bytes 47970000 | tf_op jit(solution)/shard_map/normed_back/pallas_call | solution.py:983
  147.6 5.3 %all-to-all-start.3 = ((bf16[16,24,896]{2,1,0:T(8,128)(2,1)}), bf16[16,24,896]{2,1,0:T(8,128)(2,1)S(1)}, u32[]{:S(2)}, u32[]{:S(2)}) async-start(bf16[16,24,896]{2,1,0:T(8,128)(2,1)} %add.16), calls=%async_computation.3 | async-start | bytes 1376256 | tf_op jit(solution)/shard_map/all_to_all | solution.py:1175
  155.3 3.9 %collective-permute-start.27 = (bf16[128,768]{1,0:T(8,128)(2,1)S(1)}, bf16[128,768]{1,0:T(8,128)(2,1)S(1)}, u32[]{:S(2)}, u32[]{:S(2)}) collective-permute-start(bf16[128,768]{1,0:T(8,128)(2,1)S(1)} %finish_input.1), channel_id=1, source_target_pairs={{0,0},{1,1},{16,2},{17,3},{8,4},{9,5},{24,6},{25,7},{2,8},{3,9},{1... | collective-permute-start | bytes 589832 | tf_op jit(solution)/shard_map/ppermute | solution.py:93
  160.2 2.5 %collective-permute-start.30 = (bf16[24,768]{1,0:T(8,128)(2,1)S(1)}, bf16[24,768]{1,0:T(8,128)(2,1)S(1)}, u32[]{:S(2)}, u32[]{:S(2)}) collective-permute-start(bf16[24,768]{1,0:T(8,128)(2,1)S(1)} %get-tuple-element.213), channel_id=1, source_target_pairs={{0,17},{1,16},{16,1},{17,0},{2,19},{3,18},{18,3},{19,2},{4,21},{5,... | collective-permute-start | bytes 110600 | tf_op jit(solution)/shard_map/ppermute | solution.py:61
  162.8 2.1 %finish_output.1 = bf16[128,768]{1,0:T(8,128)(2,1)} custom-call(f32[128,768]{1,0:T(8,128)} %copy-done.12, f32[8,768]{1,0:T(8,128)} %copy-done.18, bf16[128,768]{1,0:T(8,128)(2,1)} %copy-done.13, bf16[128,768]{1,0:T(8,128)(2,1)} %copy-done.37, bf16[128,768]{1,0:T(8,128)(2,1)} %copy-done.38, bf16[128,768]{1,0:T(8,128)(2,1)} %copy-done.39), custom_call_target="tpu_custom_call" | custom-call | flops 483000000 | bytes 7749000 | tf_op jit(solution)/shard_map/finish_output/pallas_call | solution.py:861
  168.3 8.2 %collective-permute-done.27.second_ref = bf16[128,768]{1,0:T(8,128)(2,1)S(1)} collective-permute-done((bf16[128,768]{1,0:T(8,128)(2,1)S(1)}, bf16[128,768]{1,0:T(8,128)(2,1)S(1)}, u32[]{:S(2)}, u32[]{:S(2)}) %collective-permute-start.27) | collective-permute-done | bytes 196640 | tf_op jit(solution)/shard_map/ppermute | solution.py:93
  176.4 2.1 %collective-permute-done.23.first_ref = bf16[128,768]{1,0:T(8,128)(2,1)S(1)} collective-permute-done((bf16[128,768]{1,0:T(8,128)(2,1)}, bf16[128,768]{1,0:T(8,128)(2,1)S(1)}, u32[]{:S(2)}, u32[]{:S(2)}) %collective-permute-start.23) | collective-permute-done | bytes 196640 | tf_op jit(solution)/shard_map/ppermute | solution.py:93
  (159 shorter events, 55.5 us)
Async XLA Ops:
  2.4 24.0 %collective-permute-start.3 = (bf16[136,768]{1,0:T(8,128)(2,1)S(1)}, bf16[136,768]{1,0:T(8,128)(2,1)S(1)}, u32[]{:S(2)}, u32[]{:S(2)}) collective-permute-start(bf16[136,768]{1,0:T(8,128)(2,1)S(1)} %pad_maximum_fusion.1), channel_id=1, source_target_pairs={{0,0},{1,1},{2,16},{3,17},{4,8},{5,9},{6,24},{7,25},{8,2},{9,3},{1... | collective-permute-start | bytes 626696 | tf_op jit(solution)/shard_map/ppermute | solution.py:93
  8.9 11.8 %all-to-all-start = ((bf16[4,24,2176]{2,1,0:T(8,128)(2,1)}), bf16[4,24,2176]{2,1,0:T(8,128)(2,1)S(1)}, u32[]{:S(2)}, u32[]{:S(2)}) async-start(bf16[4,24,2176]{2,1,0:T(8,128)(2,1)} %prepare.1), calls=%async_computation | async-start | bytes 835584 | tf_op jit(solution)/shard_map/all_to_all | solution.py:1073
  13.2 13.1 %collective-permute-start.4 = (bf16[128,768]{1,0:T(8,128)(2,1)S(1)}, bf16[128,768]{1,0:T(8,128)(2,1)S(1)}, u32[]{:S(2)}, u32[]{:S(2)}) collective-permute-start(bf16[128,768]{1,0:T(8,128)(2,1)S(1)} %fusion), channel_id=1, source_target_pairs={{0,0},{1,1},{2,16},{3,17},{4,8},{5,9},{6,24},{7,25},{8,2},{9,3},{1... | collective-permute-start | bytes 589832 | tf_op jit(solution)/shard_map/ppermute | solution.py:93
  22.6 12.0 %collective-permute-start.1 = (bf16[96,640]{1,0:T(8,128)(2,1)S(1)}, bf16[96,640]{1,0:T(8,128)(2,1)S(1)}, u32[]{:S(2)}, u32[]{:S(2)}) collective-permute-start(bf16[96,640]{1,0:T(8,128)(2,1)S(1)} %get-tuple-element.120), channel_id=1, source_target_pairs={{0,4},{2,6},{4,0},{6,2},{1,5},{3,7},{5,1},{7,3},{8,12},{10,14},{12... | collective-permute-start | bytes 368648 | tf_op jit(solution)/shard_map/ppermute | solution.py:71
  26.3 8.3 %collective-permute-start = (bf16[96,640]{1,0:T(8,128)(2,1)S(1)}, bf16[96,640]{1,0:T(8,128)(2,1)S(1)}, u32[]{:S(2)}, u32[]{:S(2)}) collective-permute-start(bf16[96,640]{1,0:T(8,128)(2,1)S(1)} %get-tuple-element.120), channel_id=1, source_target_pairs={{0,6},{2,0},{4,2},{6,4},{1,7},{3,1},{5,3},{7,5},{8,14},{10,8},{12,... | collective-permute-start | bytes 368648 | tf_op jit(solution)/shard_map/ppermute | solution.py:71
  34.6 48.1 %all-to-all-start.1 = ((bf16[4,296,768]{2,1,0:T(8,128)(2,1)}), bf16[4,296,768]{2,1,0:T(8,128)(2,1)S(1)}, u32[]{:S(2)}, u32[]{:S(2)}) async-start(bf16[4,296,768]{2,1,0:T(8,128)(2,1)} %get-tuple-element.125), calls=%async_computation.1 | async-start | bytes 3637248 | tf_op jit(solution)/shard_map/all_to_all | solution.py:1080
  40.2 13.0 %collective-permute-start.5 = (bf16[4,96,640]{2,1,0:T(8,128)(2,1)S(1)}, bf16[4,96,640]{2,1,0:T(8,128)(2,1)}, u32[]{:S(2)}, u32[]{:S(2)}) collective-permute-start(bf16[4,96,640]{2,1,0:T(8,128)(2,1)S(1)} %pad_maximum_fusion.refs_0_), channel_id=1, source_target_pairs={{0,8},{8,0},{1,9},{9,1},{2,10},{10,2},{3,11},{11,3},{4,12},{12,4},... | collective-permute-start | bytes 1474568 | tf_op jit(solution)/shard_map/ppermute | solution.py:52
  59.2 21.8 %collective-permute-start.9 = (bf16[128,768]{1,0:T(8,128)(2,1)S(1)}, bf16[128,768]{1,0:T(8,128)(2,1)S(1)}, u32[]{:S(2)}, u32[]{:S(2)}) collective-permute-start(bf16[128,768]{1,0:T(8,128)(2,1)S(1)} %collective-permute-done.4.refs_0_.dm_ref), channel_id=1, source_target_pairs={{0,17},{1,16},{16,1},{17,0},{2,19},{3,18},{18,3},{19,2},{4,21},{5,... | collective-permute-start | bytes 589832 | tf_op jit(solution)/shard_map/ppermute | solution.py:61
  60.8 20.3 %collective-permute-start.8 = (bf16[128,768]{1,0:T(8,128)(2,1)S(1)}, bf16[128,768]{1,0:T(8,128)(2,1)S(1)}, u32[]{:S(2)}, u32[]{:S(2)}) collective-permute-start(bf16[128,768]{1,0:T(8,128)(2,1)S(1)} %collective-permute-done.4.refs_0_.dm_ref), channel_id=1, source_target_pairs={{0,16},{1,17},{16,0},{17,1},{2,18},{3,19},{18,2},{19,3},{4,20},{5,... | collective-permute-start | bytes 589832 | tf_op jit(solution)/shard_map/ppermute | solution.py:61
  61.7 19.3 %collective-permute-start.7 = (bf16[128,768]{1,0:T(8,128)(2,1)S(1)}, bf16[128,768]{1,0:T(8,128)(2,1)S(1)}, u32[]{:S(2)}, u32[]{:S(2)}) collective-permute-start(bf16[128,768]{1,0:T(8,128)(2,1)S(1)} %collective-permute-done.4.refs_0_.dm_ref), channel_id=1, source_target_pairs={{0,1},{1,0},{16,17},{17,16},{2,3},{3,2},{18,19},{19,18},{4,5},{5,4... | collective-permute-start | bytes 589832 | tf_op jit(solution)/shard_map/ppermute | solution.py:61
  95.8 10.0 %collective-permute-start.13 = (bf16[128,768]{1,0:T(8,128)(2,1)S(1)}, bf16[128,768]{1,0:T(8,128)(2,1)S(1)}, u32[]{:S(2)}, u32[]{:S(2)}) collective-permute-start(bf16[128,768]{1,0:T(8,128)(2,1)S(1)} %get-tuple-element.146), channel_id=1, source_target_pairs={{0,17},{1,16},{16,1},{17,0},{2,19},{3,18},{18,3},{19,2},{4,21},{5,... | collective-permute-start | bytes 589832 | tf_op jit(solution)/shard_map/ppermute | solution.py:61
  107.6 11.1 %collective-permute-start.16 = (bf16[128,768]{1,0:T(8,128)(2,1)S(1)}, bf16[128,768]{1,0:T(8,128)(2,1)}, u32[]{:S(2)}, u32[]{:S(2)}) collective-permute-start(bf16[128,768]{1,0:T(8,128)(2,1)S(1)} %get-tuple-element.160.refs_2_.refs_0_), channel_id=1, source_target_pairs={{0,17},{1,16},{16,1},{17,0},{2,19},{3,18},{18,3},{19,2},{4,21},{5,... | collective-permute-start | bytes 589832 | tf_op jit(solution)/shard_map/ppermute | solution.py:61
  109.4 11.1 %collective-permute-start.15 = (bf16[128,768]{1,0:T(8,128)(2,1)S(1)}, bf16[128,768]{1,0:T(8,128)(2,1)}, u32[]{:S(2)}, u32[]{:S(2)}) collective-permute-start(bf16[128,768]{1,0:T(8,128)(2,1)S(1)} %get-tuple-element.160.refs_2_.refs_0_), channel_id=1, source_target_pairs={{0,16},{1,17},{16,0},{17,1},{2,18},{3,19},{18,2},{19,3},{4,20},{5,... | collective-permute-start | bytes 589832 | tf_op jit(solution)/shard_map/ppermute | solution.py:61
  110.6 9.9 %collective-permute-start.14 = (bf16[128,768]{1,0:T(8,128)(2,1)S(1)}, bf16[128,768]{1,0:T(8,128)(2,1)}, u32[]{:S(2)}, u32[]{:S(2)}) collective-permute-start(bf16[128,768]{1,0:T(8,128)(2,1)S(1)} %get-tuple-element.160.refs_2_.refs_0_), channel_id=1, source_target_pairs={{0,1},{1,0},{16,17},{17,16},{2,3},{3,2},{18,19},{19,18},{4,5},{5,4... | collective-permute-start | bytes 589832 | tf_op jit(solution)/shard_map/ppermute | solution.py:61
  112.4 33.7 %all-to-all-start.2 = ((bf16[4,200,768]{2,1,0:T(8,128)(2,1)}), bf16[4,200,768]{2,1,0:T(8,128)(2,1)S(1)}, u32[]{:S(2)}, u32[]{:S(2)}) async-start(bf16[4,200,768]{2,1,0:T(8,128)(2,1)} %add.15.refs_4_), calls=%async_computation.2 | async-start | bytes 2457600 | tf_op jit(solution)/shard_map/all_to_all | solution.py:1148
  116.7 16.6 %collective-permute-start.18 = (bf16[128,768]{1,0:T(8,128)(2,1)S(1)}, bf16[128,768]{1,0:T(8,128)(2,1)S(1)}, u32[]{:S(2)}, u32[]{:S(2)}) collective-permute-start(bf16[128,768]{1,0:T(8,128)(2,1)S(1)} %get-tuple-element.167), channel_id=1, source_target_pairs={{0,1},{1,0},{16,17},{17,16},{2,3},{3,2},{18,19},{19,18},{4,5},{5,4... | collective-permute-start | bytes 589832 | tf_op jit(solution)/shard_map/ppermute | solution.py:61
  117.9 15.4 %collective-permute-start.19 = (bf16[128,768]{1,0:T(8,128)(2,1)S(1)}, bf16[128,768]{1,0:T(8,128)(2,1)S(1)}, u32[]{:S(2)}, u32[]{:S(2)}) collective-permute-start(bf16[128,768]{1,0:T(8,128)(2,1)S(1)} %copy-done.9), channel_id=1, source_target_pairs={{0,16},{1,17},{16,0},{17,1},{2,18},{3,19},{18,2},{19,3},{4,20},{5,... | collective-permute-start | bytes 589832 | tf_op jit(solution)/shard_map/ppermute | solution.py:61
  118.7 14.6 %collective-permute-start.20 = (bf16[128,768]{1,0:T(8,128)(2,1)S(1)}, bf16[128,768]{1,0:T(8,128)(2,1)S(1)}, u32[]{:S(2)}, u32[]{:S(2)}) collective-permute-start(bf16[128,768]{1,0:T(8,128)(2,1)S(1)} %get-tuple-element.169), channel_id=1, source_target_pairs={{0,17},{1,16},{16,1},{17,0},{2,19},{3,18},{18,3},{19,2},{4,21},{5,... | collective-permute-start | bytes 589832 | tf_op jit(solution)/shard_map/ppermute | solution.py:61
  140.1 12.8 %collective-permute-start.24 = (bf16[128,768]{1,0:T(8,128)(2,1)S(1)}, bf16[128,768]{1,0:T(8,128)(2,1)S(1)}, u32[]{:S(2)}, u32[]{:S(2)}) collective-permute-start(bf16[128,768]{1,0:T(8,128)(2,1)S(1)} %get-tuple-element.194), channel_id=1, source_target_pairs={{0,1},{1,0},{16,17},{17,16},{2,3},{3,2},{18,19},{19,18},{4,5},{5,4... | collective-permute-start | bytes 589832 | tf_op jit(solution)/shard_map/ppermute | solution.py:61
  141.4 11.5 %collective-permute-start.25 = (bf16[128,768]{1,0:T(8,128)(2,1)S(1)}, bf16[128,768]{1,0:T(8,128)(2,1)S(1)}, u32[]{:S(2)}, u32[]{:S(2)}) collective-permute-start(bf16[128,768]{1,0:T(8,128)(2,1)S(1)} %get-tuple-element.195), channel_id=1, source_target_pairs={{0,16},{1,17},{16,0},{17,1},{2,18},{3,19},{18,2},{19,3},{4,20},{5,... | collective-permute-start | bytes 589832 | tf_op jit(solution)/shard_map/ppermute | solution.py:61
  142.2 10.8 %collective-permute-start.26 = (bf16[128,768]{1,0:T(8,128)(2,1)S(1)}, bf16[128,768]{1,0:T(8,128)(2,1)S(1)}, u32[]{:S(2)}, u32[]{:S(2)}) collective-permute-start(bf16[128,768]{1,0:T(8,128)(2,1)S(1)} %get-tuple-element.196), channel_id=1, source_target_pairs={{0,17},{1,16},{16,1},{17,0},{2,19},{3,18},{18,3},{19,2},{4,21},{5,... | collective-permute-start | bytes 589832 | tf_op jit(solution)/shard_map/ppermute | solution.py:61
  147.6 30.9 %all-to-all-start.3 = ((bf16[16,24,896]{2,1,0:T(8,128)(2,1)}), bf16[16,24,896]{2,1,0:T(8,128)(2,1)S(1)}, u32[]{:S(2)}, u32[]{:S(2)}) async-start(bf16[16,24,896]{2,1,0:T(8,128)(2,1)} %add.16), calls=%async_computation.3 | async-start | bytes 1376256 | tf_op jit(solution)/shard_map/all_to_all | solution.py:1175
  155.3 21.1 %collective-permute-start.27 = (bf16[128,768]{1,0:T(8,128)(2,1)S(1)}, bf16[128,768]{1,0:T(8,128)(2,1)S(1)}, u32[]{:S(2)}, u32[]{:S(2)}) collective-permute-start(bf16[128,768]{1,0:T(8,128)(2,1)S(1)} %finish_input.1), channel_id=1, source_target_pairs={{0,0},{1,1},{16,2},{17,3},{8,4},{9,5},{24,6},{25,7},{2,8},{3,9},{1... | collective-permute-start | bytes 589832 | tf_op jit(solution)/shard_map/ppermute | solution.py:93
  164.8 13.7 %collective-permute-start.23 = (bf16[128,768]{1,0:T(8,128)(2,1)}, bf16[128,768]{1,0:T(8,128)(2,1)S(1)}, u32[]{:S(2)}, u32[]{:S(2)}) collective-permute-start(bf16[128,768]{1,0:T(8,128)(2,1)} %finish_output.1), channel_id=1, source_target_pairs={{0,0},{1,1},{16,2},{17,3},{8,4},{9,5},{24,6},{25,7},{2,8},{3,9},{1... | collective-permute-start | bytes 589832 | tf_op jit(solution)/shard_map/ppermute | solution.py:93
  (52 other events, 402.7 us)

commit v8 on v7

--- a/solution.py
+++ b/solution.py
@@ -355,7 +355,7 @@
         lse_ref[head : head + 1, :] = lses[head]
 
 
-def attend(idx, ids, q, kvs, width=256):
+def attend(idx, ids, q, kvs, width=512):
     rows, cols = q.shape
     parts = len(kvs)
     span = kvs[0].shape[1]
@@ -379,7 +379,7 @@
             jax.ShapeDtypeStruct((rows, cols), bf16),
             jax.ShapeDtypeStruct((8, rows), f32),
         ],
-        compiler_params=params(parts * 7 * 1024 * 1024),
+        compiler_params=params(parts * 10 * 1024 * 1024),
         cost_estimate=takes(7.1),
         name="attend",
     )(idx, ids, q, *kvs)
@@ -447,7 +447,7 @@
             other_refs[j - 1][1] = value_acc[j].astype(bf16)
 
 
-def attend_back(idx, ids, q, das, after, w_out, lse, kvs, width=256):
+def attend_back(idx, ids, q, das, after, w_out, lse, kvs, width=512):
     rows, cols = q.shape
     step, model = das[0].shape
     parts = len(kvs)
@@ -486,7 +486,7 @@
             jax.ShapeDtypeStruct((TP, step, cols), bf16),
         ]
         + [jax.ShapeDtypeStruct((2, span, cols), bf16)] * (parts - 1),
-        compiler_params=params(parts * 7 * 1024 * 1024),
+        compiler_params=params(parts * 12 * 1024 * 1024),
         cost_estimate=takes(10.7),
         name="attend_back",
     )(idx, ids, q, w_out, lse, *das, *after, *kvs)

time: 183 us -> 183 us (level)
  Pallas kernels: 45.1 us -> 42.3 us
  blocking collectives: 25.9 us -> 28.3 us
    all_gather x1, blocking collectives: 13.1 us -> 15.5 us  [local(): o_all = lax.all_gather(mixed, plan.tp, axis=0, tiled=False)]
  transfers between devices with their start and end apart: 35 -> 35, of which waited for: 12 -> 10; matrix products, arithmetic and copies ran while one was open for 1% -> 1% of each run, Pallas kernels for 21% -> 19%
where the time goes in v8:
time: 183 us; the launch traced here: 180 us
  starting transfers between devices  57 us (31%)
  Pallas kernels  42.3 us (23%)
  waiting for transfers between devices  35.4 us (19%)
  blocking collectives  28.3 us (15%)
  local copies, waits for them, and re-layouts  13.4 us (7%)
  other arithmetic  1.91 us (1%)
    ppermute x18, starting transfers between devices, partner(): return lax.ppermute(value, self.tp, table)  21.1 us
    all_gather x1, blocking collectives, local(): o_all = lax.all_gather(mixed, plan.tp, axis=0, tiled=False)  15.5 us
    unnamed x84, local copies, waits for them, and re-layouts  13.3 us
    all_gather x1, blocking collectives, local(): x_all = lax.all_gather(x_mine, plan.tp, axis=0, tiled=True)  12.8 us
    ppermute x4, starting transfers between devices, move(): return lax.ppermute(value, ALL, table)  11.7 us
    ppermute x4, waiting for transfers between devices, move(): return lax.ppermute(value, ALL, table)  10.3 us
    ppermute x5, waiting for transfers between devices, turn(): lax.ppermute(value, axis, [(i, (i + by) % count) for i in range(count)])  10.2 us
    pallas_call x1, Pallas kernels, attend_back(): pl.pallas_call(functools.partial(bwd_kernel, parts, len(after)), grid_spe...  7.62 us
  transfers between devices with their start and end apart: 35, of which 10 were waited for; matrix products, arithmetic and copies ran while one was open for 1% of the time, Pallas kernels for 19%

profile of v8, /device:TPU:2, one launch (start us, length us, event | category | flops | bytes accessed | tf_op | source)
XLA Modules:
  0.0 179.7 jit_solution(11923041031289116879)
XLA Ops:
  2.4 4.5 %collective-permute-start.3 = (bf16[136,768]{1,0:T(8,128)(2,1)S(1)}, bf16[136,768]{1,0:T(8,128)(2,1)S(1)}, u32[]{:S(2)}, u32[]{:S(2)}) collective-permute-start(bf16[136,768]{1,0:T(8,128)(2,1)S(1)} %pad_maximum_fusion.1), channel_id=1, source_target_pairs={{0,0},{1,1},{2,16},{3,17},{4,8},{5,9},{6,24},{7,25},{8,2},{9,3},{1... | collective-permute-start | bytes 626696 | tf_op jit(solution)/shard_map/ppermute | solution.py:93
  8.9 4.2 %all-to-all-start = ((bf16[4,24,2176]{2,1,0:T(8,128)(2,1)}), bf16[4,24,2176]{2,1,0:T(8,128)(2,1)S(1)}, u32[]{:S(2)}, u32[]{:S(2)}) async-start(bf16[4,24,2176]{2,1,0:T(8,128)(2,1)} %prepare.1), calls=%async_computation | async-start | bytes 835584 | tf_op jit(solution)/shard_map/all_to_all | solution.py:1073
  15.2 5.5 %all-to-all-done.got_ref = bf16[4,24,2176]{2,1,0:T(8,128)(2,1)S(1)} async-done(((bf16[4,24,2176]{2,1,0:T(8,128)(2,1)}), bf16[4,24,2176]{2,1,0:T(8,128)(2,1)S(1)}, u32[]{:S(2)}, u32[]{:S(2)}) %all-to-all-start) | async-done | bytes 417824 | tf_op jit(solution)/shard_map/all_to_all | solution.py:1073
  22.6 3.7 %collective-permute-start.1 = (bf16[96,640]{1,0:T(8,128)(2,1)S(1)}, bf16[96,640]{1,0:T(8,128)(2,1)S(1)}, u32[]{:S(2)}, u32[]{:S(2)}) collective-permute-start(bf16[96,640]{1,0:T(8,128)(2,1)S(1)} %get-tuple-element.120), channel_id=1, source_target_pairs={{0,4},{2,6},{4,0},{6,2},{1,5},{3,7},{5,1},{7,3},{8,12},{10,14},{12... | collective-permute-start | bytes 368648 | tf_op jit(solution)/shard_map/ppermute | solution.py:71
  26.3 3.8 %collective-permute-done.2 = bf16[96,640]{1,0:T(8,128)(2,1)S(1)} collective-permute-done((bf16[96,640]{1,0:T(8,128)(2,1)S(1)}, bf16[96,640]{1,0:T(8,128)(2,1)S(1)}, u32[]{:S(2)}, u32[]{:S(2)}) %collective-permute-start.2) | collective-permute-done | bytes 122912 | tf_op jit(solution)/shard_map/ppermute | solution.py:71
  30.1 4.5 %collective-permute-done.1 = bf16[96,640]{1,0:T(8,128)(2,1)S(1)} collective-permute-done((bf16[96,640]{1,0:T(8,128)(2,1)S(1)}, bf16[96,640]{1,0:T(8,128)(2,1)S(1)}, u32[]{:S(2)}, u32[]{:S(2)}) %collective-permute-start.1) | collective-permute-done | bytes 122912 | tf_op jit(solution)/shard_map/ppermute | solution.py:71
  34.6 5.5 %all-to-all-start.1 = ((bf16[4,296,768]{2,1,0:T(8,128)(2,1)}), bf16[4,296,768]{2,1,0:T(8,128)(2,1)S(1)}, u32[]{:S(2)}, u32[]{:S(2)}) async-start(bf16[4,296,768]{2,1,0:T(8,128)(2,1)} %get-tuple-element.125), calls=%async_computation.1 | async-start | bytes 3637248 | tf_op jit(solution)/shard_map/all_to_all | solution.py:1080
  40.4 12.8 %all_gather.9.x_ref = bf16[512,768]{1,0:T(8,128)(2,1)S(1)} all-gather(bf16[128,768]{1,0:T(8,128)(2,1)S(1)} %slice.9.x_ref), channel_id=1, replica_groups=mesh['gx'=2,'c'=2,'sz'=4,'sy'=2] {'gx','sy'}, dimensions={0}, use_global_device_ids=true | all-gather | bytes 983040 | tf_op jit(solution)/shard_map/all_gather | solution.py:1079
  53.2 3.3 %qkv.1 = (bf16[512,768]{1,0:T(8,128)(2,1)S(1)}, bf16[512,192]{1,0:T(8,128)(2,1)S(1)}, bf16[2,512,192]{2,1,0:T(8,128)(2,1)S(1)}, bf16[768,640]{1,0:T(8,128)(2,1)S(1)}, f32[8,768]{1,0:T(8,128)S(1)}) custom-call(s32[4]{0:T(128)S(1)} %pad_add_fusion.idx_ref, bf16[512,768]{1,0:T(8,128)(2,1)S(1)} %all_gather.9.x_ref, ...), custom_call_target="tpu_custom_call" | custom-call | flops 1104000000 | bytes 17712000 | tf_op jit(solution)/shard_map/qkv/pallas_call | solution.py:291
  62.8 3.8 %attend.1 = (bf16[512,192]{1,0:T(8,128)(2,1)S(1)}, f32[8,512]{1,0:T(8,128)S(1)}) custom-call(s32[4]{0:T(128)S(1)} %pad_add_fusion.idx_ref, f32[1,1024]{1,0:T(1,128)S(1)} %slice_convert_fusion.ids_ref, bf16[512,192]{1,0:T(8,128)(2,1)S(1)} %get-tuple-element.124.q_ref, bf16[2,512,192]{2,1,0:T(8,128)(2,1)S(1)} %get-tuple-element.128.refs_0_.refs_5_, ...), custom_call_target="tpu_custom_call" | custom-call | flops 1632999936 | bytes 26199000 | tf_op jit(solution)/shard_map/attend/pallas_call | solution.py:362
  66.7 15.5 %all-gather = bf16[2048,192]{1,0:T(8,128)(2,1)} all-gather(bf16[512,192]{1,0:T(8,128)(2,1)S(1)} %get-tuple-element.129), channel_id=2, replica_groups=mesh['gx'=2,'c'=2,'sz'=4,'sy'=2] {'gx','sy'}, dimensions={0}, use_global_device_ids=true | all-gather | bytes 983040 | tf_op jit(solution)/shard_map/all_gather | solution.py:1112
  84.5 2.1 %collective-permute-done.10.refs_1_ = bf16[4,296,768]{2,1,0:T(8,128)(2,1)S(1)} collective-permute-done((bf16[4,296,768]{2,1,0:T(8,128)(2,1)S(1)}, bf16[4,296,768]{2,1,0:T(8,128)(2,1)S(1)}, u32[]{:S(2)}, u32[]{:S(2)}) %collective-permute-start.10) | collective-permute-done | bytes 1818656 | tf_op jit(solution)/shard_map/ppermute | solution.py:52
  86.6 6.4 %mlp.1 = (f32[128,768]{1,0:T(8,128)S(1)}, bf16[512,768]{1,0:T(8,128)(2,1)S(1)}, bf16[512,768]{1,0:T(8,128)(2,1)S(1)}, bf16[512,768]{1,0:T(8,128)(2,1)S(1)}, f32[...) custom-call(s32[4]{0:T(128)S(1)} %pad_add_fusion.idx_ref, ...), custom_call_target="tpu_custom_call" | custom-call | flops 2415000064 | bytes 38745000 | tf_op jit(solution)/shard_map/mlp/pallas_call | solution.py:636
  97.1 4.1 %mlp_weight_grads.1 = (bf16[4,200,768]{2,1,0:T(8,128)(2,1)S(1)}, bf16[4,200,768]{2,1,0:T(8,128)(2,1)S(1)}, bf16[128,768]{1,0:T(8,128)(2,1)S(1)}, bf16[128,768]{1...) custom-call(s32[4]{0:T(128)S(1)} %pad_add_fusion.idx_ref, ...), custom_call_target="tpu_custom_call" | custom-call | flops 1748000000 | bytes 28044000 | tf_op jit(solution)/shard_map/mlp_weight_grads/pallas_call | solution.py:722
  102.8 3.1 %collective-permute-done.13.refs_3_ = bf16[128,768]{1,0:T(8,128)(2,1)S(1)} collective-permute-done((bf16[128,768]{1,0:T(8,128)(2,1)S(1)}, bf16[128,768]{1,0:T(8,128)(2,1)S(1)}, u32[]{:S(2)}, u32[]{:S(2)}) %collective-permute-start.13) | collective-permute-done | bytes 196640 | tf_op jit(solution)/shard_map/ppermute | solution.py:61
  112.6 5.2 %all-to-all-start.2 = ((bf16[4,200,768]{2,1,0:T(8,128)(2,1)}), bf16[4,200,768]{2,1,0:T(8,128)(2,1)S(1)}, u32[]{:S(2)}, u32[]{:S(2)}) async-start(bf16[4,200,768]{2,1,0:T(8,128)(2,1)} %add.15.refs_4_), calls=%async_computation.2 | async-start | bytes 2457600 | tf_op jit(solution)/shard_map/all_to_all | solution.py:1148
  125.0 7.6 %attend_back.1 = (bf16[512,192]{1,0:T(8,128)(2,1)S(1)}, f32[2,512,192]{2,1,0:T(8,128)S(1)}, bf16[4,128,192]{2,1,0:T(8,128)(2,1)S(1)}, bf16[2,512,192]{2,1,0:T(8,128)(2,1)S(1)}) custom-call(s32[4]{0:T(128)S(1)} %pad_add_fusion.idx_ref, f32[1,1024]{1,0:T(1,128)S(1)} %slice_convert_fusion.ids_ref, bf16[512,192]{1,0:T(8,128)(2,1)S(1)} %copy-done.24, ...), custom_call_target="tpu_custom_call" | custom-call | flops 2460999936 | bytes 39483000 | tf_op jit(solution)/shard_map/attend_back/pallas_call | solution.py:455
  134.7 3.9 %normed_back.1 = (bf16[128,768]{1,0:T(8,128)(2,1)S(1)}, bf16[128,768]{1,0:T(8,128)(2,1)S(1)}, bf16[128,768]{1,0:T(8,128)(2,1)S(1)}, bf16[128,768]{1,0:T(8,128)(2...) custom-call(s32[4]{0:T(128)S(1)} %pad_add_fusion.idx_ref, ...), custom_call_target="tpu_custom_call" | custom-call | flops 2990000128 | bytes 47970000 | tf_op jit(solution)/shard_map/normed_back/pallas_call | solution.py:983
  143.9 3.3 %all-to-all-done.2.refs_0_ = bf16[4,200,768]{2,1,0:T(8,128)(2,1)S(1)} async-done(((bf16[4,200,768]{2,1,0:T(8,128)(2,1)}), bf16[4,200,768]{2,1,0:T(8,128)(2,1)S(1)}, u32[]{:S(2)}, u32[]{:S(2)}) %all-to-all-start.2) | async-done | bytes 1228832 | tf_op jit(solution)/shard_map/all_to_all | solution.py:1148
  148.7 4.7 %all-to-all-start.3 = ((bf16[16,24,896]{2,1,0:T(8,128)(2,1)}), bf16[16,24,896]{2,1,0:T(8,128)(2,1)S(1)}, u32[]{:S(2)}, u32[]{:S(2)}) async-start(bf16[16,24,896]{2,1,0:T(8,128)(2,1)} %add.16), calls=%async_computation.3 | async-start | bytes 1376256 | tf_op jit(solution)/shard_map/all_to_all | solution.py:1175
  155.8 3.4 %collective-permute-start.27 = (bf16[128,768]{1,0:T(8,128)(2,1)S(1)}, bf16[128,768]{1,0:T(8,128)(2,1)S(1)}, u32[]{:S(2)}, u32[]{:S(2)}) collective-permute-start(bf16[128,768]{1,0:T(8,128)(2,1)S(1)} %finish_input.1), channel_id=1, source_target_pairs={{0,0},{1,1},{16,2},{17,3},{8,4},{9,5},{24,6},{25,7},{2,8},{3,9},{1... | collective-permute-start | bytes 589832 | tf_op jit(solution)/shard_map/ppermute | solution.py:93
  162.7 2.1 %finish_output.1 = bf16[128,768]{1,0:T(8,128)(2,1)} custom-call(f32[128,768]{1,0:T(8,128)} %copy-done.12, f32[8,768]{1,0:T(8,128)} %copy-done.18, bf16[128,768]{1,0:T(8,128)(2,1)} %copy-done.13, bf16[128,768]{1,0:T(8,128)(2,1)} %copy-done.37, bf16[128,768]{1,0:T(8,128)(2,1)} %copy-done.38, bf16[128,768]{1,0:T(8,128)(2,1)} %copy-done.39), custom_call_target="tpu_custom_call" | custom-call | flops 483000000 | bytes 7749000 | tf_op jit(solution)/shard_map/finish_output/pallas_call | solution.py:861
  168.3 8.2 %collective-permute-done.27.second_ref = bf16[128,768]{1,0:T(8,128)(2,1)S(1)} collective-permute-done((bf16[128,768]{1,0:T(8,128)(2,1)S(1)}, bf16[128,768]{1,0:T(8,128)(2,1)S(1)}, u32[]{:S(2)}, u32[]{:S(2)}) %collective-permute-start.27) | collective-permute-done | bytes 196640 | tf_op jit(solution)/shard_map/ppermute | solution.py:93
  176.5 2.1 %collective-permute-done.23.first_ref = bf16[128,768]{1,0:T(8,128)(2,1)S(1)} collective-permute-done((bf16[128,768]{1,0:T(8,128)(2,1)}, bf16[128,768]{1,0:T(8,128)(2,1)S(1)}, u32[]{:S(2)}, u32[]{:S(2)}) %collective-permute-start.23) | collective-permute-done | bytes 196640 | tf_op jit(solution)/shard_map/ppermute | solution.py:93
  (159 shorter events, 55.1 us)
Async XLA Ops:
  2.4 24.0 %collective-permute-start.3 = (bf16[136,768]{1,0:T(8,128)(2,1)S(1)}, bf16[136,768]{1,0:T(8,128)(2,1)S(1)}, u32[]{:S(2)}, u32[]{:S(2)}) collective-permute-start(bf16[136,768]{1,0:T(8,128)(2,1)S(1)} %pad_maximum_fusion.1), channel_id=1, source_target_pairs={{0,0},{1,1},{2,16},{3,17},{4,8},{5,9},{6,24},{7,25},{8,2},{9,3},{1... | collective-permute-start | bytes 626696 | tf_op jit(solution)/shard_map/ppermute | solution.py:93
  8.9 11.8 %all-to-all-start = ((bf16[4,24,2176]{2,1,0:T(8,128)(2,1)}), bf16[4,24,2176]{2,1,0:T(8,128)(2,1)S(1)}, u32[]{:S(2)}, u32[]{:S(2)}) async-start(bf16[4,24,2176]{2,1,0:T(8,128)(2,1)} %prepare.1), calls=%async_computation | async-start | bytes 835584 | tf_op jit(solution)/shard_map/all_to_all | solution.py:1073
  13.2 13.1 %collective-permute-start.4 = (bf16[128,768]{1,0:T(8,128)(2,1)S(1)}, bf16[128,768]{1,0:T(8,128)(2,1)S(1)}, u32[]{:S(2)}, u32[]{:S(2)}) collective-permute-start(bf16[128,768]{1,0:T(8,128)(2,1)S(1)} %fusion), channel_id=1, source_target_pairs={{0,0},{1,1},{2,16},{3,17},{4,8},{5,9},{6,24},{7,25},{8,2},{9,3},{1... | collective-permute-start | bytes 589832 | tf_op jit(solution)/shard_map/ppermute | solution.py:93
  22.6 12.0 %collective-permute-start.1 = (bf16[96,640]{1,0:T(8,128)(2,1)S(1)}, bf16[96,640]{1,0:T(8,128)(2,1)S(1)}, u32[]{:S(2)}, u32[]{:S(2)}) collective-permute-start(bf16[96,640]{1,0:T(8,128)(2,1)S(1)} %get-tuple-element.120), channel_id=1, source_target_pairs={{0,4},{2,6},{4,0},{6,2},{1,5},{3,7},{5,1},{7,3},{8,12},{10,14},{12... | collective-permute-start | bytes 368648 | tf_op jit(solution)/shard_map/ppermute | solution.py:71
  26.3 8.3 %collective-permute-start = (bf16[96,640]{1,0:T(8,128)(2,1)S(1)}, bf16[96,640]{1,0:T(8,128)(2,1)S(1)}, u32[]{:S(2)}, u32[]{:S(2)}) collective-permute-start(bf16[96,640]{1,0:T(8,128)(2,1)S(1)} %get-tuple-element.120), channel_id=1, source_target_pairs={{0,6},{2,0},{4,2},{6,4},{1,7},{3,1},{5,3},{7,5},{8,14},{10,8},{12,... | collective-permute-start | bytes 368648 | tf_op jit(solution)/shard_map/ppermute | solution.py:71
  34.6 48.2 %all-to-all-start.1 = ((bf16[4,296,768]{2,1,0:T(8,128)(2,1)}), bf16[4,296,768]{2,1,0:T(8,128)(2,1)S(1)}, u32[]{:S(2)}, u32[]{:S(2)}) async-start(bf16[4,296,768]{2,1,0:T(8,128)(2,1)} %get-tuple-element.125), calls=%async_computation.1 | async-start | bytes 3637248 | tf_op jit(solution)/shard_map/all_to_all | solution.py:1080
  40.2 13.0 %collective-permute-start.5 = (bf16[4,96,640]{2,1,0:T(8,128)(2,1)S(1)}, bf16[4,96,640]{2,1,0:T(8,128)(2,1)}, u32[]{:S(2)}, u32[]{:S(2)}) collective-permute-start(bf16[4,96,640]{2,1,0:T(8,128)(2,1)S(1)} %pad_maximum_fusion.refs_0_), channel_id=1, source_target_pairs={{0,8},{8,0},{1,9},{9,1},{2,10},{10,2},{3,11},{11,3},{4,12},{12,4},... | collective-permute-start | bytes 1474568 | tf_op jit(solution)/shard_map/ppermute | solution.py:52
  59.2 22.9 %collective-permute-start.9 = (bf16[128,768]{1,0:T(8,128)(2,1)S(1)}, bf16[128,768]{1,0:T(8,128)(2,1)S(1)}, u32[]{:S(2)}, u32[]{:S(2)}) collective-permute-start(bf16[128,768]{1,0:T(8,128)(2,1)S(1)} %collective-permute-done.4.refs_0_.dm_ref), channel_id=1, source_target_pairs={{0,17},{1,16},{16,1},{17,0},{2,19},{3,18},{18,3},{19,2},{4,21},{5,... | collective-permute-start | bytes 589832 | tf_op jit(solution)/shard_map/ppermute | solution.py:61
  60.8 21.4 %collective-permute-start.8 = (bf16[128,768]{1,0:T(8,128)(2,1)S(1)}, bf16[128,768]{1,0:T(8,128)(2,1)S(1)}, u32[]{:S(2)}, u32[]{:S(2)}) collective-permute-start(bf16[128,768]{1,0:T(8,128)(2,1)S(1)} %collective-permute-done.4.refs_0_.dm_ref), channel_id=1, source_target_pairs={{0,16},{1,17},{16,0},{17,1},{2,18},{3,19},{18,2},{19,3},{4,20},{5,... | collective-permute-start | bytes 589832 | tf_op jit(solution)/shard_map/ppermute | solution.py:61
  61.7 20.4 %collective-permute-start.7 = (bf16[128,768]{1,0:T(8,128)(2,1)S(1)}, bf16[128,768]{1,0:T(8,128)(2,1)S(1)}, u32[]{:S(2)}, u32[]{:S(2)}) collective-permute-start(bf16[128,768]{1,0:T(8,128)(2,1)S(1)} %collective-permute-done.4.refs_0_.dm_ref), channel_id=1, source_target_pairs={{0,1},{1,0},{16,17},{17,16},{2,3},{3,2},{18,19},{19,18},{4,5},{5,4... | collective-permute-start | bytes 589832 | tf_op jit(solution)/shard_map/ppermute | solution.py:61
  95.8 10.1 %collective-permute-start.13 = (bf16[128,768]{1,0:T(8,128)(2,1)S(1)}, bf16[128,768]{1,0:T(8,128)(2,1)S(1)}, u32[]{:S(2)}, u32[]{:S(2)}) collective-permute-start(bf16[128,768]{1,0:T(8,128)(2,1)S(1)} %get-tuple-element.146), channel_id=1, source_target_pairs={{0,17},{1,16},{16,1},{17,0},{2,19},{3,18},{18,3},{19,2},{4,21},{5,... | collective-permute-start | bytes 589832 | tf_op jit(solution)/shard_map/ppermute | solution.py:61
  107.7 12.1 %collective-permute-start.16 = (bf16[128,768]{1,0:T(8,128)(2,1)S(1)}, bf16[128,768]{1,0:T(8,128)(2,1)}, u32[]{:S(2)}, u32[]{:S(2)}) collective-permute-start(bf16[128,768]{1,0:T(8,128)(2,1)S(1)} %get-tuple-element.160.refs_2_.refs_0_), channel_id=1, source_target_pairs={{0,17},{1,16},{16,1},{17,0},{2,19},{3,18},{18,3},{19,2},{4,21},{5,... | collective-permute-start | bytes 589832 | tf_op jit(solution)/shard_map/ppermute | solution.py:61
  109.4 11.9 %collective-permute-start.15 = (bf16[128,768]{1,0:T(8,128)(2,1)S(1)}, bf16[128,768]{1,0:T(8,128)(2,1)}, u32[]{:S(2)}, u32[]{:S(2)}) collective-permute-start(bf16[128,768]{1,0:T(8,128)(2,1)S(1)} %get-tuple-element.160.refs_2_.refs_0_), channel_id=1, source_target_pairs={{0,16},{1,17},{16,0},{17,1},{2,18},{3,19},{18,2},{19,3},{4,20},{5,... | collective-permute-start | bytes 589832 | tf_op jit(solution)/shard_map/ppermute | solution.py:61
  110.6 10.7 %collective-permute-start.14 = (bf16[128,768]{1,0:T(8,128)(2,1)S(1)}, bf16[128,768]{1,0:T(8,128)(2,1)}, u32[]{:S(2)}, u32[]{:S(2)}) collective-permute-start(bf16[128,768]{1,0:T(8,128)(2,1)S(1)} %get-tuple-element.160.refs_2_.refs_0_), channel_id=1, source_target_pairs={{0,1},{1,0},{16,17},{17,16},{2,3},{3,2},{18,19},{19,18},{4,5},{5,4... | collective-permute-start | bytes 589832 | tf_op jit(solution)/shard_map/ppermute | solution.py:61
  112.6 34.6 %all-to-all-start.2 = ((bf16[4,200,768]{2,1,0:T(8,128)(2,1)}), bf16[4,200,768]{2,1,0:T(8,128)(2,1)S(1)}, u32[]{:S(2)}, u32[]{:S(2)}) async-start(bf16[4,200,768]{2,1,0:T(8,128)(2,1)} %add.15.refs_4_), calls=%async_computation.2 | async-start | bytes 2457600 | tf_op jit(solution)/shard_map/all_to_all | solution.py:1148
  117.8 14.8 %collective-permute-start.18 = (bf16[128,768]{1,0:T(8,128)(2,1)S(1)}, bf16[128,768]{1,0:T(8,128)(2,1)S(1)}, u32[]{:S(2)}, u32[]{:S(2)}) collective-permute-start(bf16[128,768]{1,0:T(8,128)(2,1)S(1)} %get-tuple-element.167), channel_id=1, source_target_pairs={{0,1},{1,0},{16,17},{17,16},{2,3},{3,2},{18,19},{19,18},{4,5},{5,4... | collective-permute-start | bytes 589832 | tf_op jit(solution)/shard_map/ppermute | solution.py:61
  118.9 13.8 %collective-permute-start.19 = (bf16[128,768]{1,0:T(8,128)(2,1)S(1)}, bf16[128,768]{1,0:T(8,128)(2,1)S(1)}, u32[]{:S(2)}, u32[]{:S(2)}) collective-permute-start(bf16[128,768]{1,0:T(8,128)(2,1)S(1)} %copy-done.9), channel_id=1, source_target_pairs={{0,16},{1,17},{16,0},{17,1},{2,18},{3,19},{18,2},{19,3},{4,20},{5,... | collective-permute-start | bytes 589832 | tf_op jit(solution)/shard_map/ppermute | solution.py:61
  119.8 12.8 %collective-permute-start.20 = (bf16[128,768]{1,0:T(8,128)(2,1)S(1)}, bf16[128,768]{1,0:T(8,128)(2,1)S(1)}, u32[]{:S(2)}, u32[]{:S(2)}) collective-permute-start(bf16[128,768]{1,0:T(8,128)(2,1)S(1)} %get-tuple-element.169), channel_id=1, source_target_pairs={{0,17},{1,16},{16,1},{17,0},{2,19},{3,18},{18,3},{19,2},{4,21},{5,... | collective-permute-start | bytes 589832 | tf_op jit(solution)/shard_map/ppermute | solution.py:61
  139.4 14.0 %collective-permute-start.24 = (bf16[128,768]{1,0:T(8,128)(2,1)S(1)}, bf16[128,768]{1,0:T(8,128)(2,1)S(1)}, u32[]{:S(2)}, u32[]{:S(2)}) collective-permute-start(bf16[128,768]{1,0:T(8,128)(2,1)S(1)} %get-tuple-element.194), channel_id=1, source_target_pairs={{0,1},{1,0},{16,17},{17,16},{2,3},{3,2},{18,19},{19,18},{4,5},{5,4... | collective-permute-start | bytes 589832 | tf_op jit(solution)/shard_map/ppermute | solution.py:61
  140.5 12.9 %collective-permute-start.25 = (bf16[128,768]{1,0:T(8,128)(2,1)S(1)}, bf16[128,768]{1,0:T(8,128)(2,1)S(1)}, u32[]{:S(2)}, u32[]{:S(2)}) collective-permute-start(bf16[128,768]{1,0:T(8,128)(2,1)S(1)} %get-tuple-element.195), channel_id=1, source_target_pairs={{0,16},{1,17},{16,0},{17,1},{2,18},{3,19},{18,2},{19,3},{4,20},{5,... | collective-permute-start | bytes 589832 | tf_op jit(solution)/shard_map/ppermute | solution.py:61
  141.5 12.0 %collective-permute-start.26 = (bf16[128,768]{1,0:T(8,128)(2,1)S(1)}, bf16[128,768]{1,0:T(8,128)(2,1)S(1)}, u32[]{:S(2)}, u32[]{:S(2)}) collective-permute-start(bf16[128,768]{1,0:T(8,128)(2,1)S(1)} %get-tuple-element.196), channel_id=1, source_target_pairs={{0,17},{1,16},{16,1},{17,0},{2,19},{3,18},{18,3},{19,2},{4,21},{5,... | collective-permute-start | bytes 589832 | tf_op jit(solution)/shard_map/ppermute | solution.py:61
  148.7 29.9 %all-to-all-start.3 = ((bf16[16,24,896]{2,1,0:T(8,128)(2,1)}), bf16[16,24,896]{2,1,0:T(8,128)(2,1)S(1)}, u32[]{:S(2)}, u32[]{:S(2)}) async-start(bf16[16,24,896]{2,1,0:T(8,128)(2,1)} %add.16), calls=%async_computation.3 | async-start | bytes 1376256 | tf_op jit(solution)/shard_map/all_to_all | solution.py:1175
  155.8 20.7 %collective-permute-start.27 = (bf16[128,768]{1,0:T(8,128)(2,1)S(1)}, bf16[128,768]{1,0:T(8,128)(2,1)S(1)}, u32[]{:S(2)}, u32[]{:S(2)}) collective-permute-start(bf16[128,768]{1,0:T(8,128)(2,1)S(1)} %finish_input.1), channel_id=1, source_target_pairs={{0,0},{1,1},{16,2},{17,3},{8,4},{9,5},{24,6},{25,7},{2,8},{3,9},{1... | collective-permute-start | bytes 589832 | tf_op jit(solution)/shard_map/ppermute | solution.py:93
  164.8 13.8 %collective-permute-start.23 = (bf16[128,768]{1,0:T(8,128)(2,1)}, bf16[128,768]{1,0:T(8,128)(2,1)S(1)}, u32[]{:S(2)}, u32[]{:S(2)}) collective-permute-start(bf16[128,768]{1,0:T(8,128)(2,1)} %finish_output.1), channel_id=1, source_target_pairs={{0,0},{1,1},{16,2},{17,3},{8,4},{9,5},{24,6},{25,7},{2,8},{3,9},{1... | collective-permute-start | bytes 589832 | tf_op jit(solution)/shard_map/ppermute | solution.py:93
  (52 other events, 392.9 us)

commit v9 on v8

--- a/solution.py
+++ b/solution.py
@@ -861,6 +861,7 @@
     return pl.pallas_call(
         output_kernel,
         out_shape=jax.ShapeDtypeStruct(r_own.shape, bf16),
+        compiler_params=small_params(),
         cost_estimate=takes(2.1),
         name="finish_output",
     )(r_own, vecs, *parts)

time: 183 us -> 183 us (level)
  Pallas kernels: 42.3 us -> 40.4 us
    pallas_call x1, Pallas kernels: 2.08 us -> 0.13 us  [finish_output(): pl.pallas_call(output_kernel, out_shape=jax.ShapeDtypeStruct(r_own.shape,...]
    unnamed x84 -> x90, local copies, waits for them, and re-layouts: 13.3 us -> 13.4 us
  transfers between devices with their start and end apart: 35 -> 35, of which waited for: 10 -> 11; matrix products, arithmetic and copies ran while one was open for 1% -> 1% of each run, Pallas kernels for 19% -> 18%
where the time goes in v9:
time: 183 us; the launch traced here: 180 us
  starting transfers between devices  58.1 us (32%)
  Pallas kernels  40.4 us (22%)
  waiting for transfers between devices  36.5 us (20%)
  blocking collectives  28.3 us (15%)
  local copies, waits for them, and re-layouts  13.5 us (7%)
  other arithmetic  1.91 us (1%)
    ppermute x18, starting transfers between devices, partner(): return lax.ppermute(value, self.tp, table)  21.1 us
    all_gather x1, blocking collectives, local(): o_all = lax.all_gather(mixed, plan.tp, axis=0, tiled=False)  15.5 us
    unnamed x90, local copies, waits for them, and re-layouts  13.4 us
    all_gather x1, blocking collectives, local(): x_all = lax.all_gather(x_mine, plan.tp, axis=0, tiled=True)  12.8 us
    ppermute x4, starting transfers between devices, move(): return lax.ppermute(value, ALL, table)  12.3 us
    ppermute x4, waiting for transfers between devices, move(): return lax.ppermute(value, ALL, table)  11.6 us
    ppermute x5, waiting for transfers between devices, turn(): lax.ppermute(value, axis, [(i, (i + by) % count) for i in range(count)])  10.2 us
    pallas_call x1, Pallas kernels, attend_back(): pl.pallas_call(functools.partial(bwd_kernel, parts, len(after)), grid_spe...  7.61 us
  transfers between devices with their start and end apart: 35, of which 11 were waited for; matrix products, arithmetic and copies ran while one was open for 1% of the time, Pallas kernels for 18%

profile of v9, /device:TPU:2, one launch (start us, length us, event | category | flops | bytes accessed | tf_op | source)
XLA Modules:
  0.0 180.0 jit_solution(12654548931229755549)
XLA Ops:
  2.4 4.5 %collective-permute-start.3 = (bf16[136,768]{1,0:T(8,128)(2,1)S(1)}, bf16[136,768]{1,0:T(8,128)(2,1)S(1)}, u32[]{:S(2)}, u32[]{:S(2)}) collective-permute-start(bf16[136,768]{1,0:T(8,128)(2,1)S(1)} %pad_maximum_fusion.1), channel_id=1, source_target_pairs={{0,0},{1,1},{2,16},{3,17},{4,8},{5,9},{6,24},{7,25},{8,2},{9,3},{1... | collective-permute-start | bytes 626696 | tf_op jit(solution)/shard_map/ppermute | solution.py:93
  6.9 2.0 %prepare.1 = bf16[4,24,2176]{2,1,0:T(8,128)(2,1)} custom-call(bf16[24,768]{1,0:T(8,128)(2,1)} %q_ref.1, bf16[24,768]{1,0:T(8,128)(2,1)} %k_ref.1, bf16[24,768]{1,0:T(8,128)(2,1)} %v_ref.1, bf16[24,3072]{1,0:T(8,128)(2,1)} %up_ref.1, bf16[24,768]{1,0:T(8,128)(2,1)} %out_ref.1, bf16[1,24]{1,0:T(2,128)(2,1)} %bitcast.50, bf16[1,24]{1,0:T(2,128)(2,1)} %bitcast.51, ...), custom_call_target="tpu_custom_call" | custom-call | flops 437000000 | bytes 7011000 | tf_op jit(solution)/shard_map/prepare/pallas_call | solution.py:188
  8.9 4.2 %all-to-all-start = ((bf16[4,24,2176]{2,1,0:T(8,128)(2,1)}), bf16[4,24,2176]{2,1,0:T(8,128)(2,1)S(1)}, u32[]{:S(2)}, u32[]{:S(2)}) async-start(bf16[4,24,2176]{2,1,0:T(8,128)(2,1)} %prepare.1), calls=%async_computation | async-start | bytes 835584 | tf_op jit(solution)/shard_map/all_to_all | solution.py:1074
  15.2 5.5 %all-to-all-done.got_ref = bf16[4,24,2176]{2,1,0:T(8,128)(2,1)S(1)} async-done(((bf16[4,24,2176]{2,1,0:T(8,128)(2,1)}), bf16[4,24,2176]{2,1,0:T(8,128)(2,1)S(1)}, u32[]{:S(2)}, u32[]{:S(2)}) %all-to-all-start) | async-done | bytes 417824 | tf_op jit(solution)/shard_map/all_to_all | solution.py:1074
  22.6 3.7 %collective-permute-start.1 = (bf16[96,640]{1,0:T(8,128)(2,1)S(1)}, bf16[96,640]{1,0:T(8,128)(2,1)S(1)}, u32[]{:S(2)}, u32[]{:S(2)}) collective-permute-start(bf16[96,640]{1,0:T(8,128)(2,1)S(1)} %get-tuple-element.120), channel_id=1, source_target_pairs={{0,4},{2,6},{4,0},{6,2},{1,5},{3,7},{5,1},{7,3},{8,12},{10,14},{12... | collective-permute-start | bytes 368648 | tf_op jit(solution)/shard_map/ppermute | solution.py:71
  26.3 3.8 %collective-permute-done.2 = bf16[96,640]{1,0:T(8,128)(2,1)S(1)} collective-permute-done((bf16[96,640]{1,0:T(8,128)(2,1)S(1)}, bf16[96,640]{1,0:T(8,128)(2,1)S(1)}, u32[]{:S(2)}, u32[]{:S(2)}) %collective-permute-start.2) | collective-permute-done | bytes 122912 | tf_op jit(solution)/shard_map/ppermute | solution.py:71
  30.1 4.5 %collective-permute-done.1 = bf16[96,640]{1,0:T(8,128)(2,1)S(1)} collective-permute-done((bf16[96,640]{1,0:T(8,128)(2,1)S(1)}, bf16[96,640]{1,0:T(8,128)(2,1)S(1)}, u32[]{:S(2)}, u32[]{:S(2)}) %collective-permute-start.1) | collective-permute-done | bytes 122912 | tf_op jit(solution)/shard_map/ppermute | solution.py:71
  34.6 5.5 %all-to-all-start.1 = ((bf16[4,296,768]{2,1,0:T(8,128)(2,1)}), bf16[4,296,768]{2,1,0:T(8,128)(2,1)S(1)}, u32[]{:S(2)}, u32[]{:S(2)}) async-start(bf16[4,296,768]{2,1,0:T(8,128)(2,1)} %get-tuple-element.125), calls=%async_computation.1 | async-start | bytes 3637248 | tf_op jit(solution)/shard_map/all_to_all | solution.py:1081
  40.4 12.8 %all_gather.9.x_ref = bf16[512,768]{1,0:T(8,128)(2,1)S(1)} all-gather(bf16[128,768]{1,0:T(8,128)(2,1)S(1)} %slice.9.x_ref), channel_id=1, replica_groups=mesh['gx'=2,'c'=2,'sz'=4,'sy'=2] {'gx','sy'}, dimensions={0}, use_global_device_ids=true | all-gather | bytes 983040 | tf_op jit(solution)/shard_map/all_gather | solution.py:1080
  53.2 3.3 %qkv.1 = (bf16[512,768]{1,0:T(8,128)(2,1)S(1)}, bf16[512,192]{1,0:T(8,128)(2,1)S(1)}, bf16[2,512,192]{2,1,0:T(8,128)(2,1)S(1)}, bf16[768,640]{1,0:T(8,128)(2,1)S(1)}, f32[8,768]{1,0:T(8,128)S(1)}) custom-call(s32[4]{0:T(128)S(1)} %pad_add_fusion.idx_ref, bf16[512,768]{1,0:T(8,128)(2,1)S(1)} %all_gather.9.x_ref, ...), custom_call_target="tpu_custom_call" | custom-call | flops 1104000000 | bytes 17712000 | tf_op jit(solution)/shard_map/qkv/pallas_call | solution.py:291
  62.7 3.8 %attend.1 = (bf16[512,192]{1,0:T(8,128)(2,1)S(1)}, f32[8,512]{1,0:T(8,128)S(1)}) custom-call(s32[4]{0:T(128)S(1)} %pad_add_fusion.idx_ref, f32[1,1024]{1,0:T(1,128)S(1)} %slice_convert_fusion.ids_ref, bf16[512,192]{1,0:T(8,128)(2,1)S(1)} %get-tuple-element.124.q_ref, bf16[2,512,192]{2,1,0:T(8,128)(2,1)S(1)} %get-tuple-element.128.refs_0_.refs_5_, ...), custom_call_target="tpu_custom_call" | custom-call | flops 1632999936 | bytes 26199000 | tf_op jit(solution)/shard_map/attend/pallas_call | solution.py:362
  66.6 15.5 %all-gather = bf16[2048,192]{1,0:T(8,128)(2,1)} all-gather(bf16[512,192]{1,0:T(8,128)(2,1)S(1)} %get-tuple-element.129), channel_id=2, replica_groups=mesh['gx'=2,'c'=2,'sz'=4,'sy'=2] {'gx','sy'}, dimensions={0}, use_global_device_ids=true | all-gather | bytes 983040 | tf_op jit(solution)/shard_map/all_gather | solution.py:1113
  84.5 2.1 %collective-permute-done.10.refs_1_ = bf16[4,296,768]{2,1,0:T(8,128)(2,1)S(1)} collective-permute-done((bf16[4,296,768]{2,1,0:T(8,128)(2,1)S(1)}, bf16[4,296,768]{2,1,0:T(8,128)(2,1)S(1)}, u32[]{:S(2)}, u32[]{:S(2)}) %collective-permute-start.10) | collective-permute-done | bytes 1818656 | tf_op jit(solution)/shard_map/ppermute | solution.py:52
  86.6 6.4 %mlp.1 = (f32[128,768]{1,0:T(8,128)S(1)}, bf16[512,768]{1,0:T(8,128)(2,1)S(1)}, bf16[512,768]{1,0:T(8,128)(2,1)S(1)}, bf16[512,768]{1,0:T(8,128)(2,1)S(1)}, f32[...) custom-call(s32[4]{0:T(128)S(1)} %pad_add_fusion.idx_ref, ...), custom_call_target="tpu_custom_call" | custom-call | flops 2415000064 | bytes 38745000 | tf_op jit(solution)/shard_map/mlp/pallas_call | solution.py:636
  96.6 4.1 %mlp_weight_grads.1 = (bf16[4,200,768]{2,1,0:T(8,128)(2,1)S(1)}, bf16[4,200,768]{2,1,0:T(8,128)(2,1)S(1)}, bf16[128,768]{1,0:T(8,128)(2,1)S(1)}, bf16[128,768]{1...) custom-call(s32[4]{0:T(128)S(1)} %pad_add_fusion.idx_ref, ...), custom_call_target="tpu_custom_call" | custom-call | flops 1748000000 | bytes 28044000 | tf_op jit(solution)/shard_map/mlp_weight_grads/pallas_call | solution.py:722
  102.3 3.1 %collective-permute-done.13.refs_3_ = bf16[128,768]{1,0:T(8,128)(2,1)S(1)} collective-permute-done((bf16[128,768]{1,0:T(8,128)(2,1)S(1)}, bf16[128,768]{1,0:T(8,128)(2,1)S(1)}, u32[]{:S(2)}, u32[]{:S(2)}) %collective-permute-start.13) | collective-permute-done | bytes 196640 | tf_op jit(solution)/shard_map/ppermute | solution.py:61
  112.0 5.2 %all-to-all-start.2 = ((bf16[4,200,768]{2,1,0:T(8,128)(2,1)}), bf16[4,200,768]{2,1,0:T(8,128)(2,1)S(1)}, u32[]{:S(2)}, u32[]{:S(2)}) async-start(bf16[4,200,768]{2,1,0:T(8,128)(2,1)} %add.15.refs_4_), calls=%async_computation.2 | async-start | bytes 2457600 | tf_op jit(solution)/shard_map/all_to_all | solution.py:1149
  124.5 7.6 %attend_back.1 = (bf16[512,192]{1,0:T(8,128)(2,1)S(1)}, f32[2,512,192]{2,1,0:T(8,128)S(1)}, bf16[4,128,192]{2,1,0:T(8,128)(2,1)S(1)}, bf16[2,512,192]{2,1,0:T(8,128)(2,1)S(1)}) custom-call(s32[4]{0:T(128)S(1)} %pad_add_fusion.idx_ref, f32[1,1024]{1,0:T(1,128)S(1)} %slice_convert_fusion.ids_ref, bf16[512,192]{1,0:T(8,128)(2,1)S(1)} %copy-done.30, ...), custom_call_target="tpu_custom_call" | custom-call | flops 2460999936 | bytes 39483000 | tf_op jit(solution)/shard_map/attend_back/pallas_call | solution.py:455
  135.5 3.9 %normed_back.1 = (bf16[128,768]{1,0:T(8,128)(2,1)S(1)}, bf16[128,768]{1,0:T(8,128)(2,1)S(1)}, bf16[128,768]{1,0:T(8,128)(2,1)S(1)}, bf16[128,768]{1,0:T(8,128)(2...) custom-call(s32[4]{0:T(128)S(1)} %pad_add_fusion.idx_ref, ...), custom_call_target="tpu_custom_call" | custom-call | flops 2990000128 | bytes 47970000 | tf_op jit(solution)/shard_map/normed_back/pallas_call | solution.py:984
  148.2 5.2 %all-to-all-start.3 = ((bf16[16,24,896]{2,1,0:T(8,128)(2,1)}), bf16[16,24,896]{2,1,0:T(8,128)(2,1)S(1)}, u32[]{:S(2)}, u32[]{:S(2)}) async-start(bf16[16,24,896]{2,1,0:T(8,128)(2,1)} %add.16), calls=%async_computation.3 | async-start | bytes 1376256 | tf_op jit(solution)/shard_map/all_to_all | solution.py:1176
  155.8 4.0 %collective-permute-start.27 = (bf16[128,768]{1,0:T(8,128)(2,1)S(1)}, bf16[128,768]{1,0:T(8,128)(2,1)S(1)}, u32[]{:S(2)}, u32[]{:S(2)}) collective-permute-start(bf16[128,768]{1,0:T(8,128)(2,1)S(1)} %finish_input.1), channel_id=1, source_target_pairs={{0,0},{1,1},{16,2},{17,3},{8,4},{9,5},{24,6},{25,7},{2,8},{3,9},{1... | collective-permute-start | bytes 589832 | tf_op jit(solution)/shard_map/ppermute | solution.py:93
  160.8 2.5 %collective-permute-start.30 = (bf16[24,768]{1,0:T(8,128)(2,1)S(1)}, bf16[24,768]{1,0:T(8,128)(2,1)S(1)}, u32[]{:S(2)}, u32[]{:S(2)}) collective-permute-start(bf16[24,768]{1,0:T(8,128)(2,1)S(1)} %get-tuple-element.213), channel_id=1, source_target_pairs={{0,17},{1,16},{16,1},{17,0},{2,19},{3,18},{18,3},{19,2},{4,21},{5,... | collective-permute-start | bytes 110600 | tf_op jit(solution)/shard_map/ppermute | solution.py:61
  167.4 9.5 %collective-permute-done.27.second_ref = bf16[128,768]{1,0:T(8,128)(2,1)S(1)} collective-permute-done((bf16[128,768]{1,0:T(8,128)(2,1)S(1)}, bf16[128,768]{1,0:T(8,128)(2,1)S(1)}, u32[]{:S(2)}, u32[]{:S(2)}) %collective-permute-start.27) | collective-permute-done | bytes 196640 | tf_op jit(solution)/shard_map/ppermute | solution.py:93
  176.8 2.1 %collective-permute-done.23.first_ref = bf16[128,768]{1,0:T(8,128)(2,1)S(1)} collective-permute-done((bf16[128,768]{1,0:T(8,128)(2,1)S(1)}, bf16[128,768]{1,0:T(8,128)(2,1)S(1)}, u32[]{:S(2)}, u32[]{:S(2)}) %collective-permute-start.23) | collective-permute-done | bytes 196640 | tf_op jit(solution)/shard_map/ppermute | solution.py:93
  (165 shorter events, 53.9 us)
Async XLA Ops:
  2.4 24.0 %collective-permute-start.3 = (bf16[136,768]{1,0:T(8,128)(2,1)S(1)}, bf16[136,768]{1,0:T(8,128)(2,1)S(1)}, u32[]{:S(2)}, u32[]{:S(2)}) collective-permute-start(bf16[136,768]{1,0:T(8,128)(2,1)S(1)} %pad_maximum_fusion.1), channel_id=1, source_target_pairs={{0,0},{1,1},{2,16},{3,17},{4,8},{5,9},{6,24},{7,25},{8,2},{9,3},{1... | collective-permute-start | bytes 626696 | tf_op jit(solution)/shard_map/ppermute | solution.py:93
  8.9 11.8 %all-to-all-start = ((bf16[4,24,2176]{2,1,0:T(8,128)(2,1)}), bf16[4,24,2176]{2,1,0:T(8,128)(2,1)S(1)}, u32[]{:S(2)}, u32[]{:S(2)}) async-start(bf16[4,24,2176]{2,1,0:T(8,128)(2,1)} %prepare.1), calls=%async_computation | async-start | bytes 835584 | tf_op jit(solution)/shard_map/all_to_all | solution.py:1074
  13.2 13.1 %collective-permute-start.4 = (bf16[128,768]{1,0:T(8,128)(2,1)S(1)}, bf16[128,768]{1,0:T(8,128)(2,1)S(1)}, u32[]{:S(2)}, u32[]{:S(2)}) collective-permute-start(bf16[128,768]{1,0:T(8,128)(2,1)S(1)} %fusion), channel_id=1, source_target_pairs={{0,0},{1,1},{2,16},{3,17},{4,8},{5,9},{6,24},{7,25},{8,2},{9,3},{1... | collective-permute-start | bytes 589832 | tf_op jit(solution)/shard_map/ppermute | solution.py:93
  22.6 12.0 %collective-permute-start.1 = (bf16[96,640]{1,0:T(8,128)(2,1)S(1)}, bf16[96,640]{1,0:T(8,128)(2,1)S(1)}, u32[]{:S(2)}, u32[]{:S(2)}) collective-permute-start(bf16[96,640]{1,0:T(8,128)(2,1)S(1)} %get-tuple-element.120), channel_id=1, source_target_pairs={{0,4},{2,6},{4,0},{6,2},{1,5},{3,7},{5,1},{7,3},{8,12},{10,14},{12... | collective-permute-start | bytes 368648 | tf_op jit(solution)/shard_map/ppermute | solution.py:71
  26.3 8.3 %collective-permute-start = (bf16[96,640]{1,0:T(8,128)(2,1)S(1)}, bf16[96,640]{1,0:T(8,128)(2,1)S(1)}, u32[]{:S(2)}, u32[]{:S(2)}) collective-permute-start(bf16[96,640]{1,0:T(8,128)(2,1)S(1)} %get-tuple-element.120), channel_id=1, source_target_pairs={{0,6},{2,0},{4,2},{6,4},{1,7},{3,1},{5,3},{7,5},{8,14},{10,8},{12,... | collective-permute-start | bytes 368648 | tf_op jit(solution)/shard_map/ppermute | solution.py:71
  34.6 48.2 %all-to-all-start.1 = ((bf16[4,296,768]{2,1,0:T(8,128)(2,1)}), bf16[4,296,768]{2,1,0:T(8,128)(2,1)S(1)}, u32[]{:S(2)}, u32[]{:S(2)}) async-start(bf16[4,296,768]{2,1,0:T(8,128)(2,1)} %get-tuple-element.125), calls=%async_computation.1 | async-start | bytes 3637248 | tf_op jit(solution)/shard_map/all_to_all | solution.py:1081
  40.2 13.0 %collective-permute-start.5 = (bf16[4,96,640]{2,1,0:T(8,128)(2,1)S(1)}, bf16[4,96,640]{2,1,0:T(8,128)(2,1)}, u32[]{:S(2)}, u32[]{:S(2)}) collective-permute-start(bf16[4,96,640]{2,1,0:T(8,128)(2,1)S(1)} %pad_maximum_fusion.refs_0_), channel_id=1, source_target_pairs={{0,8},{8,0},{1,9},{9,1},{2,10},{10,2},{3,11},{11,3},{4,12},{12,4},... | collective-permute-start | bytes 1474568 | tf_op jit(solution)/shard_map/ppermute | solution.py:52
  59.2 22.9 %collective-permute-start.9 = (bf16[128,768]{1,0:T(8,128)(2,1)S(1)}, bf16[128,768]{1,0:T(8,128)(2,1)S(1)}, u32[]{:S(2)}, u32[]{:S(2)}) collective-permute-start(bf16[128,768]{1,0:T(8,128)(2,1)S(1)} %collective-permute-done.4.refs_0_.dm_ref), channel_id=1, source_target_pairs={{0,17},{1,16},{16,1},{17,0},{2,19},{3,18},{18,3},{19,2},{4,21},{5,... | collective-permute-start | bytes 589832 | tf_op jit(solution)/shard_map/ppermute | solution.py:61
  60.7 21.4 %collective-permute-start.8 = (bf16[128,768]{1,0:T(8,128)(2,1)S(1)}, bf16[128,768]{1,0:T(8,128)(2,1)S(1)}, u32[]{:S(2)}, u32[]{:S(2)}) collective-permute-start(bf16[128,768]{1,0:T(8,128)(2,1)S(1)} %collective-permute-done.4.refs_0_.dm_ref), channel_id=1, source_target_pairs={{0,16},{1,17},{16,0},{17,1},{2,18},{3,19},{18,2},{19,3},{4,20},{5,... | collective-permute-start | bytes 589832 | tf_op jit(solution)/shard_map/ppermute | solution.py:61
  61.6 20.5 %collective-permute-start.7 = (bf16[128,768]{1,0:T(8,128)(2,1)S(1)}, bf16[128,768]{1,0:T(8,128)(2,1)S(1)}, u32[]{:S(2)}, u32[]{:S(2)}) collective-permute-start(bf16[128,768]{1,0:T(8,128)(2,1)S(1)} %collective-permute-done.4.refs_0_.dm_ref), channel_id=1, source_target_pairs={{0,1},{1,0},{16,17},{17,16},{2,3},{3,2},{18,19},{19,18},{4,5},{5,4... | collective-permute-start | bytes 589832 | tf_op jit(solution)/shard_map/ppermute | solution.py:61
  95.3 10.1 %collective-permute-start.13 = (bf16[128,768]{1,0:T(8,128)(2,1)S(1)}, bf16[128,768]{1,0:T(8,128)(2,1)S(1)}, u32[]{:S(2)}, u32[]{:S(2)}) collective-permute-start(bf16[128,768]{1,0:T(8,128)(2,1)S(1)} %get-tuple-element.146), channel_id=1, source_target_pairs={{0,17},{1,16},{16,1},{17,0},{2,19},{3,18},{18,3},{19,2},{4,21},{5,... | collective-permute-start | bytes 589832 | tf_op jit(solution)/shard_map/ppermute | solution.py:61
  107.2 12.1 %collective-permute-start.16 = (bf16[128,768]{1,0:T(8,128)(2,1)S(1)}, bf16[128,768]{1,0:T(8,128)(2,1)}, u32[]{:S(2)}, u32[]{:S(2)}) collective-permute-start(bf16[128,768]{1,0:T(8,128)(2,1)S(1)} %get-tuple-element.160.refs_2_.refs_0_), channel_id=1, source_target_pairs={{0,17},{1,16},{16,1},{17,0},{2,19},{3,18},{18,3},{19,2},{4,21},{5,... | collective-permute-start | bytes 589832 | tf_op jit(solution)/shard_map/ppermute | solution.py:61
  108.9 11.9 %collective-permute-start.15 = (bf16[128,768]{1,0:T(8,128)(2,1)S(1)}, bf16[128,768]{1,0:T(8,128)(2,1)}, u32[]{:S(2)}, u32[]{:S(2)}) collective-permute-start(bf16[128,768]{1,0:T(8,128)(2,1)S(1)} %get-tuple-element.160.refs_2_.refs_0_), channel_id=1, source_target_pairs={{0,16},{1,17},{16,0},{17,1},{2,18},{3,19},{18,2},{19,3},{4,20},{5,... | collective-permute-start | bytes 589832 | tf_op jit(solution)/shard_map/ppermute | solution.py:61
  110.1 10.7 %collective-permute-start.14 = (bf16[128,768]{1,0:T(8,128)(2,1)S(1)}, bf16[128,768]{1,0:T(8,128)(2,1)}, u32[]{:S(2)}, u32[]{:S(2)}) collective-permute-start(bf16[128,768]{1,0:T(8,128)(2,1)S(1)} %get-tuple-element.160.refs_2_.refs_0_), channel_id=1, source_target_pairs={{0,1},{1,0},{16,17},{17,16},{2,3},{3,2},{18,19},{19,18},{4,5},{5,4... | collective-permute-start | bytes 589832 | tf_op jit(solution)/shard_map/ppermute | solution.py:61
  112.0 34.7 %all-to-all-start.2 = ((bf16[4,200,768]{2,1,0:T(8,128)(2,1)}), bf16[4,200,768]{2,1,0:T(8,128)(2,1)S(1)}, u32[]{:S(2)}, u32[]{:S(2)}) async-start(bf16[4,200,768]{2,1,0:T(8,128)(2,1)} %add.15.refs_4_), calls=%async_computation.2 | async-start | bytes 2457600 | tf_op jit(solution)/shard_map/all_to_all | solution.py:1149
  117.3 14.8 %collective-permute-start.18 = (bf16[128,768]{1,0:T(8,128)(2,1)}, bf16[128,768]{1,0:T(8,128)(2,1)S(1)}, u32[]{:S(2)}, u32[]{:S(2)}) collective-permute-start(bf16[128,768]{1,0:T(8,128)(2,1)} %copy-done.14), channel_id=1, source_target_pairs={{0,1},{1,0},{16,17},{17,16},{2,3},{3,2},{18,19},{19,18},{4,5},{5,4... | collective-permute-start | bytes 589832 | tf_op jit(solution)/shard_map/ppermute | solution.py:61
  118.4 13.8 %collective-permute-start.19 = (bf16[128,768]{1,0:T(8,128)(2,1)S(1)}, bf16[128,768]{1,0:T(8,128)(2,1)S(1)}, u32[]{:S(2)}, u32[]{:S(2)}) collective-permute-start(bf16[128,768]{1,0:T(8,128)(2,1)S(1)} %get-tuple-element.168), channel_id=1, source_target_pairs={{0,16},{1,17},{16,0},{17,1},{2,18},{3,19},{18,2},{19,3},{4,20},{5,... | collective-permute-start | bytes 589832 | tf_op jit(solution)/shard_map/ppermute | solution.py:61
  119.3 13.6 %collective-permute-start.20 = (bf16[128,768]{1,0:T(8,128)(2,1)S(1)}, bf16[128,768]{1,0:T(8,128)(2,1)S(1)}, u32[]{:S(2)}, u32[]{:S(2)}) collective-permute-start(bf16[128,768]{1,0:T(8,128)(2,1)S(1)} %get-tuple-element.169), channel_id=1, source_target_pairs={{0,17},{1,16},{16,1},{17,0},{2,19},{3,18},{18,3},{19,2},{4,21},{5,... | collective-permute-start | bytes 589832 | tf_op jit(solution)/shard_map/ppermute | solution.py:61
  140.2 13.1 %collective-permute-start.24 = (bf16[128,768]{1,0:T(8,128)(2,1)S(1)}, bf16[128,768]{1,0:T(8,128)(2,1)S(1)}, u32[]{:S(2)}, u32[]{:S(2)}) collective-permute-start(bf16[128,768]{1,0:T(8,128)(2,1)S(1)} %get-tuple-element.194), channel_id=1, source_target_pairs={{0,1},{1,0},{16,17},{17,16},{2,3},{3,2},{18,19},{19,18},{4,5},{5,4... | collective-permute-start | bytes 589832 | tf_op jit(solution)/shard_map/ppermute | solution.py:61
  141.3 12.0 %collective-permute-start.25 = (bf16[128,768]{1,0:T(8,128)(2,1)S(1)}, bf16[128,768]{1,0:T(8,128)(2,1)S(1)}, u32[]{:S(2)}, u32[]{:S(2)}) collective-permute-start(bf16[128,768]{1,0:T(8,128)(2,1)S(1)} %get-tuple-element.195), channel_id=1, source_target_pairs={{0,16},{1,17},{16,0},{17,1},{2,18},{3,19},{18,2},{19,3},{4,20},{5,... | collective-permute-start | bytes 589832 | tf_op jit(solution)/shard_map/ppermute | solution.py:61
  142.3 11.1 %collective-permute-start.26 = (bf16[128,768]{1,0:T(8,128)(2,1)S(1)}, bf16[128,768]{1,0:T(8,128)(2,1)S(1)}, u32[]{:S(2)}, u32[]{:S(2)}) collective-permute-start(bf16[128,768]{1,0:T(8,128)(2,1)S(1)} %get-tuple-element.196), channel_id=1, source_target_pairs={{0,17},{1,16},{16,1},{17,0},{2,19},{3,18},{18,3},{19,2},{4,21},{5,... | collective-permute-start | bytes 589832 | tf_op jit(solution)/shard_map/ppermute | solution.py:61
  148.2 30.8 %all-to-all-start.3 = ((bf16[16,24,896]{2,1,0:T(8,128)(2,1)}), bf16[16,24,896]{2,1,0:T(8,128)(2,1)S(1)}, u32[]{:S(2)}, u32[]{:S(2)}) async-start(bf16[16,24,896]{2,1,0:T(8,128)(2,1)} %add.16), calls=%async_computation.3 | async-start | bytes 1376256 | tf_op jit(solution)/shard_map/all_to_all | solution.py:1176
  155.8 21.1 %collective-permute-start.27 = (bf16[128,768]{1,0:T(8,128)(2,1)S(1)}, bf16[128,768]{1,0:T(8,128)(2,1)S(1)}, u32[]{:S(2)}, u32[]{:S(2)}) collective-permute-start(bf16[128,768]{1,0:T(8,128)(2,1)S(1)} %finish_input.1), channel_id=1, source_target_pairs={{0,0},{1,1},{16,2},{17,3},{8,4},{9,5},{24,6},{25,7},{2,8},{3,9},{1... | collective-permute-start | bytes 589832 | tf_op jit(solution)/shard_map/ppermute | solution.py:93
  163.5 15.5 %collective-permute-start.23 = (bf16[128,768]{1,0:T(8,128)(2,1)S(1)}, bf16[128,768]{1,0:T(8,128)(2,1)S(1)}, u32[]{:S(2)}, u32[]{:S(2)}) collective-permute-start(bf16[128,768]{1,0:T(8,128)(2,1)S(1)} %finish_output.1), channel_id=1, source_target_pairs={{0,0},{1,1},{16,2},{17,3},{8,4},{9,5},{24,6},{25,7},{2,8},{3,9},{1... | collective-permute-start | bytes 589832 | tf_op jit(solution)/shard_map/ppermute | solution.py:93
  (55 other events, 340.8 us)
